TPU v7x, 128 devices: a whole 4x4x4 slice. The times are simulated.
128 devices in a mesh: fac: 32 (over y, x, core), freq: 4 (over z).
Axes of the slice: x: 4, y: 4, z: 4, core: 2. Of those that a mesh axis runs over, the one named last changes fastest.
Arguments:
- right_side: float32 [16, 36864, 128], P('freq', 'fac'), may hold values from -6 to 6
- factors: bfloat16 [36864, 1024], P('fac'), may hold values from -0.03125 to 0.03125
- pair_weight: float32 [16, 36864], P('freq', 'fac'), may hold values from -2 to 2
- second_order: float32 [16, 36864], P('freq', 'fac'), may hold values from -1 to 1
- forward: float32 [16, 16], replicated, may hold values from -3 to 3
- backward: float32 [16, 16], replicated, may hold values from -3 to 3
Outputs:
- amplitude: float32 [16, 36864, 128], P('freq', 'fac')
- sources: float32 [16, 36864, 128], P('freq', 'fac')
All inputs are finite; a program needn't handle non-finite values.
Results may differ from a plain program's by a relative error of at most 0.0015.
Values may be sent and summed in bfloat16 or wider, within the bound.
No kernel may reach another device: no remote copies, remote signals or barrier semaphores. Data moves between devices by JAX's collectives and lax.ppermute only.
A program may use at most 64 MiB of HBM per device.

v0:
```python
import jax
import jax.numpy as jnp
from jax import lax
from jax.experimental import pallas as pl
from jax.experimental.pallas import tpu as pltpu
from jax.sharding import PartitionSpec as P

OUTER = 2
INNER = 2
F32 = jnp.float32
BF16 = jnp.bfloat16
F16 = jnp.float16
SIDE = 4
RUN = 16
INTERPRET = False


def place(y, x, k):
    return ((y % SIDE) * SIDE + x % SIDE) * 2 + k


def along(d, first):
    pairs = []
    for y in range(SIDE):
        for x in range(SIDE):
            for k in range(2):
                on_x = (k == 0) == first
                there = place(y, x + d, k) if on_x else place(y + d, x, k)
                pairs.append((place(y, x, k), there))
    return pairs


CORES = [(i, i ^ 1) for i in range(2 * SIDE * SIDE)]


def ring(d):
    return [(z, (z + d) % SIDE) for z in range(SIDE)]


def scale_of(peak):
    power = jnp.ceil(jnp.log2(jnp.maximum(peak, 1e-30))) - 14.0
    return power, jnp.exp2(-power)


def pack_body(z_ref, amp_ref, own_ref, *sent):
    nf, rows, cols = amp_ref.shape
    quarter = rows // SIDE
    groups = quarter // RUN
    z = z_ref[0]
    peak = jnp.max(jnp.abs(amp_ref[0]), axis=0, keepdims=True)
    for f in range(1, nf):
        peak = jnp.maximum(peak, jnp.max(jnp.abs(amp_ref[f]), axis=0, keepdims=True))
    peak = jnp.broadcast_to(jnp.max(peak, axis=1, keepdims=True), (1, cols))
    power, scale = scale_of(peak)
    scale = jnp.broadcast_to(scale, (RUN, cols))
    for d in range(SIDE):
        base = ((z + d) % SIDE) * quarter

        def step(g, carry, d=d, base=base):
            for f in range(nf):
                tile = amp_ref[f, pl.ds(pl.multiple_of(base + g * RUN, RUN), RUN), :]
                spot = pl.ds(pl.multiple_of((g * nf + f) * RUN, RUN), RUN)
                if d == 0:
                    own_ref[spot, :] = tile
                else:
                    sent[d - 1][spot, :] = tile * scale
            return carry

        lax.fori_loop(0, groups, step, 0)
        if d:
            sent[d - 1][nf * quarter :, :] = jnp.broadcast_to(power, (RUN, cols))


def mix_body(own_ref, got1, got2, got3, kernel_ref, into_ref, out_ref, kept, *sent):
    body, cols = own_ref.shape
    block = body * SIDE // kernel_ref.shape[0]
    size = into_ref.shape[1]
    part = size // SIDE
    got = (got1, got2, got3)
    gains = [jnp.exp2(jnp.broadcast_to(g[body : body + 1, :], (part, cols))) for g in got]

    def apply(table, value):
        high = value.astype(BF16)
        low = (value - high.astype(F32)).astype(BF16)
        both = jnp.dot(table[...], high, preferred_element_type=F32)
        rest = jnp.dot(table[:size, :], low, preferred_element_type=F32)
        return both[:size] + (both[size:] + rest)

    def step(g, peaks):
        sides = []
        kernels = []
        for half in range(2):
            at = pl.ds(pl.multiple_of((2 * g + half) * part, part), part)
            sides.append(
                jnp.concatenate(
                    [own_ref[at, :]] + [r[at, :] * s for r, s in zip(got, gains)], axis=0
                )
            )
            kernels.append(
                kernel_ref[pl.ds(pl.multiple_of((2 * g + half) * size, size), size), :]
            )
        timed = apply(into_ref, jnp.concatenate(sides, axis=1))
        renewed = apply(out_ref, jnp.concatenate(kernels, axis=1) * timed)
        fresh = list(peaks)
        for half in range(2):
            at = pl.ds(pl.multiple_of((2 * g + half) * part, part), part)
            for d in range(SIDE):
                tile = renewed[d * part : (d + 1) * part, half * cols : (half + 1) * cols]
                if d == 0:
                    kept[at, :] = tile
                else:
                    sent[d - 1][at, :] = tile
                    fresh[d - 1] = jnp.maximum(fresh[d - 1], jnp.abs(tile))
        return tuple(fresh)

    start = tuple(jnp.zeros((part, cols), F32) for _ in range(3))
    peaks = lax.fori_loop(0, body // part // 2, step, start)
    for ref, peak in zip(sent, peaks):
        peak = jnp.max(jnp.max(peak, axis=0, keepdims=True), axis=1, keepdims=True)
        power, scale = scale_of(jnp.broadcast_to(peak, (1, cols)))
        ref[:body, :] = ref[:body, :] * jnp.broadcast_to(scale, (body, cols))
        ref[body:, :] = jnp.broadcast_to(power, (RUN, cols))


def unpack_body(z_ref, right_ref, own_ref, got1, got2, got3, sources_ref, rounded_ref):
    nf, rows, cols = right_ref.shape
    quarter = rows // SIDE
    groups = quarter // RUN
    body = nf * quarter
    z = z_ref[0]
    for d, ref in enumerate((own_ref, got1, got2, got3)):
        base = ((z - d + SIDE) % SIDE) * quarter
        if d:
            gain = jnp.exp2(jnp.broadcast_to(ref[body : body + 1, :], (RUN, cols)))

        def step(g, carry, d=d, base=base, ref=ref, gain=gain if d else None):
            for f in range(nf):
                tile = ref[pl.ds(pl.multiple_of((g * nf + f) * RUN, RUN), RUN), :]
                if d:
                    tile = tile * gain
                at = pl.ds(pl.multiple_of(base + g * RUN, RUN), RUN)
                tile = right_ref[f, at, :] + tile
                sources_ref[f, at, :] = tile
                rounded_ref[f, at, :] = tile.astype(BF16)
            return carry

        lax.fori_loop(0, groups, step, 0)


def call(body, outs, name, scalars=0, args=()):
    spec = pl.BlockSpec(memory_space=pltpu.VMEM)
    flat = pl.BlockSpec(memory_space=pltpu.SMEM)
    return pl.pallas_call(
        body,
        out_shape=[jax.ShapeDtypeStruct(s, t) for s, t in outs],
        in_specs=[flat] * scalars + [spec] * (len(args) - scalars),
        out_specs=[spec] * len(outs),
        compiler_params=pltpu.CompilerParams(vmem_limit_bytes=40 << 20),
        interpret=INTERPRET,
        name=name,
    )(*args)


def shards(right_side, factors, pair_weight, second_order, forward, backward):
    nf, rows, cols = right_side.shape
    naux = factors.shape[1]
    half = naux // 2
    chunk = half // SIDE
    quarter = rows // SIDE
    wide = nf * cols
    me = lax.axis_index("fac")
    z = lax.axis_index("freq")
    core = me % 2
    chip = me // 2
    spot = jnp.where(core == 0, chip % SIDE, chip // SIDE)
    factors_keep = lax.dynamic_slice(factors, (0, core * half), (rows, half))
    factors_send = lax.dynamic_slice(factors, (0, (1 - core) * half), (rows, half))

    def project(table, rounded):
        return jnp.einsum(
            "pa,fpc->afc", table, rounded, preferred_element_type=F32
        ).reshape(half, wide)

    def reduce_all(rounded):
        sent = project(factors_send, rounded)
        got = lax.ppermute(sent, "fac", CORES)
        mine = project(factors_keep, rounded) + got
        own = lax.dynamic_slice(mine, (spot * chunk, 0), (chunk, wide))
        for d in (1, 2, 3):
            piece = lax.dynamic_slice(
                mine, (((spot + d) % SIDE) * chunk, 0), (chunk, wide)
            ).astype(BF16)
            own = own + lax.ppermute(piece, "fac", along(d, True)).astype(F32)
        own = own.astype(BF16)
        total = own.astype(F32)
        for d in (1, 2, 3):
            total = total + lax.ppermute(own, "fac", along(d, False)).astype(F32)
        total = total.astype(BF16)
        gathered = jnp.zeros((half, wide), BF16)
        gathered = lax.dynamic_update_slice(gathered, total, (spot * chunk, 0))
        for d in (1, 2, 3):
            piece = lax.ppermute(total, "fac", along(d, True))
            gathered = lax.dynamic_update_slice(
                gathered, piece, (((spot - d) % SIDE) * chunk, 0)
            )
        other = lax.ppermute(gathered, "fac", CORES)
        return gathered, other

    def spread_of(parts):
        gathered, other = parts
        return (
            jnp.einsum("pa,afc->fpc", factors_keep, gathered.reshape(half, nf, cols),
                       preferred_element_type=F32)
            + jnp.einsum("pa,afc->fpc", factors_send, other.reshape(half, nf, cols),
                         preferred_element_type=F32)
        )

    def exchange(sent):
        return [
            lax.ppermute(load.astype(F16), "freq", ring(d + 1)).astype(F32)
            for d, load in enumerate(sent)
        ]

    body = nf * quarter
    size = SIDE * nf * RUN
    weight = pair_weight[:, :, None]
    place_z = jnp.full((1,), z, jnp.int32)
    kernel = [lax.dynamic_slice(second_order, (0, z * quarter), (nf, quarter))]
    for d in (1, 2, 3):
        piece = lax.dynamic_slice(
            second_order, (0, ((z + d) % SIDE) * quarter), (nf, quarter)
        )
        kernel.append(lax.ppermute(piece, "freq", ring(d)))
    kernel = jnp.concatenate(kernel, axis=0).reshape(SIDE * nf, quarter // RUN, RUN)
    kernel = kernel.transpose(1, 0, 2).reshape(body * SIDE, 1)
    kernel = jnp.broadcast_to(kernel, (body * SIDE, cols))

    row = jnp.arange(size)
    ring_at, f_at = row // (nf * RUN), row // RUN % nf
    names = jnp.arange(SIDE * nf)
    source = (((z - ring_at) % SIDE) * nf + f_at)[:, None] == names[None, :]
    target = (((z + ring_at) % SIDE) * nf + f_at)[:, None] == names[None, :]
    same = (row % RUN)[:, None] == (row % RUN)[None, :]

    def spread_table(left, table, right):
        left, right = left.astype(F32), right.astype(F32)
        full = jnp.einsum("it,tw,jw->ij", left, table, right, precision=lax.Precision.HIGHEST)
        full = jnp.where(same, full, 0.0)
        high = lax.reduce_precision(full, 8, 7)
        return jnp.concatenate([high, full - high], axis=0).astype(BF16)

    table_in = spread_table(source, forward, source)
    table_out = spread_table(target, backward, source)
    loads = [((body, cols), F32)] + [((body + RUN, cols), F32)] * 3

    sources = right_side
    rounded = right_side.astype(BF16)
    for outer in range(OUTER):
        for inner in range(INNER):
            amplitude = sources + weight * spread_of(reduce_all(rounded))
            rounded = amplitude.astype(BF16)
        own, *sent = call(pack_body, loads, "pack", 1, (place_z, amplitude))
        got = exchange(sent)
        own, *sent = call(mix_body, loads, "mix", 0, (own, *got, kernel, table_in, table_out))
        got = exchange(sent)
        sources, rounded = call(
            unpack_body,
            [(right_side.shape, F32), (right_side.shape, BF16)],
            "unpack", 1, (place_z, right_side, own, *got),
        )
    return (amplitude, sources)


def solution(mesh):
    return jax.shard_map(
        shards,
        mesh=mesh,
        in_specs=(
            P("freq", "fac", None),
            P("fac", None),
            P("freq", "fac"),
            P("freq", "fac"),
            P(),
            P(),
        ),
        out_specs=(P("freq", "fac", None), P("freq", "fac", None)),
        check_vma=False,
    )
```

profile of v0, /device:TPU:1, one launch (start us, length us, event | category | flops | bytes accessed | tf_op | source)
XLA Modules:
  0.0 281.2 jit_solution(4188763524562768942)
XLA Ops:
  4.1 3.2 %convolution_bitcast_fusion.6 = f32[512,512]{0,1:T(8,128)} fusion(bf16[1152,512]{0,1:T(8,128)(2,1)} %bitcast.132, bf16[1152,1024]{1,0:T(8,128)(2,1)S(1)} %copy-done, s32[]{:T(128)S(6)} %select_n.239), kind=kOutput, calls=%fused_computation.24 | convolution fusion | flops 603979776 | bytes 3407876
  8.7 2.6 collective-permute-done
  20.1 3.0 %collective-permute-done.2 = bf16[128,512]{0,1:T(8,128)(2,1)S(1)} collective-permute-done((bf16[128,512]{0,1:T(8,128)(2,1)S(1)}, bf16[128,512]{0,1:T(8,128)(2,1)S(1)}, u32[]{:S(2)}, u32[]{:S(2)}) %collective-permute-start.2) | collective-permute-done | bytes 131104 | tf_op jit(solution)/shard_map/ppermute | solution.py:193
  24.1 2.5 collective-permute-start.6
  27.5 2.5 collective-permute-done.6
  34.1 2.3 collective-permute-start.8
  37.4 2.9 %collective-permute-done.7 = bf16[128,512]{0,1:T(8,128)(2,1)S(1)} collective-permute-done((bf16[128,512]{0,1:T(8,128)(2,1)S(1)}, bf16[128,512]{0,1:T(8,128)(2,1)S(1)}, u32[]{:S(2)}, u32[]{:S(2)}) %collective-permute-start.7) | collective-permute-done | bytes 131104 | tf_op jit(solution)/shard_map/ppermute | solution.py:202
  40.9 4.6 %collective-permute-start.10 = (bf16[512,512]{0,1:T(8,128)(2,1)S(1)}, bf16[512,512]{0,1:T(8,128)(2,1)S(1)}, u32[]{:S(2)}, u32[]{:S(2)}) collective-permute-start(bf16[512,512]{0,1:T(8,128)(2,1)S(1)} %constant_dynamic-update-slice_fusion.12), channel_id=1, source_target_pairs={{0,4},{4,0},{8,12},{12,8},{16,20},{20,16},{24,28},{28,24},{32,36},... | collective-permute-start | bytes 1572872 | tf_op jit(solution)/shard_map/ppermute | solution.py:206
  51.5 3.2 %convolution_bitcast_fusion.4 = f32[512,512]{0,1:T(8,128)} fusion(bf16[1152,512]{0,1:T(8,128)(2,1)} %bitcast.134, bf16[1152,1024]{1,0:T(8,128)(2,1)S(1)} %copy-done, s32[]{:T(128)S(6)} %select_n.239), kind=kOutput, calls=%fused_computation.22 | convolution fusion | flops 603979776 | bytes 3407876
  55.1 2.6 collective-permute-done.11
  60.0 2.7 collective-permute-start.14
  68.4 2.5 collective-permute-start.17
  74.2 2.3 collective-permute-done.16
  79.7 2.5 collective-permute-start.20
  82.2 2.9 %collective-permute-done.18 = bf16[128,512]{0,1:T(8,128)(2,1)S(1)} collective-permute-done((bf16[128,512]{0,1:T(8,128)(2,1)S(1)}, bf16[128,512]{0,1:T(8,128)(2,1)S(1)}, u32[]{:S(2)}, u32[]{:S(2)}) %collective-permute-start.18) | collective-permute-done | bytes 131104 | tf_op jit(solution)/shard_map/ppermute | solution.py:202
  93.3 3.8 %collective-permute-start.24 = (f16[1168,128]{1,0:T(8,128)(2,1)}, f16[1168,128]{1,0:T(8,128)(2,1)}, u32[]{:S(2)}, u32[]{:S(2)}) collective-permute-start(f16[1168,128]{1,0:T(8,128)(2,1)} %convert_element_type.261), channel_id=1, source_target_pairs={{0,3},{1,0},{2,1},{3,2},{4,7},{5,4},{6,5},{7,6},{8,11},{9,8},{10,9... | collective-permute-start | bytes 897032 | tf_op jit(solution)/shard_map/ppermute | solution.py:220
  97.8 2.4 collective-permute-start.26
  100.2 12.9 %collective-permute-done.26 = f32[4,288]{1,0:T(4,128)S(1)} collective-permute-done((f32[4,288]{1,0:T(4,128)S(1)}, f32[4,288]{1,0:T(4,128)S(1)}, u32[]{:S(2)}, u32[]{:S(2)}) %collective-permute-start.26) | collective-permute-done | bytes 4640 | tf_op jit(solution)/shard_map/ppermute | solution.py:233
  120.2 6.3 %mix.2 = (f32[1152,128]{1,0:T(8,128)S(1)}, f32[1168,128]{1,0:T(8,128)S(1)}, f32[1168,128]{1,0:T(8,128)S(1)}, f32[1168,128]{1,0:T(8,128)S(1)}) custom-call(f32[1152,128]{1,0:T(8,128)S(1)} %get-tuple-element.21.own_ref, f32[1168,128]{1,0:T(8,128)S(1)} %convert_element_type.258.got1, f32[1168,128]{1,0:T(8,128)S(1)} %convert_element_type.260.got2, ...), custom_call_target="tpu_custom_call" | custom-call | tf_op jit(solution)/shard_map/mix/pallas_call | solution.py:153
  128.3 5.2 %collective-permute-done.30 = f16[1168,128]{1,0:T(8,128)(2,1)S(1)} collective-permute-done((f16[1168,128]{1,0:T(8,128)(2,1)S(1)}, f16[1168,128]{1,0:T(8,128)(2,1)S(1)}, u32[]{:S(2)}, u32[]{:S(2)}) %collective-permute-start.30) | collective-permute-done | bytes 299040 | tf_op jit(solution)/shard_map/ppermute | solution.py:220
  135.2 8.5 %collective-permute-done.28 = f16[1168,128]{1,0:T(8,128)(2,1)S(1)} collective-permute-done((f16[1168,128]{1,0:T(8,128)(2,1)S(1)}, f16[1168,128]{1,0:T(8,128)(2,1)S(1)}, u32[]{:S(2)}, u32[]{:S(2)}) %collective-permute-start.28) | collective-permute-done | bytes 299040 | tf_op jit(solution)/shard_map/ppermute | solution.py:220
  146.8 2.4 copy.33
  152.0 2.3 collective-permute-done.31
  155.4 2.7 collective-permute-start.34
  158.0 2.6 collective-permute-done.32
  161.3 2.3 collective-permute-done.33
  163.7 2.4 collective-permute-start.37
  166.8 2.6 collective-permute-done.37
  169.5 2.3 collective-permute-done.36
  173.0 9.2 %collective-permute-start.38 = (bf16[128,512]{0,1:T(8,128)(2,1)S(1)}, bf16[128,512]{0,1:T(8,128)(2,1)S(1)}, u32[]{:S(2)}, u32[]{:S(2)}) collective-permute-start(bf16[128,512]{0,1:T(8,128)(2,1)S(1)} %get-tuple-element.43), channel_id=1, source_target_pairs={{0,8},{4,36},{8,16},{12,44},{16,24},{20,52},{24,0},{28,60},{32,40}... | collective-permute-start | bytes 393224 | tf_op jit(solution)/shard_map/ppermute | solution.py:202
  184.9 4.0 %collective-permute-done.38 = bf16[128,512]{0,1:T(8,128)(2,1)S(1)} collective-permute-done((bf16[128,512]{0,1:T(8,128)(2,1)S(1)}, bf16[128,512]{0,1:T(8,128)(2,1)S(1)}, u32[]{:S(2)}, u32[]{:S(2)}) %collective-permute-start.38) | collective-permute-done | bytes 131104 | tf_op jit(solution)/shard_map/ppermute | solution.py:202
  189.6 3.2 %collective-permute-start.41 = (bf16[512,512]{0,1:T(8,128)(2,1)S(1)}, bf16[512,512]{0,1:T(8,128)(2,1)S(1)}, u32[]{:S(2)}, u32[]{:S(2)}) collective-permute-start(bf16[512,512]{0,1:T(8,128)(2,1)S(1)} %constant_dynamic-update-slice_fusion.4), channel_id=1, source_target_pairs={{0,4},{4,0},{8,12},{12,8},{16,20},{20,16},{24,28},{28,24},{32,36},... | collective-permute-start | bytes 1572872 | tf_op jit(solution)/shard_map/ppermute | solution.py:206
  197.2 2.4 copy.37
  202.3 2.3 collective-permute-done.42
  205.6 2.7 collective-permute-start.45
  208.3 2.6 collective-permute-done.43
  211.6 2.3 collective-permute-done.44
  214.0 2.4 collective-permute-start.48
  217.1 2.6 collective-permute-done.48
  219.7 2.3 collective-permute-done.47
  226.0 4.0 %collective-permute-done.49 = bf16[128,512]{0,1:T(8,128)(2,1)S(1)} collective-permute-done((bf16[128,512]{0,1:T(8,128)(2,1)S(1)}, bf16[128,512]{0,1:T(8,128)(2,1)S(1)}, u32[]{:S(2)}, u32[]{:S(2)}) %collective-permute-start.49) | collective-permute-done | bytes 131104 | tf_op jit(solution)/shard_map/ppermute | solution.py:202
  230.7 2.4 collective-permute-start.52
  238.9 6.7 %collective-permute-done.55 = f16[1168,128]{1,0:T(8,128)(2,1)S(1)} collective-permute-done((f16[1168,128]{1,0:T(8,128)(2,1)S(1)}, f16[1168,128]{1,0:T(8,128)(2,1)S(1)}, u32[]{:S(2)}, u32[]{:S(2)}) %collective-permute-start.55) | collective-permute-done | bytes 299040 | tf_op jit(solution)/shard_map/ppermute | solution.py:220
  247.7 7.3 %collective-permute-done.53 = f16[1168,128]{1,0:T(8,128)(2,1)S(1)} collective-permute-done((f16[1168,128]{1,0:T(8,128)(2,1)S(1)}, f16[1168,128]{1,0:T(8,128)(2,1)S(1)}, u32[]{:S(2)}, u32[]{:S(2)}) %collective-permute-start.53) | collective-permute-done | bytes 299040 | tf_op jit(solution)/shard_map/ppermute | solution.py:220
  255.0 6.3 %mix.3 = (f32[1152,128]{1,0:T(8,128)S(1)}, f32[1168,128]{1,0:T(8,128)S(1)}, f32[1168,128]{1,0:T(8,128)S(1)}, f32[1168,128]{1,0:T(8,128)S(1)}) custom-call(f32[1152,128]{1,0:T(8,128)S(1)} %get-tuple-element.31.own_ref, f32[1168,128]{1,0:T(8,128)S(1)} %convert_element_type.295.got1, f32[1168,128]{1,0:T(8,128)S(1)} %convert_element_type.297.got2, ...), custom_call_target="tpu_custom_call" | custom-call | tf_op jit(solution)/shard_map/mix/pallas_call | solution.py:153
  263.1 6.6 %collective-permute-done.58 = f16[1168,128]{1,0:T(8,128)(2,1)S(1)} collective-permute-done((f16[1168,128]{1,0:T(8,128)(2,1)S(1)}, f16[1168,128]{1,0:T(8,128)(2,1)S(1)}, u32[]{:S(2)}, u32[]{:S(2)}) %collective-permute-start.58) | collective-permute-done | bytes 299040 | tf_op jit(solution)/shard_map/ppermute | solution.py:220
  270.8 7.8 %collective-permute-done.56 = f16[1168,128]{1,0:T(8,128)(2,1)S(1)} collective-permute-done((f16[1168,128]{1,0:T(8,128)(2,1)S(1)}, f16[1168,128]{1,0:T(8,128)(2,1)S(1)}, u32[]{:S(2)}, u32[]{:S(2)}) %collective-permute-start.56) | collective-permute-done | bytes 299040 | tf_op jit(solution)/shard_map/ppermute | solution.py:220
  278.6 2.4 unpack.3
  (209 shorter events, 98.9 us)
Async XLA Ops:
  14.5 5.5 %collective-permute-start.1 = (bf16[128,512]{0,1:T(8,128)(2,1)S(1)}, bf16[128,512]{0,1:T(8,128)(2,1)S(1)}, u32[]{:S(2)}, u32[]{:S(2)}) collective-permute-start(bf16[128,512]{0,1:T(8,128)(2,1)S(1)} %get-tuple-element.57), channel_id=1, source_target_pairs={{0,8},{4,36},{8,16},{12,44},{16,24},{20,52},{24,0},{28,60},{32,40}... | collective-permute-start | bytes 393224 | tf_op jit(solution)/shard_map/ppermute | solution.py:193
  17.5 5.6 %collective-permute-start.2 = (bf16[128,512]{0,1:T(8,128)(2,1)S(1)}, bf16[128,512]{0,1:T(8,128)(2,1)S(1)}, u32[]{:S(2)}, u32[]{:S(2)}) collective-permute-start(bf16[128,512]{0,1:T(8,128)(2,1)S(1)} %get-tuple-element.59), channel_id=1, source_target_pairs={{0,16},{4,68},{8,24},{12,76},{16,0},{20,84},{24,8},{28,92},{32,48}... | collective-permute-start | bytes 393224 | tf_op jit(solution)/shard_map/ppermute | solution.py:193
  24.1 5.9 %collective-permute-start.6 = (bf16[128,512]{0,1:T(8,128)(2,1)S(1)}, bf16[128,512]{0,1:T(8,128)(2,1)S(1)}, u32[]{:S(2)}, u32[]{:S(2)}) collective-permute-start(bf16[128,512]{0,1:T(8,128)(2,1)S(1)} %add_convert_fusion.7), channel_id=1, source_target_pairs={{0,96},{4,28},{8,104},{12,4},{16,112},{20,12},{24,120},{28,20},{32... | collective-permute-start | bytes 393224 | tf_op jit(solution)/shard_map/ppermute | solution.py:197
  26.6 5.4 %collective-permute-start.5 = (bf16[128,512]{0,1:T(8,128)(2,1)S(1)}, bf16[128,512]{0,1:T(8,128)(2,1)S(1)}, u32[]{:S(2)}, u32[]{:S(2)}) collective-permute-start(bf16[128,512]{0,1:T(8,128)(2,1)S(1)} %add_convert_fusion.7), channel_id=1, source_target_pairs={{0,64},{4,20},{8,72},{12,28},{16,80},{20,4},{24,88},{28,12},{32,96... | collective-permute-start | bytes 393224 | tf_op jit(solution)/shard_map/ppermute | solution.py:197
  26.9 6.7 %collective-permute-start.4 = (bf16[128,512]{0,1:T(8,128)(2,1)S(1)}, bf16[128,512]{0,1:T(8,128)(2,1)S(1)}, u32[]{:S(2)}, u32[]{:S(2)}) collective-permute-start(bf16[128,512]{0,1:T(8,128)(2,1)S(1)} %add_convert_fusion.7), channel_id=1, source_target_pairs={{0,32},{4,12},{8,40},{12,20},{16,48},{20,28},{24,56},{28,4},{32,64... | collective-permute-start | bytes 393224 | tf_op jit(solution)/shard_map/ppermute | solution.py:197
  33.7 6.5 %collective-permute-start.7 = (bf16[128,512]{0,1:T(8,128)(2,1)S(1)}, bf16[128,512]{0,1:T(8,128)(2,1)S(1)}, u32[]{:S(2)}, u32[]{:S(2)}) collective-permute-start(bf16[128,512]{0,1:T(8,128)(2,1)S(1)} %get-tuple-element.47), channel_id=1, source_target_pairs={{0,8},{4,36},{8,16},{12,44},{16,24},{20,52},{24,0},{28,60},{32,40}... | collective-permute-start | bytes 393224 | tf_op jit(solution)/shard_map/ppermute | solution.py:202
  34.1 6.2 %collective-permute-start.8 = (bf16[128,512]{0,1:T(8,128)(2,1)S(1)}, bf16[128,512]{0,1:T(8,128)(2,1)S(1)}, u32[]{:S(2)}, u32[]{:S(2)}) collective-permute-start(bf16[128,512]{0,1:T(8,128)(2,1)S(1)} %get-tuple-element.47), channel_id=1, source_target_pairs={{0,16},{4,68},{8,24},{12,76},{16,0},{20,84},{24,8},{28,92},{32,48}... | collective-permute-start | bytes 393224 | tf_op jit(solution)/shard_map/ppermute | solution.py:202
  40.9 6.1 %collective-permute-start.10 = (bf16[512,512]{0,1:T(8,128)(2,1)S(1)}, bf16[512,512]{0,1:T(8,128)(2,1)S(1)}, u32[]{:S(2)}, u32[]{:S(2)}) collective-permute-start(bf16[512,512]{0,1:T(8,128)(2,1)S(1)} %constant_dynamic-update-slice_fusion.12), channel_id=1, source_target_pairs={{0,4},{4,0},{8,12},{12,8},{16,20},{20,16},{24,28},{28,24},{32,36},... | collective-permute-start | bytes 1572872 | tf_op jit(solution)/shard_map/ppermute | solution.py:206
  60.0 6.7 %collective-permute-start.12 = (bf16[128,512]{0,1:T(8,128)(2,1)S(1)}, bf16[128,512]{0,1:T(8,128)(2,1)S(1)}, u32[]{:S(2)}, u32[]{:S(2)}) collective-permute-start(bf16[128,512]{0,1:T(8,128)(2,1)S(1)} %get-tuple-element.54), channel_id=1, source_target_pairs={{0,8},{4,36},{8,16},{12,44},{16,24},{20,52},{24,0},{28,60},{32,40}... | collective-permute-start | bytes 393224 | tf_op jit(solution)/shard_map/ppermute | solution.py:193
  60.0 6.7 %collective-permute-start.14 = (bf16[128,512]{0,1:T(8,128)(2,1)S(1)}, bf16[128,512]{0,1:T(8,128)(2,1)S(1)}, u32[]{:S(2)}, u32[]{:S(2)}) collective-permute-start(bf16[128,512]{0,1:T(8,128)(2,1)S(1)} %get-tuple-element.55), channel_id=1, source_target_pairs={{0,24},{4,100},{8,0},{12,108},{16,8},{20,116},{24,16},{28,124},{32... | collective-permute-start | bytes 393224 | tf_op jit(solution)/shard_map/ppermute | solution.py:193
  62.7 5.6 %collective-permute-start.13 = (bf16[128,512]{0,1:T(8,128)(2,1)S(1)}, bf16[128,512]{0,1:T(8,128)(2,1)S(1)}, u32[]{:S(2)}, u32[]{:S(2)}) collective-permute-start(bf16[128,512]{0,1:T(8,128)(2,1)S(1)} %get-tuple-element.56), channel_id=1, source_target_pairs={{0,16},{4,68},{8,24},{12,76},{16,0},{20,84},{24,8},{28,92},{32,48}... | collective-permute-start | bytes 393224 | tf_op jit(solution)/shard_map/ppermute | solution.py:193
  62.8 35.0 %collective-permute-start.25 = (f32[4,288]{1,0:T(4,128)S(1)}, f32[4,288]{1,0:T(4,128)S(1)}, u32[]{:S(2)}, u32[]{:S(2)}) collective-permute-start(f32[4,288]{1,0:T(4,128)S(1)} %get-tuple-element.65), channel_id=1, source_target_pairs={{0,1},{1,2},{2,3},{3,0},{4,5},{5,6},{6,7},{7,4},{8,9},{9,10},{10,1... | collective-permute-start | bytes 13832 | tf_op jit(solution)/shard_map/ppermute | solution.py:233
  64.5 35.7 %collective-permute-start.27 = (f32[4,288]{1,0:T(4,128)S(1)}, f32[4,288]{1,0:T(4,128)S(1)}, u32[]{:S(2)}, u32[]{:S(2)}) collective-permute-start(f32[4,288]{1,0:T(4,128)S(1)} %get-tuple-element.66), channel_id=1, source_target_pairs={{0,3},{1,0},{2,1},{3,2},{4,7},{5,4},{6,5},{7,6},{8,11},{9,8},{10,9... | collective-permute-start | bytes 13832 | tf_op jit(solution)/shard_map/ppermute | solution.py:233
  68.4 5.8 %collective-permute-start.17 = (bf16[128,512]{0,1:T(8,128)(2,1)S(1)}, bf16[128,512]{0,1:T(8,128)(2,1)S(1)}, u32[]{:S(2)}, u32[]{:S(2)}) collective-permute-start(bf16[128,512]{0,1:T(8,128)(2,1)S(1)} %add_convert_fusion.5), channel_id=1, source_target_pairs={{0,96},{4,28},{8,104},{12,4},{16,112},{20,12},{24,120},{28,20},{32... | collective-permute-start | bytes 393224 | tf_op jit(solution)/shard_map/ppermute | solution.py:197
  70.9 5.6 %collective-permute-start.16 = (bf16[128,512]{0,1:T(8,128)(2,1)S(1)}, bf16[128,512]{0,1:T(8,128)(2,1)S(1)}, u32[]{:S(2)}, u32[]{:S(2)}) collective-permute-start(bf16[128,512]{0,1:T(8,128)(2,1)S(1)} %add_convert_fusion.5), channel_id=1, source_target_pairs={{0,64},{4,20},{8,72},{12,28},{16,80},{20,4},{24,88},{28,12},{32,96... | collective-permute-start | bytes 393224 | tf_op jit(solution)/shard_map/ppermute | solution.py:197
  70.9 7.0 %collective-permute-start.15 = (bf16[128,512]{0,1:T(8,128)(2,1)S(1)}, bf16[128,512]{0,1:T(8,128)(2,1)S(1)}, u32[]{:S(2)}, u32[]{:S(2)}) collective-permute-start(bf16[128,512]{0,1:T(8,128)(2,1)S(1)} %add_convert_fusion.5), channel_id=1, source_target_pairs={{0,32},{4,12},{8,40},{12,20},{16,48},{20,28},{24,56},{28,4},{32,64... | collective-permute-start | bytes 393224 | tf_op jit(solution)/shard_map/ppermute | solution.py:197
  78.0 7.1 %collective-permute-start.19 = (bf16[128,512]{0,1:T(8,128)(2,1)S(1)}, bf16[128,512]{0,1:T(8,128)(2,1)S(1)}, u32[]{:S(2)}, u32[]{:S(2)}) collective-permute-start(bf16[128,512]{0,1:T(8,128)(2,1)S(1)} %get-tuple-element.45), channel_id=1, source_target_pairs={{0,16},{4,68},{8,24},{12,76},{16,0},{20,84},{24,8},{28,92},{32,48}... | collective-permute-start | bytes 393224 | tf_op jit(solution)/shard_map/ppermute | solution.py:202
  79.2 6.0 %collective-permute-start.18 = (bf16[128,512]{0,1:T(8,128)(2,1)S(1)}, bf16[128,512]{0,1:T(8,128)(2,1)S(1)}, u32[]{:S(2)}, u32[]{:S(2)}) collective-permute-start(bf16[128,512]{0,1:T(8,128)(2,1)S(1)} %get-tuple-element.45), channel_id=1, source_target_pairs={{0,8},{4,36},{8,16},{12,44},{16,24},{20,52},{24,0},{28,60},{32,40}... | collective-permute-start | bytes 393224 | tf_op jit(solution)/shard_map/ppermute | solution.py:202
  79.7 5.6 %collective-permute-start.20 = (bf16[128,512]{0,1:T(8,128)(2,1)S(1)}, bf16[128,512]{0,1:T(8,128)(2,1)S(1)}, u32[]{:S(2)}, u32[]{:S(2)}) collective-permute-start(bf16[128,512]{0,1:T(8,128)(2,1)S(1)} %get-tuple-element.45), channel_id=1, source_target_pairs={{0,24},{4,100},{8,0},{12,108},{16,8},{20,116},{24,16},{28,124},{32... | collective-permute-start | bytes 393224 | tf_op jit(solution)/shard_map/ppermute | solution.py:202
  93.3 23.2 %collective-permute-start.24 = (f16[1168,128]{1,0:T(8,128)(2,1)}, f16[1168,128]{1,0:T(8,128)(2,1)}, u32[]{:S(2)}, u32[]{:S(2)}) collective-permute-start(f16[1168,128]{1,0:T(8,128)(2,1)} %convert_element_type.261), channel_id=1, source_target_pairs={{0,3},{1,0},{2,1},{3,2},{4,7},{5,4},{6,5},{7,6},{8,11},{9,8},{10,9... | collective-permute-start | bytes 897032 | tf_op jit(solution)/shard_map/ppermute | solution.py:220
  97.0 20.5 %collective-permute-start.23 = (f16[1168,128]{1,0:T(8,128)(2,1)}, f16[1168,128]{1,0:T(8,128)(2,1)}, u32[]{:S(2)}, u32[]{:S(2)}) collective-permute-start(f16[1168,128]{1,0:T(8,128)(2,1)} %convert_element_type.259), channel_id=1, source_target_pairs={{0,2},{1,3},{2,0},{3,1},{4,6},{5,7},{6,4},{7,5},{8,10},{9,11},{10,... | collective-permute-start | bytes 897032 | tf_op jit(solution)/shard_map/ppermute | solution.py:220
  97.0 21.5 %collective-permute-start.22 = (f16[1168,128]{1,0:T(8,128)(2,1)}, f16[1168,128]{1,0:T(8,128)(2,1)}, u32[]{:S(2)}, u32[]{:S(2)}) collective-permute-start(f16[1168,128]{1,0:T(8,128)(2,1)} %convert_element_type.257), channel_id=1, source_target_pairs={{0,1},{1,2},{2,3},{3,0},{4,5},{5,6},{6,7},{7,4},{8,9},{9,10},{10,1... | collective-permute-start | bytes 897032 | tf_op jit(solution)/shard_map/ppermute | solution.py:220
  97.8 15.3 %collective-permute-start.26 = (f32[4,288]{1,0:T(4,128)S(1)}, f32[4,288]{1,0:T(4,128)S(1)}, u32[]{:S(2)}, u32[]{:S(2)}) collective-permute-start(f32[4,288]{1,0:T(4,128)S(1)} %get-tuple-element.67), channel_id=1, source_target_pairs={{0,2},{1,3},{2,0},{3,1},{4,6},{5,7},{6,4},{7,5},{8,10},{9,11},{10,... | collective-permute-start | bytes 13832 | tf_op jit(solution)/shard_map/ppermute | solution.py:233
  126.7 6.9 %collective-permute-start.30 = (f16[1168,128]{1,0:T(8,128)(2,1)S(1)}, f16[1168,128]{1,0:T(8,128)(2,1)S(1)}, u32[]{:S(2)}, u32[]{:S(2)}) collective-permute-start(f16[1168,128]{1,0:T(8,128)(2,1)S(1)} %convert_element_type.267), channel_id=1, source_target_pairs={{0,3},{1,0},{2,1},{3,2},{4,7},{5,4},{6,5},{7,6},{8,11},{9,8},{10,9... | collective-permute-start | bytes 897032 | tf_op jit(solution)/shard_map/ppermute | solution.py:220
  126.8 8.4 %collective-permute-start.29 = (f16[1168,128]{1,0:T(8,128)(2,1)S(1)}, f16[1168,128]{1,0:T(8,128)(2,1)S(1)}, u32[]{:S(2)}, u32[]{:S(2)}) collective-permute-start(f16[1168,128]{1,0:T(8,128)(2,1)S(1)} %convert_element_type.265), channel_id=1, source_target_pairs={{0,2},{1,3},{2,0},{3,1},{4,6},{5,7},{6,4},{7,5},{8,10},{9,11},{10,... | collective-permute-start | bytes 897032 | tf_op jit(solution)/shard_map/ppermute | solution.py:220
  127.2 16.6 %collective-permute-start.28 = (f16[1168,128]{1,0:T(8,128)(2,1)S(1)}, f16[1168,128]{1,0:T(8,128)(2,1)S(1)}, u32[]{:S(2)}, u32[]{:S(2)}) collective-permute-start(f16[1168,128]{1,0:T(8,128)(2,1)S(1)} %convert_element_type.263), channel_id=1, source_target_pairs={{0,1},{1,2},{2,3},{3,0},{4,5},{5,6},{6,7},{7,4},{8,9},{9,10},{10,1... | collective-permute-start | bytes 897032 | tf_op jit(solution)/shard_map/ppermute | solution.py:220
  155.3 5.4 %collective-permute-start.32 = (bf16[128,512]{0,1:T(8,128)(2,1)S(1)}, bf16[128,512]{0,1:T(8,128)(2,1)S(1)}, u32[]{:S(2)}, u32[]{:S(2)}) collective-permute-start(bf16[128,512]{0,1:T(8,128)(2,1)S(1)} %get-tuple-element.51), channel_id=1, source_target_pairs={{0,8},{4,36},{8,16},{12,44},{16,24},{20,52},{24,0},{28,60},{32,40}... | collective-permute-start | bytes 393224 | tf_op jit(solution)/shard_map/ppermute | solution.py:193
  155.4 6.0 %collective-permute-start.34 = (bf16[128,512]{0,1:T(8,128)(2,1)S(1)}, bf16[128,512]{0,1:T(8,128)(2,1)S(1)}, u32[]{:S(2)}, u32[]{:S(2)}) collective-permute-start(bf16[128,512]{0,1:T(8,128)(2,1)S(1)} %get-tuple-element.52), channel_id=1, source_target_pairs={{0,24},{4,100},{8,0},{12,108},{16,8},{20,116},{24,16},{28,124},{32... | collective-permute-start | bytes 393224 | tf_op jit(solution)/shard_map/ppermute | solution.py:193
  158.0 5.6 %collective-permute-start.33 = (bf16[128,512]{0,1:T(8,128)(2,1)S(1)}, bf16[128,512]{0,1:T(8,128)(2,1)S(1)}, u32[]{:S(2)}, u32[]{:S(2)}) collective-permute-start(bf16[128,512]{0,1:T(8,128)(2,1)S(1)} %get-tuple-element.53), channel_id=1, source_target_pairs={{0,16},{4,68},{8,24},{12,76},{16,0},{20,84},{24,8},{28,92},{32,48}... | collective-permute-start | bytes 393224 | tf_op jit(solution)/shard_map/ppermute | solution.py:193
  163.7 5.8 %collective-permute-start.37 = (bf16[128,512]{0,1:T(8,128)(2,1)S(1)}, bf16[128,512]{0,1:T(8,128)(2,1)S(1)}, u32[]{:S(2)}, u32[]{:S(2)}) collective-permute-start(bf16[128,512]{0,1:T(8,128)(2,1)S(1)} %add_convert_fusion.3), channel_id=1, source_target_pairs={{0,96},{4,28},{8,104},{12,4},{16,112},{20,12},{24,120},{28,20},{32... | collective-permute-start | bytes 393224 | tf_op jit(solution)/shard_map/ppermute | solution.py:197
  166.2 5.7 %collective-permute-start.36 = (bf16[128,512]{0,1:T(8,128)(2,1)S(1)}, bf16[128,512]{0,1:T(8,128)(2,1)S(1)}, u32[]{:S(2)}, u32[]{:S(2)}) collective-permute-start(bf16[128,512]{0,1:T(8,128)(2,1)S(1)} %add_convert_fusion.3), channel_id=1, source_target_pairs={{0,64},{4,20},{8,72},{12,28},{16,80},{20,4},{24,88},{28,12},{32,96... | collective-permute-start | bytes 393224 | tf_op jit(solution)/shard_map/ppermute | solution.py:197
  166.2 6.7 %collective-permute-start.35 = (bf16[128,512]{0,1:T(8,128)(2,1)S(1)}, bf16[128,512]{0,1:T(8,128)(2,1)S(1)}, u32[]{:S(2)}, u32[]{:S(2)}) collective-permute-start(bf16[128,512]{0,1:T(8,128)(2,1)S(1)} %add_convert_fusion.3), channel_id=1, source_target_pairs={{0,32},{4,12},{8,40},{12,20},{16,48},{20,28},{24,56},{28,4},{32,64... | collective-permute-start | bytes 393224 | tf_op jit(solution)/shard_map/ppermute | solution.py:197
  173.0 15.9 %collective-permute-start.38 = (bf16[128,512]{0,1:T(8,128)(2,1)S(1)}, bf16[128,512]{0,1:T(8,128)(2,1)S(1)}, u32[]{:S(2)}, u32[]{:S(2)}) collective-permute-start(bf16[128,512]{0,1:T(8,128)(2,1)S(1)} %get-tuple-element.43), channel_id=1, source_target_pairs={{0,8},{4,36},{8,16},{12,44},{16,24},{20,52},{24,0},{28,60},{32,40}... | collective-permute-start | bytes 393224 | tf_op jit(solution)/shard_map/ppermute | solution.py:202
  182.2 6.8 %collective-permute-start.39 = (bf16[128,512]{0,1:T(8,128)(2,1)S(1)}, bf16[128,512]{0,1:T(8,128)(2,1)S(1)}, u32[]{:S(2)}, u32[]{:S(2)}) collective-permute-start(bf16[128,512]{0,1:T(8,128)(2,1)S(1)} %get-tuple-element.43), channel_id=1, source_target_pairs={{0,16},{4,68},{8,24},{12,76},{16,0},{20,84},{24,8},{28,92},{32,48}... | collective-permute-start | bytes 393224 | tf_op jit(solution)/shard_map/ppermute | solution.py:202
  205.5 5.4 %collective-permute-start.43 = (bf16[128,512]{0,1:T(8,128)(2,1)S(1)}, bf16[128,512]{0,1:T(8,128)(2,1)S(1)}, u32[]{:S(2)}, u32[]{:S(2)}) collective-permute-start(bf16[128,512]{0,1:T(8,128)(2,1)S(1)} %get-tuple-element.48), channel_id=1, source_target_pairs={{0,8},{4,36},{8,16},{12,44},{16,24},{20,52},{24,0},{28,60},{32,40}... | collective-permute-start | bytes 393224 | tf_op jit(solution)/shard_map/ppermute | solution.py:193
  205.6 6.0 %collective-permute-start.45 = (bf16[128,512]{0,1:T(8,128)(2,1)S(1)}, bf16[128,512]{0,1:T(8,128)(2,1)S(1)}, u32[]{:S(2)}, u32[]{:S(2)}) collective-permute-start(bf16[128,512]{0,1:T(8,128)(2,1)S(1)} %get-tuple-element.49), channel_id=1, source_target_pairs={{0,24},{4,100},{8,0},{12,108},{16,8},{20,116},{24,16},{28,124},{32... | collective-permute-start | bytes 393224 | tf_op jit(solution)/shard_map/ppermute | solution.py:193
  208.3 5.6 %collective-permute-start.44 = (bf16[128,512]{0,1:T(8,128)(2,1)S(1)}, bf16[128,512]{0,1:T(8,128)(2,1)S(1)}, u32[]{:S(2)}, u32[]{:S(2)}) collective-permute-start(bf16[128,512]{0,1:T(8,128)(2,1)S(1)} %get-tuple-element.50), channel_id=1, source_target_pairs={{0,16},{4,68},{8,24},{12,76},{16,0},{20,84},{24,8},{28,92},{32,48}... | collective-permute-start | bytes 393224 | tf_op jit(solution)/shard_map/ppermute | solution.py:193
  214.0 5.7 %collective-permute-start.48 = (bf16[128,512]{0,1:T(8,128)(2,1)S(1)}, bf16[128,512]{0,1:T(8,128)(2,1)S(1)}, u32[]{:S(2)}, u32[]{:S(2)}) collective-permute-start(bf16[128,512]{0,1:T(8,128)(2,1)S(1)} %add_convert_fusion.1), channel_id=1, source_target_pairs={{0,96},{4,28},{8,104},{12,4},{16,112},{20,12},{24,120},{28,20},{32... | collective-permute-start | bytes 393224 | tf_op jit(solution)/shard_map/ppermute | solution.py:197
  216.4 5.7 %collective-permute-start.47 = (bf16[128,512]{0,1:T(8,128)(2,1)S(1)}, bf16[128,512]{0,1:T(8,128)(2,1)S(1)}, u32[]{:S(2)}, u32[]{:S(2)}) collective-permute-start(bf16[128,512]{0,1:T(8,128)(2,1)S(1)} %add_convert_fusion.1), channel_id=1, source_target_pairs={{0,64},{4,20},{8,72},{12,28},{16,80},{20,4},{24,88},{28,12},{32,96... | collective-permute-start | bytes 393224 | tf_op jit(solution)/shard_map/ppermute | solution.py:197
  216.4 6.7 %collective-permute-start.46 = (bf16[128,512]{0,1:T(8,128)(2,1)S(1)}, bf16[128,512]{0,1:T(8,128)(2,1)S(1)}, u32[]{:S(2)}, u32[]{:S(2)}) collective-permute-start(bf16[128,512]{0,1:T(8,128)(2,1)S(1)} %add_convert_fusion.1), channel_id=1, source_target_pairs={{0,32},{4,12},{8,40},{12,20},{16,48},{20,28},{24,56},{28,4},{32,64... | collective-permute-start | bytes 393224 | tf_op jit(solution)/shard_map/ppermute | solution.py:197
  223.3 6.8 %collective-permute-start.49 = (bf16[128,512]{0,1:T(8,128)(2,1)S(1)}, bf16[128,512]{0,1:T(8,128)(2,1)S(1)}, u32[]{:S(2)}, u32[]{:S(2)}) collective-permute-start(bf16[128,512]{0,1:T(8,128)(2,1)S(1)} %get-tuple-element.41), channel_id=1, source_target_pairs={{0,8},{4,36},{8,16},{12,44},{16,24},{20,52},{24,0},{28,60},{32,40}... | collective-permute-start | bytes 393224 | tf_op jit(solution)/shard_map/ppermute | solution.py:202
  223.3 6.8 %collective-permute-start.50 = (bf16[128,512]{0,1:T(8,128)(2,1)S(1)}, bf16[128,512]{0,1:T(8,128)(2,1)S(1)}, u32[]{:S(2)}, u32[]{:S(2)}) collective-permute-start(bf16[128,512]{0,1:T(8,128)(2,1)S(1)} %get-tuple-element.41), channel_id=1, source_target_pairs={{0,16},{4,68},{8,24},{12,76},{16,0},{20,84},{24,8},{28,92},{32,48}... | collective-permute-start | bytes 393224 | tf_op jit(solution)/shard_map/ppermute | solution.py:202
  237.1 8.4 %collective-permute-start.55 = (f16[1168,128]{1,0:T(8,128)(2,1)S(1)}, f16[1168,128]{1,0:T(8,128)(2,1)S(1)}, u32[]{:S(2)}, u32[]{:S(2)}) collective-permute-start(f16[1168,128]{1,0:T(8,128)(2,1)S(1)} %convert_element_type.298), channel_id=1, source_target_pairs={{0,3},{1,0},{2,1},{3,2},{4,7},{5,4},{6,5},{7,6},{8,11},{9,8},{10,9... | collective-permute-start | bytes 897032 | tf_op jit(solution)/shard_map/ppermute | solution.py:220
  238.1 9.6 %collective-permute-start.54 = (f16[1168,128]{1,0:T(8,128)(2,1)S(1)}, f16[1168,128]{1,0:T(8,128)(2,1)S(1)}, u32[]{:S(2)}, u32[]{:S(2)}) collective-permute-start(f16[1168,128]{1,0:T(8,128)(2,1)S(1)} %convert_element_type.296), channel_id=1, source_target_pairs={{0,2},{1,3},{2,0},{3,1},{4,6},{5,7},{6,4},{7,5},{8,10},{9,11},{10,... | collective-permute-start | bytes 897032 | tf_op jit(solution)/shard_map/ppermute | solution.py:220
  238.1 16.9 %collective-permute-start.53 = (f16[1168,128]{1,0:T(8,128)(2,1)S(1)}, f16[1168,128]{1,0:T(8,128)(2,1)S(1)}, u32[]{:S(2)}, u32[]{:S(2)}) collective-permute-start(f16[1168,128]{1,0:T(8,128)(2,1)S(1)} %convert_element_type.294), channel_id=1, source_target_pairs={{0,1},{1,2},{2,3},{3,0},{4,5},{5,6},{6,7},{7,4},{8,9},{9,10},{10,1... | collective-permute-start | bytes 897032 | tf_op jit(solution)/shard_map/ppermute | solution.py:220
  261.5 8.2 %collective-permute-start.58 = (f16[1168,128]{1,0:T(8,128)(2,1)S(1)}, f16[1168,128]{1,0:T(8,128)(2,1)S(1)}, u32[]{:S(2)}, u32[]{:S(2)}) collective-permute-start(f16[1168,128]{1,0:T(8,128)(2,1)S(1)} %convert_element_type.304), channel_id=1, source_target_pairs={{0,3},{1,0},{2,1},{3,2},{4,7},{5,4},{6,5},{7,6},{8,11},{9,8},{10,9... | collective-permute-start | bytes 897032 | tf_op jit(solution)/shard_map/ppermute | solution.py:220
  261.6 9.2 %collective-permute-start.57 = (f16[1168,128]{1,0:T(8,128)(2,1)S(1)}, f16[1168,128]{1,0:T(8,128)(2,1)S(1)}, u32[]{:S(2)}, u32[]{:S(2)}) collective-permute-start(f16[1168,128]{1,0:T(8,128)(2,1)S(1)} %convert_element_type.302), channel_id=1, source_target_pairs={{0,2},{1,3},{2,0},{3,1},{4,6},{5,7},{6,4},{7,5},{8,10},{9,11},{10,... | collective-permute-start | bytes 897032 | tf_op jit(solution)/shard_map/ppermute | solution.py:220
  261.7 16.9 %collective-permute-start.56 = (f16[1168,128]{1,0:T(8,128)(2,1)S(1)}, f16[1168,128]{1,0:T(8,128)(2,1)S(1)}, u32[]{:S(2)}, u32[]{:S(2)}) collective-permute-start(f16[1168,128]{1,0:T(8,128)(2,1)S(1)} %convert_element_type.300), channel_id=1, source_target_pairs={{0,1},{1,2},{2,3},{3,0},{4,5},{5,6},{6,7},{7,4},{8,9},{9,10},{10,1... | collective-permute-start | bytes 897032 | tf_op jit(solution)/shard_map/ppermute | solution.py:220
  (34 other events, 216.0 us)
where the time goes:
time: 286 us; the launch traced here: 281 us
  waiting for transfers between devices  131 us (46%)
  starting transfers between devices  78.2 us (27%)
  matrix products  27.2 us (10%)
  Pallas kernels  16.9 us (6%)
  local copies, waits for them, and re-layouts  16.2 us (6%)
  other arithmetic  9.69 us (3%)
    ppermute x12, waiting for transfers between devices, exchange(): lax.ppermute(load.astype(F16), 'freq', ring(d + 1)).astype(F32)  46.8 us
    ppermute x12, waiting for transfers between devices, reduce_all(): total = total + lax.ppermute(own, 'fac', along(d, False)).astype(F32)  24.1 us
    ppermute x12, starting transfers between devices, reduce_all(): piece = lax.ppermute(total, 'fac', along(d, True))  22.1 us
    pallas_call x6, Pallas kernels, call(): pl.pallas_call(body, out_shape=[jax.ShapeDtypeStruct(s, t) for s, t in ou...  16.9 us
    ppermute x12, waiting for transfers between devices, reduce_all(): own = own + lax.ppermute(piece, 'fac', along(d, True)).astype(F32)  16.9 us
    unnamed x8, matrix products  16.7 us
    ppermute x12, waiting for transfers between devices, reduce_all(): piece = lax.ppermute(total, 'fac', along(d, True))  15.4 us
    ppermute x12, starting transfers between devices, reduce_all(): total = total + lax.ppermute(own, 'fac', along(d, False)).astype(F32)  12.9 us
  transfers between devices with their start and end apart: 59, of which 46 were waited for; matrix products, arithmetic and copies ran while one was open for 4% of the time, Pallas kernels for 0%

commit v1 on v0

--- a/solution.py
+++ b/solution.py
@@ -16,7 +16,7 @@
 
 
 def place(y, x, k):
-    return ((y % SIDE) * SIDE + x % SIDE) * 2 + k
+    return (y * SIDE + x) * 2 + k
 
 
 def along(d, first):
@@ -25,7 +25,7 @@
         for x in range(SIDE):
             for k in range(2):
                 on_x = (k == 0) == first
-                there = place(y, x + d, k) if on_x else place(y + d, x, k)
+                there = place(y, x ^ d, k) if on_x else place(y ^ d, x, k)
                 pairs.append((place(y, x, k), there))
     return pairs
 
@@ -33,8 +33,8 @@
 CORES = [(i, i ^ 1) for i in range(2 * SIDE * SIDE)]
 
 
-def ring(d):
-    return [(z, (z + d) % SIDE) for z in range(SIDE)]
+def swap(d):
+    return [(z, z ^ d) for z in range(SIDE)]
 
 
 def scale_of(peak):
@@ -54,7 +54,7 @@
     power, scale = scale_of(peak)
     scale = jnp.broadcast_to(scale, (RUN, cols))
     for d in range(SIDE):
-        base = ((z + d) % SIDE) * quarter
+        base = (z ^ d) * quarter
 
         def step(g, carry, d=d, base=base):
             for f in range(nf):
@@ -129,7 +129,7 @@
     body = nf * quarter
     z = z_ref[0]
     for d, ref in enumerate((own_ref, got1, got2, got3)):
-        base = ((z - d + SIDE) % SIDE) * quarter
+        base = (z ^ d) * quarter
         if d:
             gain = jnp.exp2(jnp.broadcast_to(ref[body : body + 1, :], (RUN, cols)))
 
@@ -188,7 +188,7 @@
         own = lax.dynamic_slice(mine, (spot * chunk, 0), (chunk, wide))
         for d in (1, 2, 3):
             piece = lax.dynamic_slice(
-                mine, (((spot + d) % SIDE) * chunk, 0), (chunk, wide)
+                mine, ((spot ^ d) * chunk, 0), (chunk, wide)
             ).astype(BF16)
             own = own + lax.ppermute(piece, "fac", along(d, True)).astype(F32)
         own = own.astype(BF16)
@@ -201,7 +201,7 @@
         for d in (1, 2, 3):
             piece = lax.ppermute(total, "fac", along(d, True))
             gathered = lax.dynamic_update_slice(
-                gathered, piece, (((spot - d) % SIDE) * chunk, 0)
+                gathered, piece, ((spot ^ d) * chunk, 0)
             )
         other = lax.ppermute(gathered, "fac", CORES)
         return gathered, other
@@ -217,7 +217,7 @@
 
     def exchange(sent):
         return [
-            lax.ppermute(load.astype(F16), "freq", ring(d + 1)).astype(F32)
+            lax.ppermute(load.astype(F16), "freq", swap(d + 1)).astype(F32)
             for d, load in enumerate(sent)
         ]
 
@@ -228,9 +228,9 @@
     kernel = [lax.dynamic_slice(second_order, (0, z * quarter), (nf, quarter))]
     for d in (1, 2, 3):
         piece = lax.dynamic_slice(
-            second_order, (0, ((z + d) % SIDE) * quarter), (nf, quarter)
+            second_order, (0, (z ^ d) * quarter), (nf, quarter)
         )
-        kernel.append(lax.ppermute(piece, "freq", ring(d)))
+        kernel.append(lax.ppermute(piece, "freq", swap(d)))
     kernel = jnp.concatenate(kernel, axis=0).reshape(SIDE * nf, quarter // RUN, RUN)
     kernel = kernel.transpose(1, 0, 2).reshape(body * SIDE, 1)
     kernel = jnp.broadcast_to(kernel, (body * SIDE, cols))
@@ -238,8 +238,7 @@
     row = jnp.arange(size)
     ring_at, f_at = row // (nf * RUN), row // RUN % nf
     names = jnp.arange(SIDE * nf)
-    source = (((z - ring_at) % SIDE) * nf + f_at)[:, None] == names[None, :]
-    target = (((z + ring_at) % SIDE) * nf + f_at)[:, None] == names[None, :]
+    source = ((z ^ ring_at) * nf + f_at)[:, None] == names[None, :]
     same = (row % RUN)[:, None] == (row % RUN)[None, :]
 
     def spread_table(left, table, right):
@@ -250,7 +249,7 @@
         return jnp.concatenate([high, full - high], axis=0).astype(BF16)
 
     table_in = spread_table(source, forward, source)
-    table_out = spread_table(target, backward, source)
+    table_out = spread_table(source, backward, source)
     loads = [((body, cols), F32)] + [((body + RUN, cols), F32)] * 3
 
     sources = right_side

time: 286 us -> 269 us (0.941); the launches traced: 281 us -> 267 us
  waiting for transfers between devices: 131 us -> 115 us
  starting transfers between devices: 78.2 us -> 81.8 us
  matrix products: 27.2 us -> 24 us
    ppermute x12, waiting for transfers between devices: 24.1 us -> 12.9 us  [reduce_all(): total = total + lax.ppermute(own, 'fac', along(d, False)).astype(F32)]
    ppermute x15, waiting for transfers between devices: 59.7 us -> 50.8 us  [the longest x12 38 us: exchange(): lax.ppermute(load.astype(F16), 'freq', swap(d + 1)).astype(F32)]
    ppermute x12, starting transfers between devices: 22.1 us -> 15.2 us  [reduce_all(): piece = lax.ppermute(total, 'fac', along(d, True))]
    ppermute x15, starting transfers between devices: 15.5 us -> 20.3 us  [the longest x12 13.8 us: exchange(): lax.ppermute(load.astype(F16), 'freq', swap(d + 1)).astype(F32)]
    ppermute x12, waiting for transfers between devices: 16.9 us -> 20.5 us  [reduce_all(): own = own + lax.ppermute(piece, 'fac', along(d, True)).astype(F32)]
  transfers between devices with their start and end apart: 59 -> 59, of which waited for: 46 -> 39; matrix products, arithmetic and copies ran while one was open for 4% -> 5% of each run, Pallas kernels for 0% -> 0%
where the time goes in v1:
time: 269 us; the launch traced here: 267 us
  waiting for transfers between devices  115 us (43%)
  starting transfers between devices  81.8 us (30%)
  matrix products  24 us (9%)
  local copies, waits for them, and re-layouts  17.6 us (7%)
  Pallas kernels  16.9 us (6%)
  other arithmetic  10.7 us (4%)
    ppermute x12, waiting for transfers between devices, exchange(): lax.ppermute(load.astype(F16), 'freq', swap(d + 1)).astype(F32)  38 us
    ppermute x12, waiting for transfers between devices, reduce_all(): own = own + lax.ppermute(piece, 'fac', along(d, True)).astype(F32)  20.5 us
    pallas_call x6, Pallas kernels, call(): pl.pallas_call(body, out_shape=[jax.ShapeDtypeStruct(s, t) for s, t in ou...  16.9 us
    ppermute x12, waiting for transfers between devices, reduce_all(): piece = lax.ppermute(total, 'fac', along(d, True))  15.9 us
    ppermute x12, starting transfers between devices, reduce_all(): piece = lax.ppermute(total, 'fac', along(d, True))  15.2 us
    unnamed x8, matrix products  14.5 us
    ppermute x4, starting transfers between devices, reduce_all(): other = lax.ppermute(gathered, 'fac', CORES)  14.5 us
    ppermute x12, starting transfers between devices, reduce_all(): own = own + lax.ppermute(piece, 'fac', along(d, True)).astype(F32)  14.3 us
  transfers between devices with their start and end apart: 59, of which 39 were waited for; matrix products, arithmetic and copies ran while one was open for 5% of the time, Pallas kernels for 0%

profile of v1, /device:TPU:1, one launch (start us, length us, event | category | flops | bytes accessed | tf_op | source)
XLA Modules:
  0.0 267.1 jit_solution(1579227470853432774)
XLA Ops:
  4.1 3.2 %convolution_bitcast_fusion.6 = f32[512,512]{0,1:T(8,128)} fusion(bf16[1152,512]{0,1:T(8,128)(2,1)} %bitcast.132, bf16[1152,1024]{1,0:T(8,128)(2,1)S(1)} %copy-done, s32[]{:T(128)S(6)} %select_n.130), kind=kOutput, calls=%fused_computation.24 | convolution fusion | flops 603979776 | bytes 3407876
  8.7 2.6 collective-permute-done
  11.3 2.1 fusion.14
  18.7 2.6 collective-permute-done.3
  21.3 2.2 collective-permute-done.2
  24.5 2.3 collective-permute-start.6
  27.8 2.2 collective-permute-done.6
  36.2 3.0 %collective-permute-done.8 = bf16[128,512]{0,1:T(8,128)(2,1)S(1)} collective-permute-done((bf16[128,512]{0,1:T(8,128)(2,1)S(1)}, bf16[128,512]{0,1:T(8,128)(2,1)S(1)}, u32[]{:S(2)}, u32[]{:S(2)}) %collective-permute-start.8) | collective-permute-done | bytes 131104 | tf_op jit(solution)/shard_map/ppermute | solution.py:202
  40.6 4.2 %collective-permute-start.10 = (bf16[512,512]{0,1:T(8,128)(2,1)S(1)}, bf16[512,512]{0,1:T(8,128)(2,1)S(1)}, u32[]{:S(2)}, u32[]{:S(2)}) collective-permute-start(bf16[512,512]{0,1:T(8,128)(2,1)S(1)} %constant_dynamic-update-slice_fusion.12), channel_id=1, source_target_pairs={{0,4},{4,0},{8,12},{12,8},{16,20},{20,16},{24,28},{28,24},{32,36},... | collective-permute-start | bytes 1572872 | tf_op jit(solution)/shard_map/ppermute | solution.py:206
  49.8 2.2 convolution_bitcast_fusion.4
  52.5 2.3 collective-permute-done.11
  56.7 2.4 collective-permute-start.14
  62.7 2.3 collective-permute-done.13
  66.0 2.0 collective-permute-start.17
  71.9 2.3 collective-permute-start.27
  81.8 3.7 %collective-permute-start.21 = (bf16[512,512]{0,1:T(8,128)(2,1)S(1)}, bf16[512,512]{0,1:T(8,128)(2,1)S(1)}, u32[]{:S(2)}, u32[]{:S(2)}) collective-permute-start(bf16[512,512]{0,1:T(8,128)(2,1)S(1)} %constant_dynamic-update-slice_fusion.8), channel_id=1, source_target_pairs={{0,4},{4,0},{8,12},{12,8},{16,20},{20,16},{24,28},{28,24},{32,36},... | collective-permute-start | bytes 1572872 | tf_op jit(solution)/shard_map/ppermute | solution.py:206
  91.7 3.0 %collective-permute-start.24 = (f16[1168,128]{1,0:T(8,128)(2,1)}, f16[1168,128]{1,0:T(8,128)(2,1)}, u32[]{:S(2)}, u32[]{:S(2)}) collective-permute-start(f16[1168,128]{1,0:T(8,128)(2,1)} %convert_element_type.261), channel_id=1, source_target_pairs={{0,3},{1,2},{2,1},{3,0},{4,7},{5,6},{6,5},{7,4},{8,11},{9,10},{10,... | collective-permute-start | bytes 897032 | tf_op jit(solution)/shard_map/ppermute | solution.py:220
  95.4 2.6 collective-permute-start.26
  98.0 12.8 %collective-permute-done.26 = f32[4,288]{1,0:T(4,128)S(1)} collective-permute-done((f32[4,288]{1,0:T(4,128)S(1)}, f32[4,288]{1,0:T(4,128)S(1)}, u32[]{:S(2)}, u32[]{:S(2)}) %collective-permute-start.26) | collective-permute-done | bytes 4640 | tf_op jit(solution)/shard_map/ppermute | solution.py:233
  117.9 6.3 %mix.2 = (f32[1152,128]{1,0:T(8,128)S(1)}, f32[1168,128]{1,0:T(8,128)S(1)}, f32[1168,128]{1,0:T(8,128)S(1)}, f32[1168,128]{1,0:T(8,128)S(1)}) custom-call(f32[1152,128]{1,0:T(8,128)S(1)} %get-tuple-element.21.own_ref, f32[1168,128]{1,0:T(8,128)S(1)} %convert_element_type.258.got1, f32[1168,128]{1,0:T(8,128)S(1)} %convert_element_type.260.got2, ...), custom_call_target="tpu_custom_call" | custom-call | tf_op jit(solution)/shard_map/mix/pallas_call | solution.py:153
  125.8 2.0 collective-permute-start.28
  127.8 12.6 %collective-permute-done.30 = f16[1168,128]{1,0:T(8,128)(2,1)S(1)} collective-permute-done((f16[1168,128]{1,0:T(8,128)(2,1)S(1)}, f16[1168,128]{1,0:T(8,128)(2,1)S(1)}, u32[]{:S(2)}, u32[]{:S(2)}) %collective-permute-start.30) | collective-permute-done | bytes 299040 | tf_op jit(solution)/shard_map/ppermute | solution.py:220
  143.6 2.4 copy.33
  146.0 2.2 convolution_bitcast_fusion.2
  149.9 2.3 collective-permute-done.31
  153.6 2.2 collective-permute-start.34
  159.2 2.3 collective-permute-done.33
  161.6 2.1 collective-permute-start.37
  164.9 2.1 collective-permute-done.37
  169.2 2.6 collective-permute-start.39
  173.1 2.4 collective-permute-done.39
  177.3 3.7 %collective-permute-start.41 = (bf16[512,512]{0,1:T(8,128)(2,1)S(1)}, bf16[512,512]{0,1:T(8,128)(2,1)S(1)}, u32[]{:S(2)}, u32[]{:S(2)}) collective-permute-start(bf16[512,512]{0,1:T(8,128)(2,1)S(1)} %constant_dynamic-update-slice_fusion.4), channel_id=1, source_target_pairs={{0,4},{4,0},{8,12},{12,8},{16,20},{20,16},{24,28},{28,24},{32,36},... | collective-permute-start | bytes 1572872 | tf_op jit(solution)/shard_map/ppermute | solution.py:206
  183.4 2.0 fusion.13
  185.4 2.4 copy.37
  187.8 2.2 convolution_bitcast_fusion
  190.4 2.3 collective-permute-done.42
  194.6 2.8 %collective-permute-start.45 = (bf16[128,512]{0,1:T(8,128)(2,1)S(1)}, bf16[128,512]{0,1:T(8,128)(2,1)S(1)}, u32[]{:S(2)}, u32[]{:S(2)}) collective-permute-start(bf16[128,512]{0,1:T(8,128)(2,1)S(1)} %get-tuple-element.49), channel_id=1, source_target_pairs={{0,24},{4,100},{8,16},{12,108},{16,8},{20,116},{24,0},{28,124},{32... | collective-permute-start | bytes 393224 | tf_op jit(solution)/shard_map/ppermute | solution.py:193
  197.9 2.8 %collective-permute-done.45 = bf16[128,512]{0,1:T(8,128)(2,1)S(1)} collective-permute-done((bf16[128,512]{0,1:T(8,128)(2,1)S(1)}, bf16[128,512]{0,1:T(8,128)(2,1)S(1)}, u32[]{:S(2)}, u32[]{:S(2)}) %collective-permute-start.45) | collective-permute-done | bytes 131104 | tf_op jit(solution)/shard_map/ppermute | solution.py:193
  202.7 2.3 collective-permute-start.48
  206.1 2.3 collective-permute-done.48
  208.3 2.3 collective-permute-done.47
  210.9 2.3 collective-permute-start.50
  214.8 2.2 collective-permute-done.50
  218.7 3.0 %collective-permute-start.52 = (bf16[512,512]{0,1:T(8,128)(2,1)S(1)}, bf16[512,512]{0,1:T(8,128)(2,1)S(1)}, u32[]{:S(2)}, u32[]{:S(2)}) collective-permute-start(bf16[512,512]{0,1:T(8,128)(2,1)S(1)} %constant_dynamic-update-slice_fusion), channel_id=1, source_target_pairs={{0,4},{4,0},{8,12},{12,8},{16,20},{20,16},{24,28},{28,24},{32,36},... | collective-permute-start | bytes 1572872 | tf_op jit(solution)/shard_map/ppermute | solution.py:206
  229.2 12.7 %collective-permute-done.55 = f16[1168,128]{1,0:T(8,128)(2,1)S(1)} collective-permute-done((f16[1168,128]{1,0:T(8,128)(2,1)S(1)}, f16[1168,128]{1,0:T(8,128)(2,1)S(1)}, u32[]{:S(2)}, u32[]{:S(2)}) %collective-permute-start.55) | collective-permute-done | bytes 299040 | tf_op jit(solution)/shard_map/ppermute | solution.py:220
  242.1 6.3 %mix.3 = (f32[1152,128]{1,0:T(8,128)S(1)}, f32[1168,128]{1,0:T(8,128)S(1)}, f32[1168,128]{1,0:T(8,128)S(1)}, f32[1168,128]{1,0:T(8,128)S(1)}) custom-call(f32[1152,128]{1,0:T(8,128)S(1)} %get-tuple-element.31.own_ref, f32[1168,128]{1,0:T(8,128)S(1)} %convert_element_type.295.got1, f32[1168,128]{1,0:T(8,128)S(1)} %convert_element_type.297.got2, ...), custom_call_target="tpu_custom_call" | custom-call | tf_op jit(solution)/shard_map/mix/pallas_call | solution.py:153
  252.0 12.6 %collective-permute-done.58 = f16[1168,128]{1,0:T(8,128)(2,1)S(1)} collective-permute-done((f16[1168,128]{1,0:T(8,128)(2,1)S(1)}, f16[1168,128]{1,0:T(8,128)(2,1)S(1)}, u32[]{:S(2)}, u32[]{:S(2)}) %collective-permute-start.58) | collective-permute-done | bytes 299040 | tf_op jit(solution)/shard_map/ppermute | solution.py:220
  264.8 2.4 unpack.3
  (204 shorter events, 98.0 us)
Async XLA Ops:
  16.0 5.3 %collective-permute-start.3 = (bf16[128,512]{0,1:T(8,128)(2,1)S(1)}, bf16[128,512]{0,1:T(8,128)(2,1)S(1)}, u32[]{:S(2)}, u32[]{:S(2)}) collective-permute-start(bf16[128,512]{0,1:T(8,128)(2,1)S(1)} %get-tuple-element.58), channel_id=1, source_target_pairs={{0,24},{4,100},{8,16},{12,108},{16,8},{20,116},{24,0},{28,124},{32... | collective-permute-start | bytes 393224 | tf_op jit(solution)/shard_map/ppermute | solution.py:193
  17.9 5.6 %collective-permute-start.2 = (bf16[128,512]{0,1:T(8,128)(2,1)S(1)}, bf16[128,512]{0,1:T(8,128)(2,1)S(1)}, u32[]{:S(2)}, u32[]{:S(2)}) collective-permute-start(bf16[128,512]{0,1:T(8,128)(2,1)S(1)} %get-tuple-element.59), channel_id=1, source_target_pairs={{0,16},{4,68},{8,24},{12,76},{16,0},{20,84},{24,8},{28,92},{32,48}... | collective-permute-start | bytes 393224 | tf_op jit(solution)/shard_map/ppermute | solution.py:193
  24.5 5.6 %collective-permute-start.6 = (bf16[128,512]{0,1:T(8,128)(2,1)S(1)}, bf16[128,512]{0,1:T(8,128)(2,1)S(1)}, u32[]{:S(2)}, u32[]{:S(2)}) collective-permute-start(bf16[128,512]{0,1:T(8,128)(2,1)S(1)} %add_convert_fusion.7), channel_id=1, source_target_pairs={{0,96},{4,28},{8,104},{12,20},{16,112},{20,12},{24,120},{28,4},{32... | collective-permute-start | bytes 393224 | tf_op jit(solution)/shard_map/ppermute | solution.py:197
  26.8 5.3 %collective-permute-start.5 = (bf16[128,512]{0,1:T(8,128)(2,1)S(1)}, bf16[128,512]{0,1:T(8,128)(2,1)S(1)}, u32[]{:S(2)}, u32[]{:S(2)}) collective-permute-start(bf16[128,512]{0,1:T(8,128)(2,1)S(1)} %add_convert_fusion.7), channel_id=1, source_target_pairs={{0,64},{4,20},{8,72},{12,28},{16,80},{20,4},{24,88},{28,12},{32,96... | collective-permute-start | bytes 393224 | tf_op jit(solution)/shard_map/ppermute | solution.py:197
  27.3 4.8 %collective-permute-start.4 = (bf16[128,512]{0,1:T(8,128)(2,1)S(1)}, bf16[128,512]{0,1:T(8,128)(2,1)S(1)}, u32[]{:S(2)}, u32[]{:S(2)}) collective-permute-start(bf16[128,512]{0,1:T(8,128)(2,1)S(1)} %add_convert_fusion.7), channel_id=1, source_target_pairs={{0,32},{4,12},{8,40},{12,4},{16,48},{20,28},{24,56},{28,20},{32,0}... | collective-permute-start | bytes 393224 | tf_op jit(solution)/shard_map/ppermute | solution.py:197
  33.0 6.2 %collective-permute-start.8 = (bf16[128,512]{0,1:T(8,128)(2,1)S(1)}, bf16[128,512]{0,1:T(8,128)(2,1)S(1)}, u32[]{:S(2)}, u32[]{:S(2)}) collective-permute-start(bf16[128,512]{0,1:T(8,128)(2,1)S(1)} %get-tuple-element.47), channel_id=1, source_target_pairs={{0,16},{4,68},{8,24},{12,76},{16,0},{20,84},{24,8},{28,92},{32,48}... | collective-permute-start | bytes 393224 | tf_op jit(solution)/shard_map/ppermute | solution.py:202
  34.9 5.7 %collective-permute-start.9 = (bf16[128,512]{0,1:T(8,128)(2,1)S(1)}, bf16[128,512]{0,1:T(8,128)(2,1)S(1)}, u32[]{:S(2)}, u32[]{:S(2)}) collective-permute-start(bf16[128,512]{0,1:T(8,128)(2,1)S(1)} %get-tuple-element.47), channel_id=1, source_target_pairs={{0,24},{4,100},{8,16},{12,108},{16,8},{20,116},{24,0},{28,124},{32... | collective-permute-start | bytes 393224 | tf_op jit(solution)/shard_map/ppermute | solution.py:202
  40.6 5.7 %collective-permute-start.10 = (bf16[512,512]{0,1:T(8,128)(2,1)S(1)}, bf16[512,512]{0,1:T(8,128)(2,1)S(1)}, u32[]{:S(2)}, u32[]{:S(2)}) collective-permute-start(bf16[512,512]{0,1:T(8,128)(2,1)S(1)} %constant_dynamic-update-slice_fusion.12), channel_id=1, source_target_pairs={{0,4},{4,0},{8,12},{12,8},{16,20},{20,16},{24,28},{28,24},{32,36},... | collective-permute-start | bytes 1572872 | tf_op jit(solution)/shard_map/ppermute | solution.py:206
  56.7 6.0 %collective-permute-start.14 = (bf16[128,512]{0,1:T(8,128)(2,1)}, bf16[128,512]{0,1:T(8,128)(2,1)}, u32[]{:S(2)}, u32[]{:S(2)}) collective-permute-start(bf16[128,512]{0,1:T(8,128)(2,1)} %get-tuple-element.55), channel_id=1, source_target_pairs={{0,24},{4,100},{8,16},{12,108},{16,8},{20,116},{24,0},{28,124},{32... | collective-permute-start | bytes 393224 | tf_op jit(solution)/shard_map/ppermute | solution.py:193
  59.1 5.9 %collective-permute-start.13 = (bf16[128,512]{0,1:T(8,128)(2,1)}, bf16[128,512]{0,1:T(8,128)(2,1)}, u32[]{:S(2)}, u32[]{:S(2)}) collective-permute-start(bf16[128,512]{0,1:T(8,128)(2,1)} %get-tuple-element.56), channel_id=1, source_target_pairs={{0,16},{4,68},{8,24},{12,76},{16,0},{20,84},{24,8},{28,92},{32,48}... | collective-permute-start | bytes 393224 | tf_op jit(solution)/shard_map/ppermute | solution.py:193
  66.0 8.1 %collective-permute-start.17 = (bf16[128,512]{0,1:T(8,128)(2,1)S(1)}, bf16[128,512]{0,1:T(8,128)(2,1)S(1)}, u32[]{:S(2)}, u32[]{:S(2)}) collective-permute-start(bf16[128,512]{0,1:T(8,128)(2,1)S(1)} %add_convert_fusion.5), channel_id=1, source_target_pairs={{0,96},{4,28},{8,104},{12,20},{16,112},{20,12},{24,120},{28,4},{32... | collective-permute-start | bytes 393224 | tf_op jit(solution)/shard_map/ppermute | solution.py:197
  68.1 6.1 %collective-permute-start.16 = (bf16[128,512]{0,1:T(8,128)(2,1)S(1)}, bf16[128,512]{0,1:T(8,128)(2,1)S(1)}, u32[]{:S(2)}, u32[]{:S(2)}) collective-permute-start(bf16[128,512]{0,1:T(8,128)(2,1)S(1)} %add_convert_fusion.5), channel_id=1, source_target_pairs={{0,64},{4,20},{8,72},{12,28},{16,80},{20,4},{24,88},{28,12},{32,96... | collective-permute-start | bytes 393224 | tf_op jit(solution)/shard_map/ppermute | solution.py:197
  68.1 6.1 %collective-permute-start.15 = (bf16[128,512]{0,1:T(8,128)(2,1)S(1)}, bf16[128,512]{0,1:T(8,128)(2,1)S(1)}, u32[]{:S(2)}, u32[]{:S(2)}) collective-permute-start(bf16[128,512]{0,1:T(8,128)(2,1)S(1)} %add_convert_fusion.5), channel_id=1, source_target_pairs={{0,32},{4,12},{8,40},{12,4},{16,48},{20,28},{24,56},{28,20},{32,0}... | collective-permute-start | bytes 393224 | tf_op jit(solution)/shard_map/ppermute | solution.py:197
  70.2 25.1 %collective-permute-start.25 = (f32[4,288]{1,0:T(4,128)S(1)}, f32[4,288]{1,0:T(4,128)S(1)}, u32[]{:S(2)}, u32[]{:S(2)}) collective-permute-start(f32[4,288]{1,0:T(4,128)S(1)} %get-tuple-element.65), channel_id=1, source_target_pairs={{0,1},{1,0},{2,3},{3,2},{4,5},{5,4},{6,7},{7,6},{8,9},{9,8},{10,11... | collective-permute-start | bytes 13832 | tf_op jit(solution)/shard_map/ppermute | solution.py:233
  71.9 26.1 %collective-permute-start.27 = (f32[4,288]{1,0:T(4,128)S(1)}, f32[4,288]{1,0:T(4,128)S(1)}, u32[]{:S(2)}, u32[]{:S(2)}) collective-permute-start(f32[4,288]{1,0:T(4,128)S(1)} %get-tuple-element.66), channel_id=1, source_target_pairs={{0,3},{1,2},{2,1},{3,0},{4,7},{5,6},{6,5},{7,4},{8,11},{9,10},{10,... | collective-permute-start | bytes 13832 | tf_op jit(solution)/shard_map/ppermute | solution.py:233
  74.3 5.6 %collective-permute-start.19 = (bf16[128,512]{0,1:T(8,128)(2,1)S(1)}, bf16[128,512]{0,1:T(8,128)(2,1)S(1)}, u32[]{:S(2)}, u32[]{:S(2)}) collective-permute-start(bf16[128,512]{0,1:T(8,128)(2,1)S(1)} %get-tuple-element.45), channel_id=1, source_target_pairs={{0,16},{4,68},{8,24},{12,76},{16,0},{20,84},{24,8},{28,92},{32,48}... | collective-permute-start | bytes 393224 | tf_op jit(solution)/shard_map/ppermute | solution.py:202
  74.8 5.0 %collective-permute-start.18 = (bf16[128,512]{0,1:T(8,128)(2,1)S(1)}, bf16[128,512]{0,1:T(8,128)(2,1)S(1)}, u32[]{:S(2)}, u32[]{:S(2)}) collective-permute-start(bf16[128,512]{0,1:T(8,128)(2,1)S(1)} %get-tuple-element.45), channel_id=1, source_target_pairs={{0,8},{4,36},{8,0},{12,44},{16,24},{20,52},{24,16},{28,60},{32,40}... | collective-permute-start | bytes 393224 | tf_op jit(solution)/shard_map/ppermute | solution.py:202
  76.4 5.4 %collective-permute-start.20 = (bf16[128,512]{0,1:T(8,128)(2,1)S(1)}, bf16[128,512]{0,1:T(8,128)(2,1)S(1)}, u32[]{:S(2)}, u32[]{:S(2)}) collective-permute-start(bf16[128,512]{0,1:T(8,128)(2,1)S(1)} %get-tuple-element.45), channel_id=1, source_target_pairs={{0,24},{4,100},{8,16},{12,108},{16,8},{20,116},{24,0},{28,124},{32... | collective-permute-start | bytes 393224 | tf_op jit(solution)/shard_map/ppermute | solution.py:202
  81.8 5.2 %collective-permute-start.21 = (bf16[512,512]{0,1:T(8,128)(2,1)S(1)}, bf16[512,512]{0,1:T(8,128)(2,1)S(1)}, u32[]{:S(2)}, u32[]{:S(2)}) collective-permute-start(bf16[512,512]{0,1:T(8,128)(2,1)S(1)} %constant_dynamic-update-slice_fusion.8), channel_id=1, source_target_pairs={{0,4},{4,0},{8,12},{12,8},{16,20},{20,16},{24,28},{28,24},{32,36},... | collective-permute-start | bytes 1572872 | tf_op jit(solution)/shard_map/ppermute | solution.py:206
  91.7 22.4 %collective-permute-start.24 = (f16[1168,128]{1,0:T(8,128)(2,1)}, f16[1168,128]{1,0:T(8,128)(2,1)}, u32[]{:S(2)}, u32[]{:S(2)}) collective-permute-start(f16[1168,128]{1,0:T(8,128)(2,1)} %convert_element_type.261), channel_id=1, source_target_pairs={{0,3},{1,2},{2,1},{3,0},{4,7},{5,6},{6,5},{7,4},{8,11},{9,10},{10,... | collective-permute-start | bytes 897032 | tf_op jit(solution)/shard_map/ppermute | solution.py:220
  94.8 20.5 %collective-permute-start.23 = (f16[1168,128]{1,0:T(8,128)(2,1)}, f16[1168,128]{1,0:T(8,128)(2,1)}, u32[]{:S(2)}, u32[]{:S(2)}) collective-permute-start(f16[1168,128]{1,0:T(8,128)(2,1)} %convert_element_type.259), channel_id=1, source_target_pairs={{0,2},{1,3},{2,0},{3,1},{4,6},{5,7},{6,4},{7,5},{8,10},{9,11},{10,... | collective-permute-start | bytes 897032 | tf_op jit(solution)/shard_map/ppermute | solution.py:220
  94.8 21.5 %collective-permute-start.22 = (f16[1168,128]{1,0:T(8,128)(2,1)}, f16[1168,128]{1,0:T(8,128)(2,1)}, u32[]{:S(2)}, u32[]{:S(2)}) collective-permute-start(f16[1168,128]{1,0:T(8,128)(2,1)} %convert_element_type.257), channel_id=1, source_target_pairs={{0,1},{1,0},{2,3},{3,2},{4,5},{5,4},{6,7},{7,6},{8,9},{9,8},{10,11... | collective-permute-start | bytes 897032 | tf_op jit(solution)/shard_map/ppermute | solution.py:220
  95.4 15.4 %collective-permute-start.26 = (f32[4,288]{1,0:T(4,128)S(1)}, f32[4,288]{1,0:T(4,128)S(1)}, u32[]{:S(2)}, u32[]{:S(2)}) collective-permute-start(f32[4,288]{1,0:T(4,128)S(1)} %get-tuple-element.67), channel_id=1, source_target_pairs={{0,2},{1,3},{2,0},{3,1},{4,6},{5,7},{6,4},{7,5},{8,10},{9,11},{10,... | collective-permute-start | bytes 13832 | tf_op jit(solution)/shard_map/ppermute | solution.py:233
  124.4 16.1 %collective-permute-start.30 = (f16[1168,128]{1,0:T(8,128)(2,1)S(1)}, f16[1168,128]{1,0:T(8,128)(2,1)S(1)}, u32[]{:S(2)}, u32[]{:S(2)}) collective-permute-start(f16[1168,128]{1,0:T(8,128)(2,1)S(1)} %convert_element_type.267), channel_id=1, source_target_pairs={{0,3},{1,2},{2,1},{3,0},{4,7},{5,6},{6,5},{7,4},{8,11},{9,10},{10,... | collective-permute-start | bytes 897032 | tf_op jit(solution)/shard_map/ppermute | solution.py:220
  124.7 15.8 %collective-permute-start.29 = (f16[1168,128]{1,0:T(8,128)(2,1)S(1)}, f16[1168,128]{1,0:T(8,128)(2,1)S(1)}, u32[]{:S(2)}, u32[]{:S(2)}) collective-permute-start(f16[1168,128]{1,0:T(8,128)(2,1)S(1)} %convert_element_type.265), channel_id=1, source_target_pairs={{0,2},{1,3},{2,0},{3,1},{4,6},{5,7},{6,4},{7,5},{8,10},{9,11},{10,... | collective-permute-start | bytes 897032 | tf_op jit(solution)/shard_map/ppermute | solution.py:220
  125.8 14.7 %collective-permute-start.28 = (f16[1168,128]{1,0:T(8,128)(2,1)S(1)}, f16[1168,128]{1,0:T(8,128)(2,1)S(1)}, u32[]{:S(2)}, u32[]{:S(2)}) collective-permute-start(f16[1168,128]{1,0:T(8,128)(2,1)S(1)} %convert_element_type.263), channel_id=1, source_target_pairs={{0,1},{1,0},{2,3},{3,2},{4,5},{5,4},{6,7},{7,6},{8,9},{9,8},{10,11... | collective-permute-start | bytes 897032 | tf_op jit(solution)/shard_map/ppermute | solution.py:220
  153.6 5.6 %collective-permute-start.34 = (bf16[128,512]{0,1:T(8,128)(2,1)S(1)}, bf16[128,512]{0,1:T(8,128)(2,1)S(1)}, u32[]{:S(2)}, u32[]{:S(2)}) collective-permute-start(bf16[128,512]{0,1:T(8,128)(2,1)S(1)} %get-tuple-element.52), channel_id=1, source_target_pairs={{0,24},{4,100},{8,16},{12,108},{16,8},{20,116},{24,0},{28,124},{32... | collective-permute-start | bytes 393224 | tf_op jit(solution)/shard_map/ppermute | solution.py:193
  155.9 5.6 %collective-permute-start.33 = (bf16[128,512]{0,1:T(8,128)(2,1)S(1)}, bf16[128,512]{0,1:T(8,128)(2,1)S(1)}, u32[]{:S(2)}, u32[]{:S(2)}) collective-permute-start(bf16[128,512]{0,1:T(8,128)(2,1)S(1)} %get-tuple-element.53), channel_id=1, source_target_pairs={{0,16},{4,68},{8,24},{12,76},{16,0},{20,84},{24,8},{28,92},{32,48}... | collective-permute-start | bytes 393224 | tf_op jit(solution)/shard_map/ppermute | solution.py:193
  161.6 5.4 %collective-permute-start.37 = (bf16[128,512]{0,1:T(8,128)(2,1)S(1)}, bf16[128,512]{0,1:T(8,128)(2,1)S(1)}, u32[]{:S(2)}, u32[]{:S(2)}) collective-permute-start(bf16[128,512]{0,1:T(8,128)(2,1)S(1)} %add_convert_fusion.3), channel_id=1, source_target_pairs={{0,96},{4,28},{8,104},{12,20},{16,112},{20,12},{24,120},{28,4},{32... | collective-permute-start | bytes 393224 | tf_op jit(solution)/shard_map/ppermute | solution.py:197
  163.7 5.3 %collective-permute-start.36 = (bf16[128,512]{0,1:T(8,128)(2,1)S(1)}, bf16[128,512]{0,1:T(8,128)(2,1)S(1)}, u32[]{:S(2)}, u32[]{:S(2)}) collective-permute-start(bf16[128,512]{0,1:T(8,128)(2,1)S(1)} %add_convert_fusion.3), channel_id=1, source_target_pairs={{0,64},{4,20},{8,72},{12,28},{16,80},{20,4},{24,88},{28,12},{32,96... | collective-permute-start | bytes 393224 | tf_op jit(solution)/shard_map/ppermute | solution.py:197
  164.1 4.9 %collective-permute-start.35 = (bf16[128,512]{0,1:T(8,128)(2,1)S(1)}, bf16[128,512]{0,1:T(8,128)(2,1)S(1)}, u32[]{:S(2)}, u32[]{:S(2)}) collective-permute-start(bf16[128,512]{0,1:T(8,128)(2,1)S(1)} %add_convert_fusion.3), channel_id=1, source_target_pairs={{0,32},{4,12},{8,40},{12,4},{16,48},{20,28},{24,56},{28,20},{32,0}... | collective-permute-start | bytes 393224 | tf_op jit(solution)/shard_map/ppermute | solution.py:197
  169.2 6.3 %collective-permute-start.39 = (bf16[128,512]{0,1:T(8,128)(2,1)S(1)}, bf16[128,512]{0,1:T(8,128)(2,1)S(1)}, u32[]{:S(2)}, u32[]{:S(2)}) collective-permute-start(bf16[128,512]{0,1:T(8,128)(2,1)S(1)} %get-tuple-element.43), channel_id=1, source_target_pairs={{0,16},{4,68},{8,24},{12,76},{16,0},{20,84},{24,8},{28,92},{32,48}... | collective-permute-start | bytes 393224 | tf_op jit(solution)/shard_map/ppermute | solution.py:202
  171.8 5.5 %collective-permute-start.40 = (bf16[128,512]{0,1:T(8,128)(2,1)S(1)}, bf16[128,512]{0,1:T(8,128)(2,1)S(1)}, u32[]{:S(2)}, u32[]{:S(2)}) collective-permute-start(bf16[128,512]{0,1:T(8,128)(2,1)S(1)} %get-tuple-element.43), channel_id=1, source_target_pairs={{0,24},{4,100},{8,16},{12,108},{16,8},{20,116},{24,0},{28,124},{32... | collective-permute-start | bytes 393224 | tf_op jit(solution)/shard_map/ppermute | solution.py:202
  177.3 5.2 %collective-permute-start.41 = (bf16[512,512]{0,1:T(8,128)(2,1)S(1)}, bf16[512,512]{0,1:T(8,128)(2,1)S(1)}, u32[]{:S(2)}, u32[]{:S(2)}) collective-permute-start(bf16[512,512]{0,1:T(8,128)(2,1)S(1)} %constant_dynamic-update-slice_fusion.4), channel_id=1, source_target_pairs={{0,4},{4,0},{8,12},{12,8},{16,20},{20,16},{24,28},{28,24},{32,36},... | collective-permute-start | bytes 1572872 | tf_op jit(solution)/shard_map/ppermute | solution.py:206
  194.6 6.1 %collective-permute-start.45 = (bf16[128,512]{0,1:T(8,128)(2,1)S(1)}, bf16[128,512]{0,1:T(8,128)(2,1)S(1)}, u32[]{:S(2)}, u32[]{:S(2)}) collective-permute-start(bf16[128,512]{0,1:T(8,128)(2,1)S(1)} %get-tuple-element.49), channel_id=1, source_target_pairs={{0,24},{4,100},{8,16},{12,108},{16,8},{20,116},{24,0},{28,124},{32... | collective-permute-start | bytes 393224 | tf_op jit(solution)/shard_map/ppermute | solution.py:193
  197.4 5.3 %collective-permute-start.44 = (bf16[128,512]{0,1:T(8,128)(2,1)S(1)}, bf16[128,512]{0,1:T(8,128)(2,1)S(1)}, u32[]{:S(2)}, u32[]{:S(2)}) collective-permute-start(bf16[128,512]{0,1:T(8,128)(2,1)S(1)} %get-tuple-element.50), channel_id=1, source_target_pairs={{0,16},{4,68},{8,24},{12,76},{16,0},{20,84},{24,8},{28,92},{32,48}... | collective-permute-start | bytes 393224 | tf_op jit(solution)/shard_map/ppermute | solution.py:193
  202.7 5.6 %collective-permute-start.48 = (bf16[128,512]{0,1:T(8,128)(2,1)S(1)}, bf16[128,512]{0,1:T(8,128)(2,1)S(1)}, u32[]{:S(2)}, u32[]{:S(2)}) collective-permute-start(bf16[128,512]{0,1:T(8,128)(2,1)S(1)} %add_convert_fusion.1), channel_id=1, source_target_pairs={{0,96},{4,28},{8,104},{12,20},{16,112},{20,12},{24,120},{28,4},{32... | collective-permute-start | bytes 393224 | tf_op jit(solution)/shard_map/ppermute | solution.py:197
  205.0 5.6 %collective-permute-start.47 = (bf16[128,512]{0,1:T(8,128)(2,1)S(1)}, bf16[128,512]{0,1:T(8,128)(2,1)S(1)}, u32[]{:S(2)}, u32[]{:S(2)}) collective-permute-start(bf16[128,512]{0,1:T(8,128)(2,1)S(1)} %add_convert_fusion.1), channel_id=1, source_target_pairs={{0,64},{4,20},{8,72},{12,28},{16,80},{20,4},{24,88},{28,12},{32,96... | collective-permute-start | bytes 393224 | tf_op jit(solution)/shard_map/ppermute | solution.py:197
  205.0 5.6 %collective-permute-start.46 = (bf16[128,512]{0,1:T(8,128)(2,1)S(1)}, bf16[128,512]{0,1:T(8,128)(2,1)S(1)}, u32[]{:S(2)}, u32[]{:S(2)}) collective-permute-start(bf16[128,512]{0,1:T(8,128)(2,1)S(1)} %add_convert_fusion.1), channel_id=1, source_target_pairs={{0,32},{4,12},{8,40},{12,4},{16,48},{20,28},{24,56},{28,20},{32,0}... | collective-permute-start | bytes 393224 | tf_op jit(solution)/shard_map/ppermute | solution.py:197
  210.9 6.1 %collective-permute-start.50 = (bf16[128,512]{0,1:T(8,128)(2,1)S(1)}, bf16[128,512]{0,1:T(8,128)(2,1)S(1)}, u32[]{:S(2)}, u32[]{:S(2)}) collective-permute-start(bf16[128,512]{0,1:T(8,128)(2,1)S(1)} %get-tuple-element.41), channel_id=1, source_target_pairs={{0,16},{4,68},{8,24},{12,76},{16,0},{20,84},{24,8},{28,92},{32,48}... | collective-permute-start | bytes 393224 | tf_op jit(solution)/shard_map/ppermute | solution.py:202
  213.2 5.5 %collective-permute-start.51 = (bf16[128,512]{0,1:T(8,128)(2,1)S(1)}, bf16[128,512]{0,1:T(8,128)(2,1)S(1)}, u32[]{:S(2)}, u32[]{:S(2)}) collective-permute-start(bf16[128,512]{0,1:T(8,128)(2,1)S(1)} %get-tuple-element.41), channel_id=1, source_target_pairs={{0,24},{4,100},{8,16},{12,108},{16,8},{20,116},{24,0},{28,124},{32... | collective-permute-start | bytes 393224 | tf_op jit(solution)/shard_map/ppermute | solution.py:202
  218.7 4.5 %collective-permute-start.52 = (bf16[512,512]{0,1:T(8,128)(2,1)S(1)}, bf16[512,512]{0,1:T(8,128)(2,1)S(1)}, u32[]{:S(2)}, u32[]{:S(2)}) collective-permute-start(bf16[512,512]{0,1:T(8,128)(2,1)S(1)} %constant_dynamic-update-slice_fusion), channel_id=1, source_target_pairs={{0,4},{4,0},{8,12},{12,8},{16,20},{20,16},{24,28},{28,24},{32,36},... | collective-permute-start | bytes 1572872 | tf_op jit(solution)/shard_map/ppermute | solution.py:206
  225.7 16.1 %collective-permute-start.55 = (f16[1168,128]{1,0:T(8,128)(2,1)S(1)}, f16[1168,128]{1,0:T(8,128)(2,1)S(1)}, u32[]{:S(2)}, u32[]{:S(2)}) collective-permute-start(f16[1168,128]{1,0:T(8,128)(2,1)S(1)} %convert_element_type.298), channel_id=1, source_target_pairs={{0,3},{1,2},{2,1},{3,0},{4,7},{5,6},{6,5},{7,4},{8,11},{9,10},{10,... | collective-permute-start | bytes 897032 | tf_op jit(solution)/shard_map/ppermute | solution.py:220
  226.1 15.8 %collective-permute-start.54 = (f16[1168,128]{1,0:T(8,128)(2,1)S(1)}, f16[1168,128]{1,0:T(8,128)(2,1)S(1)}, u32[]{:S(2)}, u32[]{:S(2)}) collective-permute-start(f16[1168,128]{1,0:T(8,128)(2,1)S(1)} %convert_element_type.296), channel_id=1, source_target_pairs={{0,2},{1,3},{2,0},{3,1},{4,6},{5,7},{6,4},{7,5},{8,10},{9,11},{10,... | collective-permute-start | bytes 897032 | tf_op jit(solution)/shard_map/ppermute | solution.py:220
  227.2 14.9 %collective-permute-start.53 = (f16[1168,128]{1,0:T(8,128)(2,1)S(1)}, f16[1168,128]{1,0:T(8,128)(2,1)S(1)}, u32[]{:S(2)}, u32[]{:S(2)}) collective-permute-start(f16[1168,128]{1,0:T(8,128)(2,1)S(1)} %convert_element_type.294), channel_id=1, source_target_pairs={{0,1},{1,0},{2,3},{3,2},{4,5},{5,4},{6,7},{7,6},{8,9},{9,8},{10,11... | collective-permute-start | bytes 897032 | tf_op jit(solution)/shard_map/ppermute | solution.py:220
  248.5 16.1 %collective-permute-start.58 = (f16[1168,128]{1,0:T(8,128)(2,1)S(1)}, f16[1168,128]{1,0:T(8,128)(2,1)S(1)}, u32[]{:S(2)}, u32[]{:S(2)}) collective-permute-start(f16[1168,128]{1,0:T(8,128)(2,1)S(1)} %convert_element_type.304), channel_id=1, source_target_pairs={{0,3},{1,2},{2,1},{3,0},{4,7},{5,6},{6,5},{7,4},{8,11},{9,10},{10,... | collective-permute-start | bytes 897032 | tf_op jit(solution)/shard_map/ppermute | solution.py:220
  248.9 15.7 %collective-permute-start.57 = (f16[1168,128]{1,0:T(8,128)(2,1)S(1)}, f16[1168,128]{1,0:T(8,128)(2,1)S(1)}, u32[]{:S(2)}, u32[]{:S(2)}) collective-permute-start(f16[1168,128]{1,0:T(8,128)(2,1)S(1)} %convert_element_type.302), channel_id=1, source_target_pairs={{0,2},{1,3},{2,0},{3,1},{4,6},{5,7},{6,4},{7,5},{8,10},{9,11},{10,... | collective-permute-start | bytes 897032 | tf_op jit(solution)/shard_map/ppermute | solution.py:220
  250.0 14.7 %collective-permute-start.56 = (f16[1168,128]{1,0:T(8,128)(2,1)S(1)}, f16[1168,128]{1,0:T(8,128)(2,1)S(1)}, u32[]{:S(2)}, u32[]{:S(2)}) collective-permute-start(f16[1168,128]{1,0:T(8,128)(2,1)S(1)} %convert_element_type.300), channel_id=1, source_target_pairs={{0,1},{1,0},{2,3},{3,2},{4,5},{5,4},{6,7},{7,6},{8,9},{9,8},{10,11... | collective-permute-start | bytes 897032 | tf_op jit(solution)/shard_map/ppermute | solution.py:220
  (32 other events, 225.3 us)

commit v2 on v1

--- a/solution.py
+++ b/solution.py
@@ -1,3 +1,5 @@
+from functools import partial
+
 import jax
 import jax.numpy as jnp
 from jax import lax
@@ -42,38 +44,68 @@
     return power, jnp.exp2(-power)
 
 
-def pack_body(z_ref, amp_ref, own_ref, *sent):
-    nf, rows, cols = amp_ref.shape
+def round_body(right_ref, rounded_ref):
+    nf, rows, cols = right_ref.shape
+    for f in range(nf):
+        rounded_ref[:, f * cols : (f + 1) * cols] = right_ref[f].astype(BF16)
+
+
+def gather_parts(core_ref, mine_ref, other_ref, whole):
+    half = mine_ref.shape[0]
+    core = core_ref[0]
+    whole[pl.ds(pl.multiple_of(core * half, half), half), :] = mine_ref[...]
+    whole[pl.ds(pl.multiple_of((1 - core) * half, half), half), :] = other_ref[...]
+
+
+def ladder_body(core_ref, factors_ref, mine_ref, other_ref, sources_ref, weight_ref,
+                rounded_ref, whole):
+    nf, rows, cols = sources_ref.shape
+    gather_parts(core_ref, mine_ref, other_ref, whole)
+    span = rows // SIDE
+
+    def step(r, carry):
+        at = pl.ds(pl.multiple_of(r * span, RUN), span)
+        spread = jnp.dot(factors_ref[at, :], whole[...], preferred_element_type=F32)
+        for f in range(nf):
+            lanes = slice(f * cols, (f + 1) * cols)
+            value = sources_ref[f, at, :] + weight_ref[at, f : f + 1] * spread[:, lanes]
+            rounded_ref[at, lanes] = value.astype(BF16)
+        return carry
+
+    lax.fori_loop(0, SIDE, step, 0)
+
+
+def pack_body(offset, core_ref, z_ref, factors_ref, mine_ref, other_ref, sources_ref,
+              weight_ref, sent_ref, whole):
+    nf, rows, cols = sources_ref.shape
     quarter = rows // SIDE
-    groups = quarter // RUN
-    z = z_ref[0]
-    peak = jnp.max(jnp.abs(amp_ref[0]), axis=0, keepdims=True)
-    for f in range(1, nf):
-        peak = jnp.maximum(peak, jnp.max(jnp.abs(amp_ref[f]), axis=0, keepdims=True))
-    peak = jnp.broadcast_to(jnp.max(peak, axis=1, keepdims=True), (1, cols))
-    power, scale = scale_of(peak)
-    scale = jnp.broadcast_to(scale, (RUN, cols))
-    for d in range(SIDE):
-        base = (z ^ d) * quarter
-
-        def step(g, carry, d=d, base=base):
-            for f in range(nf):
-                tile = amp_ref[f, pl.ds(pl.multiple_of(base + g * RUN, RUN), RUN), :]
-                spot = pl.ds(pl.multiple_of((g * nf + f) * RUN, RUN), RUN)
-                if d == 0:
-                    own_ref[spot, :] = tile
-                else:
-                    sent[d - 1][spot, :] = tile * scale
-            return carry
-
-        lax.fori_loop(0, groups, step, 0)
-        if d:
-            sent[d - 1][nf * quarter :, :] = jnp.broadcast_to(power, (RUN, cols))
-
-
-def mix_body(own_ref, got1, got2, got3, kernel_ref, into_ref, out_ref, kept, *sent):
-    body, cols = own_ref.shape
-    block = body * SIDE // kernel_ref.shape[0]
+    body = sent_ref.shape[1] - RUN
+    length = body // nf
+    gather_parts(core_ref, mine_ref, other_ref, whole)
+
+    def block(d, peak):
+        base = pl.multiple_of((z_ref[0] ^ d) * quarter + offset, RUN)
+        at = pl.ds(base, length)
+        spread = jnp.dot(factors_ref[at, :], whole[...], preferred_element_type=F32)
+        for f in range(nf):
+            value = sources_ref[f, at, :] + weight_ref[at, f : f + 1] * spread[:, f * cols : (f + 1) * cols]
+            for g in range(length // RUN):
+                tile = value[g * RUN : (g + 1) * RUN]
+                sent_ref[d, (g * nf + f) * RUN : (g * nf + f + 1) * RUN, :] = tile
+                peak = jnp.maximum(peak, jnp.abs(tile))
+        return peak
+
+    peak = lax.fori_loop(0, SIDE, block, jnp.zeros((RUN, cols), F32))
+    peak = jnp.max(jnp.max(peak, axis=0, keepdims=True), axis=1, keepdims=True)
+    power, scale = scale_of(jnp.broadcast_to(peak, (1, cols)))
+    for d in range(1, SIDE):
+        sent_ref[d, :body, :] = sent_ref[d, :body, :] * jnp.broadcast_to(scale, (body, cols))
+        sent_ref[d, body:, :] = jnp.broadcast_to(power, (RUN, cols))
+
+
+def mix_body(own_ref, got1, got2, got3, kernel_ref, into_ref, out_ref, sent_ref):
+    cols = own_ref.shape[2]
+    body = own_ref.shape[1] - RUN
     size = into_ref.shape[1]
     part = size // SIDE
     got = (got1, got2, got3)
@@ -93,7 +125,7 @@
             at = pl.ds(pl.multiple_of((2 * g + half) * part, part), part)
             sides.append(
                 jnp.concatenate(
-                    [own_ref[at, :]] + [r[at, :] * s for r, s in zip(got, gains)], axis=0
+                    [own_ref[0, at, :]] + [r[at, :] * s for r, s in zip(got, gains)], axis=0
                 )
             )
             kernels.append(
@@ -106,48 +138,45 @@
             at = pl.ds(pl.multiple_of((2 * g + half) * part, part), part)
             for d in range(SIDE):
                 tile = renewed[d * part : (d + 1) * part, half * cols : (half + 1) * cols]
-                if d == 0:
-                    kept[at, :] = tile
-                else:
-                    sent[d - 1][at, :] = tile
+                sent_ref[d, at, :] = tile
+                if d:
                     fresh[d - 1] = jnp.maximum(fresh[d - 1], jnp.abs(tile))
         return tuple(fresh)
 
     start = tuple(jnp.zeros((part, cols), F32) for _ in range(3))
     peaks = lax.fori_loop(0, body // part // 2, step, start)
-    for ref, peak in zip(sent, peaks):
+    for d, peak in enumerate(peaks, 1):
         peak = jnp.max(jnp.max(peak, axis=0, keepdims=True), axis=1, keepdims=True)
         power, scale = scale_of(jnp.broadcast_to(peak, (1, cols)))
-        ref[:body, :] = ref[:body, :] * jnp.broadcast_to(scale, (body, cols))
-        ref[body:, :] = jnp.broadcast_to(power, (RUN, cols))
-
-
-def unpack_body(z_ref, right_ref, own_ref, got1, got2, got3, sources_ref, rounded_ref):
+        sent_ref[d, :body, :] = sent_ref[d, :body, :] * jnp.broadcast_to(scale, (body, cols))
+        sent_ref[d, body:, :] = jnp.broadcast_to(power, (RUN, cols))
+
+
+def unpack_body(splits, z_ref, right_ref, *refs):
     nf, rows, cols = right_ref.shape
     quarter = rows // SIDE
-    groups = quarter // RUN
-    body = nf * quarter
     z = z_ref[0]
-    for d, ref in enumerate((own_ref, got1, got2, got3)):
-        base = (z ^ d) * quarter
-        if d:
-            gain = jnp.exp2(jnp.broadcast_to(ref[body : body + 1, :], (RUN, cols)))
-
-        def step(g, carry, d=d, base=base, ref=ref, gain=gain if d else None):
-            for f in range(nf):
-                tile = ref[pl.ds(pl.multiple_of((g * nf + f) * RUN, RUN), RUN), :]
-                if d:
-                    tile = tile * gain
+    sources_ref, rounded_ref = refs[-2:]
+    for h, (offset, length) in enumerate(splits):
+        body = nf * length
+        for d, ref in enumerate(refs[h * SIDE : (h + 1) * SIDE]):
+            base = (z ^ d) * quarter + offset
+            gain = jnp.exp2(jnp.broadcast_to(ref[body : body + 1, :], (RUN, cols))) if d else None
+
+            def step(g, carry, d=d, base=base, ref=ref, gain=gain):
                 at = pl.ds(pl.multiple_of(base + g * RUN, RUN), RUN)
-                tile = right_ref[f, at, :] + tile
-                sources_ref[f, at, :] = tile
-                rounded_ref[f, at, :] = tile.astype(BF16)
-            return carry
-
-        lax.fori_loop(0, groups, step, 0)
-
-
-def call(body, outs, name, scalars=0, args=()):
+                for f in range(nf):
+                    spot = pl.ds(pl.multiple_of((g * nf + f) * RUN, RUN), RUN)
+                    tile = ref[spot, :] * gain if d else ref[0, spot, :]
+                    tile = right_ref[f, at, :] + tile
+                    sources_ref[f, at, :] = tile
+                    rounded_ref[at, f * cols : (f + 1) * cols] = tile.astype(BF16)
+                return carry
+
+            lax.fori_loop(0, length // RUN, step, 0)
+
+
+def call(body, outs, name, scalars=0, args=(), scratch=()):
     spec = pl.BlockSpec(memory_space=pltpu.VMEM)
     flat = pl.BlockSpec(memory_space=pltpu.SMEM)
     return pl.pallas_call(
@@ -155,6 +184,7 @@
         out_shape=[jax.ShapeDtypeStruct(s, t) for s, t in outs],
         in_specs=[flat] * scalars + [spec] * (len(args) - scalars),
         out_specs=[spec] * len(outs),
+        scratch_shapes=list(scratch),
         compiler_params=pltpu.CompilerParams(vmem_limit_bytes=40 << 20),
         interpret=INTERPRET,
         name=name,
@@ -177,9 +207,9 @@
     factors_send = lax.dynamic_slice(factors, (0, (1 - core) * half), (rows, half))
 
     def project(table, rounded):
-        return jnp.einsum(
-            "pa,fpc->afc", table, rounded, preferred_element_type=F32
-        ).reshape(half, wide)
+        return lax.dot_general(
+            table, rounded, (((0,), (0,)), ((), ())), preferred_element_type=F32
+        )
 
     def reduce_all(rounded):
         sent = project(factors_send, rounded)
@@ -217,8 +247,8 @@
 
     def exchange(sent):
         return [
-            lax.ppermute(load.astype(F16), "freq", swap(d + 1)).astype(F32)
-            for d, load in enumerate(sent)
+            lax.ppermute(sent[d].astype(F16), "freq", swap(d)).astype(F32)
+            for d in range(1, SIDE)
         ]
 
     body = nf * quarter
@@ -252,20 +282,48 @@
     table_out = spread_table(source, backward, source)
     loads = [((body, cols), F32)] + [((body + RUN, cols), F32)] * 3
 
+    core_at = jnp.full((1,), core, jnp.int32)
+    column = pair_weight.T
+    whole = [pltpu.VMEM((naux, wide), BF16)]
+    pair = 2 * RUN
+    first = (quarter // pair + 1) // 2 * pair
+    splits = ((0, first), (first, quarter - first))
+
     sources = right_side
-    rounded = right_side.astype(BF16)
+    (rounded,) = call(round_body, [((rows, wide), BF16)], "round", 0, (right_side,))
     for outer in range(OUTER):
-        for inner in range(INNER):
-            amplitude = sources + weight * spread_of(reduce_all(rounded))
-            rounded = amplitude.astype(BF16)
-        own, *sent = call(pack_body, loads, "pack", 1, (place_z, amplitude))
-        got = exchange(sent)
-        own, *sent = call(mix_body, loads, "mix", 0, (own, *got, kernel, table_in, table_out))
-        got = exchange(sent)
+        for inner in range(INNER - 1):
+            parts = reduce_all(rounded)
+            (rounded,) = call(
+                ladder_body, [((rows, wide), BF16)], "ladder", 1,
+                (core_at, factors, *parts, sources, column), whole,
+            )
+        parts = reduce_all(rounded)
+        packed = []
+        for offset, length in splits:
+            body = nf * length
+            loads = [((SIDE, body + RUN, cols), F32)]
+            (sent,) = call(
+                partial(pack_body, offset), loads, "pack", 2,
+                (core_at, place_z, factors, *parts, sources, column), whole,
+            )
+            packed.append((sent, exchange(sent)))
+        back = []
+        for (offset, length), (own, got) in zip(splits, packed):
+            body = nf * length
+            loads = [((SIDE, body + RUN, cols), F32)]
+            (sent,) = call(
+                mix_body, loads, "mix", 0,
+                (own, *got, kernel[offset * nf * SIDE : (offset + length) * nf * SIDE],
+                 table_in, table_out),
+            )
+            back += [sent, *exchange(sent)]
+        if outer == OUTER - 1:
+            amplitude = sources + weight * spread_of(parts)
         sources, rounded = call(
-            unpack_body,
-            [(right_side.shape, F32), (right_side.shape, BF16)],
-            "unpack", 1, (place_z, right_side, own, *got),
+            partial(unpack_body, splits),
+            [(right_side.shape, F32), ((rows, wide), BF16)],
+            "unpack", 1, (place_z, right_side, *back),
         )
     return (amplitude, sources)
 

time: 269 us -> 268 us (level)
  waiting for transfers between devices: 115 us -> 75 us
  starting transfers between devices: 81.8 us -> 109 us
  Pallas kernels: 16.9 us -> 31.9 us
  matrix products: 24 us -> 16.1 us
  local copies, waits for them, and re-layouts: 17.6 us -> 24.4 us
  other arithmetic: 10.7 us -> 6.14 us
    ppermute x12 -> x24, waiting for transfers between devices: 38 us -> 19.2 us  [exchange(): lax.ppermute(sent[d].astype(F16), 'freq', swap(d)).astype(F32)]
    ppermute x12 -> x24, starting transfers between devices: 13.8 us -> 29.2 us  [exchange(): lax.ppermute(sent[d].astype(F16), 'freq', swap(d)).astype(F32)]
    pallas_call x6 -> x13, Pallas kernels: 16.9 us -> 31.9 us  [call(): pl.pallas_call(body, out_shape=[jax.ShapeDtypeStruct(s, t) for s, t in ou...]
    unnamed x8 -> x0, matrix products: 14.5 us -> none
    ppermute x3, waiting for transfers between devices: 12.8 us -> 0.01 us  [shards(): kernel.append(lax.ppermute(piece, 'freq', swap(d)))]
    dot_general x0 -> x8, matrix products: none -> 11.8 us  [project(): lax.dot_general(table, rounded, (((0,), (0,)), ((), ())), preferred_eleme...]
    unnamed x42 -> x61, local copies, waits for them, and re-layouts: 3.48 us -> 9.56 us
    ppermute x4, starting transfers between devices: 14.5 us -> 20.4 us  [reduce_all(): other = lax.ppermute(gathered, 'fac', CORES)]
  transfers between devices with their start and end apart: 59 -> 71, of which waited for: 39 -> 42; matrix products, arithmetic and copies ran while one was open for 5% -> 10% of each run, Pallas kernels for 0% -> 7%
where the time goes in v2:
time: 268 us; the launch traced here: 264 us
  starting transfers between devices  109 us (41%)
  waiting for transfers between devices  75 us (28%)
  Pallas kernels  31.9 us (12%)
  local copies, waits for them, and re-layouts  24.4 us (9%)
  matrix products  16.1 us (6%)
  other arithmetic  6.14 us (2%)
    pallas_call x13, Pallas kernels, call(): pl.pallas_call(body, out_shape=[jax.ShapeDtypeStruct(s, t) for s, t in ou...  31.9 us
    ppermute x24, starting transfers between devices, exchange(): lax.ppermute(sent[d].astype(F16), 'freq', swap(d)).astype(F32)  29.2 us
    ppermute x4, starting transfers between devices, reduce_all(): other = lax.ppermute(gathered, 'fac', CORES)  20.4 us
    ppermute x24, waiting for transfers between devices, exchange(): lax.ppermute(sent[d].astype(F16), 'freq', swap(d)).astype(F32)  19.2 us
    ppermute x12, starting transfers between devices, reduce_all(): piece = lax.ppermute(total, 'fac', along(d, True))  17.2 us
    ppermute x12, waiting for transfers between devices, reduce_all(): own = own + lax.ppermute(piece, 'fac', along(d, True)).astype(F32)  16.6 us
    ppermute x12, starting transfers between devices, reduce_all(): own = own + lax.ppermute(piece, 'fac', along(d, True)).astype(F32)  15.9 us
    ppermute x12, starting transfers between devices, reduce_all(): total = total + lax.ppermute(own, 'fac', along(d, False)).astype(F32)  15.7 us
  transfers between devices with their start and end apart: 71, of which 42 were waited for; matrix products, arithmetic and copies ran while one was open for 10% of the time, Pallas kernels for 7%

profile of v2, /device:TPU:1, one launch (start us, length us, event | category | flops | bytes accessed | tf_op | source)
XLA Modules:
  0.0 264.3 jit_solution(11918655458854471858)
XLA Ops:
  7.3 2.6 collective-permute-done
  9.9 2.1 convolution_add_fusion.4
  14.5 2.6 collective-permute-start.2
  17.2 3.9 %collective-permute-done.2 = bf16[128,512]{1,0:T(8,128)(2,1)S(1)} collective-permute-done((bf16[128,512]{1,0:T(8,128)(2,1)S(1)}, bf16[128,512]{1,0:T(8,128)(2,1)S(1)}, u32[]{:S(2)}, u32[]{:S(2)}) %collective-permute-start.2) | collective-permute-done | bytes 131104 | tf_op jit(solution)/shard_map/ppermute | solution.py:223
  24.6 2.4 collective-permute-start.5
  27.5 3.3 %collective-permute-done.5 = bf16[128,512]{1,0:T(8,128)(2,1)S(1)} collective-permute-done((bf16[128,512]{1,0:T(8,128)(2,1)S(1)}, bf16[128,512]{1,0:T(8,128)(2,1)S(1)}, u32[]{:S(2)}, u32[]{:S(2)}) %collective-permute-start.5) | collective-permute-done | bytes 131104 | tf_op jit(solution)/shard_map/ppermute | solution.py:227
  32.7 2.3 collective-permute-start.8
  36.6 2.2 collective-permute-done.8
  40.2 4.5 %collective-permute-start.10 = (bf16[512,512]{1,0:T(8,128)(2,1)S(1)}, bf16[512,512]{1,0:T(8,128)(2,1)}, u32[]{:S(2)}, u32[]{:S(2)}) collective-permute-start(bf16[512,512]{1,0:T(8,128)(2,1)S(1)} %constant_dynamic-update-slice_fusion.12.mine_ref), channel_id=1, source_target_pairs={{0,4},{4,0},{8,12},{12,8},{16,20},{20,16},{24,28},{28,24},{32,36},... | collective-permute-start | bytes 1572872 | tf_op jit(solution)/shard_map/ppermute | solution.py:236
  48.1 3.0 %ladder.2 = bf16[1152,512]{1,0:T(8,128)(2,1)S(1)} custom-call(s32[1]{0:T(128)} %bitcast.1.core_ref, bf16[1152,1024]{1,0:T(8,128)(2,1)S(1)} %copy-done.2, bf16[512,512]{1,0:T(8,128)(2,1)S(1)} %constant_dynamic-update-slice_fusion.12.mine_ref, bf16[512,512]{1,0:T(8,128)(2,1)} %collective-permute-done.10.other_ref, f32[4,1152,128]{2,1,0:T(8,128)S(1)} %copy-done.4, ...), custom_call_target="tpu_custom_call" | custom-call | tf_op jit(solution)/shard_map/ladder/pallas_call | solution.py:182
  55.2 3.3 %collective-permute-start.26 = (f32[4,288]{1,0:T(4,128)S(1)}, f32[4,288]{1,0:T(4,128)S(1)}, u32[]{:S(2)}, u32[]{:S(2)}) collective-permute-start(f32[4,288]{1,0:T(4,128)S(1)} %get-tuple-element.59), channel_id=1, source_target_pairs={{0,2},{1,3},{2,0},{3,1},{4,6},{5,7},{6,4},{7,5},{8,10},{9,11},{10,... | collective-permute-start | bytes 13832 | tf_op jit(solution)/shard_map/ppermute | solution.py:263
  58.5 2.5 convolution_add_fusion.3
  68.6 2.9 %collective-permute-start.16 = (bf16[128,512]{1,0:T(8,128)(2,1)S(1)}, bf16[128,512]{1,0:T(8,128)(2,1)S(1)}, u32[]{:S(2)}, u32[]{:S(2)}) collective-permute-start(bf16[128,512]{1,0:T(8,128)(2,1)S(1)} %add_convert_fusion.5), channel_id=1, source_target_pairs={{0,64},{4,20},{8,72},{12,28},{16,80},{20,4},{24,88},{28,12},{32,96... | collective-permute-start | bytes 393224 | tf_op jit(solution)/shard_map/ppermute | solution.py:227
  78.5 3.3 %collective-permute-start.19 = (bf16[128,512]{1,0:T(8,128)(2,1)S(1)}, bf16[128,512]{1,0:T(8,128)(2,1)S(1)}, u32[]{:S(2)}, u32[]{:S(2)}) collective-permute-start(bf16[128,512]{1,0:T(8,128)(2,1)S(1)} %get-tuple-element.13), channel_id=1, source_target_pairs={{0,16},{4,68},{8,24},{12,76},{16,0},{20,84},{24,8},{28,92},{32,48}... | collective-permute-start | bytes 393224 | tf_op jit(solution)/shard_map/ppermute | solution.py:232
  82.3 2.1 collective-permute-start.20
  88.3 5.4 %collective-permute-start.21 = (bf16[512,512]{1,0:T(8,128)(2,1)}, bf16[512,512]{1,0:T(8,128)(2,1)}, u32[]{:S(2)}, u32[]{:S(2)}) collective-permute-start(bf16[512,512]{1,0:T(8,128)(2,1)} %constant_dynamic-update-slice_fusion.8.mine_ref), channel_id=1, source_target_pairs={{0,4},{4,0},{8,12},{12,8},{16,20},{20,16},{24,28},{28,24},{32,36},... | collective-permute-start | bytes 1572872 | tf_op jit(solution)/shard_map/ppermute | solution.py:236
  101.8 2.7 %pack.5.own_ref = f32[4,528,128]{2,1,0:T(8,128)S(1)} custom-call(s32[1]{0:T(128)} %bitcast.1.core_ref, s32[1]{0:T(128)} %bitcast.z_ref, bf16[1152,1024]{1,0:T(8,128)(2,1)S(1)} %copy-done.2, bf16[512,512]{1,0:T(8,128)(2,1)} %constant_dynamic-update-slice_fusion.8.mine_ref, bf16[512,512]{1,0:T(8,128)(2,1)} %collective-permute-done.21.other_ref, ...), custom_call_target="tpu_custom_call" | custom-call | tf_op jit(solution)/shard_map/pack/pallas_call | solution.py:182
  104.8 2.1 collective-permute-start.32
  108.6 2.8 %pack.4.own_ref = f32[4,656,128]{2,1,0:T(8,128)S(1)} custom-call(s32[1]{0:T(128)} %bitcast.1.core_ref, s32[1]{0:T(128)} %bitcast.z_ref, bf16[1152,1024]{1,0:T(8,128)(2,1)S(1)} %copy-done.2, bf16[512,512]{1,0:T(8,128)(2,1)} %constant_dynamic-update-slice_fusion.8.mine_ref, bf16[512,512]{1,0:T(8,128)(2,1)} %collective-permute-done.21.other_ref, ...), custom_call_target="tpu_custom_call" | custom-call | tf_op jit(solution)/shard_map/pack/pallas_call | solution.py:182
  111.8 2.1 collective-permute-start.23
  116.5 2.9 %mix.5.refs_4_ = f32[4,528,128]{2,1,0:T(8,128)S(1)} custom-call(f32[4,528,128]{2,1,0:T(8,128)S(1)} %pack.5.own_ref, f32[528,128]{1,0:T(8,128)S(1)} %convert_element_type.355.got1, f32[528,128]{1,0:T(8,128)S(1)} %convert_element_type.357.got2, f32[528,128]{1,0:T(8,128)S(1)} %convert_element_type.359.got3, f32[2048,128]{1,0:T(8,128)S(1)} %broadcast_in_dim.27.kernel_ref, ...), custom_call_target="tpu_custom_call" | custom-call | tf_op jit(solution)/shard_map/mix/pallas_call | solution.py:182
  121.1 2.8 %collective-permute-done.24 = f16[656,128]{1,0:T(8,128)(2,1)S(1)} collective-permute-done((f16[656,128]{1,0:T(8,128)(2,1)S(1)}, f16[656,128]{1,0:T(8,128)(2,1)S(1)}, u32[]{:S(2)}, u32[]{:S(2)}) %collective-permute-start.24) | collective-permute-done | bytes 167968 | tf_op jit(solution)/shard_map/ppermute | solution.py:250
  124.3 3.6 %mix.4.refs_0_ = f32[4,656,128]{2,1,0:T(8,128)S(1)} custom-call(f32[4,656,128]{2,1,0:T(8,128)S(1)} %pack.4.own_ref, f32[656,128]{1,0:T(8,128)S(1)} %convert_element_type.343.got1, f32[656,128]{1,0:T(8,128)S(1)} %convert_element_type.345.got2, f32[656,128]{1,0:T(8,128)S(1)} %convert_element_type.347.got3, f32[2560,128]{1,0:T(8,128)S(1)} %broadcast_in_dim.25.kernel_ref, ...), custom_call_target="tpu_custom_call" | custom-call | tf_op jit(solution)/shard_map/mix/pallas_call | solution.py:182
  128.2 2.8 %collective-permute-start.29 = (f16[656,128]{1,0:T(8,128)(2,1)S(1)}, f16[656,128]{1,0:T(8,128)(2,1)S(1)}, u32[]{:S(2)}, u32[]{:S(2)}) collective-permute-start(f16[656,128]{1,0:T(8,128)(2,1)S(1)} %get-tuple-element.35), channel_id=1, source_target_pairs={{0,2},{1,3},{2,0},{3,1},{4,6},{5,7},{6,4},{7,5},{8,10},{9,11},{10,... | collective-permute-start | bytes 503816 | tf_op jit(solution)/shard_map/ppermute | solution.py:250
  133.7 6.7 %collective-permute-done.35 = f16[528,128]{1,0:T(8,128)(2,1)S(1)} collective-permute-done((f16[528,128]{1,0:T(8,128)(2,1)S(1)}, f16[528,128]{1,0:T(8,128)(2,1)S(1)}, u32[]{:S(2)}, u32[]{:S(2)}) %collective-permute-start.35) | collective-permute-done | bytes 135200 | tf_op jit(solution)/shard_map/ppermute | solution.py:250
  140.5 5.7 %collective-permute-done.36 = f16[528,128]{1,0:T(8,128)(2,1)S(1)} collective-permute-done((f16[528,128]{1,0:T(8,128)(2,1)S(1)}, f16[528,128]{1,0:T(8,128)(2,1)S(1)}, u32[]{:S(2)}, u32[]{:S(2)}) %collective-permute-start.36) | collective-permute-done | bytes 135200 | tf_op jit(solution)/shard_map/ppermute | solution.py:250
  149.6 2.3 collective-permute-done.37
  152.9 3.2 %collective-permute-start.39 = (bf16[128,512]{1,0:T(8,128)(2,1)S(1)}, bf16[128,512]{1,0:T(8,128)(2,1)S(1)}, u32[]{:S(2)}, u32[]{:S(2)}) collective-permute-start(bf16[128,512]{1,0:T(8,128)(2,1)S(1)} %get-tuple-element.21), channel_id=1, source_target_pairs={{0,16},{4,68},{8,24},{12,76},{16,0},{20,84},{24,8},{28,92},{32,48}... | collective-permute-start | bytes 393224 | tf_op jit(solution)/shard_map/ppermute | solution.py:223
  157.0 2.9 %collective-permute-done.39 = bf16[128,512]{1,0:T(8,128)(2,1)S(1)} collective-permute-done((bf16[128,512]{1,0:T(8,128)(2,1)S(1)}, bf16[128,512]{1,0:T(8,128)(2,1)S(1)}, u32[]{:S(2)}, u32[]{:S(2)}) %collective-permute-start.39) | collective-permute-done | bytes 131104 | tf_op jit(solution)/shard_map/ppermute | solution.py:223
  171.2 2.0 collective-permute-start.46
  176.4 6.1 %collective-permute-start.47 = (bf16[512,512]{1,0:T(8,128)(2,1)S(1)}, bf16[512,512]{1,0:T(8,128)(2,1)S(1)}, u32[]{:S(2)}, u32[]{:S(2)}) collective-permute-start(bf16[512,512]{1,0:T(8,128)(2,1)S(1)} %constant_dynamic-update-slice_fusion.4.mine_ref), channel_id=1, source_target_pairs={{0,4},{4,0},{8,12},{12,8},{16,20},{20,16},{24,28},{28,24},{32,36},... | collective-permute-start | bytes 1572872 | tf_op jit(solution)/shard_map/ppermute | solution.py:236
  187.3 2.3 collective-permute-done.48
  192.5 2.0 collective-permute-start.51
  197.8 2.3 collective-permute-start.53
  201.6 2.2 collective-permute-done.53
  205.7 3.2 %collective-permute-start.56 = (bf16[128,512]{1,0:T(8,128)(2,1)S(1)}, bf16[128,512]{1,0:T(8,128)(2,1)S(1)}, u32[]{:S(2)}, u32[]{:S(2)}) collective-permute-start(bf16[128,512]{1,0:T(8,128)(2,1)S(1)} %get-tuple-element.9), channel_id=1, source_target_pairs={{0,16},{4,68},{8,24},{12,76},{16,0},{20,84},{24,8},{28,92},{32,48}... | collective-permute-start | bytes 393224 | tf_op jit(solution)/shard_map/ppermute | solution.py:232
  209.6 3.1 %collective-permute-done.56 = bf16[128,512]{1,0:T(8,128)(2,1)S(1)} collective-permute-done((bf16[128,512]{1,0:T(8,128)(2,1)S(1)}, bf16[128,512]{1,0:T(8,128)(2,1)S(1)}, u32[]{:S(2)}, u32[]{:S(2)}) %collective-permute-start.56) | collective-permute-done | bytes 131104 | tf_op jit(solution)/shard_map/ppermute | solution.py:232
  214.1 4.4 %collective-permute-start.58 = (bf16[512,512]{1,0:T(8,128)(2,1)S(1)}, bf16[512,512]{1,0:T(8,128)(2,1)}, u32[]{:S(2)}, u32[]{:S(2)}) collective-permute-start(bf16[512,512]{1,0:T(8,128)(2,1)S(1)} %constant_dynamic-update-slice_fusion.mine_ref), channel_id=1, source_target_pairs={{0,4},{4,0},{8,12},{12,8},{16,20},{20,16},{24,28},{28,24},{32,36},... | collective-permute-start | bytes 1572872 | tf_op jit(solution)/shard_map/ppermute | solution.py:236
  221.9 2.6 pack.7.own_ref
  225.6 2.2 collective-permute-start.66
  229.4 2.7 %pack.6.own_ref = f32[4,656,128]{2,1,0:T(8,128)S(1)} custom-call(s32[1]{0:T(128)} %bitcast.1.core_ref, s32[1]{0:T(128)} %bitcast.z_ref, bf16[1152,1024]{1,0:T(8,128)(2,1)S(1)} %copy-done.2, bf16[512,512]{1,0:T(8,128)(2,1)S(1)} %constant_dynamic-update-slice_fusion.mine_ref, bf16[512,512]{1,0:T(8,128)(2,1)} %collective-permute-done.58.other_ref, ...), custom_call_target="tpu_custom_call" | custom-call | tf_op jit(solution)/shard_map/pack/pallas_call | solution.py:182
  233.3 2.2 collective-permute-start.60
  242.3 2.9 %mix.7.refs_4_ = f32[4,528,128]{2,1,0:T(8,128)S(1)} custom-call(f32[4,528,128]{2,1,0:T(8,128)S(1)} %copy-done.16, f32[528,128]{1,0:T(8,128)S(1)} %convert_element_type.403.got1, f32[528,128]{1,0:T(8,128)S(1)} %convert_element_type.405.got2, f32[528,128]{1,0:T(8,128)S(1)} %convert_element_type.407.got3, f32[2048,128]{1,0:T(8,128)S(1)} %copy-done.18, ...), custom_call_target="tpu_custom_call" | custom-call | tf_op jit(solution)/shard_map/mix/pallas_call | solution.py:182
  245.4 2.2 collective-permute-start.69
  249.4 3.6 %mix.6.refs_0_ = f32[4,656,128]{2,1,0:T(8,128)S(1)} custom-call(f32[4,656,128]{2,1,0:T(8,128)S(1)} %copy-done.12, f32[656,128]{1,0:T(8,128)S(1)} %convert_element_type.391.got1, f32[656,128]{1,0:T(8,128)S(1)} %convert_element_type.393.got2, f32[656,128]{1,0:T(8,128)S(1)} %convert_element_type.395.got3, f32[2560,128]{1,0:T(8,128)S(1)} %copy-done.14, ...), custom_call_target="tpu_custom_call" | custom-call | tf_op jit(solution)/shard_map/mix/pallas_call | solution.py:182
  253.3 2.2 collective-permute-start.63
  257.2 2.3 fusion.2
  261.9 2.4 unpack.3
  (266 shorter events, 118.3 us)
Async XLA Ops:
  14.5 6.7 %collective-permute-start.2 = (bf16[128,512]{1,0:T(8,128)(2,1)S(1)}, bf16[128,512]{1,0:T(8,128)(2,1)S(1)}, u32[]{:S(2)}, u32[]{:S(2)}) collective-permute-start(bf16[128,512]{1,0:T(8,128)(2,1)S(1)} %get-tuple-element.27), channel_id=1, source_target_pairs={{0,16},{4,68},{8,24},{12,76},{16,0},{20,84},{24,8},{28,92},{32,48}... | collective-permute-start | bytes 393224 | tf_op jit(solution)/shard_map/ppermute | solution.py:223
  17.1 5.5 %collective-permute-start.3 = (bf16[128,512]{1,0:T(8,128)(2,1)S(1)}, bf16[128,512]{1,0:T(8,128)(2,1)S(1)}, u32[]{:S(2)}, u32[]{:S(2)}) collective-permute-start(bf16[128,512]{1,0:T(8,128)(2,1)S(1)} %get-tuple-element.26), channel_id=1, source_target_pairs={{0,24},{4,100},{8,16},{12,108},{16,8},{20,116},{24,0},{28,124},{32... | collective-permute-start | bytes 393224 | tf_op jit(solution)/shard_map/ppermute | solution.py:223
  24.6 6.2 %collective-permute-start.5 = (bf16[128,512]{1,0:T(8,128)(2,1)S(1)}, bf16[128,512]{1,0:T(8,128)(2,1)S(1)}, u32[]{:S(2)}, u32[]{:S(2)}) collective-permute-start(bf16[128,512]{1,0:T(8,128)(2,1)S(1)} %add_convert_fusion.7), channel_id=1, source_target_pairs={{0,64},{4,20},{8,72},{12,28},{16,80},{20,4},{24,88},{28,12},{32,96... | collective-permute-start | bytes 393224 | tf_op jit(solution)/shard_map/ppermute | solution.py:227
  27.1 5.5 %collective-permute-start.6 = (bf16[128,512]{1,0:T(8,128)(2,1)S(1)}, bf16[128,512]{1,0:T(8,128)(2,1)S(1)}, u32[]{:S(2)}, u32[]{:S(2)}) collective-permute-start(bf16[128,512]{1,0:T(8,128)(2,1)S(1)} %add_convert_fusion.7), channel_id=1, source_target_pairs={{0,96},{4,28},{8,104},{12,20},{16,112},{20,12},{24,120},{28,4},{32... | collective-permute-start | bytes 393224 | tf_op jit(solution)/shard_map/ppermute | solution.py:227
  32.7 6.1 %collective-permute-start.8 = (bf16[128,512]{1,0:T(8,128)(2,1)S(1)}, bf16[128,512]{1,0:T(8,128)(2,1)S(1)}, u32[]{:S(2)}, u32[]{:S(2)}) collective-permute-start(bf16[128,512]{1,0:T(8,128)(2,1)S(1)} %get-tuple-element.15), channel_id=1, source_target_pairs={{0,16},{4,68},{8,24},{12,76},{16,0},{20,84},{24,8},{28,92},{32,48}... | collective-permute-start | bytes 393224 | tf_op jit(solution)/shard_map/ppermute | solution.py:232
  40.2 6.2 %collective-permute-start.10 = (bf16[512,512]{1,0:T(8,128)(2,1)S(1)}, bf16[512,512]{1,0:T(8,128)(2,1)}, u32[]{:S(2)}, u32[]{:S(2)}) collective-permute-start(bf16[512,512]{1,0:T(8,128)(2,1)S(1)} %constant_dynamic-update-slice_fusion.12.mine_ref), channel_id=1, source_target_pairs={{0,4},{4,0},{8,12},{12,8},{16,20},{20,16},{24,28},{28,24},{32,36},... | collective-permute-start | bytes 1572872 | tf_op jit(solution)/shard_map/ppermute | solution.py:236
  53.0 5.5 %collective-permute-start.11 = (f32[512,512]{1,0:T(8,128)}, f32[512,512]{1,0:T(8,128)}, u32[]{:S(2)}, u32[]{:S(2)}) collective-permute-start(f32[512,512]{1,0:T(8,128)} %fusion.11), channel_id=1, source_target_pairs={{0,4},{4,0},{8,12},{12,8},{16,20},{20,16},{24,28},{28,24},{32,36},... | collective-permute-start | bytes 3145736 | tf_op jit(solution)/shard_map/ppermute | solution.py:216
  53.5 40.7 %collective-permute-start.25 = (f32[4,288]{1,0:T(4,128)S(1)}, f32[4,288]{1,0:T(4,128)S(1)}, u32[]{:S(2)}, u32[]{:S(2)}) collective-permute-start(f32[4,288]{1,0:T(4,128)S(1)} %get-tuple-element.57), channel_id=1, source_target_pairs={{0,1},{1,0},{2,3},{3,2},{4,5},{5,4},{6,7},{7,6},{8,9},{9,8},{10,11... | collective-permute-start | bytes 13832 | tf_op jit(solution)/shard_map/ppermute | solution.py:263
  55.2 39.0 %collective-permute-start.26 = (f32[4,288]{1,0:T(4,128)S(1)}, f32[4,288]{1,0:T(4,128)S(1)}, u32[]{:S(2)}, u32[]{:S(2)}) collective-permute-start(f32[4,288]{1,0:T(4,128)S(1)} %get-tuple-element.59), channel_id=1, source_target_pairs={{0,2},{1,3},{2,0},{3,1},{4,6},{5,7},{6,4},{7,5},{8,10},{9,11},{10,... | collective-permute-start | bytes 13832 | tf_op jit(solution)/shard_map/ppermute | solution.py:263
  61.1 5.6 %collective-permute-start.13 = (bf16[128,512]{1,0:T(8,128)(2,1)S(1)}, bf16[128,512]{1,0:T(8,128)(2,1)S(1)}, u32[]{:S(2)}, u32[]{:S(2)}) collective-permute-start(bf16[128,512]{1,0:T(8,128)(2,1)S(1)} %get-tuple-element.24), channel_id=1, source_target_pairs={{0,16},{4,68},{8,24},{12,76},{16,0},{20,84},{24,8},{28,92},{32,48}... | collective-permute-start | bytes 393224 | tf_op jit(solution)/shard_map/ppermute | solution.py:223
  63.0 5.5 %collective-permute-start.14 = (bf16[128,512]{1,0:T(8,128)(2,1)S(1)}, bf16[128,512]{1,0:T(8,128)(2,1)S(1)}, u32[]{:S(2)}, u32[]{:S(2)}) collective-permute-start(bf16[128,512]{1,0:T(8,128)(2,1)S(1)} %get-tuple-element.23), channel_id=1, source_target_pairs={{0,24},{4,100},{8,16},{12,108},{16,8},{20,116},{24,0},{28,124},{32... | collective-permute-start | bytes 393224 | tf_op jit(solution)/shard_map/ppermute | solution.py:223
  68.6 6.7 %collective-permute-start.16 = (bf16[128,512]{1,0:T(8,128)(2,1)S(1)}, bf16[128,512]{1,0:T(8,128)(2,1)S(1)}, u32[]{:S(2)}, u32[]{:S(2)}) collective-permute-start(bf16[128,512]{1,0:T(8,128)(2,1)S(1)} %add_convert_fusion.5), channel_id=1, source_target_pairs={{0,64},{4,20},{8,72},{12,28},{16,80},{20,4},{24,88},{28,12},{32,96... | collective-permute-start | bytes 393224 | tf_op jit(solution)/shard_map/ppermute | solution.py:227
  71.5 5.5 %collective-permute-start.17 = (bf16[128,512]{1,0:T(8,128)(2,1)S(1)}, bf16[128,512]{1,0:T(8,128)(2,1)S(1)}, u32[]{:S(2)}, u32[]{:S(2)}) collective-permute-start(bf16[128,512]{1,0:T(8,128)(2,1)S(1)} %add_convert_fusion.5), channel_id=1, source_target_pairs={{0,96},{4,28},{8,104},{12,20},{16,112},{20,12},{24,120},{28,4},{32... | collective-permute-start | bytes 393224 | tf_op jit(solution)/shard_map/ppermute | solution.py:227
  72.8 21.4 %collective-permute-start.27 = (f32[4,288]{1,0:T(4,128)S(1)}, f32[4,288]{1,0:T(4,128)S(1)}, u32[]{:S(2)}, u32[]{:S(2)}) collective-permute-start(f32[4,288]{1,0:T(4,128)S(1)} %get-tuple-element.58), channel_id=1, source_target_pairs={{0,3},{1,2},{2,1},{3,0},{4,7},{5,6},{6,5},{7,4},{8,11},{9,10},{10,... | collective-permute-start | bytes 13832 | tf_op jit(solution)/shard_map/ppermute | solution.py:263
  78.5 7.1 %collective-permute-start.19 = (bf16[128,512]{1,0:T(8,128)(2,1)S(1)}, bf16[128,512]{1,0:T(8,128)(2,1)S(1)}, u32[]{:S(2)}, u32[]{:S(2)}) collective-permute-start(bf16[128,512]{1,0:T(8,128)(2,1)S(1)} %get-tuple-element.13), channel_id=1, source_target_pairs={{0,16},{4,68},{8,24},{12,76},{16,0},{20,84},{24,8},{28,92},{32,48}... | collective-permute-start | bytes 393224 | tf_op jit(solution)/shard_map/ppermute | solution.py:232
  88.3 11.8 %collective-permute-start.21 = (bf16[512,512]{1,0:T(8,128)(2,1)}, bf16[512,512]{1,0:T(8,128)(2,1)}, u32[]{:S(2)}, u32[]{:S(2)}) collective-permute-start(bf16[512,512]{1,0:T(8,128)(2,1)} %constant_dynamic-update-slice_fusion.8.mine_ref), channel_id=1, source_target_pairs={{0,4},{4,0},{8,12},{12,8},{16,20},{20,16},{24,28},{28,24},{32,36},... | collective-permute-start | bytes 1572872 | tf_op jit(solution)/shard_map/ppermute | solution.py:236
  104.7 9.2 %collective-permute-start.31 = (f16[528,128]{1,0:T(8,128)(2,1)S(1)}, f16[528,128]{1,0:T(8,128)(2,1)S(1)}, u32[]{:S(2)}, u32[]{:S(2)}) collective-permute-start(f16[528,128]{1,0:T(8,128)(2,1)S(1)} %get-tuple-element.51), channel_id=1, source_target_pairs={{0,1},{1,0},{2,3},{3,2},{4,5},{5,4},{6,7},{7,6},{8,9},{9,8},{10,11... | collective-permute-start | bytes 405512 | tf_op jit(solution)/shard_map/ppermute | solution.py:250
  104.8 10.9 %collective-permute-start.32 = (f16[528,128]{1,0:T(8,128)(2,1)S(1)}, f16[528,128]{1,0:T(8,128)(2,1)S(1)}, u32[]{:S(2)}, u32[]{:S(2)}) collective-permute-start(f16[528,128]{1,0:T(8,128)(2,1)S(1)} %get-tuple-element.50), channel_id=1, source_target_pairs={{0,2},{1,3},{2,0},{3,1},{4,6},{5,7},{6,4},{7,5},{8,10},{9,11},{10,... | collective-permute-start | bytes 405512 | tf_op jit(solution)/shard_map/ppermute | solution.py:250
  106.9 9.2 %collective-permute-start.33 = (f16[528,128]{1,0:T(8,128)(2,1)S(1)}, f16[528,128]{1,0:T(8,128)(2,1)S(1)}, u32[]{:S(2)}, u32[]{:S(2)}) collective-permute-start(f16[528,128]{1,0:T(8,128)(2,1)S(1)} %get-tuple-element.49), channel_id=1, source_target_pairs={{0,3},{1,2},{2,1},{3,0},{4,7},{5,6},{6,5},{7,4},{8,11},{9,10},{10,... | collective-permute-start | bytes 405512 | tf_op jit(solution)/shard_map/ppermute | solution.py:250
  111.7 8.0 %collective-permute-start.22 = (f16[656,128]{1,0:T(8,128)(2,1)S(1)}, f16[656,128]{1,0:T(8,128)(2,1)S(1)}, u32[]{:S(2)}, u32[]{:S(2)}) collective-permute-start(f16[656,128]{1,0:T(8,128)(2,1)S(1)} %get-tuple-element.39), channel_id=1, source_target_pairs={{0,1},{1,0},{2,3},{3,2},{4,5},{5,4},{6,7},{7,6},{8,9},{9,8},{10,11... | collective-permute-start | bytes 503816 | tf_op jit(solution)/shard_map/ppermute | solution.py:250
  111.8 9.2 %collective-permute-start.23 = (f16[656,128]{1,0:T(8,128)(2,1)S(1)}, f16[656,128]{1,0:T(8,128)(2,1)S(1)}, u32[]{:S(2)}, u32[]{:S(2)}) collective-permute-start(f16[656,128]{1,0:T(8,128)(2,1)S(1)} %get-tuple-element.38), channel_id=1, source_target_pairs={{0,2},{1,3},{2,0},{3,1},{4,6},{5,7},{6,4},{7,5},{8,10},{9,11},{10,... | collective-permute-start | bytes 503816 | tf_op jit(solution)/shard_map/ppermute | solution.py:250
  113.9 9.9 %collective-permute-start.24 = (f16[656,128]{1,0:T(8,128)(2,1)S(1)}, f16[656,128]{1,0:T(8,128)(2,1)S(1)}, u32[]{:S(2)}, u32[]{:S(2)}) collective-permute-start(f16[656,128]{1,0:T(8,128)(2,1)S(1)} %get-tuple-element.37), channel_id=1, source_target_pairs={{0,3},{1,2},{2,1},{3,0},{4,7},{5,6},{6,5},{7,4},{8,11},{9,10},{10,... | collective-permute-start | bytes 503816 | tf_op jit(solution)/shard_map/ppermute | solution.py:250
  119.6 12.7 %collective-permute-start.34 = (f16[528,128]{1,0:T(8,128)(2,1)S(1)}, f16[528,128]{1,0:T(8,128)(2,1)S(1)}, u32[]{:S(2)}, u32[]{:S(2)}) collective-permute-start(f16[528,128]{1,0:T(8,128)(2,1)S(1)} %get-tuple-element.48), channel_id=1, source_target_pairs={{0,1},{1,0},{2,3},{3,2},{4,5},{5,4},{6,7},{7,6},{8,9},{9,8},{10,11... | collective-permute-start | bytes 405512 | tf_op jit(solution)/shard_map/ppermute | solution.py:250
  128.1 18.1 %collective-permute-start.28 = (f16[656,128]{1,0:T(8,128)(2,1)S(1)}, f16[656,128]{1,0:T(8,128)(2,1)S(1)}, u32[]{:S(2)}, u32[]{:S(2)}) collective-permute-start(f16[656,128]{1,0:T(8,128)(2,1)S(1)} %get-tuple-element.36), channel_id=1, source_target_pairs={{0,1},{1,0},{2,3},{3,2},{4,5},{5,4},{6,7},{7,6},{8,9},{9,8},{10,11... | collective-permute-start | bytes 503816 | tf_op jit(solution)/shard_map/ppermute | solution.py:250
  128.2 18.0 %collective-permute-start.29 = (f16[656,128]{1,0:T(8,128)(2,1)S(1)}, f16[656,128]{1,0:T(8,128)(2,1)S(1)}, u32[]{:S(2)}, u32[]{:S(2)}) collective-permute-start(f16[656,128]{1,0:T(8,128)(2,1)S(1)} %get-tuple-element.35), channel_id=1, source_target_pairs={{0,2},{1,3},{2,0},{3,1},{4,6},{5,7},{6,4},{7,5},{8,10},{9,11},{10,... | collective-permute-start | bytes 503816 | tf_op jit(solution)/shard_map/ppermute | solution.py:250
  131.0 15.2 %collective-permute-start.30 = (f16[656,128]{1,0:T(8,128)(2,1)S(1)}, f16[656,128]{1,0:T(8,128)(2,1)S(1)}, u32[]{:S(2)}, u32[]{:S(2)}) collective-permute-start(f16[656,128]{1,0:T(8,128)(2,1)S(1)} %get-tuple-element.34), channel_id=1, source_target_pairs={{0,3},{1,2},{2,1},{3,0},{4,7},{5,6},{6,5},{7,4},{8,11},{9,10},{10,... | collective-permute-start | bytes 503816 | tf_op jit(solution)/shard_map/ppermute | solution.py:250
  132.0 8.4 %collective-permute-start.35 = (f16[528,128]{1,0:T(8,128)(2,1)S(1)}, f16[528,128]{1,0:T(8,128)(2,1)S(1)}, u32[]{:S(2)}, u32[]{:S(2)}) collective-permute-start(f16[528,128]{1,0:T(8,128)(2,1)S(1)} %get-tuple-element.47), channel_id=1, source_target_pairs={{0,2},{1,3},{2,0},{3,1},{4,6},{5,7},{6,4},{7,5},{8,10},{9,11},{10,... | collective-permute-start | bytes 405512 | tf_op jit(solution)/shard_map/ppermute | solution.py:250
  132.3 13.8 %collective-permute-start.36 = (f16[528,128]{1,0:T(8,128)(2,1)S(1)}, f16[528,128]{1,0:T(8,128)(2,1)S(1)}, u32[]{:S(2)}, u32[]{:S(2)}) collective-permute-start(f16[528,128]{1,0:T(8,128)(2,1)S(1)} %get-tuple-element.46), channel_id=1, source_target_pairs={{0,3},{1,2},{2,1},{3,0},{4,7},{5,6},{6,5},{7,4},{8,11},{9,10},{10,... | collective-permute-start | bytes 405512 | tf_op jit(solution)/shard_map/ppermute | solution.py:250
  152.9 7.0 %collective-permute-start.39 = (bf16[128,512]{1,0:T(8,128)(2,1)S(1)}, bf16[128,512]{1,0:T(8,128)(2,1)S(1)}, u32[]{:S(2)}, u32[]{:S(2)}) collective-permute-start(bf16[128,512]{1,0:T(8,128)(2,1)S(1)} %get-tuple-element.21), channel_id=1, source_target_pairs={{0,16},{4,68},{8,24},{12,76},{16,0},{20,84},{24,8},{28,92},{32,48}... | collective-permute-start | bytes 393224 | tf_op jit(solution)/shard_map/ppermute | solution.py:223
  161.7 5.7 %collective-permute-start.42 = (bf16[128,512]{1,0:T(8,128)(2,1)S(1)}, bf16[128,512]{1,0:T(8,128)(2,1)S(1)}, u32[]{:S(2)}, u32[]{:S(2)}) collective-permute-start(bf16[128,512]{1,0:T(8,128)(2,1)S(1)} %add_convert_fusion.3), channel_id=1, source_target_pairs={{0,64},{4,20},{8,72},{12,28},{16,80},{20,4},{24,88},{28,12},{32,96... | collective-permute-start | bytes 393224 | tf_op jit(solution)/shard_map/ppermute | solution.py:227
  169.4 5.6 %collective-permute-start.45 = (bf16[128,512]{1,0:T(8,128)(2,1)S(1)}, bf16[128,512]{1,0:T(8,128)(2,1)S(1)}, u32[]{:S(2)}, u32[]{:S(2)}) collective-permute-start(bf16[128,512]{1,0:T(8,128)(2,1)S(1)} %get-tuple-element.11), channel_id=1, source_target_pairs={{0,16},{4,68},{8,24},{12,76},{16,0},{20,84},{24,8},{28,92},{32,48}... | collective-permute-start | bytes 393224 | tf_op jit(solution)/shard_map/ppermute | solution.py:232
  176.4 7.6 %collective-permute-start.47 = (bf16[512,512]{1,0:T(8,128)(2,1)S(1)}, bf16[512,512]{1,0:T(8,128)(2,1)S(1)}, u32[]{:S(2)}, u32[]{:S(2)}) collective-permute-start(bf16[512,512]{1,0:T(8,128)(2,1)S(1)} %constant_dynamic-update-slice_fusion.4.mine_ref), channel_id=1, source_target_pairs={{0,4},{4,0},{8,12},{12,8},{16,20},{20,16},{24,28},{28,24},{32,36},... | collective-permute-start | bytes 1572872 | tf_op jit(solution)/shard_map/ppermute | solution.py:236
  190.7 5.8 %collective-permute-start.50 = (bf16[128,512]{1,0:T(8,128)(2,1)S(1)}, bf16[128,512]{1,0:T(8,128)(2,1)S(1)}, u32[]{:S(2)}, u32[]{:S(2)}) collective-permute-start(bf16[128,512]{1,0:T(8,128)(2,1)S(1)} %get-tuple-element.18), channel_id=1, source_target_pairs={{0,16},{4,68},{8,24},{12,76},{16,0},{20,84},{24,8},{28,92},{32,48}... | collective-permute-start | bytes 393224 | tf_op jit(solution)/shard_map/ppermute | solution.py:223
  197.8 6.0 %collective-permute-start.53 = (bf16[128,512]{1,0:T(8,128)(2,1)S(1)}, bf16[128,512]{1,0:T(8,128)(2,1)S(1)}, u32[]{:S(2)}, u32[]{:S(2)}) collective-permute-start(bf16[128,512]{1,0:T(8,128)(2,1)S(1)} %add_convert_fusion.1), channel_id=1, source_target_pairs={{0,64},{4,20},{8,72},{12,28},{16,80},{20,4},{24,88},{28,12},{32,96... | collective-permute-start | bytes 393224 | tf_op jit(solution)/shard_map/ppermute | solution.py:227
  205.7 7.0 %collective-permute-start.56 = (bf16[128,512]{1,0:T(8,128)(2,1)S(1)}, bf16[128,512]{1,0:T(8,128)(2,1)S(1)}, u32[]{:S(2)}, u32[]{:S(2)}) collective-permute-start(bf16[128,512]{1,0:T(8,128)(2,1)S(1)} %get-tuple-element.9), channel_id=1, source_target_pairs={{0,16},{4,68},{8,24},{12,76},{16,0},{20,84},{24,8},{28,92},{32,48}... | collective-permute-start | bytes 393224 | tf_op jit(solution)/shard_map/ppermute | solution.py:232
  214.1 6.1 %collective-permute-start.58 = (bf16[512,512]{1,0:T(8,128)(2,1)S(1)}, bf16[512,512]{1,0:T(8,128)(2,1)}, u32[]{:S(2)}, u32[]{:S(2)}) collective-permute-start(bf16[512,512]{1,0:T(8,128)(2,1)S(1)} %constant_dynamic-update-slice_fusion.mine_ref), channel_id=1, source_target_pairs={{0,4},{4,0},{8,12},{12,8},{16,20},{20,16},{24,28},{28,24},{32,36},... | collective-permute-start | bytes 1572872 | tf_op jit(solution)/shard_map/ppermute | solution.py:236
  225.6 12.1 %collective-permute-start.65 = (f16[528,128]{1,0:T(8,128)(2,1)}, f16[528,128]{1,0:T(8,128)(2,1)}, u32[]{:S(2)}, u32[]{:S(2)}) collective-permute-start(f16[528,128]{1,0:T(8,128)(2,1)} %get-tuple-element.45), channel_id=1, source_target_pairs={{0,1},{1,0},{2,3},{3,2},{4,5},{5,4},{6,7},{7,6},{8,9},{9,8},{10,11... | collective-permute-start | bytes 405512 | tf_op jit(solution)/shard_map/ppermute | solution.py:250
  225.6 14.8 %collective-permute-start.66 = (f16[528,128]{1,0:T(8,128)(2,1)}, f16[528,128]{1,0:T(8,128)(2,1)}, u32[]{:S(2)}, u32[]{:S(2)}) collective-permute-start(f16[528,128]{1,0:T(8,128)(2,1)} %get-tuple-element.44), channel_id=1, source_target_pairs={{0,2},{1,3},{2,0},{3,1},{4,6},{5,7},{6,4},{7,5},{8,10},{9,11},{10,... | collective-permute-start | bytes 405512 | tf_op jit(solution)/shard_map/ppermute | solution.py:250
  227.8 13.5 %collective-permute-start.67 = (f16[528,128]{1,0:T(8,128)(2,1)}, f16[528,128]{1,0:T(8,128)(2,1)}, u32[]{:S(2)}, u32[]{:S(2)}) collective-permute-start(f16[528,128]{1,0:T(8,128)(2,1)} %get-tuple-element.43), channel_id=1, source_target_pairs={{0,3},{1,2},{2,1},{3,0},{4,7},{5,6},{6,5},{7,4},{8,11},{9,10},{10,... | collective-permute-start | bytes 405512 | tf_op jit(solution)/shard_map/ppermute | solution.py:250
  233.3 14.3 %collective-permute-start.59 = (f16[656,128]{1,0:T(8,128)(2,1)}, f16[656,128]{1,0:T(8,128)(2,1)S(1)}, u32[]{:S(2)}, u32[]{:S(2)}) collective-permute-start(f16[656,128]{1,0:T(8,128)(2,1)} %get-tuple-element.33), channel_id=1, source_target_pairs={{0,1},{1,0},{2,3},{3,2},{4,5},{5,4},{6,7},{7,6},{8,9},{9,8},{10,11... | collective-permute-start | bytes 503816 | tf_op jit(solution)/shard_map/ppermute | solution.py:250
  233.3 16.0 %collective-permute-start.60 = (f16[656,128]{1,0:T(8,128)(2,1)}, f16[656,128]{1,0:T(8,128)(2,1)S(1)}, u32[]{:S(2)}, u32[]{:S(2)}) collective-permute-start(f16[656,128]{1,0:T(8,128)(2,1)} %get-tuple-element.32), channel_id=1, source_target_pairs={{0,2},{1,3},{2,0},{3,1},{4,6},{5,7},{6,4},{7,5},{8,10},{9,11},{10,... | collective-permute-start | bytes 503816 | tf_op jit(solution)/shard_map/ppermute | solution.py:250
  237.7 11.7 %collective-permute-start.61 = (f16[656,128]{1,0:T(8,128)(2,1)S(1)}, f16[656,128]{1,0:T(8,128)(2,1)S(1)}, u32[]{:S(2)}, u32[]{:S(2)}) collective-permute-start(f16[656,128]{1,0:T(8,128)(2,1)S(1)} %get-tuple-element.31), channel_id=1, source_target_pairs={{0,3},{1,2},{2,1},{3,0},{4,7},{5,6},{6,5},{7,4},{8,11},{9,10},{10,... | collective-permute-start | bytes 503816 | tf_op jit(solution)/shard_map/ppermute | solution.py:250
  245.3 10.2 %collective-permute-start.68 = (f16[528,128]{1,0:T(8,128)(2,1)S(1)}, f16[528,128]{1,0:T(8,128)(2,1)S(1)}, u32[]{:S(2)}, u32[]{:S(2)}) collective-permute-start(f16[528,128]{1,0:T(8,128)(2,1)S(1)} %get-tuple-element.42), channel_id=1, source_target_pairs={{0,1},{1,0},{2,3},{3,2},{4,5},{5,4},{6,7},{7,6},{8,9},{9,8},{10,11... | collective-permute-start | bytes 405512 | tf_op jit(solution)/shard_map/ppermute | solution.py:250
  245.4 14.1 %collective-permute-start.69 = (f16[528,128]{1,0:T(8,128)(2,1)S(1)}, f16[528,128]{1,0:T(8,128)(2,1)S(1)}, u32[]{:S(2)}, u32[]{:S(2)}) collective-permute-start(f16[528,128]{1,0:T(8,128)(2,1)S(1)} %get-tuple-element.41), channel_id=1, source_target_pairs={{0,2},{1,3},{2,0},{3,1},{4,6},{5,7},{6,4},{7,5},{8,10},{9,11},{10,... | collective-permute-start | bytes 405512 | tf_op jit(solution)/shard_map/ppermute | solution.py:250
  247.6 11.9 %collective-permute-start.70 = (f16[528,128]{1,0:T(8,128)(2,1)S(1)}, f16[528,128]{1,0:T(8,128)(2,1)S(1)}, u32[]{:S(2)}, u32[]{:S(2)}) collective-permute-start(f16[528,128]{1,0:T(8,128)(2,1)S(1)} %get-tuple-element.40), channel_id=1, source_target_pairs={{0,3},{1,2},{2,1},{3,0},{4,7},{5,6},{6,5},{7,4},{8,11},{9,10},{10,... | collective-permute-start | bytes 405512 | tf_op jit(solution)/shard_map/ppermute | solution.py:250
  253.2 6.4 %collective-permute-start.62 = (f16[656,128]{1,0:T(8,128)(2,1)S(1)}, f16[656,128]{1,0:T(8,128)(2,1)S(1)}, u32[]{:S(2)}, u32[]{:S(2)}) collective-permute-start(f16[656,128]{1,0:T(8,128)(2,1)S(1)} %get-tuple-element.30), channel_id=1, source_target_pairs={{0,1},{1,0},{2,3},{3,2},{4,5},{5,4},{6,7},{7,6},{8,9},{9,8},{10,11... | collective-permute-start | bytes 503816 | tf_op jit(solution)/shard_map/ppermute | solution.py:250
  253.3 6.9 %collective-permute-start.63 = (f16[656,128]{1,0:T(8,128)(2,1)S(1)}, f16[656,128]{1,0:T(8,128)(2,1)S(1)}, u32[]{:S(2)}, u32[]{:S(2)}) collective-permute-start(f16[656,128]{1,0:T(8,128)(2,1)S(1)} %get-tuple-element.29), channel_id=1, source_target_pairs={{0,2},{1,3},{2,0},{3,1},{4,6},{5,7},{6,4},{7,5},{8,10},{9,11},{10,... | collective-permute-start | bytes 503816 | tf_op jit(solution)/shard_map/ppermute | solution.py:250
  255.5 6.3 %collective-permute-start.64 = (f16[656,128]{1,0:T(8,128)(2,1)S(1)}, f16[656,128]{1,0:T(8,128)(2,1)S(1)}, u32[]{:S(2)}, u32[]{:S(2)}) collective-permute-start(f16[656,128]{1,0:T(8,128)(2,1)S(1)} %get-tuple-element.28), channel_id=1, source_target_pairs={{0,3},{1,2},{2,1},{3,0},{4,7},{5,6},{6,5},{7,4},{8,11},{9,10},{10,... | collective-permute-start | bytes 503816 | tf_op jit(solution)/shard_map/ppermute | solution.py:250
  (53 other events, 383.2 us)

commit v3 on v2

--- a/solution.py
+++ b/solution.py
@@ -1,5 +1,3 @@
-from functools import partial
-
 import jax
 import jax.numpy as jnp
 from jax import lax
@@ -14,6 +12,8 @@
 F16 = jnp.float16
 SIDE = 4
 RUN = 16
+LANES = 128
+PARTNERS = (2, 1, 3)
 INTERPRET = False
 
 
@@ -75,16 +75,16 @@
     lax.fori_loop(0, SIDE, step, 0)
 
 
-def pack_body(offset, core_ref, z_ref, factors_ref, mine_ref, other_ref, sources_ref,
-              weight_ref, sent_ref, whole):
+def pack_body(core_ref, z_ref, factors_ref, mine_ref, other_ref, sources_ref,
+              weight_ref, kernel_ref, sent_ref, whole):
     nf, rows, cols = sources_ref.shape
     quarter = rows // SIDE
-    body = sent_ref.shape[1] - RUN
-    length = body // nf
+    length = quarter
+    body = nf * length
     gather_parts(core_ref, mine_ref, other_ref, whole)
 
     def block(d, peak):
-        base = pl.multiple_of((z_ref[0] ^ d) * quarter + offset, RUN)
+        base = pl.multiple_of((z_ref[0] ^ d) * quarter, RUN)
         at = pl.ds(base, length)
         spread = jnp.dot(factors_ref[at, :], whole[...], preferred_element_type=F32)
         for f in range(nf):
@@ -93,6 +93,10 @@
                 tile = value[g * RUN : (g + 1) * RUN]
                 sent_ref[d, (g * nf + f) * RUN : (g * nf + f + 1) * RUN, :] = tile
                 peak = jnp.maximum(peak, jnp.abs(tile))
+        kernel = kernel_ref[z_ref[0] ^ d]
+        high = kernel.astype(BF16).astype(F32)
+        sent_ref[d, body + RUN : body + 2 * RUN, :] = high
+        sent_ref[d, body + 2 * RUN :, :] = kernel - high
         return peak
 
     peak = lax.fori_loop(0, SIDE, block, jnp.zeros((RUN, cols), F32))
@@ -100,15 +104,34 @@
     power, scale = scale_of(jnp.broadcast_to(peak, (1, cols)))
     for d in range(1, SIDE):
         sent_ref[d, :body, :] = sent_ref[d, :body, :] * jnp.broadcast_to(scale, (body, cols))
-        sent_ref[d, body:, :] = jnp.broadcast_to(power, (RUN, cols))
-
-
-def mix_body(own_ref, got1, got2, got3, kernel_ref, into_ref, out_ref, sent_ref):
+        sent_ref[d, body : body + RUN, :] = jnp.broadcast_to(power, (RUN, cols))
+
+
+def mix_body(own_ref, got1, got2, got3, into_ref, out_ref, sent_ref, turned, kernel_ref):
     cols = own_ref.shape[2]
-    body = own_ref.shape[1] - RUN
+    body = own_ref.shape[1] - 3 * RUN
     size = into_ref.shape[1]
     part = size // SIDE
     got = (got1, got2, got3)
+    nf = part // RUN
+    groups = body // part
+    each = LANES // RUN
+    for d, ref in enumerate((own_ref.at[0], *got)):
+        table = ref[body + RUN : body + 2 * RUN, :] + ref[body + 2 * RUN :, :]
+        turned[d] = table.T
+    strips = -(-groups // each)
+    for strip in range(strips):
+
+        def expand(j, carry, strip=strip):
+            for d in range(SIDE):
+                rows = turned[d, pl.ds(pl.multiple_of(j * RUN, RUN), RUN), :]
+                for f in range(nf):
+                    column = rows[:, f * strips + strip : f * strips + strip + 1]
+                    spot = (strip * each + j) * size + (d * nf + f) * RUN
+                    kernel_ref[pl.ds(pl.multiple_of(spot, RUN), RUN), :] = jnp.broadcast_to(column, (RUN, cols))
+            return carry
+
+        lax.fori_loop(0, min(each, groups - strip * each), expand, 0)
     gains = [jnp.exp2(jnp.broadcast_to(g[body : body + 1, :], (part, cols))) for g in got]
 
     def apply(table, value):
@@ -152,28 +175,27 @@
         sent_ref[d, body:, :] = jnp.broadcast_to(power, (RUN, cols))
 
 
-def unpack_body(splits, z_ref, right_ref, *refs):
+def unpack_body(z_ref, right_ref, *refs):
     nf, rows, cols = right_ref.shape
     quarter = rows // SIDE
     z = z_ref[0]
     sources_ref, rounded_ref = refs[-2:]
-    for h, (offset, length) in enumerate(splits):
-        body = nf * length
-        for d, ref in enumerate(refs[h * SIDE : (h + 1) * SIDE]):
-            base = (z ^ d) * quarter + offset
-            gain = jnp.exp2(jnp.broadcast_to(ref[body : body + 1, :], (RUN, cols))) if d else None
-
-            def step(g, carry, d=d, base=base, ref=ref, gain=gain):
-                at = pl.ds(pl.multiple_of(base + g * RUN, RUN), RUN)
-                for f in range(nf):
-                    spot = pl.ds(pl.multiple_of((g * nf + f) * RUN, RUN), RUN)
-                    tile = ref[spot, :] * gain if d else ref[0, spot, :]
-                    tile = right_ref[f, at, :] + tile
-                    sources_ref[f, at, :] = tile
-                    rounded_ref[at, f * cols : (f + 1) * cols] = tile.astype(BF16)
-                return carry
-
-            lax.fori_loop(0, length // RUN, step, 0)
+    body = nf * quarter
+    for d, ref in enumerate(refs[:SIDE]):
+        base = (z ^ d) * quarter
+        gain = jnp.exp2(jnp.broadcast_to(ref[body : body + 1, :], (RUN, cols))) if d else None
+
+        def step(g, carry, d=d, base=base, ref=ref, gain=gain):
+            at = pl.ds(pl.multiple_of(base + g * RUN, RUN), RUN)
+            for f in range(nf):
+                spot = pl.ds(pl.multiple_of((g * nf + f) * RUN, RUN), RUN)
+                tile = ref[spot, :] * gain if d else ref[0, spot, :]
+                tile = right_ref[f, at, :] + tile
+                sources_ref[f, at, :] = tile
+                rounded_ref[at, f * cols : (f + 1) * cols] = tile.astype(BF16)
+            return carry
+
+        lax.fori_loop(0, quarter // RUN, step, 0)
 
 
 def call(body, outs, name, scalars=0, args=(), scratch=()):
@@ -216,19 +238,19 @@
         got = lax.ppermute(sent, "fac", CORES)
         mine = project(factors_keep, rounded) + got
         own = lax.dynamic_slice(mine, (spot * chunk, 0), (chunk, wide))
-        for d in (1, 2, 3):
+        for d in PARTNERS:
             piece = lax.dynamic_slice(
                 mine, ((spot ^ d) * chunk, 0), (chunk, wide)
             ).astype(BF16)
             own = own + lax.ppermute(piece, "fac", along(d, True)).astype(F32)
         own = own.astype(BF16)
         total = own.astype(F32)
-        for d in (1, 2, 3):
+        for d in PARTNERS:
             total = total + lax.ppermute(own, "fac", along(d, False)).astype(F32)
         total = total.astype(BF16)
         gathered = jnp.zeros((half, wide), BF16)
         gathered = lax.dynamic_update_slice(gathered, total, (spot * chunk, 0))
-        for d in (1, 2, 3):
+        for d in PARTNERS:
             piece = lax.ppermute(total, "fac", along(d, True))
             gathered = lax.dynamic_update_slice(
                 gathered, piece, ((spot ^ d) * chunk, 0)
@@ -246,24 +268,20 @@
         )
 
     def exchange(sent):
-        return [
-            lax.ppermute(sent[d].astype(F16), "freq", swap(d)).astype(F32)
-            for d in range(1, SIDE)
-        ]
+        got = {}
+        for d in PARTNERS:
+            got[d] = lax.ppermute(sent[d].astype(F16), "freq", swap(d)).astype(F32)
+        return [got[d] for d in range(1, SIDE)]
 
     body = nf * quarter
     size = SIDE * nf * RUN
     weight = pair_weight[:, :, None]
     place_z = jnp.full((1,), z, jnp.int32)
-    kernel = [lax.dynamic_slice(second_order, (0, z * quarter), (nf, quarter))]
-    for d in (1, 2, 3):
-        piece = lax.dynamic_slice(
-            second_order, (0, (z ^ d) * quarter), (nf, quarter)
-        )
-        kernel.append(lax.ppermute(piece, "freq", swap(d)))
-    kernel = jnp.concatenate(kernel, axis=0).reshape(SIDE * nf, quarter // RUN, RUN)
-    kernel = kernel.transpose(1, 0, 2).reshape(body * SIDE, 1)
-    kernel = jnp.broadcast_to(kernel, (body * SIDE, cols))
+    strips = -(-quarter // LANES)
+    kernel = second_order.reshape(nf, SIDE, quarter).transpose(1, 0, 2)
+    kernel = jnp.pad(kernel, ((0, 0), (0, 0), (0, strips * LANES - quarter)))
+    kernel = kernel.reshape(SIDE, nf * strips, LANES)
+    kernel = jnp.pad(kernel, ((0, 0), (0, RUN - nf * strips), (0, 0)))
 
     row = jnp.arange(size)
     ring_at, f_at = row // (nf * RUN), row // RUN % nf
@@ -280,15 +298,10 @@
 
     table_in = spread_table(source, forward, source)
     table_out = spread_table(source, backward, source)
-    loads = [((body, cols), F32)] + [((body + RUN, cols), F32)] * 3
 
     core_at = jnp.full((1,), core, jnp.int32)
     column = pair_weight.T
     whole = [pltpu.VMEM((naux, wide), BF16)]
-    pair = 2 * RUN
-    first = (quarter // pair + 1) // 2 * pair
-    splits = ((0, first), (first, quarter - first))
-
     sources = right_side
     (rounded,) = call(round_body, [((rows, wide), BF16)], "round", 0, (right_side,))
     for outer in range(OUTER):
@@ -299,29 +312,21 @@
                 (core_at, factors, *parts, sources, column), whole,
             )
         parts = reduce_all(rounded)
-        packed = []
-        for offset, length in splits:
-            body = nf * length
-            loads = [((SIDE, body + RUN, cols), F32)]
-            (sent,) = call(
-                partial(pack_body, offset), loads, "pack", 2,
-                (core_at, place_z, factors, *parts, sources, column), whole,
-            )
-            packed.append((sent, exchange(sent)))
-        back = []
-        for (offset, length), (own, got) in zip(splits, packed):
-            body = nf * length
-            loads = [((SIDE, body + RUN, cols), F32)]
-            (sent,) = call(
-                mix_body, loads, "mix", 0,
-                (own, *got, kernel[offset * nf * SIDE : (offset + length) * nf * SIDE],
-                 table_in, table_out),
-            )
-            back += [sent, *exchange(sent)]
+        (sent,) = call(
+            pack_body, [((SIDE, body + 3 * RUN, cols), F32)], "pack", 2,
+            (core_at, place_z, factors, *parts, sources, column, kernel), whole,
+        )
+        got = exchange(sent)
+        (sent,) = call(
+            mix_body, [((SIDE, body + RUN, cols), F32)], "mix", 0,
+            (sent, *got, table_in, table_out),
+            [pltpu.VMEM((SIDE, LANES, RUN), F32), pltpu.VMEM((SIDE * body, cols), F32)],
+        )
+        back = [sent, *exchange(sent)]
         if outer == OUTER - 1:
             amplitude = sources + weight * spread_of(parts)
         sources, rounded = call(
-            partial(unpack_body, splits),
+            unpack_body,
             [(right_side.shape, F32), ((rows, wide), BF16)],
             "unpack", 1, (place_z, right_side, *back),
         )

time: 268 us -> 266 us (level)
  waiting for transfers between devices: 75 us -> 110 us
  starting transfers between devices: 109 us -> 83.9 us
  local copies, waits for them, and re-layouts: 24.4 us -> 15.1 us
    ppermute x27 -> x12, waiting for transfers between devices: 19.2 us -> 48.6 us  [exchange(): got[d] = lax.ppermute(sent[d].astype(F16), 'freq', swap(d)).astype(F32)]
    ppermute x27 -> x12, starting transfers between devices: 35.6 us -> 16.7 us  [exchange(): got[d] = lax.ppermute(sent[d].astype(F16), 'freq', swap(d)).astype(F32)]
    ppermute x4, starting transfers between devices: 20.4 us -> 15.2 us  [reduce_all(): other = lax.ppermute(gathered, 'fac', CORES)]
    slice x6 -> x0, local copies, waits for them, and re-layouts: 5.11 us -> none  [shards(): kernel[offset * nf * SIDE:(offset + length) * nf * SIDE]]
    pallas_call x13 -> x9, Pallas kernels: 31.9 us -> 29.8 us  [call(): pl.pallas_call(body, out_shape=[jax.ShapeDtypeStruct(s, t) for s, t in ou...]
    unnamed x61 -> x49, local copies, waits for them, and re-layouts: 9.56 us -> 8.68 us
  transfers between devices with their start and end apart: 71 -> 56, of which waited for: 42 -> 53; matrix products, arithmetic and copies ran while one was open for 10% -> 4% of each run, Pallas kernels for 7% -> 0%
where the time goes in v3:
time: 266 us; the launch traced here: 264 us
  waiting for transfers between devices  110 us (41%)
  starting transfers between devices  83.9 us (32%)
  Pallas kernels  29.8 us (11%)
  matrix products  16.3 us (6%)
  local copies, waits for them, and re-layouts  15.1 us (6%)
  other arithmetic  8 us (3%)
    ppermute x12, waiting for transfers between devices, exchange(): got[d] = lax.ppermute(sent[d].astype(F16), 'freq', swap(d)).astype(F32)  48.6 us
    pallas_call x9, Pallas kernels, call(): pl.pallas_call(body, out_shape=[jax.ShapeDtypeStruct(s, t) for s, t in ou...  29.8 us
    ppermute x12, starting transfers between devices, exchange(): got[d] = lax.ppermute(sent[d].astype(F16), 'freq', swap(d)).astype(F32)  16.7 us
    ppermute x12, waiting for transfers between devices, reduce_all(): own = own + lax.ppermute(piece, 'fac', along(d, True)).astype(F32)  16.5 us
    ppermute x12, starting transfers between devices, reduce_all(): own = own + lax.ppermute(piece, 'fac', along(d, True)).astype(F32)  16 us
    ppermute x12, starting transfers between devices, reduce_all(): total = total + lax.ppermute(own, 'fac', along(d, False)).astype(F32)  15.7 us
    ppermute x12, waiting for transfers between devices, reduce_all(): piece = lax.ppermute(total, 'fac', along(d, True))  15.5 us
    ppermute x12, starting transfers between devices, reduce_all(): piece = lax.ppermute(total, 'fac', along(d, True))  15.3 us
  transfers between devices with their start and end apart: 56, of which 53 were waited for; matrix products, arithmetic and copies ran while one was open for 4% of the time, Pallas kernels for 0%

profile of v3, /device:TPU:1, one launch (start us, length us, event | category | flops | bytes accessed | tf_op | source)
XLA Modules:
  0.0 263.9 jit_solution(5438561037551492571)
XLA Ops:
  4.0 1.8 fusion.13
  7.3 2.6 collective-permute-done
  9.9 3.1 %convolution_add_fusion.4 = f32[512,512]{1,0:T(8,128)} fusion(f32[512,512]{1,0:T(8,128)} %collective-permute-done, bf16[1152,512]{1,0:T(8,128)(2,1)S(1)} %round.1, bf16[1152,1024]{1,0:T(8,128)(2,1)S(1)} %copy-done.2, s32[]{:T(128)S(6)} %select_n.117), kind=kOutput, calls=%fused_computation.7 | convolution fusion | flops 604241920 | bytes 4456452 | tf_op jit(solution)/shard_map/dot_general | solution.py:232
  14.1 2.9 %collective-permute-start.3 = (bf16[128,512]{1,0:T(8,128)(2,1)S(1)}, bf16[128,512]{1,0:T(8,128)(2,1)S(1)}, u32[]{:S(2)}, u32[]{:S(2)}) collective-permute-start(bf16[128,512]{1,0:T(8,128)(2,1)S(1)} %get-tuple-element.38), channel_id=1, source_target_pairs={{0,24},{4,100},{8,16},{12,108},{16,8},{20,116},{24,0},{28,124},{32... | collective-permute-start | bytes 393224 | tf_op jit(solution)/shard_map/ppermute | solution.py:245
  23.7 2.6 collective-permute-start.6
  40.0 4.6 %collective-permute-start.10 = (bf16[512,512]{1,0:T(8,128)(2,1)S(1)}, bf16[512,512]{1,0:T(8,128)(2,1)}, u32[]{:S(2)}, u32[]{:S(2)}) collective-permute-start(bf16[512,512]{1,0:T(8,128)(2,1)S(1)} %constant_dynamic-update-slice_fusion.12.mine_ref), channel_id=1, source_target_pairs={{0,4},{4,0},{8,12},{12,8},{16,20},{20,16},{24,28},{28,24},{32,36},... | collective-permute-start | bytes 1572872 | tf_op jit(solution)/shard_map/ppermute | solution.py:258
  47.9 3.1 %ladder.2 = bf16[1152,512]{1,0:T(8,128)(2,1)S(1)} custom-call(s32[1]{0:T(128)} %bitcast.1.core_ref, bf16[1152,1024]{1,0:T(8,128)(2,1)S(1)} %copy-done.2, bf16[512,512]{1,0:T(8,128)(2,1)S(1)} %constant_dynamic-update-slice_fusion.12.mine_ref, bf16[512,512]{1,0:T(8,128)(2,1)} %collective-permute-done.10.other_ref, f32[4,1152,128]{2,1,0:T(8,128)S(1)} %copy-done.4, ...), custom_call_target="tpu_custom_call" | custom-call | tf_op jit(solution)/shard_map/ladder/pallas_call | solution.py:204
  52.3 2.3 collective-permute-done.11
  55.6 2.2 collective-permute-start.14
  57.8 1.7 collective-permute-start.12
  61.9 1.7 collective-permute-done.12
  65.3 2.9 %collective-permute-start.15 = (bf16[128,512]{1,0:T(8,128)(2,1)}, bf16[128,512]{1,0:T(8,128)(2,1)}, u32[]{:S(2)}, u32[]{:S(2)}) collective-permute-start(bf16[128,512]{1,0:T(8,128)(2,1)} %add_convert_fusion.5), channel_id=1, source_target_pairs={{0,64},{4,20},{8,72},{12,28},{16,80},{20,4},{24,88},{28,12},{32,96... | collective-permute-start | bytes 393224 | tf_op jit(solution)/shard_map/ppermute | solution.py:249
  70.3 1.9 collective-permute-done.15
  72.3 1.8 constant_dynamic-update-slice_fusion.11
  83.4 3.4 %collective-permute-start.21 = (bf16[512,512]{1,0:T(8,128)(2,1)S(1)}, bf16[512,512]{1,0:T(8,128)(2,1)S(1)}, u32[]{:S(2)}, u32[]{:S(2)}) collective-permute-start(bf16[512,512]{1,0:T(8,128)(2,1)S(1)} %constant_dynamic-update-slice_fusion.8.mine_ref), channel_id=1, source_target_pairs={{0,4},{4,0},{8,12},{12,8},{16,20},{20,16},{24,28},{28,24},{32,36},... | collective-permute-start | bytes 1572872 | tf_op jit(solution)/shard_map/ppermute | solution.py:258
  90.0 2.2 pack.2.own_ref
  94.3 3.3 %collective-permute-start.23 = (f16[1200,128]{1,0:T(8,128)(2,1)S(1)}, f16[1200,128]{1,0:T(8,128)(2,1)S(1)}, u32[]{:S(2)}, u32[]{:S(2)}) collective-permute-start(f16[1200,128]{1,0:T(8,128)(2,1)S(1)} %get-tuple-element.20), channel_id=1, source_target_pairs={{0,2},{1,3},{2,0},{3,1},{4,6},{5,7},{6,4},{7,5},{8,10},{9,11},{10,... | collective-permute-start | bytes 921608 | tf_op jit(solution)/shard_map/ppermute | solution.py:273
  98.0 3.6 %collective-permute-done.22 = f16[1200,128]{1,0:T(8,128)(2,1)S(1)} collective-permute-done((f16[1200,128]{1,0:T(8,128)(2,1)S(1)}, f16[1200,128]{1,0:T(8,128)(2,1)S(1)}, u32[]{:S(2)}, u32[]{:S(2)}) %collective-permute-start.22) | collective-permute-done | bytes 307232 | tf_op jit(solution)/shard_map/ppermute | solution.py:273
  101.6 9.7 %collective-permute-done.23 = f16[1200,128]{1,0:T(8,128)(2,1)S(1)} collective-permute-done((f16[1200,128]{1,0:T(8,128)(2,1)S(1)}, f16[1200,128]{1,0:T(8,128)(2,1)S(1)}, u32[]{:S(2)}, u32[]{:S(2)}) %collective-permute-start.23) | collective-permute-done | bytes 307232 | tf_op jit(solution)/shard_map/ppermute | solution.py:273
  111.4 1.9 collective-permute-done.24
  113.4 8.6 %mix.2.refs_0_ = f32[4,1168,128]{2,1,0:T(8,128)S(1)} custom-call(f32[4,1200,128]{2,1,0:T(8,128)S(1)} %pack.2.own_ref, f32[1200,128]{1,0:T(8,128)S(1)} %convert_element_type.263.got1, f32[1200,128]{1,0:T(8,128)S(1)} %convert_element_type.265.got2, f32[1200,128]{1,0:T(8,128)S(1)} %convert_element_type.267.got3, bf16[512,256]{1,0:T(8,128)(2,1)S(1)} %pad_maximum_fusion.into_ref, ...), custom_call_target="tpu_custom_call" | custom-call | tf_op jit(solution)/shard_map/mix/pallas_call | solution.py:204
  123.9 2.3 collective-permute-start.27
  126.2 2.9 %collective-permute-done.25 = f16[1168,128]{1,0:T(8,128)(2,1)S(1)} collective-permute-done((f16[1168,128]{1,0:T(8,128)(2,1)S(1)}, f16[1168,128]{1,0:T(8,128)(2,1)S(1)}, u32[]{:S(2)}, u32[]{:S(2)}) %collective-permute-start.25) | collective-permute-done | bytes 299040 | tf_op jit(solution)/shard_map/ppermute | solution.py:273
  129.2 6.8 %collective-permute-done.26 = f16[1168,128]{1,0:T(8,128)(2,1)S(1)} collective-permute-done((f16[1168,128]{1,0:T(8,128)(2,1)S(1)}, f16[1168,128]{1,0:T(8,128)(2,1)S(1)}, u32[]{:S(2)}, u32[]{:S(2)}) %collective-permute-start.26) | collective-permute-done | bytes 299040 | tf_op jit(solution)/shard_map/ppermute | solution.py:273
  136.0 2.4 collective-permute-done.27
  140.0 2.6 %collective-permute-start.28 = (f32[512,512]{1,0:T(8,128)S(1)}, f32[512,512]{1,0:T(8,128)S(1)}, u32[]{:S(2)}, u32[]{:S(2)}) collective-permute-start(f32[512,512]{1,0:T(8,128)S(1)} %fusion.9), channel_id=1, source_target_pairs={{0,4},{4,0},{8,12},{12,8},{16,20},{20,16},{24,28},{28,24},{32,36},... | collective-permute-start | bytes 3145736 | tf_op jit(solution)/shard_map/ppermute | solution.py:238
  142.7 2.3 collective-permute-done.28
  145.9 2.3 collective-permute-start.31
  154.0 1.8 collective-permute-start.34
  155.8 2.1 collective-permute-start.32
  159.6 2.1 collective-permute-done.32
  170.0 4.0 %collective-permute-start.38 = (bf16[512,512]{1,0:T(8,128)(2,1)S(1)}, bf16[512,512]{1,0:T(8,128)(2,1)S(1)}, u32[]{:S(2)}, u32[]{:S(2)}) collective-permute-start(bf16[512,512]{1,0:T(8,128)(2,1)S(1)} %constant_dynamic-update-slice_fusion.4.mine_ref), channel_id=1, source_target_pairs={{0,4},{4,0},{8,12},{12,8},{16,20},{20,16},{24,28},{28,24},{32,36},... | collective-permute-start | bytes 1572872 | tf_op jit(solution)/shard_map/ppermute | solution.py:258
  175.5 2.0 ladder.3
  178.9 2.3 collective-permute-done.39
  182.2 2.2 collective-permute-start.42
  191.3 2.9 %collective-permute-start.43 = (bf16[128,512]{1,0:T(8,128)(2,1)S(1)}, bf16[128,512]{1,0:T(8,128)(2,1)S(1)}, u32[]{:S(2)}, u32[]{:S(2)}) collective-permute-start(bf16[128,512]{1,0:T(8,128)(2,1)S(1)} %add_convert_fusion.1), channel_id=1, source_target_pairs={{0,64},{4,20},{8,72},{12,28},{16,80},{20,4},{24,88},{28,12},{32,96... | collective-permute-start | bytes 393224 | tf_op jit(solution)/shard_map/ppermute | solution.py:249
  195.3 2.6 collective-permute-done.43
  206.2 3.3 %collective-permute-start.49 = (bf16[512,512]{1,0:T(8,128)(2,1)S(1)}, bf16[512,512]{1,0:T(8,128)(2,1)S(1)}, u32[]{:S(2)}, u32[]{:S(2)}) collective-permute-start(bf16[512,512]{1,0:T(8,128)(2,1)S(1)} %constant_dynamic-update-slice_fusion.mine_ref), channel_id=1, source_target_pairs={{0,4},{4,0},{8,12},{12,8},{16,20},{20,16},{24,28},{28,24},{32,36},... | collective-permute-start | bytes 1572872 | tf_op jit(solution)/shard_map/ppermute | solution.py:258
  211.0 2.3 pack.3.own_ref
  215.8 3.5 %collective-permute-start.51 = (f16[1200,128]{1,0:T(8,128)(2,1)}, f16[1200,128]{1,0:T(8,128)(2,1)}, u32[]{:S(2)}, u32[]{:S(2)}) collective-permute-start(f16[1200,128]{1,0:T(8,128)(2,1)} %get-tuple-element.17), channel_id=1, source_target_pairs={{0,2},{1,3},{2,0},{3,1},{4,6},{5,7},{6,4},{7,5},{8,10},{9,11},{10,... | collective-permute-start | bytes 921608 | tf_op jit(solution)/shard_map/ppermute | solution.py:273
  221.7 2.9 %collective-permute-done.50 = f16[1200,128]{1,0:T(8,128)(2,1)} collective-permute-done((f16[1200,128]{1,0:T(8,128)(2,1)}, f16[1200,128]{1,0:T(8,128)(2,1)}, u32[]{:S(2)}, u32[]{:S(2)}) %collective-permute-start.50) | collective-permute-done | bytes 307232 | tf_op jit(solution)/shard_map/ppermute | solution.py:273
  225.6 7.7 %collective-permute-done.51 = f16[1200,128]{1,0:T(8,128)(2,1)} collective-permute-done((f16[1200,128]{1,0:T(8,128)(2,1)}, f16[1200,128]{1,0:T(8,128)(2,1)}, u32[]{:S(2)}, u32[]{:S(2)}) %collective-permute-start.51) | collective-permute-done | bytes 307232 | tf_op jit(solution)/shard_map/ppermute | solution.py:273
  236.3 8.5 %mix.3.refs_0_ = f32[4,1168,128]{2,1,0:T(8,128)S(1)} custom-call(f32[4,1200,128]{2,1,0:T(8,128)S(1)} %copy-done.9, f32[1200,128]{1,0:T(8,128)S(1)} %convert_element_type.299.got1, f32[1200,128]{1,0:T(8,128)S(1)} %convert_element_type.301.got2, f32[1200,128]{1,0:T(8,128)S(1)} %convert_element_type.303.got3, bf16[512,256]{1,0:T(8,128)(2,1)S(1)} %copy-done.13, ...), custom_call_target="tpu_custom_call" | custom-call | tf_op jit(solution)/shard_map/mix/pallas_call | solution.py:204
  246.9 2.3 collective-permute-start.55
  249.2 2.3 fusion.2
  252.2 6.5 %collective-permute-done.54 = f16[1168,128]{1,0:T(8,128)(2,1)S(1)} collective-permute-done((f16[1168,128]{1,0:T(8,128)(2,1)S(1)}, f16[1168,128]{1,0:T(8,128)(2,1)S(1)}, u32[]{:S(2)}, u32[]{:S(2)}) %collective-permute-start.54) | collective-permute-done | bytes 299040 | tf_op jit(solution)/shard_map/ppermute | solution.py:273
  258.7 2.7 %collective-permute-done.55 = f16[1168,128]{1,0:T(8,128)(2,1)S(1)} collective-permute-done((f16[1168,128]{1,0:T(8,128)(2,1)S(1)}, f16[1168,128]{1,0:T(8,128)(2,1)S(1)}, u32[]{:S(2)}, u32[]{:S(2)}) %collective-permute-start.55) | collective-permute-done | bytes 299040 | tf_op jit(solution)/shard_map/ppermute | solution.py:273
  261.5 2.4 unpack.3
  (194 shorter events, 106.6 us)
Async XLA Ops:
  14.1 5.5 %collective-permute-start.3 = (bf16[128,512]{1,0:T(8,128)(2,1)S(1)}, bf16[128,512]{1,0:T(8,128)(2,1)S(1)}, u32[]{:S(2)}, u32[]{:S(2)}) collective-permute-start(bf16[128,512]{1,0:T(8,128)(2,1)S(1)} %get-tuple-element.38), channel_id=1, source_target_pairs={{0,24},{4,100},{8,16},{12,108},{16,8},{20,116},{24,0},{28,124},{32... | collective-permute-start | bytes 393224 | tf_op jit(solution)/shard_map/ppermute | solution.py:245
  17.0 4.1 %collective-permute-start.2 = (bf16[128,512]{1,0:T(8,128)(2,1)S(1)}, bf16[128,512]{1,0:T(8,128)(2,1)S(1)}, u32[]{:S(2)}, u32[]{:S(2)}) collective-permute-start(bf16[128,512]{1,0:T(8,128)(2,1)S(1)} %get-tuple-element.39), channel_id=1, source_target_pairs={{0,8},{4,36},{8,0},{12,44},{16,24},{20,52},{24,16},{28,60},{32,40}... | collective-permute-start | bytes 393224 | tf_op jit(solution)/shard_map/ppermute | solution.py:245
  17.0 5.6 %collective-permute-start.1 = (bf16[128,512]{1,0:T(8,128)(2,1)S(1)}, bf16[128,512]{1,0:T(8,128)(2,1)S(1)}, u32[]{:S(2)}, u32[]{:S(2)}) collective-permute-start(bf16[128,512]{1,0:T(8,128)(2,1)S(1)} %get-tuple-element.37), channel_id=1, source_target_pairs={{0,16},{4,68},{8,24},{12,76},{16,0},{20,84},{24,8},{28,92},{32,48}... | collective-permute-start | bytes 393224 | tf_op jit(solution)/shard_map/ppermute | solution.py:245
  23.7 5.1 %collective-permute-start.6 = (bf16[128,512]{1,0:T(8,128)(2,1)S(1)}, bf16[128,512]{1,0:T(8,128)(2,1)S(1)}, u32[]{:S(2)}, u32[]{:S(2)}) collective-permute-start(bf16[128,512]{1,0:T(8,128)(2,1)S(1)} %add_convert_fusion.7), channel_id=1, source_target_pairs={{0,96},{4,28},{8,104},{12,20},{16,112},{20,12},{24,120},{28,4},{32... | collective-permute-start | bytes 393224 | tf_op jit(solution)/shard_map/ppermute | solution.py:249
  26.2 4.1 %collective-permute-start.5 = (bf16[128,512]{1,0:T(8,128)(2,1)S(1)}, bf16[128,512]{1,0:T(8,128)(2,1)S(1)}, u32[]{:S(2)}, u32[]{:S(2)}) collective-permute-start(bf16[128,512]{1,0:T(8,128)(2,1)S(1)} %add_convert_fusion.7), channel_id=1, source_target_pairs={{0,32},{4,12},{8,40},{12,4},{16,48},{20,28},{24,56},{28,20},{32,0}... | collective-permute-start | bytes 393224 | tf_op jit(solution)/shard_map/ppermute | solution.py:249
  26.2 5.3 %collective-permute-start.4 = (bf16[128,512]{1,0:T(8,128)(2,1)S(1)}, bf16[128,512]{1,0:T(8,128)(2,1)S(1)}, u32[]{:S(2)}, u32[]{:S(2)}) collective-permute-start(bf16[128,512]{1,0:T(8,128)(2,1)S(1)} %add_convert_fusion.7), channel_id=1, source_target_pairs={{0,64},{4,20},{8,72},{12,28},{16,80},{20,4},{24,88},{28,12},{32,96... | collective-permute-start | bytes 393224 | tf_op jit(solution)/shard_map/ppermute | solution.py:249
  31.7 5.4 %collective-permute-start.7 = (bf16[128,512]{1,0:T(8,128)(2,1)S(1)}, bf16[128,512]{1,0:T(8,128)(2,1)S(1)}, u32[]{:S(2)}, u32[]{:S(2)}) collective-permute-start(bf16[128,512]{1,0:T(8,128)(2,1)S(1)} %get-tuple-element.15), channel_id=1, source_target_pairs={{0,16},{4,68},{8,24},{12,76},{16,0},{20,84},{24,8},{28,92},{32,48}... | collective-permute-start | bytes 393224 | tf_op jit(solution)/shard_map/ppermute | solution.py:254
  33.1 5.3 %collective-permute-start.8 = (bf16[128,512]{1,0:T(8,128)(2,1)S(1)}, bf16[128,512]{1,0:T(8,128)(2,1)S(1)}, u32[]{:S(2)}, u32[]{:S(2)}) collective-permute-start(bf16[128,512]{1,0:T(8,128)(2,1)S(1)} %get-tuple-element.15), channel_id=1, source_target_pairs={{0,8},{4,36},{8,0},{12,44},{16,24},{20,52},{24,16},{28,60},{32,40}... | collective-permute-start | bytes 393224 | tf_op jit(solution)/shard_map/ppermute | solution.py:254
  34.6 5.3 %collective-permute-start.9 = (bf16[128,512]{1,0:T(8,128)(2,1)S(1)}, bf16[128,512]{1,0:T(8,128)(2,1)S(1)}, u32[]{:S(2)}, u32[]{:S(2)}) collective-permute-start(bf16[128,512]{1,0:T(8,128)(2,1)S(1)} %get-tuple-element.15), channel_id=1, source_target_pairs={{0,24},{4,100},{8,16},{12,108},{16,8},{20,116},{24,0},{28,124},{32... | collective-permute-start | bytes 393224 | tf_op jit(solution)/shard_map/ppermute | solution.py:254
  40.0 6.2 %collective-permute-start.10 = (bf16[512,512]{1,0:T(8,128)(2,1)S(1)}, bf16[512,512]{1,0:T(8,128)(2,1)}, u32[]{:S(2)}, u32[]{:S(2)}) collective-permute-start(bf16[512,512]{1,0:T(8,128)(2,1)S(1)} %constant_dynamic-update-slice_fusion.12.mine_ref), channel_id=1, source_target_pairs={{0,4},{4,0},{8,12},{12,8},{16,20},{20,16},{24,28},{28,24},{32,36},... | collective-permute-start | bytes 1572872 | tf_op jit(solution)/shard_map/ppermute | solution.py:258
  55.6 5.4 %collective-permute-start.14 = (bf16[128,512]{1,0:T(8,128)(2,1)S(1)}, bf16[128,512]{1,0:T(8,128)(2,1)S(1)}, u32[]{:S(2)}, u32[]{:S(2)}) collective-permute-start(bf16[128,512]{1,0:T(8,128)(2,1)S(1)} %get-tuple-element.35), channel_id=1, source_target_pairs={{0,24},{4,100},{8,16},{12,108},{16,8},{20,116},{24,0},{28,124},{32... | collective-permute-start | bytes 393224 | tf_op jit(solution)/shard_map/ppermute | solution.py:245
  57.8 5.8 %collective-permute-start.12 = (bf16[128,512]{1,0:T(8,128)(2,1)S(1)}, bf16[128,512]{1,0:T(8,128)(2,1)S(1)}, u32[]{:S(2)}, u32[]{:S(2)}) collective-permute-start(bf16[128,512]{1,0:T(8,128)(2,1)S(1)} %get-tuple-element.34), channel_id=1, source_target_pairs={{0,16},{4,68},{8,24},{12,76},{16,0},{20,84},{24,8},{28,92},{32,48}... | collective-permute-start | bytes 393224 | tf_op jit(solution)/shard_map/ppermute | solution.py:245
  64.3 5.3 %collective-permute-start.17 = (bf16[128,512]{1,0:T(8,128)(2,1)}, bf16[128,512]{1,0:T(8,128)(2,1)}, u32[]{:S(2)}, u32[]{:S(2)}) collective-permute-start(bf16[128,512]{1,0:T(8,128)(2,1)} %add_convert_fusion.5), channel_id=1, source_target_pairs={{0,96},{4,28},{8,104},{12,20},{16,112},{20,12},{24,120},{28,4},{32... | collective-permute-start | bytes 393224 | tf_op jit(solution)/shard_map/ppermute | solution.py:249
  65.3 4.4 %collective-permute-start.16 = (bf16[128,512]{1,0:T(8,128)(2,1)}, bf16[128,512]{1,0:T(8,128)(2,1)S(1)}, u32[]{:S(2)}, u32[]{:S(2)}) collective-permute-start(bf16[128,512]{1,0:T(8,128)(2,1)} %add_convert_fusion.5), channel_id=1, source_target_pairs={{0,32},{4,12},{8,40},{12,4},{16,48},{20,28},{24,56},{28,20},{32,0}... | collective-permute-start | bytes 393224 | tf_op jit(solution)/shard_map/ppermute | solution.py:249
  65.3 7.0 %collective-permute-start.15 = (bf16[128,512]{1,0:T(8,128)(2,1)}, bf16[128,512]{1,0:T(8,128)(2,1)}, u32[]{:S(2)}, u32[]{:S(2)}) collective-permute-start(bf16[128,512]{1,0:T(8,128)(2,1)} %add_convert_fusion.5), channel_id=1, source_target_pairs={{0,64},{4,20},{8,72},{12,28},{16,80},{20,4},{24,88},{28,12},{32,96... | collective-permute-start | bytes 393224 | tf_op jit(solution)/shard_map/ppermute | solution.py:249
  74.1 5.6 %collective-permute-start.18 = (bf16[128,512]{1,0:T(8,128)(2,1)}, bf16[128,512]{1,0:T(8,128)(2,1)}, u32[]{:S(2)}, u32[]{:S(2)}) collective-permute-start(bf16[128,512]{1,0:T(8,128)(2,1)} %get-tuple-element.13), channel_id=1, source_target_pairs={{0,16},{4,68},{8,24},{12,76},{16,0},{20,84},{24,8},{28,92},{32,48}... | collective-permute-start | bytes 393224 | tf_op jit(solution)/shard_map/ppermute | solution.py:254
  75.7 5.2 %collective-permute-start.19 = (bf16[128,512]{1,0:T(8,128)(2,1)}, bf16[128,512]{1,0:T(8,128)(2,1)}, u32[]{:S(2)}, u32[]{:S(2)}) collective-permute-start(bf16[128,512]{1,0:T(8,128)(2,1)} %get-tuple-element.13), channel_id=1, source_target_pairs={{0,8},{4,36},{8,0},{12,44},{16,24},{20,52},{24,16},{28,60},{32,40}... | collective-permute-start | bytes 393224 | tf_op jit(solution)/shard_map/ppermute | solution.py:254
  77.9 5.5 %collective-permute-start.20 = (bf16[128,512]{1,0:T(8,128)(2,1)}, bf16[128,512]{1,0:T(8,128)(2,1)S(1)}, u32[]{:S(2)}, u32[]{:S(2)}) collective-permute-start(bf16[128,512]{1,0:T(8,128)(2,1)} %get-tuple-element.13), channel_id=1, source_target_pairs={{0,24},{4,100},{8,16},{12,108},{16,8},{20,116},{24,0},{28,124},{32... | collective-permute-start | bytes 393224 | tf_op jit(solution)/shard_map/ppermute | solution.py:254
  83.4 4.9 %collective-permute-start.21 = (bf16[512,512]{1,0:T(8,128)(2,1)S(1)}, bf16[512,512]{1,0:T(8,128)(2,1)S(1)}, u32[]{:S(2)}, u32[]{:S(2)}) collective-permute-start(bf16[512,512]{1,0:T(8,128)(2,1)S(1)} %constant_dynamic-update-slice_fusion.8.mine_ref), channel_id=1, source_target_pairs={{0,4},{4,0},{8,12},{12,8},{16,20},{20,16},{24,28},{28,24},{32,36},... | collective-permute-start | bytes 1572872 | tf_op jit(solution)/shard_map/ppermute | solution.py:258
  92.6 9.0 %collective-permute-start.22 = (f16[1200,128]{1,0:T(8,128)(2,1)S(1)}, f16[1200,128]{1,0:T(8,128)(2,1)S(1)}, u32[]{:S(2)}, u32[]{:S(2)}) collective-permute-start(f16[1200,128]{1,0:T(8,128)(2,1)S(1)} %get-tuple-element.21), channel_id=1, source_target_pairs={{0,1},{1,0},{2,3},{3,2},{4,5},{5,4},{6,7},{7,6},{8,9},{9,8},{10,11... | collective-permute-start | bytes 921608 | tf_op jit(solution)/shard_map/ppermute | solution.py:273
  94.3 17.0 %collective-permute-start.23 = (f16[1200,128]{1,0:T(8,128)(2,1)S(1)}, f16[1200,128]{1,0:T(8,128)(2,1)S(1)}, u32[]{:S(2)}, u32[]{:S(2)}) collective-permute-start(f16[1200,128]{1,0:T(8,128)(2,1)S(1)} %get-tuple-element.20), channel_id=1, source_target_pairs={{0,2},{1,3},{2,0},{3,1},{4,6},{5,7},{6,4},{7,5},{8,10},{9,11},{10,... | collective-permute-start | bytes 921608 | tf_op jit(solution)/shard_map/ppermute | solution.py:273
  97.6 15.7 %collective-permute-start.24 = (f16[1200,128]{1,0:T(8,128)(2,1)S(1)}, f16[1200,128]{1,0:T(8,128)(2,1)S(1)}, u32[]{:S(2)}, u32[]{:S(2)}) collective-permute-start(f16[1200,128]{1,0:T(8,128)(2,1)S(1)} %get-tuple-element.19), channel_id=1, source_target_pairs={{0,3},{1,2},{2,1},{3,0},{4,7},{5,6},{6,5},{7,4},{8,11},{9,10},{10,... | collective-permute-start | bytes 921608 | tf_op jit(solution)/shard_map/ppermute | solution.py:273
  122.3 6.9 %collective-permute-start.25 = (f16[1168,128]{1,0:T(8,128)(2,1)S(1)}, f16[1168,128]{1,0:T(8,128)(2,1)S(1)}, u32[]{:S(2)}, u32[]{:S(2)}) collective-permute-start(f16[1168,128]{1,0:T(8,128)(2,1)S(1)} %get-tuple-element.27), channel_id=1, source_target_pairs={{0,1},{1,0},{2,3},{3,2},{4,5},{5,4},{6,7},{7,6},{8,9},{9,8},{10,11... | collective-permute-start | bytes 897032 | tf_op jit(solution)/shard_map/ppermute | solution.py:273
  122.4 13.6 %collective-permute-start.26 = (f16[1168,128]{1,0:T(8,128)(2,1)S(1)}, f16[1168,128]{1,0:T(8,128)(2,1)S(1)}, u32[]{:S(2)}, u32[]{:S(2)}) collective-permute-start(f16[1168,128]{1,0:T(8,128)(2,1)S(1)} %get-tuple-element.26), channel_id=1, source_target_pairs={{0,2},{1,3},{2,0},{3,1},{4,6},{5,7},{6,4},{7,5},{8,10},{9,11},{10,... | collective-permute-start | bytes 897032 | tf_op jit(solution)/shard_map/ppermute | solution.py:273
  123.9 14.6 %collective-permute-start.27 = (f16[1168,128]{1,0:T(8,128)(2,1)S(1)}, f16[1168,128]{1,0:T(8,128)(2,1)S(1)}, u32[]{:S(2)}, u32[]{:S(2)}) collective-permute-start(f16[1168,128]{1,0:T(8,128)(2,1)S(1)} %get-tuple-element.25), channel_id=1, source_target_pairs={{0,3},{1,2},{2,1},{3,0},{4,7},{5,6},{6,5},{7,4},{8,11},{9,10},{10,... | collective-permute-start | bytes 897032 | tf_op jit(solution)/shard_map/ppermute | solution.py:273
  140.0 4.9 %collective-permute-start.28 = (f32[512,512]{1,0:T(8,128)S(1)}, f32[512,512]{1,0:T(8,128)S(1)}, u32[]{:S(2)}, u32[]{:S(2)}) collective-permute-start(f32[512,512]{1,0:T(8,128)S(1)} %fusion.9), channel_id=1, source_target_pairs={{0,4},{4,0},{8,12},{12,8},{16,20},{20,16},{24,28},{28,24},{32,36},... | collective-permute-start | bytes 3145736 | tf_op jit(solution)/shard_map/ppermute | solution.py:238
  145.9 5.4 %collective-permute-start.31 = (bf16[128,512]{1,0:T(8,128)(2,1)S(1)}, bf16[128,512]{1,0:T(8,128)(2,1)S(1)}, u32[]{:S(2)}, u32[]{:S(2)}) collective-permute-start(bf16[128,512]{1,0:T(8,128)(2,1)S(1)} %get-tuple-element.32), channel_id=1, source_target_pairs={{0,24},{4,100},{8,16},{12,108},{16,8},{20,116},{24,0},{28,124},{32... | collective-permute-start | bytes 393224 | tf_op jit(solution)/shard_map/ppermute | solution.py:245
  148.2 5.7 %collective-permute-start.29 = (bf16[128,512]{1,0:T(8,128)(2,1)S(1)}, bf16[128,512]{1,0:T(8,128)(2,1)S(1)}, u32[]{:S(2)}, u32[]{:S(2)}) collective-permute-start(bf16[128,512]{1,0:T(8,128)(2,1)S(1)} %get-tuple-element.31), channel_id=1, source_target_pairs={{0,16},{4,68},{8,24},{12,76},{16,0},{20,84},{24,8},{28,92},{32,48}... | collective-permute-start | bytes 393224 | tf_op jit(solution)/shard_map/ppermute | solution.py:245
  154.0 5.1 %collective-permute-start.34 = (bf16[128,512]{1,0:T(8,128)(2,1)S(1)}, bf16[128,512]{1,0:T(8,128)(2,1)S(1)}, u32[]{:S(2)}, u32[]{:S(2)}) collective-permute-start(bf16[128,512]{1,0:T(8,128)(2,1)S(1)} %add_convert_fusion.3), channel_id=1, source_target_pairs={{0,96},{4,28},{8,104},{12,20},{16,112},{20,12},{24,120},{28,4},{32... | collective-permute-start | bytes 393224 | tf_op jit(solution)/shard_map/ppermute | solution.py:249
  155.8 5.9 %collective-permute-start.32 = (bf16[128,512]{1,0:T(8,128)(2,1)S(1)}, bf16[128,512]{1,0:T(8,128)(2,1)S(1)}, u32[]{:S(2)}, u32[]{:S(2)}) collective-permute-start(bf16[128,512]{1,0:T(8,128)(2,1)S(1)} %add_convert_fusion.3), channel_id=1, source_target_pairs={{0,64},{4,20},{8,72},{12,28},{16,80},{20,4},{24,88},{28,12},{32,96... | collective-permute-start | bytes 393224 | tf_op jit(solution)/shard_map/ppermute | solution.py:249
  161.8 5.4 %collective-permute-start.35 = (bf16[128,512]{1,0:T(8,128)(2,1)S(1)}, bf16[128,512]{1,0:T(8,128)(2,1)S(1)}, u32[]{:S(2)}, u32[]{:S(2)}) collective-permute-start(bf16[128,512]{1,0:T(8,128)(2,1)S(1)} %get-tuple-element.11), channel_id=1, source_target_pairs={{0,16},{4,68},{8,24},{12,76},{16,0},{20,84},{24,8},{28,92},{32,48}... | collective-permute-start | bytes 393224 | tf_op jit(solution)/shard_map/ppermute | solution.py:254
  163.2 5.2 %collective-permute-start.36 = (bf16[128,512]{1,0:T(8,128)(2,1)S(1)}, bf16[128,512]{1,0:T(8,128)(2,1)S(1)}, u32[]{:S(2)}, u32[]{:S(2)}) collective-permute-start(bf16[128,512]{1,0:T(8,128)(2,1)S(1)} %get-tuple-element.11), channel_id=1, source_target_pairs={{0,8},{4,36},{8,0},{12,44},{16,24},{20,52},{24,16},{28,60},{32,40}... | collective-permute-start | bytes 393224 | tf_op jit(solution)/shard_map/ppermute | solution.py:254
  164.6 5.3 %collective-permute-start.37 = (bf16[128,512]{1,0:T(8,128)(2,1)S(1)}, bf16[128,512]{1,0:T(8,128)(2,1)S(1)}, u32[]{:S(2)}, u32[]{:S(2)}) collective-permute-start(bf16[128,512]{1,0:T(8,128)(2,1)S(1)} %get-tuple-element.11), channel_id=1, source_target_pairs={{0,24},{4,100},{8,16},{12,108},{16,8},{20,116},{24,0},{28,124},{32... | collective-permute-start | bytes 393224 | tf_op jit(solution)/shard_map/ppermute | solution.py:254
  170.0 5.5 %collective-permute-start.38 = (bf16[512,512]{1,0:T(8,128)(2,1)S(1)}, bf16[512,512]{1,0:T(8,128)(2,1)S(1)}, u32[]{:S(2)}, u32[]{:S(2)}) collective-permute-start(bf16[512,512]{1,0:T(8,128)(2,1)S(1)} %constant_dynamic-update-slice_fusion.4.mine_ref), channel_id=1, source_target_pairs={{0,4},{4,0},{8,12},{12,8},{16,20},{20,16},{24,28},{28,24},{32,36},... | collective-permute-start | bytes 1572872 | tf_op jit(solution)/shard_map/ppermute | solution.py:258
  182.2 5.4 %collective-permute-start.42 = (bf16[128,512]{1,0:T(8,128)(2,1)S(1)}, bf16[128,512]{1,0:T(8,128)(2,1)S(1)}, u32[]{:S(2)}, u32[]{:S(2)}) collective-permute-start(bf16[128,512]{1,0:T(8,128)(2,1)S(1)} %get-tuple-element.29), channel_id=1, source_target_pairs={{0,24},{4,100},{8,16},{12,108},{16,8},{20,116},{24,0},{28,124},{32... | collective-permute-start | bytes 393224 | tf_op jit(solution)/shard_map/ppermute | solution.py:245
  184.4 5.8 %collective-permute-start.40 = (bf16[128,512]{1,0:T(8,128)(2,1)S(1)}, bf16[128,512]{1,0:T(8,128)(2,1)S(1)}, u32[]{:S(2)}, u32[]{:S(2)}) collective-permute-start(bf16[128,512]{1,0:T(8,128)(2,1)S(1)} %get-tuple-element.28), channel_id=1, source_target_pairs={{0,16},{4,68},{8,24},{12,76},{16,0},{20,84},{24,8},{28,92},{32,48}... | collective-permute-start | bytes 393224 | tf_op jit(solution)/shard_map/ppermute | solution.py:245
  190.2 5.1 %collective-permute-start.45 = (bf16[128,512]{1,0:T(8,128)(2,1)S(1)}, bf16[128,512]{1,0:T(8,128)(2,1)S(1)}, u32[]{:S(2)}, u32[]{:S(2)}) collective-permute-start(bf16[128,512]{1,0:T(8,128)(2,1)S(1)} %add_convert_fusion.1), channel_id=1, source_target_pairs={{0,96},{4,28},{8,104},{12,20},{16,112},{20,12},{24,120},{28,4},{32... | collective-permute-start | bytes 393224 | tf_op jit(solution)/shard_map/ppermute | solution.py:249
  191.3 6.6 %collective-permute-start.43 = (bf16[128,512]{1,0:T(8,128)(2,1)S(1)}, bf16[128,512]{1,0:T(8,128)(2,1)S(1)}, u32[]{:S(2)}, u32[]{:S(2)}) collective-permute-start(bf16[128,512]{1,0:T(8,128)(2,1)S(1)} %add_convert_fusion.1), channel_id=1, source_target_pairs={{0,64},{4,20},{8,72},{12,28},{16,80},{20,4},{24,88},{28,12},{32,96... | collective-permute-start | bytes 393224 | tf_op jit(solution)/shard_map/ppermute | solution.py:249
  198.0 5.4 %collective-permute-start.46 = (bf16[128,512]{1,0:T(8,128)(2,1)S(1)}, bf16[128,512]{1,0:T(8,128)(2,1)S(1)}, u32[]{:S(2)}, u32[]{:S(2)}) collective-permute-start(bf16[128,512]{1,0:T(8,128)(2,1)S(1)} %get-tuple-element.9), channel_id=1, source_target_pairs={{0,16},{4,68},{8,24},{12,76},{16,0},{20,84},{24,8},{28,92},{32,48}... | collective-permute-start | bytes 393224 | tf_op jit(solution)/shard_map/ppermute | solution.py:254
  199.7 4.9 %collective-permute-start.47 = (bf16[128,512]{1,0:T(8,128)(2,1)S(1)}, bf16[128,512]{1,0:T(8,128)(2,1)S(1)}, u32[]{:S(2)}, u32[]{:S(2)}) collective-permute-start(bf16[128,512]{1,0:T(8,128)(2,1)S(1)} %get-tuple-element.9), channel_id=1, source_target_pairs={{0,8},{4,36},{8,0},{12,44},{16,24},{20,52},{24,16},{28,60},{32,40}... | collective-permute-start | bytes 393224 | tf_op jit(solution)/shard_map/ppermute | solution.py:254
  200.8 5.3 %collective-permute-start.48 = (bf16[128,512]{1,0:T(8,128)(2,1)S(1)}, bf16[128,512]{1,0:T(8,128)(2,1)S(1)}, u32[]{:S(2)}, u32[]{:S(2)}) collective-permute-start(bf16[128,512]{1,0:T(8,128)(2,1)S(1)} %get-tuple-element.9), channel_id=1, source_target_pairs={{0,24},{4,100},{8,16},{12,108},{16,8},{20,116},{24,0},{28,124},{32... | collective-permute-start | bytes 393224 | tf_op jit(solution)/shard_map/ppermute | solution.py:254
  206.2 4.8 %collective-permute-start.49 = (bf16[512,512]{1,0:T(8,128)(2,1)S(1)}, bf16[512,512]{1,0:T(8,128)(2,1)S(1)}, u32[]{:S(2)}, u32[]{:S(2)}) collective-permute-start(bf16[512,512]{1,0:T(8,128)(2,1)S(1)} %constant_dynamic-update-slice_fusion.mine_ref), channel_id=1, source_target_pairs={{0,4},{4,0},{8,12},{12,8},{16,20},{20,16},{24,28},{28,24},{32,36},... | collective-permute-start | bytes 1572872 | tf_op jit(solution)/shard_map/ppermute | solution.py:258
  215.8 8.8 %collective-permute-start.50 = (f16[1200,128]{1,0:T(8,128)(2,1)}, f16[1200,128]{1,0:T(8,128)(2,1)}, u32[]{:S(2)}, u32[]{:S(2)}) collective-permute-start(f16[1200,128]{1,0:T(8,128)(2,1)} %get-tuple-element.18), channel_id=1, source_target_pairs={{0,1},{1,0},{2,3},{3,2},{4,5},{5,4},{6,7},{7,6},{8,9},{9,8},{10,11... | collective-permute-start | bytes 921608 | tf_op jit(solution)/shard_map/ppermute | solution.py:273
  215.8 17.5 %collective-permute-start.51 = (f16[1200,128]{1,0:T(8,128)(2,1)}, f16[1200,128]{1,0:T(8,128)(2,1)}, u32[]{:S(2)}, u32[]{:S(2)}) collective-permute-start(f16[1200,128]{1,0:T(8,128)(2,1)} %get-tuple-element.17), channel_id=1, source_target_pairs={{0,2},{1,3},{2,0},{3,1},{4,6},{5,7},{6,4},{7,5},{8,10},{9,11},{10,... | collective-permute-start | bytes 921608 | tf_op jit(solution)/shard_map/ppermute | solution.py:273
  219.3 16.0 %collective-permute-start.52 = (f16[1200,128]{1,0:T(8,128)(2,1)}, f16[1200,128]{1,0:T(8,128)(2,1)}, u32[]{:S(2)}, u32[]{:S(2)}) collective-permute-start(f16[1200,128]{1,0:T(8,128)(2,1)} %get-tuple-element.16), channel_id=1, source_target_pairs={{0,3},{1,2},{2,1},{3,0},{4,7},{5,6},{6,5},{7,4},{8,11},{9,10},{10,... | collective-permute-start | bytes 921608 | tf_op jit(solution)/shard_map/ppermute | solution.py:273
  245.3 6.9 %collective-permute-start.53 = (f16[1168,128]{1,0:T(8,128)(2,1)S(1)}, f16[1168,128]{1,0:T(8,128)(2,1)S(1)}, u32[]{:S(2)}, u32[]{:S(2)}) collective-permute-start(f16[1168,128]{1,0:T(8,128)(2,1)S(1)} %get-tuple-element.24), channel_id=1, source_target_pairs={{0,1},{1,0},{2,3},{3,2},{4,5},{5,4},{6,7},{7,6},{8,9},{9,8},{10,11... | collective-permute-start | bytes 897032 | tf_op jit(solution)/shard_map/ppermute | solution.py:273
  245.4 13.3 %collective-permute-start.54 = (f16[1168,128]{1,0:T(8,128)(2,1)S(1)}, f16[1168,128]{1,0:T(8,128)(2,1)S(1)}, u32[]{:S(2)}, u32[]{:S(2)}) collective-permute-start(f16[1168,128]{1,0:T(8,128)(2,1)S(1)} %get-tuple-element.23), channel_id=1, source_target_pairs={{0,2},{1,3},{2,0},{3,1},{4,6},{5,7},{6,4},{7,5},{8,10},{9,11},{10,... | collective-permute-start | bytes 897032 | tf_op jit(solution)/shard_map/ppermute | solution.py:273
  246.9 14.6 %collective-permute-start.55 = (f16[1168,128]{1,0:T(8,128)(2,1)S(1)}, f16[1168,128]{1,0:T(8,128)(2,1)S(1)}, u32[]{:S(2)}, u32[]{:S(2)}) collective-permute-start(f16[1168,128]{1,0:T(8,128)(2,1)S(1)} %get-tuple-element.22), channel_id=1, source_target_pairs={{0,3},{1,2},{2,1},{3,0},{4,7},{5,6},{6,5},{7,4},{8,11},{9,10},{10,... | collective-permute-start | bytes 897032 | tf_op jit(solution)/shard_map/ppermute | solution.py:273
  (32 other events, 376.5 us)

commit v4 on v3

--- a/solution.py
+++ b/solution.py
@@ -1,3 +1,5 @@
+from functools import partial
+
 import jax
 import jax.numpy as jnp
 from jax import lax
@@ -107,7 +109,11 @@
         sent_ref[d, body : body + RUN, :] = jnp.broadcast_to(power, (RUN, cols))
 
 
-def mix_body(own_ref, got1, got2, got3, into_ref, out_ref, sent_ref, turned, kernel_ref):
+def mix_body(first, own_ref, got1, got2, got3, into_ref, out_ref, *refs):
+    if first:
+        sent_ref, kernel_ref, turned = refs
+    else:
+        kernel_ref, sent_ref = refs
     cols = own_ref.shape[2]
     body = own_ref.shape[1] - 3 * RUN
     size = into_ref.shape[1]
@@ -116,22 +122,24 @@
     nf = part // RUN
     groups = body // part
     each = LANES // RUN
-    for d, ref in enumerate((own_ref.at[0], *got)):
-        table = ref[body + RUN : body + 2 * RUN, :] + ref[body + 2 * RUN :, :]
-        turned[d] = table.T
     strips = -(-groups // each)
-    for strip in range(strips):
-
-        def expand(j, carry, strip=strip):
-            for d in range(SIDE):
-                rows = turned[d, pl.ds(pl.multiple_of(j * RUN, RUN), RUN), :]
-                for f in range(nf):
-                    column = rows[:, f * strips + strip : f * strips + strip + 1]
-                    spot = (strip * each + j) * size + (d * nf + f) * RUN
-                    kernel_ref[pl.ds(pl.multiple_of(spot, RUN), RUN), :] = jnp.broadcast_to(column, (RUN, cols))
-            return carry
-
-        lax.fori_loop(0, min(each, groups - strip * each), expand, 0)
+    if first:
+        for d, ref in enumerate((own_ref.at[0], *got)):
+            table = ref[body + RUN : body + 2 * RUN, :] + ref[body + 2 * RUN :, :]
+            turned[d] = table.T
+        for strip in range(strips):
+
+            def expand(j, carry, strip=strip):
+                for d in range(SIDE):
+                    rows = turned[d, pl.ds(pl.multiple_of(j * RUN, RUN), RUN), :]
+                    for f in range(nf):
+                        column = rows[:, f * strips + strip : f * strips + strip + 1]
+                        spot = (strip * each + j) * size + (d * nf + f) * RUN
+                        kernel_ref[pl.ds(pl.multiple_of(spot, RUN), RUN), :] = jnp.broadcast_to(column, (RUN, cols))
+                return carry
+
+            lax.fori_loop(0, min(each, groups - strip * each), expand, 0)
+    wide = 6 if groups % 6 == 0 else 2
     gains = [jnp.exp2(jnp.broadcast_to(g[body : body + 1, :], (part, cols))) for g in got]
 
     def apply(table, value):
@@ -144,21 +152,21 @@
     def step(g, peaks):
         sides = []
         kernels = []
-        for half in range(2):
-            at = pl.ds(pl.multiple_of((2 * g + half) * part, part), part)
+        for half in range(wide):
+            at = pl.ds(pl.multiple_of((wide * g + half) * part, part), part)
             sides.append(
                 jnp.concatenate(
                     [own_ref[0, at, :]] + [r[at, :] * s for r, s in zip(got, gains)], axis=0
                 )
             )
             kernels.append(
-                kernel_ref[pl.ds(pl.multiple_of((2 * g + half) * size, size), size), :]
+                kernel_ref[pl.ds(pl.multiple_of((wide * g + half) * size, size), size), :]
             )
         timed = apply(into_ref, jnp.concatenate(sides, axis=1))
         renewed = apply(out_ref, jnp.concatenate(kernels, axis=1) * timed)
         fresh = list(peaks)
-        for half in range(2):
-            at = pl.ds(pl.multiple_of((2 * g + half) * part, part), part)
+        for half in range(wide):
+            at = pl.ds(pl.multiple_of((wide * g + half) * part, part), part)
             for d in range(SIDE):
                 tile = renewed[d * part : (d + 1) * part, half * cols : (half + 1) * cols]
                 sent_ref[d, at, :] = tile
@@ -167,7 +175,7 @@
         return tuple(fresh)
 
     start = tuple(jnp.zeros((part, cols), F32) for _ in range(3))
-    peaks = lax.fori_loop(0, body // part // 2, step, start)
+    peaks = lax.fori_loop(0, groups // wide, step, start)
     for d, peak in enumerate(peaks, 1):
         peak = jnp.max(jnp.max(peak, axis=0, keepdims=True), axis=1, keepdims=True)
         power, scale = scale_of(jnp.broadcast_to(peak, (1, cols)))
@@ -198,7 +206,7 @@
         lax.fori_loop(0, quarter // RUN, step, 0)
 
 
-def call(body, outs, name, scalars=0, args=(), scratch=()):
+def call(body, outs, name, limit, scalars=0, args=(), scratch=()):
     spec = pl.BlockSpec(memory_space=pltpu.VMEM)
     flat = pl.BlockSpec(memory_space=pltpu.SMEM)
     return pl.pallas_call(
@@ -207,7 +215,7 @@
         in_specs=[flat] * scalars + [spec] * (len(args) - scalars),
         out_specs=[spec] * len(outs),
         scratch_shapes=list(scratch),
-        compiler_params=pltpu.CompilerParams(vmem_limit_bytes=40 << 20),
+        compiler_params=pltpu.CompilerParams(vmem_limit_bytes=limit << 20),
         interpret=INTERPRET,
         name=name,
     )(*args)
@@ -303,32 +311,39 @@
     column = pair_weight.T
     whole = [pltpu.VMEM((naux, wide), BF16)]
     sources = right_side
-    (rounded,) = call(round_body, [((rows, wide), BF16)], "round", 0, (right_side,))
+    (rounded,) = call(round_body, [((rows, wide), BF16)], "round", 4, 0, (right_side,))
     for outer in range(OUTER):
         for inner in range(INNER - 1):
             parts = reduce_all(rounded)
             (rounded,) = call(
-                ladder_body, [((rows, wide), BF16)], "ladder", 1,
+                ladder_body, [((rows, wide), BF16)], "ladder", 10, 1,
                 (core_at, factors, *parts, sources, column), whole,
             )
         parts = reduce_all(rounded)
         (sent,) = call(
-            pack_body, [((SIDE, body + 3 * RUN, cols), F32)], "pack", 2,
+            pack_body, [((SIDE, body + 3 * RUN, cols), F32)], "pack", 12, 2,
             (core_at, place_z, factors, *parts, sources, column, kernel), whole,
         )
         got = exchange(sent)
-        (sent,) = call(
-            mix_body, [((SIDE, body + RUN, cols), F32)], "mix", 0,
-            (sent, *got, table_in, table_out),
-            [pltpu.VMEM((SIDE, LANES, RUN), F32), pltpu.VMEM((SIDE * body, cols), F32)],
-        )
+        mixed = [((SIDE, body + RUN, cols), F32)]
+        tables = (table_in, table_out)
+        if outer == 0:
+            sent, spread_kernel = call(
+                partial(mix_body, True), mixed + [((SIDE * body, cols), F32)], "mix", 16, 0,
+                (sent, *got, *tables), [pltpu.VMEM((SIDE, LANES, RUN), F32)],
+            )
+        else:
+            (sent,) = call(
+                partial(mix_body, False), mixed, "mix", 16, 0,
+                (sent, *got, *tables, spread_kernel),
+            )
         back = [sent, *exchange(sent)]
         if outer == OUTER - 1:
             amplitude = sources + weight * spread_of(parts)
         sources, rounded = call(
             unpack_body,
             [(right_side.shape, F32), ((rows, wide), BF16)],
-            "unpack", 1, (place_z, right_side, *back),
+            "unpack", 4, 1, (place_z, right_side, *back),
         )
     return (amplitude, sources)
 

time: 266 us -> 260 us (0.977)
  Pallas kernels: 29.8 us -> 21.6 us
    pallas_call x9, Pallas kernels: 29.8 us -> 21.6 us  [call(): pl.pallas_call(body, out_shape=[jax.ShapeDtypeStruct(s, t) for s, t in ou...]
    unnamed x49 -> x53, local copies, waits for them, and re-layouts: 8.68 us -> 10.7 us
where the time goes in v4:
time: 260 us; the launch traced here: 258 us
  waiting for transfers between devices  110 us (42%)
  starting transfers between devices  83.9 us (32%)
  Pallas kernels  21.6 us (8%)
  local copies, waits for them, and re-layouts  17 us (7%)
  matrix products  16.1 us (6%)
  other arithmetic  8 us (3%)
    ppermute x12, waiting for transfers between devices, exchange(): got[d] = lax.ppermute(sent[d].astype(F16), 'freq', swap(d)).astype(F32)  48.8 us
    pallas_call x9, Pallas kernels, call(): pl.pallas_call(body, out_shape=[jax.ShapeDtypeStruct(s, t) for s, t in ou...  21.6 us
    ppermute x12, starting transfers between devices, exchange(): got[d] = lax.ppermute(sent[d].astype(F16), 'freq', swap(d)).astype(F32)  16.7 us
    ppermute x12, waiting for transfers between devices, reduce_all(): own = own + lax.ppermute(piece, 'fac', along(d, True)).astype(F32)  16.5 us
    ppermute x12, starting transfers between devices, reduce_all(): own = own + lax.ppermute(piece, 'fac', along(d, True)).astype(F32)  16 us
    ppermute x12, starting transfers between devices, reduce_all(): total = total + lax.ppermute(own, 'fac', along(d, False)).astype(F32)  15.7 us
    ppermute x12, waiting for transfers between devices, reduce_all(): piece = lax.ppermute(total, 'fac', along(d, True))  15.5 us
    ppermute x12, starting transfers between devices, reduce_all(): piece = lax.ppermute(total, 'fac', along(d, True))  15.3 us
  transfers between devices with their start and end apart: 56, of which 53 were waited for; matrix products, arithmetic and copies ran while one was open for 4% of the time, Pallas kernels for 0%

profile of v4, /device:TPU:1, one launch (start us, length us, event | category | flops | bytes accessed | tf_op | source)
XLA Modules:
  0.0 257.6 jit_solution(6428532708830363951)
XLA Ops:
  4.0 1.8 fusion.13
  7.3 2.6 %collective-permute-done = f32[512,512]{1,0:T(8,128)} collective-permute-done((f32[512,512]{1,0:T(8,128)}, f32[512,512]{1,0:T(8,128)}, u32[]{:S(2)}, u32[]{:S(2)}) %collective-permute-start) | collective-permute-done | bytes 1048608 | tf_op jit(solution)/shard_map/ppermute | solution.py:246
  9.9 3.1 %convolution_add_fusion.4 = f32[512,512]{1,0:T(8,128)} fusion(f32[512,512]{1,0:T(8,128)} %collective-permute-done, bf16[1152,512]{1,0:T(8,128)(2,1)S(1)} %round.1, bf16[1152,1024]{1,0:T(8,128)(2,1)S(1)} %copy-done.2, s32[]{:T(128)S(6)} %select_n.117), kind=kOutput, calls=%fused_computation.7 | convolution fusion | flops 604241920 | bytes 4456452 | tf_op jit(solution)/shard_map/dot_general | solution.py:240
  14.1 2.9 %collective-permute-start.3 = (bf16[128,512]{1,0:T(8,128)(2,1)S(1)}, bf16[128,512]{1,0:T(8,128)(2,1)S(1)}, u32[]{:S(2)}, u32[]{:S(2)}) collective-permute-start(bf16[128,512]{1,0:T(8,128)(2,1)S(1)} %get-tuple-element.42), channel_id=1, source_target_pairs={{0,24},{4,100},{8,16},{12,108},{16,8},{20,116},{24,0},{28,124},{32... | collective-permute-start | bytes 393224 | tf_op jit(solution)/shard_map/ppermute | solution.py:253
  23.7 2.6 collective-permute-start.6
  40.0 4.6 %collective-permute-start.10 = (bf16[512,512]{1,0:T(8,128)(2,1)S(1)}, bf16[512,512]{1,0:T(8,128)(2,1)}, u32[]{:S(2)}, u32[]{:S(2)}) collective-permute-start(bf16[512,512]{1,0:T(8,128)(2,1)S(1)} %constant_dynamic-update-slice_fusion.12.mine_ref), channel_id=1, source_target_pairs={{0,4},{4,0},{8,12},{12,8},{16,20},{20,16},{24,28},{28,24},{32,36},... | collective-permute-start | bytes 1572872 | tf_op jit(solution)/shard_map/ppermute | solution.py:266
  47.9 3.1 %ladder.2 = bf16[1152,512]{1,0:T(8,128)(2,1)S(1)} custom-call(s32[1]{0:T(128)} %bitcast.1.core_ref, bf16[1152,1024]{1,0:T(8,128)(2,1)S(1)} %copy-done.2, bf16[512,512]{1,0:T(8,128)(2,1)S(1)} %constant_dynamic-update-slice_fusion.12.mine_ref, bf16[512,512]{1,0:T(8,128)(2,1)} %collective-permute-done.10.other_ref, f32[4,1152,128]{2,1,0:T(8,128)S(1)} %copy-done.4, ...), custom_call_target="tpu_custom_call" | custom-call | tf_op jit(solution)/shard_map/ladder/pallas_call | solution.py:212
  52.3 2.3 collective-permute-done.11
  55.6 2.2 collective-permute-start.14
  57.8 1.7 collective-permute-start.12
  61.9 1.7 collective-permute-done.12
  65.3 2.9 %collective-permute-start.15 = (bf16[128,512]{1,0:T(8,128)(2,1)}, bf16[128,512]{1,0:T(8,128)(2,1)}, u32[]{:S(2)}, u32[]{:S(2)}) collective-permute-start(bf16[128,512]{1,0:T(8,128)(2,1)} %add_convert_fusion.5), channel_id=1, source_target_pairs={{0,64},{4,20},{8,72},{12,28},{16,80},{20,4},{24,88},{28,12},{32,96... | collective-permute-start | bytes 393224 | tf_op jit(solution)/shard_map/ppermute | solution.py:257
  70.3 1.9 collective-permute-done.15
  72.3 1.8 constant_dynamic-update-slice_fusion.11
  83.4 3.4 %collective-permute-start.21 = (bf16[512,512]{1,0:T(8,128)(2,1)S(1)}, bf16[512,512]{1,0:T(8,128)(2,1)S(1)}, u32[]{:S(2)}, u32[]{:S(2)}) collective-permute-start(bf16[512,512]{1,0:T(8,128)(2,1)S(1)} %constant_dynamic-update-slice_fusion.8.mine_ref), channel_id=1, source_target_pairs={{0,4},{4,0},{8,12},{12,8},{16,20},{20,16},{24,28},{28,24},{32,36},... | collective-permute-start | bytes 1572872 | tf_op jit(solution)/shard_map/ppermute | solution.py:266
  90.0 2.2 pack.2.own_ref
  94.3 3.3 %collective-permute-start.23 = (f16[1200,128]{1,0:T(8,128)(2,1)S(1)}, f16[1200,128]{1,0:T(8,128)(2,1)S(1)}, u32[]{:S(2)}, u32[]{:S(2)}) collective-permute-start(f16[1200,128]{1,0:T(8,128)(2,1)S(1)} %get-tuple-element.24), channel_id=1, source_target_pairs={{0,2},{1,3},{2,0},{3,1},{4,6},{5,7},{6,4},{7,5},{8,10},{9,11},{10,... | collective-permute-start | bytes 921608 | tf_op jit(solution)/shard_map/ppermute | solution.py:281
  98.0 3.6 %collective-permute-done.22 = f16[1200,128]{1,0:T(8,128)(2,1)S(1)} collective-permute-done((f16[1200,128]{1,0:T(8,128)(2,1)S(1)}, f16[1200,128]{1,0:T(8,128)(2,1)S(1)}, u32[]{:S(2)}, u32[]{:S(2)}) %collective-permute-start.22) | collective-permute-done | bytes 307232 | tf_op jit(solution)/shard_map/ppermute | solution.py:281
  101.6 9.7 %collective-permute-done.23 = f16[1200,128]{1,0:T(8,128)(2,1)S(1)} collective-permute-done((f16[1200,128]{1,0:T(8,128)(2,1)S(1)}, f16[1200,128]{1,0:T(8,128)(2,1)S(1)}, u32[]{:S(2)}, u32[]{:S(2)}) %collective-permute-start.23) | collective-permute-done | bytes 307232 | tf_op jit(solution)/shard_map/ppermute | solution.py:281
  111.4 1.9 collective-permute-done.24
  113.4 5.6 %mix.2 = (f32[4,1168,128]{2,1,0:T(8,128)S(1)}, f32[4608,128]{1,0:T(8,128)S(1)}) custom-call(f32[4,1200,128]{2,1,0:T(8,128)S(1)} %pack.2.own_ref, f32[1200,128]{1,0:T(8,128)S(1)} %convert_element_type.263.got1, f32[1200,128]{1,0:T(8,128)S(1)} %convert_element_type.265.got2, f32[1200,128]{1,0:T(8,128)S(1)} %convert_element_type.267.got3, ...), custom_call_target="tpu_custom_call" | custom-call | tf_op jit(solution)/shard_map/mix/pallas_call | solution.py:212
  122.1 2.4 collective-permute-start.27
  124.5 2.9 %collective-permute-done.25 = f16[1168,128]{1,0:T(8,128)(2,1)S(1)} collective-permute-done((f16[1168,128]{1,0:T(8,128)(2,1)S(1)}, f16[1168,128]{1,0:T(8,128)(2,1)S(1)}, u32[]{:S(2)}, u32[]{:S(2)}) %collective-permute-start.25) | collective-permute-done | bytes 299040 | tf_op jit(solution)/shard_map/ppermute | solution.py:281
  127.4 6.8 %collective-permute-done.26 = f16[1168,128]{1,0:T(8,128)(2,1)S(1)} collective-permute-done((f16[1168,128]{1,0:T(8,128)(2,1)S(1)}, f16[1168,128]{1,0:T(8,128)(2,1)S(1)}, u32[]{:S(2)}, u32[]{:S(2)}) %collective-permute-start.26) | collective-permute-done | bytes 299040 | tf_op jit(solution)/shard_map/ppermute | solution.py:281
  134.3 2.4 collective-permute-done.27
  138.2 2.6 %collective-permute-start.28 = (f32[512,512]{1,0:T(8,128)S(1)}, f32[512,512]{1,0:T(8,128)S(1)}, u32[]{:S(2)}, u32[]{:S(2)}) collective-permute-start(f32[512,512]{1,0:T(8,128)S(1)} %fusion.9), channel_id=1, source_target_pairs={{0,4},{4,0},{8,12},{12,8},{16,20},{20,16},{24,28},{28,24},{32,36},... | collective-permute-start | bytes 3145736 | tf_op jit(solution)/shard_map/ppermute | solution.py:246
  140.9 2.3 collective-permute-done.28
  144.1 2.2 collective-permute-start.31
  152.2 1.8 collective-permute-start.34
  154.0 2.2 collective-permute-start.32
  157.8 2.1 collective-permute-done.32
  168.2 4.0 %collective-permute-start.38 = (bf16[512,512]{1,0:T(8,128)(2,1)S(1)}, bf16[512,512]{1,0:T(8,128)(2,1)S(1)}, u32[]{:S(2)}, u32[]{:S(2)}) collective-permute-start(bf16[512,512]{1,0:T(8,128)(2,1)S(1)} %constant_dynamic-update-slice_fusion.4.mine_ref), channel_id=1, source_target_pairs={{0,4},{4,0},{8,12},{12,8},{16,20},{20,16},{24,28},{28,24},{32,36},... | collective-permute-start | bytes 1572872 | tf_op jit(solution)/shard_map/ppermute | solution.py:266
  173.7 2.0 ladder.3
  177.1 2.3 collective-permute-done.39
  180.4 2.2 collective-permute-start.42
  189.5 2.9 %collective-permute-start.43 = (bf16[128,512]{1,0:T(8,128)(2,1)S(1)}, bf16[128,512]{1,0:T(8,128)(2,1)S(1)}, u32[]{:S(2)}, u32[]{:S(2)}) collective-permute-start(bf16[128,512]{1,0:T(8,128)(2,1)S(1)} %add_convert_fusion.1), channel_id=1, source_target_pairs={{0,64},{4,20},{8,72},{12,28},{16,80},{20,4},{24,88},{28,12},{32,96... | collective-permute-start | bytes 393224 | tf_op jit(solution)/shard_map/ppermute | solution.py:257
  193.5 2.6 %collective-permute-done.43 = bf16[128,512]{1,0:T(8,128)(2,1)S(1)} collective-permute-done((bf16[128,512]{1,0:T(8,128)(2,1)S(1)}, bf16[128,512]{1,0:T(8,128)(2,1)S(1)}, u32[]{:S(2)}, u32[]{:S(2)}) %collective-permute-start.43) | collective-permute-done | bytes 131104 | tf_op jit(solution)/shard_map/ppermute | solution.py:257
  204.4 3.3 %collective-permute-start.49 = (bf16[512,512]{1,0:T(8,128)(2,1)S(1)}, bf16[512,512]{1,0:T(8,128)(2,1)S(1)}, u32[]{:S(2)}, u32[]{:S(2)}) collective-permute-start(bf16[512,512]{1,0:T(8,128)(2,1)S(1)} %constant_dynamic-update-slice_fusion.mine_ref), channel_id=1, source_target_pairs={{0,4},{4,0},{8,12},{12,8},{16,20},{20,16},{24,28},{28,24},{32,36},... | collective-permute-start | bytes 1572872 | tf_op jit(solution)/shard_map/ppermute | solution.py:266
  209.2 2.2 pack.3.own_ref
  214.7 3.5 %collective-permute-start.51 = (f16[1200,128]{1,0:T(8,128)(2,1)}, f16[1200,128]{1,0:T(8,128)(2,1)}, u32[]{:S(2)}, u32[]{:S(2)}) collective-permute-start(f16[1200,128]{1,0:T(8,128)(2,1)} %get-tuple-element.21), channel_id=1, source_target_pairs={{0,2},{1,3},{2,0},{3,1},{4,6},{5,7},{6,4},{7,5},{8,10},{9,11},{10,... | collective-permute-start | bytes 921608 | tf_op jit(solution)/shard_map/ppermute | solution.py:281
  220.6 2.9 %collective-permute-done.50 = f16[1200,128]{1,0:T(8,128)(2,1)} collective-permute-done((f16[1200,128]{1,0:T(8,128)(2,1)}, f16[1200,128]{1,0:T(8,128)(2,1)}, u32[]{:S(2)}, u32[]{:S(2)}) %collective-permute-start.50) | collective-permute-done | bytes 307232 | tf_op jit(solution)/shard_map/ppermute | solution.py:281
  224.5 7.7 %collective-permute-done.51 = f16[1200,128]{1,0:T(8,128)(2,1)} collective-permute-done((f16[1200,128]{1,0:T(8,128)(2,1)}, f16[1200,128]{1,0:T(8,128)(2,1)}, u32[]{:S(2)}, u32[]{:S(2)}) %collective-permute-start.51) | collective-permute-done | bytes 307232 | tf_op jit(solution)/shard_map/ppermute | solution.py:281
  235.2 3.4 %mix.3.refs_0_ = f32[4,1168,128]{2,1,0:T(8,128)S(1)} custom-call(f32[4,1200,128]{2,1,0:T(8,128)S(1)} %copy-done.9, f32[1200,128]{1,0:T(8,128)S(1)} %convert_element_type.299.got1, f32[1200,128]{1,0:T(8,128)S(1)} %convert_element_type.301.got2, f32[1200,128]{1,0:T(8,128)S(1)} %convert_element_type.303.got3, bf16[512,256]{1,0:T(8,128)(2,1)S(1)} %copy-done.13, ...), custom_call_target="tpu_custom_call" | custom-call | tf_op jit(solution)/shard_map/mix/pallas_call | solution.py:212
  240.6 2.4 collective-permute-start.55
  242.9 2.2 fusion.2
  245.9 6.4 %collective-permute-done.54 = f16[1168,128]{1,0:T(8,128)(2,1)S(1)} collective-permute-done((f16[1168,128]{1,0:T(8,128)(2,1)S(1)}, f16[1168,128]{1,0:T(8,128)(2,1)S(1)}, u32[]{:S(2)}, u32[]{:S(2)}) %collective-permute-start.54) | collective-permute-done | bytes 299040 | tf_op jit(solution)/shard_map/ppermute | solution.py:281
  252.3 2.8 %collective-permute-done.55 = f16[1168,128]{1,0:T(8,128)(2,1)S(1)} collective-permute-done((f16[1168,128]{1,0:T(8,128)(2,1)S(1)}, f16[1168,128]{1,0:T(8,128)(2,1)S(1)}, u32[]{:S(2)}, u32[]{:S(2)}) %collective-permute-start.55) | collective-permute-done | bytes 299040 | tf_op jit(solution)/shard_map/ppermute | solution.py:281
  255.2 2.4 unpack.3
  (198 shorter events, 108.6 us)
Async XLA Ops:
  14.1 5.5 %collective-permute-start.3 = (bf16[128,512]{1,0:T(8,128)(2,1)S(1)}, bf16[128,512]{1,0:T(8,128)(2,1)S(1)}, u32[]{:S(2)}, u32[]{:S(2)}) collective-permute-start(bf16[128,512]{1,0:T(8,128)(2,1)S(1)} %get-tuple-element.42), channel_id=1, source_target_pairs={{0,24},{4,100},{8,16},{12,108},{16,8},{20,116},{24,0},{28,124},{32... | collective-permute-start | bytes 393224 | tf_op jit(solution)/shard_map/ppermute | solution.py:253
  17.0 4.1 %collective-permute-start.2 = (bf16[128,512]{1,0:T(8,128)(2,1)S(1)}, bf16[128,512]{1,0:T(8,128)(2,1)S(1)}, u32[]{:S(2)}, u32[]{:S(2)}) collective-permute-start(bf16[128,512]{1,0:T(8,128)(2,1)S(1)} %get-tuple-element.43), channel_id=1, source_target_pairs={{0,8},{4,36},{8,0},{12,44},{16,24},{20,52},{24,16},{28,60},{32,40}... | collective-permute-start | bytes 393224 | tf_op jit(solution)/shard_map/ppermute | solution.py:253
  17.0 5.6 %collective-permute-start.1 = (bf16[128,512]{1,0:T(8,128)(2,1)S(1)}, bf16[128,512]{1,0:T(8,128)(2,1)S(1)}, u32[]{:S(2)}, u32[]{:S(2)}) collective-permute-start(bf16[128,512]{1,0:T(8,128)(2,1)S(1)} %get-tuple-element.41), channel_id=1, source_target_pairs={{0,16},{4,68},{8,24},{12,76},{16,0},{20,84},{24,8},{28,92},{32,48}... | collective-permute-start | bytes 393224 | tf_op jit(solution)/shard_map/ppermute | solution.py:253
  23.7 5.1 %collective-permute-start.6 = (bf16[128,512]{1,0:T(8,128)(2,1)S(1)}, bf16[128,512]{1,0:T(8,128)(2,1)S(1)}, u32[]{:S(2)}, u32[]{:S(2)}) collective-permute-start(bf16[128,512]{1,0:T(8,128)(2,1)S(1)} %add_convert_fusion.7), channel_id=1, source_target_pairs={{0,96},{4,28},{8,104},{12,20},{16,112},{20,12},{24,120},{28,4},{32... | collective-permute-start | bytes 393224 | tf_op jit(solution)/shard_map/ppermute | solution.py:257
  26.2 4.1 %collective-permute-start.5 = (bf16[128,512]{1,0:T(8,128)(2,1)S(1)}, bf16[128,512]{1,0:T(8,128)(2,1)S(1)}, u32[]{:S(2)}, u32[]{:S(2)}) collective-permute-start(bf16[128,512]{1,0:T(8,128)(2,1)S(1)} %add_convert_fusion.7), channel_id=1, source_target_pairs={{0,32},{4,12},{8,40},{12,4},{16,48},{20,28},{24,56},{28,20},{32,0}... | collective-permute-start | bytes 393224 | tf_op jit(solution)/shard_map/ppermute | solution.py:257
  26.2 5.3 %collective-permute-start.4 = (bf16[128,512]{1,0:T(8,128)(2,1)S(1)}, bf16[128,512]{1,0:T(8,128)(2,1)S(1)}, u32[]{:S(2)}, u32[]{:S(2)}) collective-permute-start(bf16[128,512]{1,0:T(8,128)(2,1)S(1)} %add_convert_fusion.7), channel_id=1, source_target_pairs={{0,64},{4,20},{8,72},{12,28},{16,80},{20,4},{24,88},{28,12},{32,96... | collective-permute-start | bytes 393224 | tf_op jit(solution)/shard_map/ppermute | solution.py:257
  31.7 5.4 %collective-permute-start.7 = (bf16[128,512]{1,0:T(8,128)(2,1)S(1)}, bf16[128,512]{1,0:T(8,128)(2,1)S(1)}, u32[]{:S(2)}, u32[]{:S(2)}) collective-permute-start(bf16[128,512]{1,0:T(8,128)(2,1)S(1)} %get-tuple-element.19), channel_id=1, source_target_pairs={{0,16},{4,68},{8,24},{12,76},{16,0},{20,84},{24,8},{28,92},{32,48}... | collective-permute-start | bytes 393224 | tf_op jit(solution)/shard_map/ppermute | solution.py:262
  33.1 5.3 %collective-permute-start.8 = (bf16[128,512]{1,0:T(8,128)(2,1)S(1)}, bf16[128,512]{1,0:T(8,128)(2,1)S(1)}, u32[]{:S(2)}, u32[]{:S(2)}) collective-permute-start(bf16[128,512]{1,0:T(8,128)(2,1)S(1)} %get-tuple-element.19), channel_id=1, source_target_pairs={{0,8},{4,36},{8,0},{12,44},{16,24},{20,52},{24,16},{28,60},{32,40}... | collective-permute-start | bytes 393224 | tf_op jit(solution)/shard_map/ppermute | solution.py:262
  34.6 5.3 %collective-permute-start.9 = (bf16[128,512]{1,0:T(8,128)(2,1)S(1)}, bf16[128,512]{1,0:T(8,128)(2,1)S(1)}, u32[]{:S(2)}, u32[]{:S(2)}) collective-permute-start(bf16[128,512]{1,0:T(8,128)(2,1)S(1)} %get-tuple-element.19), channel_id=1, source_target_pairs={{0,24},{4,100},{8,16},{12,108},{16,8},{20,116},{24,0},{28,124},{32... | collective-permute-start | bytes 393224 | tf_op jit(solution)/shard_map/ppermute | solution.py:262
  40.0 6.2 %collective-permute-start.10 = (bf16[512,512]{1,0:T(8,128)(2,1)S(1)}, bf16[512,512]{1,0:T(8,128)(2,1)}, u32[]{:S(2)}, u32[]{:S(2)}) collective-permute-start(bf16[512,512]{1,0:T(8,128)(2,1)S(1)} %constant_dynamic-update-slice_fusion.12.mine_ref), channel_id=1, source_target_pairs={{0,4},{4,0},{8,12},{12,8},{16,20},{20,16},{24,28},{28,24},{32,36},... | collective-permute-start | bytes 1572872 | tf_op jit(solution)/shard_map/ppermute | solution.py:266
  55.6 5.4 %collective-permute-start.14 = (bf16[128,512]{1,0:T(8,128)(2,1)S(1)}, bf16[128,512]{1,0:T(8,128)(2,1)S(1)}, u32[]{:S(2)}, u32[]{:S(2)}) collective-permute-start(bf16[128,512]{1,0:T(8,128)(2,1)S(1)} %get-tuple-element.39), channel_id=1, source_target_pairs={{0,24},{4,100},{8,16},{12,108},{16,8},{20,116},{24,0},{28,124},{32... | collective-permute-start | bytes 393224 | tf_op jit(solution)/shard_map/ppermute | solution.py:253
  57.8 5.8 %collective-permute-start.12 = (bf16[128,512]{1,0:T(8,128)(2,1)S(1)}, bf16[128,512]{1,0:T(8,128)(2,1)S(1)}, u32[]{:S(2)}, u32[]{:S(2)}) collective-permute-start(bf16[128,512]{1,0:T(8,128)(2,1)S(1)} %get-tuple-element.38), channel_id=1, source_target_pairs={{0,16},{4,68},{8,24},{12,76},{16,0},{20,84},{24,8},{28,92},{32,48}... | collective-permute-start | bytes 393224 | tf_op jit(solution)/shard_map/ppermute | solution.py:253
  64.3 5.3 %collective-permute-start.17 = (bf16[128,512]{1,0:T(8,128)(2,1)}, bf16[128,512]{1,0:T(8,128)(2,1)}, u32[]{:S(2)}, u32[]{:S(2)}) collective-permute-start(bf16[128,512]{1,0:T(8,128)(2,1)} %add_convert_fusion.5), channel_id=1, source_target_pairs={{0,96},{4,28},{8,104},{12,20},{16,112},{20,12},{24,120},{28,4},{32... | collective-permute-start | bytes 393224 | tf_op jit(solution)/shard_map/ppermute | solution.py:257
  65.3 4.4 %collective-permute-start.16 = (bf16[128,512]{1,0:T(8,128)(2,1)}, bf16[128,512]{1,0:T(8,128)(2,1)S(1)}, u32[]{:S(2)}, u32[]{:S(2)}) collective-permute-start(bf16[128,512]{1,0:T(8,128)(2,1)} %add_convert_fusion.5), channel_id=1, source_target_pairs={{0,32},{4,12},{8,40},{12,4},{16,48},{20,28},{24,56},{28,20},{32,0}... | collective-permute-start | bytes 393224 | tf_op jit(solution)/shard_map/ppermute | solution.py:257
  65.3 7.0 %collective-permute-start.15 = (bf16[128,512]{1,0:T(8,128)(2,1)}, bf16[128,512]{1,0:T(8,128)(2,1)}, u32[]{:S(2)}, u32[]{:S(2)}) collective-permute-start(bf16[128,512]{1,0:T(8,128)(2,1)} %add_convert_fusion.5), channel_id=1, source_target_pairs={{0,64},{4,20},{8,72},{12,28},{16,80},{20,4},{24,88},{28,12},{32,96... | collective-permute-start | bytes 393224 | tf_op jit(solution)/shard_map/ppermute | solution.py:257
  74.1 5.6 %collective-permute-start.18 = (bf16[128,512]{1,0:T(8,128)(2,1)}, bf16[128,512]{1,0:T(8,128)(2,1)}, u32[]{:S(2)}, u32[]{:S(2)}) collective-permute-start(bf16[128,512]{1,0:T(8,128)(2,1)} %get-tuple-element.17), channel_id=1, source_target_pairs={{0,16},{4,68},{8,24},{12,76},{16,0},{20,84},{24,8},{28,92},{32,48}... | collective-permute-start | bytes 393224 | tf_op jit(solution)/shard_map/ppermute | solution.py:262
  75.7 5.2 %collective-permute-start.19 = (bf16[128,512]{1,0:T(8,128)(2,1)}, bf16[128,512]{1,0:T(8,128)(2,1)}, u32[]{:S(2)}, u32[]{:S(2)}) collective-permute-start(bf16[128,512]{1,0:T(8,128)(2,1)} %get-tuple-element.17), channel_id=1, source_target_pairs={{0,8},{4,36},{8,0},{12,44},{16,24},{20,52},{24,16},{28,60},{32,40}... | collective-permute-start | bytes 393224 | tf_op jit(solution)/shard_map/ppermute | solution.py:262
  77.9 5.5 %collective-permute-start.20 = (bf16[128,512]{1,0:T(8,128)(2,1)}, bf16[128,512]{1,0:T(8,128)(2,1)S(1)}, u32[]{:S(2)}, u32[]{:S(2)}) collective-permute-start(bf16[128,512]{1,0:T(8,128)(2,1)} %get-tuple-element.17), channel_id=1, source_target_pairs={{0,24},{4,100},{8,16},{12,108},{16,8},{20,116},{24,0},{28,124},{32... | collective-permute-start | bytes 393224 | tf_op jit(solution)/shard_map/ppermute | solution.py:262
  83.4 4.9 %collective-permute-start.21 = (bf16[512,512]{1,0:T(8,128)(2,1)S(1)}, bf16[512,512]{1,0:T(8,128)(2,1)S(1)}, u32[]{:S(2)}, u32[]{:S(2)}) collective-permute-start(bf16[512,512]{1,0:T(8,128)(2,1)S(1)} %constant_dynamic-update-slice_fusion.8.mine_ref), channel_id=1, source_target_pairs={{0,4},{4,0},{8,12},{12,8},{16,20},{20,16},{24,28},{28,24},{32,36},... | collective-permute-start | bytes 1572872 | tf_op jit(solution)/shard_map/ppermute | solution.py:266
  92.6 9.0 %collective-permute-start.22 = (f16[1200,128]{1,0:T(8,128)(2,1)S(1)}, f16[1200,128]{1,0:T(8,128)(2,1)S(1)}, u32[]{:S(2)}, u32[]{:S(2)}) collective-permute-start(f16[1200,128]{1,0:T(8,128)(2,1)S(1)} %get-tuple-element.25), channel_id=1, source_target_pairs={{0,1},{1,0},{2,3},{3,2},{4,5},{5,4},{6,7},{7,6},{8,9},{9,8},{10,11... | collective-permute-start | bytes 921608 | tf_op jit(solution)/shard_map/ppermute | solution.py:281
  94.3 17.0 %collective-permute-start.23 = (f16[1200,128]{1,0:T(8,128)(2,1)S(1)}, f16[1200,128]{1,0:T(8,128)(2,1)S(1)}, u32[]{:S(2)}, u32[]{:S(2)}) collective-permute-start(f16[1200,128]{1,0:T(8,128)(2,1)S(1)} %get-tuple-element.24), channel_id=1, source_target_pairs={{0,2},{1,3},{2,0},{3,1},{4,6},{5,7},{6,4},{7,5},{8,10},{9,11},{10,... | collective-permute-start | bytes 921608 | tf_op jit(solution)/shard_map/ppermute | solution.py:281
  97.6 15.7 %collective-permute-start.24 = (f16[1200,128]{1,0:T(8,128)(2,1)S(1)}, f16[1200,128]{1,0:T(8,128)(2,1)S(1)}, u32[]{:S(2)}, u32[]{:S(2)}) collective-permute-start(f16[1200,128]{1,0:T(8,128)(2,1)S(1)} %get-tuple-element.23), channel_id=1, source_target_pairs={{0,3},{1,2},{2,1},{3,0},{4,7},{5,6},{6,5},{7,4},{8,11},{9,10},{10,... | collective-permute-start | bytes 921608 | tf_op jit(solution)/shard_map/ppermute | solution.py:281
  120.5 6.9 %collective-permute-start.25 = (f16[1168,128]{1,0:T(8,128)(2,1)S(1)}, f16[1168,128]{1,0:T(8,128)(2,1)S(1)}, u32[]{:S(2)}, u32[]{:S(2)}) collective-permute-start(f16[1168,128]{1,0:T(8,128)(2,1)S(1)} %get-tuple-element.31), channel_id=1, source_target_pairs={{0,1},{1,0},{2,3},{3,2},{4,5},{5,4},{6,7},{7,6},{8,9},{9,8},{10,11... | collective-permute-start | bytes 897032 | tf_op jit(solution)/shard_map/ppermute | solution.py:281
  120.6 13.6 %collective-permute-start.26 = (f16[1168,128]{1,0:T(8,128)(2,1)S(1)}, f16[1168,128]{1,0:T(8,128)(2,1)S(1)}, u32[]{:S(2)}, u32[]{:S(2)}) collective-permute-start(f16[1168,128]{1,0:T(8,128)(2,1)S(1)} %get-tuple-element.30), channel_id=1, source_target_pairs={{0,2},{1,3},{2,0},{3,1},{4,6},{5,7},{6,4},{7,5},{8,10},{9,11},{10,... | collective-permute-start | bytes 897032 | tf_op jit(solution)/shard_map/ppermute | solution.py:281
  122.1 14.6 %collective-permute-start.27 = (f16[1168,128]{1,0:T(8,128)(2,1)S(1)}, f16[1168,128]{1,0:T(8,128)(2,1)S(1)}, u32[]{:S(2)}, u32[]{:S(2)}) collective-permute-start(f16[1168,128]{1,0:T(8,128)(2,1)S(1)} %get-tuple-element.29), channel_id=1, source_target_pairs={{0,3},{1,2},{2,1},{3,0},{4,7},{5,6},{6,5},{7,4},{8,11},{9,10},{10,... | collective-permute-start | bytes 897032 | tf_op jit(solution)/shard_map/ppermute | solution.py:281
  138.2 4.9 %collective-permute-start.28 = (f32[512,512]{1,0:T(8,128)S(1)}, f32[512,512]{1,0:T(8,128)S(1)}, u32[]{:S(2)}, u32[]{:S(2)}) collective-permute-start(f32[512,512]{1,0:T(8,128)S(1)} %fusion.9), channel_id=1, source_target_pairs={{0,4},{4,0},{8,12},{12,8},{16,20},{20,16},{24,28},{28,24},{32,36},... | collective-permute-start | bytes 3145736 | tf_op jit(solution)/shard_map/ppermute | solution.py:246
  144.1 5.4 %collective-permute-start.31 = (bf16[128,512]{1,0:T(8,128)(2,1)S(1)}, bf16[128,512]{1,0:T(8,128)(2,1)S(1)}, u32[]{:S(2)}, u32[]{:S(2)}) collective-permute-start(bf16[128,512]{1,0:T(8,128)(2,1)S(1)} %get-tuple-element.36), channel_id=1, source_target_pairs={{0,24},{4,100},{8,16},{12,108},{16,8},{20,116},{24,0},{28,124},{32... | collective-permute-start | bytes 393224 | tf_op jit(solution)/shard_map/ppermute | solution.py:253
  146.4 5.7 %collective-permute-start.29 = (bf16[128,512]{1,0:T(8,128)(2,1)S(1)}, bf16[128,512]{1,0:T(8,128)(2,1)S(1)}, u32[]{:S(2)}, u32[]{:S(2)}) collective-permute-start(bf16[128,512]{1,0:T(8,128)(2,1)S(1)} %get-tuple-element.35), channel_id=1, source_target_pairs={{0,16},{4,68},{8,24},{12,76},{16,0},{20,84},{24,8},{28,92},{32,48}... | collective-permute-start | bytes 393224 | tf_op jit(solution)/shard_map/ppermute | solution.py:253
  152.2 5.1 %collective-permute-start.34 = (bf16[128,512]{1,0:T(8,128)(2,1)S(1)}, bf16[128,512]{1,0:T(8,128)(2,1)S(1)}, u32[]{:S(2)}, u32[]{:S(2)}) collective-permute-start(bf16[128,512]{1,0:T(8,128)(2,1)S(1)} %add_convert_fusion.3), channel_id=1, source_target_pairs={{0,96},{4,28},{8,104},{12,20},{16,112},{20,12},{24,120},{28,4},{32... | collective-permute-start | bytes 393224 | tf_op jit(solution)/shard_map/ppermute | solution.py:257
  154.0 5.9 %collective-permute-start.32 = (bf16[128,512]{1,0:T(8,128)(2,1)S(1)}, bf16[128,512]{1,0:T(8,128)(2,1)S(1)}, u32[]{:S(2)}, u32[]{:S(2)}) collective-permute-start(bf16[128,512]{1,0:T(8,128)(2,1)S(1)} %add_convert_fusion.3), channel_id=1, source_target_pairs={{0,64},{4,20},{8,72},{12,28},{16,80},{20,4},{24,88},{28,12},{32,96... | collective-permute-start | bytes 393224 | tf_op jit(solution)/shard_map/ppermute | solution.py:257
  160.0 5.4 %collective-permute-start.35 = (bf16[128,512]{1,0:T(8,128)(2,1)S(1)}, bf16[128,512]{1,0:T(8,128)(2,1)S(1)}, u32[]{:S(2)}, u32[]{:S(2)}) collective-permute-start(bf16[128,512]{1,0:T(8,128)(2,1)S(1)} %get-tuple-element.15), channel_id=1, source_target_pairs={{0,16},{4,68},{8,24},{12,76},{16,0},{20,84},{24,8},{28,92},{32,48}... | collective-permute-start | bytes 393224 | tf_op jit(solution)/shard_map/ppermute | solution.py:262
  161.4 5.2 %collective-permute-start.36 = (bf16[128,512]{1,0:T(8,128)(2,1)S(1)}, bf16[128,512]{1,0:T(8,128)(2,1)S(1)}, u32[]{:S(2)}, u32[]{:S(2)}) collective-permute-start(bf16[128,512]{1,0:T(8,128)(2,1)S(1)} %get-tuple-element.15), channel_id=1, source_target_pairs={{0,8},{4,36},{8,0},{12,44},{16,24},{20,52},{24,16},{28,60},{32,40}... | collective-permute-start | bytes 393224 | tf_op jit(solution)/shard_map/ppermute | solution.py:262
  162.8 5.3 %collective-permute-start.37 = (bf16[128,512]{1,0:T(8,128)(2,1)S(1)}, bf16[128,512]{1,0:T(8,128)(2,1)S(1)}, u32[]{:S(2)}, u32[]{:S(2)}) collective-permute-start(bf16[128,512]{1,0:T(8,128)(2,1)S(1)} %get-tuple-element.15), channel_id=1, source_target_pairs={{0,24},{4,100},{8,16},{12,108},{16,8},{20,116},{24,0},{28,124},{32... | collective-permute-start | bytes 393224 | tf_op jit(solution)/shard_map/ppermute | solution.py:262
  168.2 5.5 %collective-permute-start.38 = (bf16[512,512]{1,0:T(8,128)(2,1)S(1)}, bf16[512,512]{1,0:T(8,128)(2,1)S(1)}, u32[]{:S(2)}, u32[]{:S(2)}) collective-permute-start(bf16[512,512]{1,0:T(8,128)(2,1)S(1)} %constant_dynamic-update-slice_fusion.4.mine_ref), channel_id=1, source_target_pairs={{0,4},{4,0},{8,12},{12,8},{16,20},{20,16},{24,28},{28,24},{32,36},... | collective-permute-start | bytes 1572872 | tf_op jit(solution)/shard_map/ppermute | solution.py:266
  180.4 5.4 %collective-permute-start.42 = (bf16[128,512]{1,0:T(8,128)(2,1)S(1)}, bf16[128,512]{1,0:T(8,128)(2,1)S(1)}, u32[]{:S(2)}, u32[]{:S(2)}) collective-permute-start(bf16[128,512]{1,0:T(8,128)(2,1)S(1)} %get-tuple-element.33), channel_id=1, source_target_pairs={{0,24},{4,100},{8,16},{12,108},{16,8},{20,116},{24,0},{28,124},{32... | collective-permute-start | bytes 393224 | tf_op jit(solution)/shard_map/ppermute | solution.py:253
  182.6 5.8 %collective-permute-start.40 = (bf16[128,512]{1,0:T(8,128)(2,1)S(1)}, bf16[128,512]{1,0:T(8,128)(2,1)S(1)}, u32[]{:S(2)}, u32[]{:S(2)}) collective-permute-start(bf16[128,512]{1,0:T(8,128)(2,1)S(1)} %get-tuple-element.32), channel_id=1, source_target_pairs={{0,16},{4,68},{8,24},{12,76},{16,0},{20,84},{24,8},{28,92},{32,48}... | collective-permute-start | bytes 393224 | tf_op jit(solution)/shard_map/ppermute | solution.py:253
  188.4 5.1 %collective-permute-start.45 = (bf16[128,512]{1,0:T(8,128)(2,1)S(1)}, bf16[128,512]{1,0:T(8,128)(2,1)S(1)}, u32[]{:S(2)}, u32[]{:S(2)}) collective-permute-start(bf16[128,512]{1,0:T(8,128)(2,1)S(1)} %add_convert_fusion.1), channel_id=1, source_target_pairs={{0,96},{4,28},{8,104},{12,20},{16,112},{20,12},{24,120},{28,4},{32... | collective-permute-start | bytes 393224 | tf_op jit(solution)/shard_map/ppermute | solution.py:257
  189.5 6.6 %collective-permute-start.43 = (bf16[128,512]{1,0:T(8,128)(2,1)S(1)}, bf16[128,512]{1,0:T(8,128)(2,1)S(1)}, u32[]{:S(2)}, u32[]{:S(2)}) collective-permute-start(bf16[128,512]{1,0:T(8,128)(2,1)S(1)} %add_convert_fusion.1), channel_id=1, source_target_pairs={{0,64},{4,20},{8,72},{12,28},{16,80},{20,4},{24,88},{28,12},{32,96... | collective-permute-start | bytes 393224 | tf_op jit(solution)/shard_map/ppermute | solution.py:257
  196.2 5.4 %collective-permute-start.46 = (bf16[128,512]{1,0:T(8,128)(2,1)S(1)}, bf16[128,512]{1,0:T(8,128)(2,1)S(1)}, u32[]{:S(2)}, u32[]{:S(2)}) collective-permute-start(bf16[128,512]{1,0:T(8,128)(2,1)S(1)} %get-tuple-element.13), channel_id=1, source_target_pairs={{0,16},{4,68},{8,24},{12,76},{16,0},{20,84},{24,8},{28,92},{32,48}... | collective-permute-start | bytes 393224 | tf_op jit(solution)/shard_map/ppermute | solution.py:262
  197.9 4.9 %collective-permute-start.47 = (bf16[128,512]{1,0:T(8,128)(2,1)S(1)}, bf16[128,512]{1,0:T(8,128)(2,1)S(1)}, u32[]{:S(2)}, u32[]{:S(2)}) collective-permute-start(bf16[128,512]{1,0:T(8,128)(2,1)S(1)} %get-tuple-element.13), channel_id=1, source_target_pairs={{0,8},{4,36},{8,0},{12,44},{16,24},{20,52},{24,16},{28,60},{32,40}... | collective-permute-start | bytes 393224 | tf_op jit(solution)/shard_map/ppermute | solution.py:262
  199.1 5.3 %collective-permute-start.48 = (bf16[128,512]{1,0:T(8,128)(2,1)S(1)}, bf16[128,512]{1,0:T(8,128)(2,1)S(1)}, u32[]{:S(2)}, u32[]{:S(2)}) collective-permute-start(bf16[128,512]{1,0:T(8,128)(2,1)S(1)} %get-tuple-element.13), channel_id=1, source_target_pairs={{0,24},{4,100},{8,16},{12,108},{16,8},{20,116},{24,0},{28,124},{32... | collective-permute-start | bytes 393224 | tf_op jit(solution)/shard_map/ppermute | solution.py:262
  204.4 4.8 %collective-permute-start.49 = (bf16[512,512]{1,0:T(8,128)(2,1)S(1)}, bf16[512,512]{1,0:T(8,128)(2,1)S(1)}, u32[]{:S(2)}, u32[]{:S(2)}) collective-permute-start(bf16[512,512]{1,0:T(8,128)(2,1)S(1)} %constant_dynamic-update-slice_fusion.mine_ref), channel_id=1, source_target_pairs={{0,4},{4,0},{8,12},{12,8},{16,20},{20,16},{24,28},{28,24},{32,36},... | collective-permute-start | bytes 1572872 | tf_op jit(solution)/shard_map/ppermute | solution.py:266
  214.7 8.8 %collective-permute-start.50 = (f16[1200,128]{1,0:T(8,128)(2,1)}, f16[1200,128]{1,0:T(8,128)(2,1)}, u32[]{:S(2)}, u32[]{:S(2)}) collective-permute-start(f16[1200,128]{1,0:T(8,128)(2,1)} %get-tuple-element.22), channel_id=1, source_target_pairs={{0,1},{1,0},{2,3},{3,2},{4,5},{5,4},{6,7},{7,6},{8,9},{9,8},{10,11... | collective-permute-start | bytes 921608 | tf_op jit(solution)/shard_map/ppermute | solution.py:281
  214.7 17.5 %collective-permute-start.51 = (f16[1200,128]{1,0:T(8,128)(2,1)}, f16[1200,128]{1,0:T(8,128)(2,1)}, u32[]{:S(2)}, u32[]{:S(2)}) collective-permute-start(f16[1200,128]{1,0:T(8,128)(2,1)} %get-tuple-element.21), channel_id=1, source_target_pairs={{0,2},{1,3},{2,0},{3,1},{4,6},{5,7},{6,4},{7,5},{8,10},{9,11},{10,... | collective-permute-start | bytes 921608 | tf_op jit(solution)/shard_map/ppermute | solution.py:281
  218.2 16.0 %collective-permute-start.52 = (f16[1200,128]{1,0:T(8,128)(2,1)}, f16[1200,128]{1,0:T(8,128)(2,1)}, u32[]{:S(2)}, u32[]{:S(2)}) collective-permute-start(f16[1200,128]{1,0:T(8,128)(2,1)} %get-tuple-element.20), channel_id=1, source_target_pairs={{0,3},{1,2},{2,1},{3,0},{4,7},{5,6},{6,5},{7,4},{8,11},{9,10},{10,... | collective-permute-start | bytes 921608 | tf_op jit(solution)/shard_map/ppermute | solution.py:281
  239.0 6.8 %collective-permute-start.53 = (f16[1168,128]{1,0:T(8,128)(2,1)S(1)}, f16[1168,128]{1,0:T(8,128)(2,1)S(1)}, u32[]{:S(2)}, u32[]{:S(2)}) collective-permute-start(f16[1168,128]{1,0:T(8,128)(2,1)S(1)} %get-tuple-element.28), channel_id=1, source_target_pairs={{0,1},{1,0},{2,3},{3,2},{4,5},{5,4},{6,7},{7,6},{8,9},{9,8},{10,11... | collective-permute-start | bytes 897032 | tf_op jit(solution)/shard_map/ppermute | solution.py:281
  239.1 13.2 %collective-permute-start.54 = (f16[1168,128]{1,0:T(8,128)(2,1)S(1)}, f16[1168,128]{1,0:T(8,128)(2,1)S(1)}, u32[]{:S(2)}, u32[]{:S(2)}) collective-permute-start(f16[1168,128]{1,0:T(8,128)(2,1)S(1)} %get-tuple-element.27), channel_id=1, source_target_pairs={{0,2},{1,3},{2,0},{3,1},{4,6},{5,7},{6,4},{7,5},{8,10},{9,11},{10,... | collective-permute-start | bytes 897032 | tf_op jit(solution)/shard_map/ppermute | solution.py:281
  240.6 14.6 %collective-permute-start.55 = (f16[1168,128]{1,0:T(8,128)(2,1)S(1)}, f16[1168,128]{1,0:T(8,128)(2,1)S(1)}, u32[]{:S(2)}, u32[]{:S(2)}) collective-permute-start(f16[1168,128]{1,0:T(8,128)(2,1)S(1)} %get-tuple-element.26), channel_id=1, source_target_pairs={{0,3},{1,2},{2,1},{3,0},{4,7},{5,6},{6,5},{7,4},{8,11},{9,10},{10,... | collective-permute-start | bytes 897032 | tf_op jit(solution)/shard_map/ppermute | solution.py:281
  (34 other events, 391.9 us)

commit v5 on v4

--- a/solution.py
+++ b/solution.py
@@ -46,52 +46,67 @@
     return power, jnp.exp2(-power)
 
 
-def round_body(right_ref, rounded_ref):
+def round_body(core_ref, right_ref, keep_ref, send_ref, moved_ref):
     nf, rows, cols = right_ref.shape
-    for f in range(nf):
-        rounded_ref[:, f * cols : (f + 1) * cols] = right_ref[f].astype(BF16)
-
-
-def gather_parts(core_ref, mine_ref, other_ref, whole):
-    half = mine_ref.shape[0]
-    core = core_ref[0]
-    whole[pl.ds(pl.multiple_of(core * half, half), half), :] = mine_ref[...]
-    whole[pl.ds(pl.multiple_of((1 - core) * half, half), half), :] = other_ref[...]
-
-
-def ladder_body(core_ref, factors_ref, mine_ref, other_ref, sources_ref, weight_ref,
-                rounded_ref, whole):
-    nf, rows, cols = sources_ref.shape
-    gather_parts(core_ref, mine_ref, other_ref, whole)
+    share = nf // 2
+    for j in range(share):
+        lanes = slice(j * cols, (j + 1) * cols)
+        keep_ref[:, lanes] = right_ref[core_ref[0] * share + j].astype(BF16)
+        value = right_ref[(1 - core_ref[0]) * share + j]
+        send_ref[:, lanes] = value.astype(BF16)
+        moved_ref[j] = value
+
+
+def ladder_body(core_ref, spot_ref, mine_ref, theirs_ref, piece0, piece1, piece2, piece3,
+                sources_ref, moved_ref, weight_ref, weight_moved_ref, own_ref, other_ref, whole):
+    share, rows, cols = moved_ref.shape
+    chunk = piece0.shape[0]
+    for d, piece in enumerate((piece0, piece1, piece2, piece3)):
+        whole[pl.ds(pl.multiple_of((spot_ref[0] ^ d) * chunk, chunk), chunk), :] = piece[...]
     span = rows // SIDE
 
     def step(r, carry):
         at = pl.ds(pl.multiple_of(r * span, RUN), span)
+        spread = jnp.dot(mine_ref[at, :], whole[...], preferred_element_type=F32)
+        for j in range(share):
+            lanes = slice(j * cols, (j + 1) * cols)
+            base = sources_ref[core_ref[0] * share + j, at, :]
+            value = base + weight_ref[at, j : j + 1] * spread[:, lanes]
+            own_ref[at, lanes] = value.astype(BF16)
+        spread = jnp.dot(theirs_ref[at, :], whole[...], preferred_element_type=F32)
+        for j in range(share):
+            lanes = slice(j * cols, (j + 1) * cols)
+            value = moved_ref[j, at, :] + weight_moved_ref[at, j : j + 1] * spread[:, lanes]
+            other_ref[at, lanes] = value.astype(BF16)
+        return carry
+
+    lax.fori_loop(0, SIDE, step, 0)
+
+
+def pack_body(last, core_ref, z_ref, factors_ref, mine_ref, other_ref, sources_ref,
+              weight_ref, kernel_ref, sent_ref, *refs):
+    if last:
+        amplitude_ref, whole = refs
+    else:
+        (whole,) = refs
+    nf, rows, cols = sources_ref.shape
+    quarter = rows // SIDE
+    body = nf * quarter
+    half = mine_ref.shape[1]
+    core = core_ref[0]
+    whole[:, pl.ds(pl.multiple_of(core * half, half), half)] = mine_ref[...]
+    whole[:, pl.ds(pl.multiple_of((1 - core) * half, half), half)] = other_ref[...]
+
+    def block(d, peak):
+        base = pl.multiple_of((z_ref[0] ^ d) * quarter, RUN)
+        at = pl.ds(base, quarter)
         spread = jnp.dot(factors_ref[at, :], whole[...], preferred_element_type=F32)
         for f in range(nf):
             lanes = slice(f * cols, (f + 1) * cols)
             value = sources_ref[f, at, :] + weight_ref[at, f : f + 1] * spread[:, lanes]
-            rounded_ref[at, lanes] = value.astype(BF16)
-        return carry
-
-    lax.fori_loop(0, SIDE, step, 0)
-
-
-def pack_body(core_ref, z_ref, factors_ref, mine_ref, other_ref, sources_ref,
-              weight_ref, kernel_ref, sent_ref, whole):
-    nf, rows, cols = sources_ref.shape
-    quarter = rows // SIDE
-    length = quarter
-    body = nf * length
-    gather_parts(core_ref, mine_ref, other_ref, whole)
-
-    def block(d, peak):
-        base = pl.multiple_of((z_ref[0] ^ d) * quarter, RUN)
-        at = pl.ds(base, length)
-        spread = jnp.dot(factors_ref[at, :], whole[...], preferred_element_type=F32)
-        for f in range(nf):
-            value = sources_ref[f, at, :] + weight_ref[at, f : f + 1] * spread[:, f * cols : (f + 1) * cols]
-            for g in range(length // RUN):
+            if last:
+                amplitude_ref[f, at, :] = value
+            for g in range(quarter // RUN):
                 tile = value[g * RUN : (g + 1) * RUN]
                 sent_ref[d, (g * nf + f) * RUN : (g * nf + f + 1) * RUN, :] = tile
                 peak = jnp.maximum(peak, jnp.abs(tile))
@@ -183,24 +198,31 @@
         sent_ref[d, body:, :] = jnp.broadcast_to(power, (RUN, cols))
 
 
-def unpack_body(z_ref, right_ref, *refs):
+def unpack_body(last, core_ref, z_ref, right_ref, own_ref, got1, got2, got3, sources_ref, *refs):
     nf, rows, cols = right_ref.shape
+    share = nf // 2
     quarter = rows // SIDE
-    z = z_ref[0]
-    sources_ref, rounded_ref = refs[-2:]
     body = nf * quarter
-    for d, ref in enumerate(refs[:SIDE]):
-        base = (z ^ d) * quarter
+    for d, ref in enumerate((own_ref, got1, got2, got3)):
+        base = (z_ref[0] ^ d) * quarter
         gain = jnp.exp2(jnp.broadcast_to(ref[body : body + 1, :], (RUN, cols))) if d else None
 
         def step(g, carry, d=d, base=base, ref=ref, gain=gain):
             at = pl.ds(pl.multiple_of(base + g * RUN, RUN), RUN)
-            for f in range(nf):
+            for i in range(nf):
+                kept = i < share
+                side = core_ref[0] if kept else 1 - core_ref[0]
+                f = side * share + i % share
                 spot = pl.ds(pl.multiple_of((g * nf + f) * RUN, RUN), RUN)
                 tile = ref[spot, :] * gain if d else ref[0, spot, :]
                 tile = right_ref[f, at, :] + tile
                 sources_ref[f, at, :] = tile
-                rounded_ref[at, f * cols : (f + 1) * cols] = tile.astype(BF16)
+                if not last:
+                    keep_ref, send_ref, moved_ref = refs
+                    lanes = slice(i % share * cols, (i % share + 1) * cols)
+                    (keep_ref if kept else send_ref)[at, lanes] = tile.astype(BF16)
+                    if not kept:
+                        moved_ref[i % share, at, :] = tile
             return carry
 
         lax.fori_loop(0, quarter // RUN, step, 0)
@@ -224,31 +246,29 @@
 def shards(right_side, factors, pair_weight, second_order, forward, backward):
     nf, rows, cols = right_side.shape
     naux = factors.shape[1]
-    half = naux // 2
-    chunk = half // SIDE
+    share = nf // 2
+    half = share * cols
+    chunk = naux // SIDE
     quarter = rows // SIDE
-    wide = nf * cols
     me = lax.axis_index("fac")
     z = lax.axis_index("freq")
     core = me % 2
     chip = me // 2
     spot = jnp.where(core == 0, chip % SIDE, chip // SIDE)
-    factors_keep = lax.dynamic_slice(factors, (0, core * half), (rows, half))
-    factors_send = lax.dynamic_slice(factors, (0, (1 - core) * half), (rows, half))
 
     def project(table, rounded):
         return lax.dot_general(
             table, rounded, (((0,), (0,)), ((), ())), preferred_element_type=F32
         )
 
-    def reduce_all(rounded):
-        sent = project(factors_send, rounded)
-        got = lax.ppermute(sent, "fac", CORES)
-        mine = project(factors_keep, rounded) + got
-        own = lax.dynamic_slice(mine, (spot * chunk, 0), (chunk, wide))
+    def swap_cores(value):
+        return lax.ppermute(value, "fac", CORES)
+
+    def reduce_chips(partial_sum):
+        own = lax.dynamic_slice(partial_sum, (spot * chunk, 0), (chunk, half))
         for d in PARTNERS:
             piece = lax.dynamic_slice(
-                mine, ((spot ^ d) * chunk, 0), (chunk, wide)
+                partial_sum, ((spot ^ d) * chunk, 0), (chunk, half)
             ).astype(BF16)
             own = own + lax.ppermute(piece, "fac", along(d, True)).astype(F32)
         own = own.astype(BF16)
@@ -256,24 +276,10 @@
         for d in PARTNERS:
             total = total + lax.ppermute(own, "fac", along(d, False)).astype(F32)
         total = total.astype(BF16)
-        gathered = jnp.zeros((half, wide), BF16)
-        gathered = lax.dynamic_update_slice(gathered, total, (spot * chunk, 0))
+        pieces = {0: total}
         for d in PARTNERS:
-            piece = lax.ppermute(total, "fac", along(d, True))
-            gathered = lax.dynamic_update_slice(
-                gathered, piece, ((spot ^ d) * chunk, 0)
-            )
-        other = lax.ppermute(gathered, "fac", CORES)
-        return gathered, other
-
-    def spread_of(parts):
-        gathered, other = parts
-        return (
-            jnp.einsum("pa,afc->fpc", factors_keep, gathered.reshape(half, nf, cols),
-                       preferred_element_type=F32)
-            + jnp.einsum("pa,afc->fpc", factors_send, other.reshape(half, nf, cols),
-                         preferred_element_type=F32)
-        )
+            pieces[d] = lax.ppermute(total, "fac", along(d, True))
+        return [pieces[d] for d in range(SIDE)]
 
     def exchange(sent):
         got = {}
@@ -283,7 +289,6 @@
 
     body = nf * quarter
     size = SIDE * nf * RUN
-    weight = pair_weight[:, :, None]
     place_z = jnp.full((1,), z, jnp.int32)
     strips = -(-quarter // LANES)
     kernel = second_order.reshape(nf, SIDE, quarter).transpose(1, 0, 2)
@@ -308,21 +313,41 @@
     table_out = spread_table(source, backward, source)
 
     core_at = jnp.full((1,), core, jnp.int32)
+    spot_at = jnp.full((1,), spot, jnp.int32)
     column = pair_weight.T
-    whole = [pltpu.VMEM((naux, wide), BF16)]
+    column_mine = lax.dynamic_slice(pair_weight, (core * share, 0), (share, rows)).T
+    column_sent = lax.dynamic_slice(pair_weight, ((1 - core) * share, 0), (share, rows))
+
     sources = right_side
-    (rounded,) = call(round_body, [((rows, wide), BF16)], "round", 4, 0, (right_side,))
+    handed = [((rows, half), BF16), ((rows, half), BF16), ((share, rows, cols), F32)]
+    keep, send, moved = call(round_body, handed, "round", 4, 1, (core_at, right_side))
     for outer in range(OUTER):
+        last = outer == OUTER - 1
+        got = swap_cores(project(factors, send))
+        partial_sum = project(factors, keep) + got
+        if outer == 0:
+            theirs = swap_cores(factors)
+            column_moved = swap_cores(column_sent).T
+        moved = swap_cores(moved)
+        pieces = reduce_chips(partial_sum)
         for inner in range(INNER - 1):
-            parts = reduce_all(rounded)
-            (rounded,) = call(
-                ladder_body, [((rows, wide), BF16)], "ladder", 10, 1,
-                (core_at, factors, *parts, sources, column), whole,
-            )
-        parts = reduce_all(rounded)
-        (sent,) = call(
-            pack_body, [((SIDE, body + 3 * RUN, cols), F32)], "pack", 12, 2,
-            (core_at, place_z, factors, *parts, sources, column, kernel), whole,
+            own, other = call(
+                ladder_body, [((rows, half), BF16)] * 2, "ladder", 8, 2,
+                (core_at, spot_at, factors, theirs, *pieces, sources, moved,
+                 column_mine, column_moved),
+                [pltpu.VMEM((naux, half), BF16)],
+            )
+            pieces = reduce_chips(project(factors, own) + project(theirs, other))
+        mine = jnp.zeros((naux, half), BF16)
+        for d, piece in enumerate(pieces):
+            mine = lax.dynamic_update_slice(mine, piece, ((spot ^ d) * chunk, 0))
+        shape = [((SIDE, body + 3 * RUN, cols), F32)]
+        if last:
+            shape.append((right_side.shape, F32))
+        sent, *amplitude = call(
+            partial(pack_body, last), shape, "pack", 12, 2,
+            (core_at, place_z, factors, mine, swap_cores(mine), sources, column, kernel),
+            [pltpu.VMEM((naux, nf * cols), BF16)],
         )
         got = exchange(sent)
         mixed = [((SIDE, body + RUN, cols), F32)]
@@ -337,15 +362,13 @@
                 partial(mix_body, False), mixed, "mix", 16, 0,
                 (sent, *got, *tables, spread_kernel),
             )
-        back = [sent, *exchange(sent)]
-        if outer == OUTER - 1:
-            amplitude = sources + weight * spread_of(parts)
-        sources, rounded = call(
-            unpack_body,
-            [(right_side.shape, F32), ((rows, wide), BF16)],
-            "unpack", 4, 1, (place_z, right_side, *back),
+        sources, *rest = call(
+            partial(unpack_body, last), [(right_side.shape, F32)] + ([] if last else handed),
+            "unpack", 4, 2, (core_at, place_z, right_side, sent, *exchange(sent)),
         )
-    return (amplitude, sources)
+        if not last:
+            keep, send, moved = rest
+    return (amplitude[0], sources)
 
 
 def solution(mesh):

time: 260 us -> 270 us (1.038)
  Pallas kernels: 21.6 us -> 27.9 us
  local copies, waits for them, and re-layouts: 17 us -> 21.2 us
    ppermute x12, waiting for transfers between devices: 48.8 us -> 55.1 us  [exchange(): got[d] = lax.ppermute(sent[d].astype(F16), 'freq', swap(d)).astype(F32)]
    pallas_call x9, Pallas kernels: 21.6 us -> 27.9 us  [call(): pl.pallas_call(body, out_shape=[jax.ShapeDtypeStruct(s, t) for s, t in ou...]
    ppermute x44, waiting for transfers between devices: 60.9 us -> 54.7 us  [the longest x12 17.1 us: reduce_chips(): own = own + lax.ppermute(piece, 'fac', along(d, True)).astype(F32)]
    dot_general x8, matrix products: 10.3 us -> 14.3 us  [project(): lax.dot_general(table, rounded, (((0,), (0,)), ((), ())), preferred_eleme...]
    dot_general x2 -> x0, matrix products: 3 us -> none  [the longest x1 2.19 us: spread_of(): jnp.einsum('pa,afc->fpc', factors_keep, gathered.reshape(half, nf, cols),...]
    convert_element_type x12, other arithmetic: 3.39 us -> 0.49 us  [exchange(): got[d] = lax.ppermute(sent[d].astype(F16), 'freq', swap(d)).astype(F32)]
    unnamed x53 -> x25, local copies, waits for them, and re-layouts: 10.7 us -> 8.04 us
  transfers between devices with their start and end apart: 56 -> 56, of which waited for: 53 -> 45; matrix products, arithmetic and copies ran while one was open for 4% -> 7% of each run, Pallas kernels for 0% -> 0%
where the time goes in v5:
time: 270 us; the launch traced here: 268 us
  waiting for transfers between devices  110 us (41%)
  starting transfers between devices  84.5 us (31%)
  Pallas kernels  27.9 us (10%)
  local copies, waits for them, and re-layouts  21.2 us (8%)
  matrix products  17.5 us (6%)
  other arithmetic  5.88 us (2%)
    ppermute x12, waiting for transfers between devices, exchange(): got[d] = lax.ppermute(sent[d].astype(F16), 'freq', swap(d)).astype(F32)  55.1 us
    pallas_call x9, Pallas kernels, call(): pl.pallas_call(body, out_shape=[jax.ShapeDtypeStruct(s, t) for s, t in ou...  27.9 us
    ppermute x8, starting transfers between devices, swap_cores(): return lax.ppermute(value, 'fac', CORES)  24 us
    ppermute x12, waiting for transfers between devices, reduce_chips(): own = own + lax.ppermute(piece, 'fac', along(d, True)).astype(F32)  17.1 us
    ppermute x12, starting transfers between devices, exchange(): got[d] = lax.ppermute(sent[d].astype(F16), 'freq', swap(d)).astype(F32)  16.8 us
    ppermute x12, starting transfers between devices, reduce_chips(): pieces[d] = lax.ppermute(total, 'fac', along(d, True))  15.7 us
    ppermute x12, waiting for transfers between devices, reduce_chips(): total = total + lax.ppermute(own, 'fac', along(d, False)).astype(F32)  15.6 us
    ppermute x12, starting transfers between devices, reduce_chips(): own = own + lax.ppermute(piece, 'fac', along(d, True)).astype(F32)  14.7 us
  transfers between devices with their start and end apart: 56, of which 45 were waited for; matrix products, arithmetic and copies ran while one was open for 7% of the time, Pallas kernels for 0%

profile of v5, /device:TPU:1, one launch (start us, length us, event | category | flops | bytes accessed | tf_op | source)
XLA Modules:
  0.0 268.0 jit_solution(16188842002504411430)
XLA Ops:
  3.7 2.1 convolution_bitcast_fusion.2
  7.7 3.6 %collective-permute-done.1 = f32[1024,256]{1,0:T(8,128)} collective-permute-done((f32[1024,256]{1,0:T(8,128)}, f32[1024,256]{1,0:T(8,128)}, u32[]{:S(2)}, u32[]{:S(2)}) %collective-permute-start.1) | collective-permute-done | bytes 1048608 | tf_op jit(solution)/shard_map/ppermute | solution.py:265
  11.3 2.3 fusion.1
  15.3 3.0 %collective-permute-start.2 = (bf16[256,256]{1,0:T(8,128)(2,1)}, bf16[256,256]{1,0:T(8,128)(2,1)S(1)}, u32[]{:S(2)}, u32[]{:S(2)}) collective-permute-start(bf16[256,256]{1,0:T(8,128)(2,1)} %get-tuple-element.57), channel_id=1, source_target_pairs={{0,16},{4,68},{8,24},{12,76},{16,0},{20,84},{24,8},{28,92},{32,48}... | collective-permute-start | bytes 393224 | tf_op jit(solution)/shard_map/ppermute | solution.py:273
  25.3 2.5 collective-permute-start.5
  28.7 2.0 collective-permute-done.5
  30.7 2.7 %collective-permute-start.12 = (f32[2,1152]{1,0:T(2,128)S(1)}, f32[2,1152]{1,0:T(2,128)S(1)}, u32[]{:S(2)}, u32[]{:S(2)}) collective-permute-start(f32[2,1152]{1,0:T(2,128)S(1)} %constant_dynamic-slice_fusion), channel_id=1, source_target_pairs={{0,4},{4,0},{8,12},{12,8},{16,20},{20,16},{24,28},{28,24},{32,36},... | collective-permute-start | bytes 27656 | tf_op jit(solution)/shard_map/ppermute | solution.py:265
  34.1 2.8 %collective-permute-start.10 = (bf16[256,256]{1,0:T(8,128)(2,1)}, bf16[256,256]{1,0:T(8,128)(2,1)}, u32[]{:S(2)}, u32[]{:S(2)}) collective-permute-start(bf16[256,256]{1,0:T(8,128)(2,1)} %add_convert_fusion.4.piece0), channel_id=1, source_target_pairs={{0,24},{4,100},{8,16},{12,108},{16,8},{20,116},{24,0},{28,124},{32... | collective-permute-start | bytes 393224 | tf_op jit(solution)/shard_map/ppermute | solution.py:281
  41.0 2.1 collective-permute-done.9.piece2
  45.9 4.2 %ladder.2 = (bf16[1152,256]{1,0:T(8,128)(2,1)S(1)}, bf16[1152,256]{1,0:T(8,128)(2,1)S(1)}) custom-call(s32[1]{0:T(128)} %bitcast.core_ref, s32[1]{0:T(128)} %bitcast.2.spot_ref, bf16[1152,1024]{1,0:T(8,128)(2,1)S(1)} %copy-done.2, bf16[1152,1024]{1,0:T(8,128)(2,1)} %collective-permute-done.theirs_ref, bf16[256,256]{1,0:T(8,128)(2,1)} %add_convert_fusion.4.piece0, ...), custom_call_target="tpu_custom_call" | custom-call | tf_op jit(solution)/shard_map/ladder/pallas_call | solution.py:234
  50.1 2.7 %fusion.28 = f32[256,1024]{0,1:T(8,128)S(1)} fusion(bf16[1152,256]{1,0:T(8,128)(2,1)S(1)} %get-tuple-element.21, bf16[1152,1024]{1,0:T(8,128)(2,1)} %collective-permute-done.theirs_ref), kind=kOutput, calls=%fused_computation.96 | convolution fusion | flops 603979776 | bytes 3997696 | tf_op jit(solution)/shard_map/dot_general | solution.py:260
  65.4 2.4 collective-permute-done.16
  87.0 7.5 %collective-permute-start.22 = (bf16[1024,256]{1,0:T(8,128)(2,1)}, bf16[1024,256]{1,0:T(8,128)(2,1)S(1)}, u32[]{:S(2)}, u32[]{:S(2)}) collective-permute-start(bf16[1024,256]{1,0:T(8,128)(2,1)} %constant_dynamic-update-slice_fusion.4.mine_ref), channel_id=1, source_target_pairs={{0,4},{4,0},{8,12},{12,8},{16,20},{20,16},{24,28},{28,24},{32,36},... | collective-permute-start | bytes 1572872 | tf_op jit(solution)/shard_map/ppermute | solution.py:265
  98.3 3.3 %pack.2.own_ref = f32[4,1200,128]{2,1,0:T(8,128)S(1)} custom-call(s32[1]{0:T(128)} %bitcast.core_ref, s32[1]{0:T(128)} %bitcast.1.z_ref, bf16[1152,1024]{1,0:T(8,128)(2,1)S(1)} %copy-done.2, bf16[1024,256]{1,0:T(8,128)(2,1)} %constant_dynamic-update-slice_fusion.4.mine_ref, bf16[1024,256]{1,0:T(8,128)(2,1)S(1)} %collective-permute-done.22.other_ref, ...), custom_call_target="tpu_custom_call" | custom-call | tf_op jit(solution)/shard_map/pack/pallas_call | solution.py:234
  103.6 3.3 %collective-permute-start.24 = (f16[1200,128]{1,0:T(8,128)(2,1)S(1)}, f16[1200,128]{1,0:T(8,128)(2,1)S(1)}, u32[]{:S(2)}, u32[]{:S(2)}) collective-permute-start(f16[1200,128]{1,0:T(8,128)(2,1)S(1)} %get-tuple-element.40), channel_id=1, source_target_pairs={{0,2},{1,3},{2,0},{3,1},{4,6},{5,7},{6,4},{7,5},{8,10},{9,11},{10,... | collective-permute-start | bytes 921608 | tf_op jit(solution)/shard_map/ppermute | solution.py:287
  107.3 3.8 %collective-permute-done.23 = f16[1200,128]{1,0:T(8,128)(2,1)S(1)} collective-permute-done((f16[1200,128]{1,0:T(8,128)(2,1)S(1)}, f16[1200,128]{1,0:T(8,128)(2,1)S(1)}, u32[]{:S(2)}, u32[]{:S(2)}) %collective-permute-start.23) | collective-permute-done | bytes 307232 | tf_op jit(solution)/shard_map/ppermute | solution.py:287
  111.1 9.9 %collective-permute-done.24 = f16[1200,128]{1,0:T(8,128)(2,1)S(1)} collective-permute-done((f16[1200,128]{1,0:T(8,128)(2,1)S(1)}, f16[1200,128]{1,0:T(8,128)(2,1)S(1)}, u32[]{:S(2)}, u32[]{:S(2)}) %collective-permute-start.24) | collective-permute-done | bytes 307232 | tf_op jit(solution)/shard_map/ppermute | solution.py:287
  121.0 2.0 collective-permute-done.25
  123.0 5.5 %mix.2 = (f32[4,1168,128]{2,1,0:T(8,128)S(1)}, f32[4608,128]{1,0:T(8,128)S(1)}) custom-call(f32[4,1200,128]{2,1,0:T(8,128)S(1)} %pack.2.own_ref, f32[1200,128]{1,0:T(8,128)S(1)} %convert_element_type.284.got1, f32[1200,128]{1,0:T(8,128)S(1)} %convert_element_type.286.got2, f32[1200,128]{1,0:T(8,128)S(1)} %convert_element_type.288.got3, ...), custom_call_target="tpu_custom_call" | custom-call | tf_op jit(solution)/shard_map/mix/pallas_call | solution.py:234
  130.5 2.4 collective-permute-start.28
  132.9 3.3 %collective-permute-done.26 = f16[1168,128]{1,0:T(8,128)(2,1)S(1)} collective-permute-done((f16[1168,128]{1,0:T(8,128)(2,1)S(1)}, f16[1168,128]{1,0:T(8,128)(2,1)S(1)}, u32[]{:S(2)}, u32[]{:S(2)}) %collective-permute-start.26) | collective-permute-done | bytes 299040 | tf_op jit(solution)/shard_map/ppermute | solution.py:287
  136.3 6.8 %collective-permute-done.27 = f16[1168,128]{1,0:T(8,128)(2,1)S(1)} collective-permute-done((f16[1168,128]{1,0:T(8,128)(2,1)S(1)}, f16[1168,128]{1,0:T(8,128)(2,1)S(1)}, u32[]{:S(2)}, u32[]{:S(2)}) %collective-permute-start.27) | collective-permute-done | bytes 299040 | tf_op jit(solution)/shard_map/ppermute | solution.py:287
  143.1 2.0 collective-permute-done.28
  147.2 2.7 collective-permute-start.29
  150.0 2.2 collective-permute-done.29
  154.5 2.5 collective-permute-start.31
  157.0 2.1 collective-permute-done.30
  165.7 2.4 collective-permute-done.33
  170.4 2.9 %collective-permute-start.37 = (bf16[256,256]{1,0:T(8,128)(2,1)S(1)}, bf16[256,256]{1,0:T(8,128)(2,1)S(1)}, u32[]{:S(2)}, u32[]{:S(2)}) collective-permute-start(bf16[256,256]{1,0:T(8,128)(2,1)S(1)} %add_convert_fusion.1.piece0), channel_id=1, source_target_pairs={{0,16},{4,68},{8,24},{12,76},{16,0},{20,84},{24,8},{28,92},{32,48}... | collective-permute-start | bytes 393224 | tf_op jit(solution)/shard_map/ppermute | solution.py:281
  174.2 2.8 %collective-permute-done.37.piece2 = bf16[256,256]{1,0:T(8,128)(2,1)S(1)} collective-permute-done((bf16[256,256]{1,0:T(8,128)(2,1)S(1)}, bf16[256,256]{1,0:T(8,128)(2,1)S(1)}, u32[]{:S(2)}, u32[]{:S(2)}) %collective-permute-start.37) | collective-permute-done | bytes 131104 | tf_op jit(solution)/shard_map/ppermute | solution.py:281
  178.4 3.6 %ladder.3 = (bf16[1152,256]{1,0:T(8,128)(2,1)S(1)}, bf16[1152,256]{1,0:T(8,128)(2,1)S(1)}) custom-call(s32[1]{0:T(128)} %bitcast.core_ref, s32[1]{0:T(128)} %bitcast.2.spot_ref, bf16[1152,1024]{1,0:T(8,128)(2,1)S(1)} %copy-done.2, bf16[1152,1024]{1,0:T(8,128)(2,1)} %collective-permute-done.theirs_ref, bf16[256,256]{1,0:T(8,128)(2,1)S(1)} %add_convert_fusion.1.piece0, ...), custom_call_target="tpu_custom_call" | custom-call | tf_op jit(solution)/shard_map/ladder/pallas_call | solution.py:234
  182.1 2.7 %fusion.29 = f32[256,1024]{0,1:T(8,128)S(1)} fusion(bf16[1152,256]{1,0:T(8,128)(2,1)S(1)} %get-tuple-element.28, bf16[1152,1024]{1,0:T(8,128)(2,1)} %collective-permute-done.theirs_ref), kind=kOutput, calls=%fused_computation.97 | convolution fusion | flops 603979776 | bytes 3997696 | tf_op jit(solution)/shard_map/dot_general | solution.py:260
  189.3 2.1 collective-permute-done.40
  196.4 2.7 collective-permute-done.43
  206.5 2.3 collective-permute-done.47
  208.8 3.2 %collective-permute-done.48 = bf16[256,256]{1,0:T(8,128)(2,1)S(1)} collective-permute-done((bf16[256,256]{1,0:T(8,128)(2,1)S(1)}, bf16[256,256]{1,0:T(8,128)(2,1)S(1)}, u32[]{:S(2)}, u32[]{:S(2)}) %collective-permute-start.48) | collective-permute-done | bytes 131104 | tf_op jit(solution)/shard_map/ppermute | solution.py:281
  212.0 9.2 %collective-permute-start.49 = (bf16[1024,256]{1,0:T(8,128)(2,1)S(1)}, bf16[1024,256]{1,0:T(8,128)(2,1)S(1)}, u32[]{:S(2)}, u32[]{:S(2)}) collective-permute-start(bf16[1024,256]{1,0:T(8,128)(2,1)S(1)} %constant_dynamic-update-slice_fusion.mine_ref), channel_id=1, source_target_pairs={{0,4},{4,0},{8,12},{12,8},{16,20},{20,16},{24,28},{28,24},{32,36},... | collective-permute-start | bytes 1572872 | tf_op jit(solution)/shard_map/ppermute | solution.py:265
  222.7 3.5 %pack.3 = (f32[4,1200,128]{2,1,0:T(8,128)S(1)}, f32[4,1152,128]{2,1,0:T(8,128)}) custom-call(s32[1]{0:T(128)} %bitcast.core_ref, s32[1]{0:T(128)} %bitcast.1.z_ref, bf16[1152,1024]{1,0:T(8,128)(2,1)S(1)} %copy-done.2, bf16[1024,256]{1,0:T(8,128)(2,1)S(1)} %constant_dynamic-update-slice_fusion.mine_ref, ...), custom_call_target="tpu_custom_call" | custom-call | tf_op jit(solution)/shard_map/pack/pallas_call | solution.py:234
  226.7 3.5 %collective-permute-start.51 = (f16[1200,128]{1,0:T(8,128)(2,1)S(1)}, f16[1200,128]{1,0:T(8,128)(2,1)S(1)}, u32[]{:S(2)}, u32[]{:S(2)}) collective-permute-start(f16[1200,128]{1,0:T(8,128)(2,1)S(1)} %get-tuple-element.37), channel_id=1, source_target_pairs={{0,2},{1,3},{2,0},{3,1},{4,6},{5,7},{6,4},{7,5},{8,10},{9,11},{10,... | collective-permute-start | bytes 921608 | tf_op jit(solution)/shard_map/ppermute | solution.py:287
  230.5 4.7 %collective-permute-done.50 = f16[1200,128]{1,0:T(8,128)(2,1)S(1)} collective-permute-done((f16[1200,128]{1,0:T(8,128)(2,1)S(1)}, f16[1200,128]{1,0:T(8,128)(2,1)S(1)}, u32[]{:S(2)}, u32[]{:S(2)}) %collective-permute-start.50) | collective-permute-done | bytes 307232 | tf_op jit(solution)/shard_map/ppermute | solution.py:287
  235.2 8.6 %collective-permute-done.51 = f16[1200,128]{1,0:T(8,128)(2,1)S(1)} collective-permute-done((f16[1200,128]{1,0:T(8,128)(2,1)S(1)}, f16[1200,128]{1,0:T(8,128)(2,1)S(1)}, u32[]{:S(2)}, u32[]{:S(2)}) %collective-permute-start.51) | collective-permute-done | bytes 307232 | tf_op jit(solution)/shard_map/ppermute | solution.py:287
  243.8 2.0 collective-permute-done.52
  245.8 3.3 %mix.3.own_ref = f32[4,1168,128]{2,1,0:T(8,128)S(1)} custom-call(f32[4,1200,128]{2,1,0:T(8,128)S(1)} %get-tuple-element.30.own_ref, f32[1200,128]{1,0:T(8,128)S(1)} %convert_element_type.323.got1, f32[1200,128]{1,0:T(8,128)S(1)} %convert_element_type.325.got2, f32[1200,128]{1,0:T(8,128)S(1)} %convert_element_type.327.got3, ...), custom_call_target="tpu_custom_call" | custom-call | tf_op jit(solution)/shard_map/mix/pallas_call | solution.py:234
  251.2 2.3 collective-permute-start.55
  253.4 2.9 %collective-permute-done.53 = f16[1168,128]{1,0:T(8,128)(2,1)S(1)} collective-permute-done((f16[1168,128]{1,0:T(8,128)(2,1)S(1)}, f16[1168,128]{1,0:T(8,128)(2,1)S(1)}, u32[]{:S(2)}, u32[]{:S(2)}) %collective-permute-start.53) | collective-permute-done | bytes 299040 | tf_op jit(solution)/shard_map/ppermute | solution.py:287
  256.4 6.6 %collective-permute-done.54 = f16[1168,128]{1,0:T(8,128)(2,1)S(1)} collective-permute-done((f16[1168,128]{1,0:T(8,128)(2,1)S(1)}, f16[1168,128]{1,0:T(8,128)(2,1)S(1)}, u32[]{:S(2)}, u32[]{:S(2)}) %collective-permute-start.54) | collective-permute-done | bytes 299040 | tf_op jit(solution)/shard_map/ppermute | solution.py:287
  263.0 2.7 %collective-permute-done.55 = f16[1168,128]{1,0:T(8,128)(2,1)S(1)} collective-permute-done((f16[1168,128]{1,0:T(8,128)(2,1)S(1)}, f16[1168,128]{1,0:T(8,128)(2,1)S(1)}, u32[]{:S(2)}, u32[]{:S(2)}) %collective-permute-start.55) | collective-permute-done | bytes 299040 | tf_op jit(solution)/shard_map/ppermute | solution.py:287
  265.8 2.2 unpack.3
  (161 shorter events, 99.3 us)
Async XLA Ops:
  5.8 5.5 %collective-permute-start.1 = (f32[1024,256]{1,0:T(8,128)}, f32[1024,256]{1,0:T(8,128)}, u32[]{:S(2)}, u32[]{:S(2)}) collective-permute-start(f32[1024,256]{1,0:T(8,128)} %convolution_bitcast_fusion.2), channel_id=1, source_target_pairs={{0,4},{4,0},{8,12},{12,8},{16,20},{20,16},{24,28},{28,24},{32,36},... | collective-permute-start | bytes 3145736 | tf_op jit(solution)/shard_map/ppermute | solution.py:265
  7.2 35.9 %collective-permute-start = (bf16[1152,1024]{1,0:T(8,128)(2,1)S(1)}, bf16[1152,1024]{1,0:T(8,128)(2,1)}, u32[]{:S(2)}, u32[]{:S(2)}) collective-permute-start(bf16[1152,1024]{1,0:T(8,128)(2,1)S(1)} %copy-done.2), channel_id=1, source_target_pairs={{0,4},{4,0},{8,12},{12,8},{16,20},{20,16},{24,28},{28,24},{32,36},... | collective-permute-start | bytes 7077896 | tf_op jit(solution)/shard_map/ppermute | solution.py:265
  7.2 33.4 %collective-permute-start.11 = (f32[2,1152,128]{2,1,0:T(8,128)}, f32[2,1152,128]{2,1,0:T(8,128)}, u32[]{:S(2)}, u32[]{:S(2)}) collective-permute-start(f32[2,1152,128]{2,1,0:T(8,128)} %get-tuple-element.19), channel_id=1, source_target_pairs={{0,4},{4,0},{8,12},{12,8},{16,20},{20,16},{24,28},{28,24},{32,36},... | collective-permute-start | bytes 3538952 | tf_op jit(solution)/shard_map/ppermute | solution.py:265
  15.3 5.9 %collective-permute-start.2 = (bf16[256,256]{1,0:T(8,128)(2,1)}, bf16[256,256]{1,0:T(8,128)(2,1)S(1)}, u32[]{:S(2)}, u32[]{:S(2)}) collective-permute-start(bf16[256,256]{1,0:T(8,128)(2,1)} %get-tuple-element.57), channel_id=1, source_target_pairs={{0,16},{4,68},{8,24},{12,76},{16,0},{20,84},{24,8},{28,92},{32,48}... | collective-permute-start | bytes 393224 | tf_op jit(solution)/shard_map/ppermute | solution.py:273
  18.7 5.4 %collective-permute-start.4 = (bf16[256,256]{1,0:T(8,128)(2,1)S(1)}, bf16[256,256]{1,0:T(8,128)(2,1)}, u32[]{:S(2)}, u32[]{:S(2)}) collective-permute-start(bf16[256,256]{1,0:T(8,128)(2,1)S(1)} %get-tuple-element.58), channel_id=1, source_target_pairs={{0,24},{4,100},{8,16},{12,108},{16,8},{20,116},{24,0},{28,124},{32... | collective-permute-start | bytes 393224 | tf_op jit(solution)/shard_map/ppermute | solution.py:273
  25.3 5.4 %collective-permute-start.5 = (bf16[256,256]{1,0:T(8,128)(2,1)S(1)}, bf16[256,256]{1,0:T(8,128)(2,1)S(1)}, u32[]{:S(2)}, u32[]{:S(2)}) collective-permute-start(bf16[256,256]{1,0:T(8,128)(2,1)S(1)} %add_convert_fusion.5), channel_id=1, source_target_pairs={{0,64},{4,20},{8,72},{12,28},{16,80},{20,4},{24,88},{28,12},{32,96... | collective-permute-start | bytes 393224 | tf_op jit(solution)/shard_map/ppermute | solution.py:277
  27.8 5.6 %collective-permute-start.6 = (bf16[256,256]{1,0:T(8,128)(2,1)S(1)}, bf16[256,256]{1,0:T(8,128)(2,1)S(1)}, u32[]{:S(2)}, u32[]{:S(2)}) collective-permute-start(bf16[256,256]{1,0:T(8,128)(2,1)S(1)} %add_convert_fusion.5), channel_id=1, source_target_pairs={{0,32},{4,12},{8,40},{12,4},{16,48},{20,28},{24,56},{28,20},{32,0}... | collective-permute-start | bytes 393224 | tf_op jit(solution)/shard_map/ppermute | solution.py:277
  28.1 5.2 %collective-permute-start.7 = (bf16[256,256]{1,0:T(8,128)(2,1)S(1)}, bf16[256,256]{1,0:T(8,128)(2,1)S(1)}, u32[]{:S(2)}, u32[]{:S(2)}) collective-permute-start(bf16[256,256]{1,0:T(8,128)(2,1)S(1)} %add_convert_fusion.5), channel_id=1, source_target_pairs={{0,96},{4,28},{8,104},{12,20},{16,112},{20,12},{24,120},{28,4},{32... | collective-permute-start | bytes 393224 | tf_op jit(solution)/shard_map/ppermute | solution.py:277
  30.7 6.2 %collective-permute-start.12 = (f32[2,1152]{1,0:T(2,128)S(1)}, f32[2,1152]{1,0:T(2,128)S(1)}, u32[]{:S(2)}, u32[]{:S(2)}) collective-permute-start(f32[2,1152]{1,0:T(2,128)S(1)} %constant_dynamic-slice_fusion), channel_id=1, source_target_pairs={{0,4},{4,0},{8,12},{12,8},{16,20},{20,16},{24,28},{28,24},{32,36},... | collective-permute-start | bytes 27656 | tf_op jit(solution)/shard_map/ppermute | solution.py:265
  34.1 6.6 %collective-permute-start.10 = (bf16[256,256]{1,0:T(8,128)(2,1)}, bf16[256,256]{1,0:T(8,128)(2,1)}, u32[]{:S(2)}, u32[]{:S(2)}) collective-permute-start(bf16[256,256]{1,0:T(8,128)(2,1)} %add_convert_fusion.4.piece0), channel_id=1, source_target_pairs={{0,24},{4,100},{8,16},{12,108},{16,8},{20,116},{24,0},{28,124},{32... | collective-permute-start | bytes 393224 | tf_op jit(solution)/shard_map/ppermute | solution.py:281
  37.5 5.6 %collective-permute-start.9 = (bf16[256,256]{1,0:T(8,128)(2,1)}, bf16[256,256]{1,0:T(8,128)(2,1)}, u32[]{:S(2)}, u32[]{:S(2)}) collective-permute-start(bf16[256,256]{1,0:T(8,128)(2,1)} %add_convert_fusion.4.piece0), channel_id=1, source_target_pairs={{0,16},{4,68},{8,24},{12,76},{16,0},{20,84},{24,8},{28,92},{32,48}... | collective-permute-start | bytes 393224 | tf_op jit(solution)/shard_map/ppermute | solution.py:281
  54.0 5.4 %collective-permute-start.13 = (bf16[256,256]{1,0:T(8,128)(2,1)S(1)}, bf16[256,256]{1,0:T(8,128)(2,1)S(1)}, u32[]{:S(2)}, u32[]{:S(2)}) collective-permute-start(bf16[256,256]{1,0:T(8,128)(2,1)S(1)} %get-tuple-element.54), channel_id=1, source_target_pairs={{0,16},{4,68},{8,24},{12,76},{16,0},{20,84},{24,8},{28,92},{32,48}... | collective-permute-start | bytes 393224 | tf_op jit(solution)/shard_map/ppermute | solution.py:273
  56.4 5.0 %collective-permute-start.15 = (bf16[256,256]{1,0:T(8,128)(2,1)S(1)}, bf16[256,256]{1,0:T(8,128)(2,1)S(1)}, u32[]{:S(2)}, u32[]{:S(2)}) collective-permute-start(bf16[256,256]{1,0:T(8,128)(2,1)S(1)} %get-tuple-element.55), channel_id=1, source_target_pairs={{0,24},{4,100},{8,16},{12,108},{16,8},{20,116},{24,0},{28,124},{32... | collective-permute-start | bytes 393224 | tf_op jit(solution)/shard_map/ppermute | solution.py:273
  62.1 5.7 %collective-permute-start.16 = (bf16[256,256]{1,0:T(8,128)(2,1)}, bf16[256,256]{1,0:T(8,128)(2,1)}, u32[]{:S(2)}, u32[]{:S(2)}) collective-permute-start(bf16[256,256]{1,0:T(8,128)(2,1)} %fusion.9), channel_id=1, source_target_pairs={{0,64},{4,20},{8,72},{12,28},{16,80},{20,4},{24,88},{28,12},{32,96... | collective-permute-start | bytes 393224 | tf_op jit(solution)/shard_map/ppermute | solution.py:277
  63.5 5.7 %collective-permute-start.18 = (bf16[256,256]{1,0:T(8,128)(2,1)}, bf16[256,256]{1,0:T(8,128)(2,1)}, u32[]{:S(2)}, u32[]{:S(2)}) collective-permute-start(bf16[256,256]{1,0:T(8,128)(2,1)} %fusion.9), channel_id=1, source_target_pairs={{0,96},{4,28},{8,104},{12,20},{16,112},{20,12},{24,120},{28,4},{32... | collective-permute-start | bytes 393224 | tf_op jit(solution)/shard_map/ppermute | solution.py:277
  71.9 9.6 %collective-permute-start.19 = (bf16[256,256]{1,0:T(8,128)(2,1)}, bf16[256,256]{1,0:T(8,128)(2,1)}, u32[]{:S(2)}, u32[]{:S(2)}) collective-permute-start(bf16[256,256]{1,0:T(8,128)(2,1)} %get-tuple-element.35), channel_id=1, source_target_pairs={{0,8},{4,36},{8,0},{12,44},{16,24},{20,52},{24,16},{28,60},{32,40}... | collective-permute-start | bytes 393224 | tf_op jit(solution)/shard_map/ppermute | solution.py:281
  73.1 10.0 %collective-permute-start.20 = (bf16[256,256]{1,0:T(8,128)(2,1)}, bf16[256,256]{1,0:T(8,128)(2,1)}, u32[]{:S(2)}, u32[]{:S(2)}) collective-permute-start(bf16[256,256]{1,0:T(8,128)(2,1)} %get-tuple-element.35), channel_id=1, source_target_pairs={{0,16},{4,68},{8,24},{12,76},{16,0},{20,84},{24,8},{28,92},{32,48}... | collective-permute-start | bytes 393224 | tf_op jit(solution)/shard_map/ppermute | solution.py:281
  80.7 5.6 %collective-permute-start.21 = (bf16[256,256]{1,0:T(8,128)(2,1)}, bf16[256,256]{1,0:T(8,128)(2,1)S(1)}, u32[]{:S(2)}, u32[]{:S(2)}) collective-permute-start(bf16[256,256]{1,0:T(8,128)(2,1)} %get-tuple-element.35), channel_id=1, source_target_pairs={{0,24},{4,100},{8,16},{12,108},{16,8},{20,116},{24,0},{28,124},{32... | collective-permute-start | bytes 393224 | tf_op jit(solution)/shard_map/ppermute | solution.py:281
  87.0 9.5 %collective-permute-start.22 = (bf16[1024,256]{1,0:T(8,128)(2,1)}, bf16[1024,256]{1,0:T(8,128)(2,1)S(1)}, u32[]{:S(2)}, u32[]{:S(2)}) collective-permute-start(bf16[1024,256]{1,0:T(8,128)(2,1)} %constant_dynamic-update-slice_fusion.4.mine_ref), channel_id=1, source_target_pairs={{0,4},{4,0},{8,12},{12,8},{16,20},{20,16},{24,28},{28,24},{32,36},... | collective-permute-start | bytes 1572872 | tf_op jit(solution)/shard_map/ppermute | solution.py:265
  101.9 9.2 %collective-permute-start.23 = (f16[1200,128]{1,0:T(8,128)(2,1)S(1)}, f16[1200,128]{1,0:T(8,128)(2,1)S(1)}, u32[]{:S(2)}, u32[]{:S(2)}) collective-permute-start(f16[1200,128]{1,0:T(8,128)(2,1)S(1)} %get-tuple-element.41), channel_id=1, source_target_pairs={{0,1},{1,0},{2,3},{3,2},{4,5},{5,4},{6,7},{7,6},{8,9},{9,8},{10,11... | collective-permute-start | bytes 921608 | tf_op jit(solution)/shard_map/ppermute | solution.py:287
  103.6 17.4 %collective-permute-start.24 = (f16[1200,128]{1,0:T(8,128)(2,1)S(1)}, f16[1200,128]{1,0:T(8,128)(2,1)S(1)}, u32[]{:S(2)}, u32[]{:S(2)}) collective-permute-start(f16[1200,128]{1,0:T(8,128)(2,1)S(1)} %get-tuple-element.40), channel_id=1, source_target_pairs={{0,2},{1,3},{2,0},{3,1},{4,6},{5,7},{6,4},{7,5},{8,10},{9,11},{10,... | collective-permute-start | bytes 921608 | tf_op jit(solution)/shard_map/ppermute | solution.py:287
  106.9 16.1 %collective-permute-start.25 = (f16[1200,128]{1,0:T(8,128)(2,1)S(1)}, f16[1200,128]{1,0:T(8,128)(2,1)S(1)}, u32[]{:S(2)}, u32[]{:S(2)}) collective-permute-start(f16[1200,128]{1,0:T(8,128)(2,1)S(1)} %get-tuple-element.39), channel_id=1, source_target_pairs={{0,3},{1,2},{2,1},{3,0},{4,7},{5,6},{6,5},{7,4},{8,11},{9,10},{10,... | collective-permute-start | bytes 921608 | tf_op jit(solution)/shard_map/ppermute | solution.py:287
  129.0 7.3 %collective-permute-start.26 = (f16[1168,128]{1,0:T(8,128)(2,1)S(1)}, f16[1168,128]{1,0:T(8,128)(2,1)S(1)}, u32[]{:S(2)}, u32[]{:S(2)}) collective-permute-start(f16[1168,128]{1,0:T(8,128)(2,1)S(1)} %get-tuple-element.47), channel_id=1, source_target_pairs={{0,1},{1,0},{2,3},{3,2},{4,5},{5,4},{6,7},{7,6},{8,9},{9,8},{10,11... | collective-permute-start | bytes 897032 | tf_op jit(solution)/shard_map/ppermute | solution.py:287
  129.0 14.0 %collective-permute-start.27 = (f16[1168,128]{1,0:T(8,128)(2,1)S(1)}, f16[1168,128]{1,0:T(8,128)(2,1)S(1)}, u32[]{:S(2)}, u32[]{:S(2)}) collective-permute-start(f16[1168,128]{1,0:T(8,128)(2,1)S(1)} %get-tuple-element.46), channel_id=1, source_target_pairs={{0,2},{1,3},{2,0},{3,1},{4,6},{5,7},{6,4},{7,5},{8,10},{9,11},{10,... | collective-permute-start | bytes 897032 | tf_op jit(solution)/shard_map/ppermute | solution.py:287
  130.5 14.6 %collective-permute-start.28 = (f16[1168,128]{1,0:T(8,128)(2,1)S(1)}, f16[1168,128]{1,0:T(8,128)(2,1)S(1)}, u32[]{:S(2)}, u32[]{:S(2)}) collective-permute-start(f16[1168,128]{1,0:T(8,128)(2,1)S(1)} %get-tuple-element.45), channel_id=1, source_target_pairs={{0,3},{1,2},{2,1},{3,0},{4,7},{5,6},{6,5},{7,4},{8,11},{9,10},{10,... | collective-permute-start | bytes 897032 | tf_op jit(solution)/shard_map/ppermute | solution.py:287
  149.9 24.3 %collective-permute-start.39 = (f32[2,1152,128]{2,1,0:T(8,128)S(1)}, f32[2,1152,128]{2,1,0:T(8,128)S(1)}, u32[]{:S(2)}, u32[]{:S(2)}) collective-permute-start(f32[2,1152,128]{2,1,0:T(8,128)S(1)} %get-tuple-element.26), channel_id=1, source_target_pairs={{0,4},{4,0},{8,12},{12,8},{16,20},{20,16},{24,28},{28,24},{32,36},... | collective-permute-start | bytes 3538952 | tf_op jit(solution)/shard_map/ppermute | solution.py:265
  153.4 5.7 %collective-permute-start.30 = (bf16[256,256]{1,0:T(8,128)(2,1)S(1)}, bf16[256,256]{1,0:T(8,128)(2,1)S(1)}, u32[]{:S(2)}, u32[]{:S(2)}) collective-permute-start(bf16[256,256]{1,0:T(8,128)(2,1)S(1)} %get-tuple-element.51), channel_id=1, source_target_pairs={{0,16},{4,68},{8,24},{12,76},{16,0},{20,84},{24,8},{28,92},{32,48}... | collective-permute-start | bytes 393224 | tf_op jit(solution)/shard_map/ppermute | solution.py:273
  154.5 6.4 %collective-permute-start.31 = (bf16[256,256]{1,0:T(8,128)(2,1)S(1)}, bf16[256,256]{1,0:T(8,128)(2,1)S(1)}, u32[]{:S(2)}, u32[]{:S(2)}) collective-permute-start(bf16[256,256]{1,0:T(8,128)(2,1)S(1)} %get-tuple-element.53), channel_id=1, source_target_pairs={{0,8},{4,36},{8,0},{12,44},{16,24},{20,52},{24,16},{28,60},{32,40}... | collective-permute-start | bytes 393224 | tf_op jit(solution)/shard_map/ppermute | solution.py:273
  157.0 5.3 %collective-permute-start.32 = (bf16[256,256]{1,0:T(8,128)(2,1)S(1)}, bf16[256,256]{1,0:T(8,128)(2,1)S(1)}, u32[]{:S(2)}, u32[]{:S(2)}) collective-permute-start(bf16[256,256]{1,0:T(8,128)(2,1)S(1)} %get-tuple-element.52), channel_id=1, source_target_pairs={{0,24},{4,100},{8,16},{12,108},{16,8},{20,116},{24,0},{28,124},{32... | collective-permute-start | bytes 393224 | tf_op jit(solution)/shard_map/ppermute | solution.py:273
  162.4 5.7 %collective-permute-start.33 = (bf16[256,256]{1,0:T(8,128)(2,1)S(1)}, bf16[256,256]{1,0:T(8,128)(2,1)S(1)}, u32[]{:S(2)}, u32[]{:S(2)}) collective-permute-start(bf16[256,256]{1,0:T(8,128)(2,1)S(1)} %add_convert_fusion.2), channel_id=1, source_target_pairs={{0,64},{4,20},{8,72},{12,28},{16,80},{20,4},{24,88},{28,12},{32,96... | collective-permute-start | bytes 393224 | tf_op jit(solution)/shard_map/ppermute | solution.py:277
  165.2 5.0 %collective-permute-start.35 = (bf16[256,256]{1,0:T(8,128)(2,1)S(1)}, bf16[256,256]{1,0:T(8,128)(2,1)S(1)}, u32[]{:S(2)}, u32[]{:S(2)}) collective-permute-start(bf16[256,256]{1,0:T(8,128)(2,1)S(1)} %add_convert_fusion.2), channel_id=1, source_target_pairs={{0,96},{4,28},{8,104},{12,20},{16,112},{20,12},{24,120},{28,4},{32... | collective-permute-start | bytes 393224 | tf_op jit(solution)/shard_map/ppermute | solution.py:277
  170.4 6.6 %collective-permute-start.37 = (bf16[256,256]{1,0:T(8,128)(2,1)S(1)}, bf16[256,256]{1,0:T(8,128)(2,1)S(1)}, u32[]{:S(2)}, u32[]{:S(2)}) collective-permute-start(bf16[256,256]{1,0:T(8,128)(2,1)S(1)} %add_convert_fusion.1.piece0), channel_id=1, source_target_pairs={{0,16},{4,68},{8,24},{12,76},{16,0},{20,84},{24,8},{28,92},{32,48}... | collective-permute-start | bytes 393224 | tf_op jit(solution)/shard_map/ppermute | solution.py:281
  173.3 5.2 %collective-permute-start.38 = (bf16[256,256]{1,0:T(8,128)(2,1)S(1)}, bf16[256,256]{1,0:T(8,128)(2,1)S(1)}, u32[]{:S(2)}, u32[]{:S(2)}) collective-permute-start(bf16[256,256]{1,0:T(8,128)(2,1)S(1)} %add_convert_fusion.1.piece0), channel_id=1, source_target_pairs={{0,24},{4,100},{8,16},{12,108},{16,8},{20,116},{24,0},{28,124},{32... | collective-permute-start | bytes 393224 | tf_op jit(solution)/shard_map/ppermute | solution.py:281
  186.0 5.4 %collective-permute-start.40 = (bf16[256,256]{1,0:T(8,128)(2,1)S(1)}, bf16[256,256]{1,0:T(8,128)(2,1)S(1)}, u32[]{:S(2)}, u32[]{:S(2)}) collective-permute-start(bf16[256,256]{1,0:T(8,128)(2,1)S(1)} %get-tuple-element.48), channel_id=1, source_target_pairs={{0,16},{4,68},{8,24},{12,76},{16,0},{20,84},{24,8},{28,92},{32,48}... | collective-permute-start | bytes 393224 | tf_op jit(solution)/shard_map/ppermute | solution.py:273
  186.6 5.1 %collective-permute-start.41 = (bf16[256,256]{1,0:T(8,128)(2,1)S(1)}, bf16[256,256]{1,0:T(8,128)(2,1)S(1)}, u32[]{:S(2)}, u32[]{:S(2)}) collective-permute-start(bf16[256,256]{1,0:T(8,128)(2,1)S(1)} %get-tuple-element.50), channel_id=1, source_target_pairs={{0,8},{4,36},{8,0},{12,44},{16,24},{20,52},{24,16},{28,60},{32,40}... | collective-permute-start | bytes 393224 | tf_op jit(solution)/shard_map/ppermute | solution.py:273
  187.9 5.0 %collective-permute-start.42 = (bf16[256,256]{1,0:T(8,128)(2,1)S(1)}, bf16[256,256]{1,0:T(8,128)(2,1)S(1)}, u32[]{:S(2)}, u32[]{:S(2)}) collective-permute-start(bf16[256,256]{1,0:T(8,128)(2,1)S(1)} %get-tuple-element.49), channel_id=1, source_target_pairs={{0,24},{4,100},{8,16},{12,108},{16,8},{20,116},{24,0},{28,124},{32... | collective-permute-start | bytes 393224 | tf_op jit(solution)/shard_map/ppermute | solution.py:273
  193.0 6.0 %collective-permute-start.43 = (bf16[256,256]{1,0:T(8,128)(2,1)S(1)}, bf16[256,256]{1,0:T(8,128)(2,1)S(1)}, u32[]{:S(2)}, u32[]{:S(2)}) collective-permute-start(bf16[256,256]{1,0:T(8,128)(2,1)S(1)} %fusion.6), channel_id=1, source_target_pairs={{0,64},{4,20},{8,72},{12,28},{16,80},{20,4},{24,88},{28,12},{32,96... | collective-permute-start | bytes 393224 | tf_op jit(solution)/shard_map/ppermute | solution.py:277
  193.9 6.4 %collective-permute-start.44 = (bf16[256,256]{1,0:T(8,128)(2,1)S(1)}, bf16[256,256]{1,0:T(8,128)(2,1)S(1)}, u32[]{:S(2)}, u32[]{:S(2)}) collective-permute-start(bf16[256,256]{1,0:T(8,128)(2,1)S(1)} %fusion.6), channel_id=1, source_target_pairs={{0,32},{4,12},{8,40},{12,4},{16,48},{20,28},{24,56},{28,20},{32,0}... | collective-permute-start | bytes 393224 | tf_op jit(solution)/shard_map/ppermute | solution.py:277
  194.7 7.0 %collective-permute-start.45 = (bf16[256,256]{1,0:T(8,128)(2,1)S(1)}, bf16[256,256]{1,0:T(8,128)(2,1)S(1)}, u32[]{:S(2)}, u32[]{:S(2)}) collective-permute-start(bf16[256,256]{1,0:T(8,128)(2,1)S(1)} %fusion.6), channel_id=1, source_target_pairs={{0,96},{4,28},{8,104},{12,20},{16,112},{20,12},{24,120},{28,4},{32... | collective-permute-start | bytes 393224 | tf_op jit(solution)/shard_map/ppermute | solution.py:277
  201.9 6.9 %collective-permute-start.47 = (bf16[256,256]{1,0:T(8,128)(2,1)S(1)}, bf16[256,256]{1,0:T(8,128)(2,1)S(1)}, u32[]{:S(2)}, u32[]{:S(2)}) collective-permute-start(bf16[256,256]{1,0:T(8,128)(2,1)S(1)} %get-tuple-element.33), channel_id=1, source_target_pairs={{0,16},{4,68},{8,24},{12,76},{16,0},{20,84},{24,8},{28,92},{32,48}... | collective-permute-start | bytes 393224 | tf_op jit(solution)/shard_map/ppermute | solution.py:281
  203.8 8.2 %collective-permute-start.48 = (bf16[256,256]{1,0:T(8,128)(2,1)S(1)}, bf16[256,256]{1,0:T(8,128)(2,1)S(1)}, u32[]{:S(2)}, u32[]{:S(2)}) collective-permute-start(bf16[256,256]{1,0:T(8,128)(2,1)S(1)} %get-tuple-element.33), channel_id=1, source_target_pairs={{0,24},{4,100},{8,16},{12,108},{16,8},{20,116},{24,0},{28,124},{32... | collective-permute-start | bytes 393224 | tf_op jit(solution)/shard_map/ppermute | solution.py:281
  212.0 10.7 %collective-permute-start.49 = (bf16[1024,256]{1,0:T(8,128)(2,1)S(1)}, bf16[1024,256]{1,0:T(8,128)(2,1)S(1)}, u32[]{:S(2)}, u32[]{:S(2)}) collective-permute-start(bf16[1024,256]{1,0:T(8,128)(2,1)S(1)} %constant_dynamic-update-slice_fusion.mine_ref), channel_id=1, source_target_pairs={{0,4},{4,0},{8,12},{12,8},{16,20},{20,16},{24,28},{28,24},{32,36},... | collective-permute-start | bytes 1572872 | tf_op jit(solution)/shard_map/ppermute | solution.py:265
  226.6 8.6 %collective-permute-start.50 = (f16[1200,128]{1,0:T(8,128)(2,1)S(1)}, f16[1200,128]{1,0:T(8,128)(2,1)S(1)}, u32[]{:S(2)}, u32[]{:S(2)}) collective-permute-start(f16[1200,128]{1,0:T(8,128)(2,1)S(1)} %get-tuple-element.38), channel_id=1, source_target_pairs={{0,1},{1,0},{2,3},{3,2},{4,5},{5,4},{6,7},{7,6},{8,9},{9,8},{10,11... | collective-permute-start | bytes 921608 | tf_op jit(solution)/shard_map/ppermute | solution.py:287
  226.7 17.1 %collective-permute-start.51 = (f16[1200,128]{1,0:T(8,128)(2,1)S(1)}, f16[1200,128]{1,0:T(8,128)(2,1)S(1)}, u32[]{:S(2)}, u32[]{:S(2)}) collective-permute-start(f16[1200,128]{1,0:T(8,128)(2,1)S(1)} %get-tuple-element.37), channel_id=1, source_target_pairs={{0,2},{1,3},{2,0},{3,1},{4,6},{5,7},{6,4},{7,5},{8,10},{9,11},{10,... | collective-permute-start | bytes 921608 | tf_op jit(solution)/shard_map/ppermute | solution.py:287
  230.2 15.6 %collective-permute-start.52 = (f16[1200,128]{1,0:T(8,128)(2,1)S(1)}, f16[1200,128]{1,0:T(8,128)(2,1)S(1)}, u32[]{:S(2)}, u32[]{:S(2)}) collective-permute-start(f16[1200,128]{1,0:T(8,128)(2,1)S(1)} %get-tuple-element.36), channel_id=1, source_target_pairs={{0,3},{1,2},{2,1},{3,0},{4,7},{5,6},{6,5},{7,4},{8,11},{9,10},{10,... | collective-permute-start | bytes 921608 | tf_op jit(solution)/shard_map/ppermute | solution.py:287
  249.5 6.8 %collective-permute-start.53 = (f16[1168,128]{1,0:T(8,128)(2,1)S(1)}, f16[1168,128]{1,0:T(8,128)(2,1)S(1)}, u32[]{:S(2)}, u32[]{:S(2)}) collective-permute-start(f16[1168,128]{1,0:T(8,128)(2,1)S(1)} %get-tuple-element.44), channel_id=1, source_target_pairs={{0,1},{1,0},{2,3},{3,2},{4,5},{5,4},{6,7},{7,6},{8,9},{9,8},{10,11... | collective-permute-start | bytes 897032 | tf_op jit(solution)/shard_map/ppermute | solution.py:287
  249.6 13.3 %collective-permute-start.54 = (f16[1168,128]{1,0:T(8,128)(2,1)S(1)}, f16[1168,128]{1,0:T(8,128)(2,1)S(1)}, u32[]{:S(2)}, u32[]{:S(2)}) collective-permute-start(f16[1168,128]{1,0:T(8,128)(2,1)S(1)} %get-tuple-element.43), channel_id=1, source_target_pairs={{0,2},{1,3},{2,0},{3,1},{4,6},{5,7},{6,4},{7,5},{8,10},{9,11},{10,... | collective-permute-start | bytes 897032 | tf_op jit(solution)/shard_map/ppermute | solution.py:287
  251.2 14.6 %collective-permute-start.55 = (f16[1168,128]{1,0:T(8,128)(2,1)S(1)}, f16[1168,128]{1,0:T(8,128)(2,1)S(1)}, u32[]{:S(2)}, u32[]{:S(2)}) collective-permute-start(f16[1168,128]{1,0:T(8,128)(2,1)S(1)} %get-tuple-element.42), channel_id=1, source_target_pairs={{0,3},{1,2},{2,1},{3,0},{4,7},{5,6},{6,5},{7,4},{8,11},{9,10},{10,... | collective-permute-start | bytes 897032 | tf_op jit(solution)/shard_map/ppermute | solution.py:287
  (20 other events, 173.5 us)

commit v6 on v4

--- a/solution.py
+++ b/solution.py
@@ -77,36 +77,49 @@
     lax.fori_loop(0, SIDE, step, 0)
 
 
-def pack_body(core_ref, z_ref, factors_ref, mine_ref, other_ref, sources_ref,
+def pack_body(d, core_ref, z_ref, factors_ref, mine_ref, other_ref, sources_ref,
               weight_ref, kernel_ref, sent_ref, whole):
     nf, rows, cols = sources_ref.shape
     quarter = rows // SIDE
-    length = quarter
-    body = nf * length
+    body = nf * quarter
     gather_parts(core_ref, mine_ref, other_ref, whole)
-
-    def block(d, peak):
-        base = pl.multiple_of((z_ref[0] ^ d) * quarter, RUN)
-        at = pl.ds(base, length)
+    there = z_ref[0] ^ d
+    at = pl.ds(pl.multiple_of(there * quarter, RUN), quarter)
+    spread = jnp.dot(factors_ref[at, :], whole[...], preferred_element_type=F32)
+    peak = jnp.zeros((RUN, cols), F32)
+    for f in range(nf):
+        lanes = slice(f * cols, (f + 1) * cols)
+        value = sources_ref[f, at, :] + weight_ref[at, f : f + 1] * spread[:, lanes]
+        for g in range(quarter // RUN):
+            tile = value[g * RUN : (g + 1) * RUN]
+            sent_ref[(g * nf + f) * RUN : (g * nf + f + 1) * RUN, :] = tile
+            peak = jnp.maximum(peak, jnp.abs(tile))
+    kernel = kernel_ref[there]
+    high = kernel.astype(BF16).astype(F32)
+    sent_ref[body + RUN : body + 2 * RUN, :] = high
+    sent_ref[body + 2 * RUN :, :] = kernel - high
+    if d:
+        peak = jnp.max(jnp.max(peak, axis=0, keepdims=True), axis=1, keepdims=True)
+        power, scale = scale_of(jnp.broadcast_to(peak, (1, cols)))
+        sent_ref[:body, :] = sent_ref[:body, :] * jnp.broadcast_to(scale, (body, cols))
+        sent_ref[body : body + RUN, :] = jnp.broadcast_to(power, (RUN, cols))
+
+
+def amplitude_body(core_ref, factors_ref, mine_ref, other_ref, sources_ref, weight_ref,
+                   amplitude_ref, whole):
+    nf, rows, cols = sources_ref.shape
+    gather_parts(core_ref, mine_ref, other_ref, whole)
+    span = rows // SIDE
+
+    def step(r, carry):
+        at = pl.ds(pl.multiple_of(r * span, RUN), span)
         spread = jnp.dot(factors_ref[at, :], whole[...], preferred_element_type=F32)
         for f in range(nf):
-            value = sources_ref[f, at, :] + weight_ref[at, f : f + 1] * spread[:, f * cols : (f + 1) * cols]
-            for g in range(length // RUN):
-                tile = value[g * RUN : (g + 1) * RUN]
-                sent_ref[d, (g * nf + f) * RUN : (g * nf + f + 1) * RUN, :] = tile
-                peak = jnp.maximum(peak, jnp.abs(tile))
-        kernel = kernel_ref[z_ref[0] ^ d]
-        high = kernel.astype(BF16).astype(F32)
-        sent_ref[d, body + RUN : body + 2 * RUN, :] = high
-        sent_ref[d, body + 2 * RUN :, :] = kernel - high
-        return peak
-
-    peak = lax.fori_loop(0, SIDE, block, jnp.zeros((RUN, cols), F32))
-    peak = jnp.max(jnp.max(peak, axis=0, keepdims=True), axis=1, keepdims=True)
-    power, scale = scale_of(jnp.broadcast_to(peak, (1, cols)))
-    for d in range(1, SIDE):
-        sent_ref[d, :body, :] = sent_ref[d, :body, :] * jnp.broadcast_to(scale, (body, cols))
-        sent_ref[d, body : body + RUN, :] = jnp.broadcast_to(power, (RUN, cols))
+            lanes = slice(f * cols, (f + 1) * cols)
+            amplitude_ref[f, at, :] = sources_ref[f, at, :] + weight_ref[at, f : f + 1] * spread[:, lanes]
+        return carry
+
+    lax.fori_loop(0, SIDE, step, 0)
 
 
 def mix_body(first, own_ref, got1, got2, got3, into_ref, out_ref, *refs):
@@ -114,8 +127,7 @@
         sent_ref, kernel_ref, turned = refs
     else:
         kernel_ref, sent_ref = refs
-    cols = own_ref.shape[2]
-    body = own_ref.shape[1] - 3 * RUN
+    body, cols = own_ref.shape[0] - 3 * RUN, own_ref.shape[1]
     size = into_ref.shape[1]
     part = size // SIDE
     got = (got1, got2, got3)
@@ -124,7 +136,7 @@
     each = LANES // RUN
     strips = -(-groups // each)
     if first:
-        for d, ref in enumerate((own_ref.at[0], *got)):
+        for d, ref in enumerate((own_ref, *got)):
             table = ref[body + RUN : body + 2 * RUN, :] + ref[body + 2 * RUN :, :]
             turned[d] = table.T
         for strip in range(strips):
@@ -156,7 +168,7 @@
             at = pl.ds(pl.multiple_of((wide * g + half) * part, part), part)
             sides.append(
                 jnp.concatenate(
-                    [own_ref[0, at, :]] + [r[at, :] * s for r, s in zip(got, gains)], axis=0
+                    [own_ref[at, :]] + [r[at, :] * s for r, s in zip(got, gains)], axis=0
                 )
             )
             kernels.append(
@@ -183,13 +195,12 @@
         sent_ref[d, body:, :] = jnp.broadcast_to(power, (RUN, cols))
 
 
-def unpack_body(z_ref, right_ref, *refs):
+def unpack_body(z_ref, right_ref, own_ref, got1, got2, got3, sources_ref, *rounded):
     nf, rows, cols = right_ref.shape
     quarter = rows // SIDE
     z = z_ref[0]
-    sources_ref, rounded_ref = refs[-2:]
     body = nf * quarter
-    for d, ref in enumerate(refs[:SIDE]):
+    for d, ref in enumerate((own_ref, got1, got2, got3)):
         base = (z ^ d) * quarter
         gain = jnp.exp2(jnp.broadcast_to(ref[body : body + 1, :], (RUN, cols))) if d else None
 
@@ -200,7 +211,8 @@
                 tile = ref[spot, :] * gain if d else ref[0, spot, :]
                 tile = right_ref[f, at, :] + tile
                 sources_ref[f, at, :] = tile
-                rounded_ref[at, f * cols : (f + 1) * cols] = tile.astype(BF16)
+                for rounded_ref in rounded:
+                    rounded_ref[at, f * cols : (f + 1) * cols] = tile.astype(BF16)
             return carry
 
         lax.fori_loop(0, quarter // RUN, step, 0)
@@ -266,15 +278,6 @@
         other = lax.ppermute(gathered, "fac", CORES)
         return gathered, other
 
-    def spread_of(parts):
-        gathered, other = parts
-        return (
-            jnp.einsum("pa,afc->fpc", factors_keep, gathered.reshape(half, nf, cols),
-                       preferred_element_type=F32)
-            + jnp.einsum("pa,afc->fpc", factors_send, other.reshape(half, nf, cols),
-                         preferred_element_type=F32)
-        )
-
     def exchange(sent):
         got = {}
         for d in PARTNERS:
@@ -283,7 +286,6 @@
 
     body = nf * quarter
     size = SIDE * nf * RUN
-    weight = pair_weight[:, :, None]
     place_z = jnp.full((1,), z, jnp.int32)
     strips = -(-quarter // LANES)
     kernel = second_order.reshape(nf, SIDE, quarter).transpose(1, 0, 2)
@@ -320,11 +322,15 @@
                 (core_at, factors, *parts, sources, column), whole,
             )
         parts = reduce_all(rounded)
-        (sent,) = call(
-            pack_body, [((SIDE, body + 3 * RUN, cols), F32)], "pack", 12, 2,
-            (core_at, place_z, factors, *parts, sources, column, kernel), whole,
-        )
+        sent = {}
+        for d in (*PARTNERS, 0):
+            (value,) = call(
+                partial(pack_body, d), [((body + 3 * RUN, cols), F32)], "pack", 10, 2,
+                (core_at, place_z, factors, *parts, sources, column, kernel), whole,
+            )
+            sent[d] = value
         got = exchange(sent)
+        sent = sent[0]
         mixed = [((SIDE, body + RUN, cols), F32)]
         tables = (table_in, table_out)
         if outer == 0:
@@ -338,13 +344,19 @@
                 (sent, *got, *tables, spread_kernel),
             )
         back = [sent, *exchange(sent)]
-        if outer == OUTER - 1:
-            amplitude = sources + weight * spread_of(parts)
-        sources, rounded = call(
+        last = outer == OUTER - 1
+        if last:
+            (amplitude,) = call(
+                amplitude_body, [(right_side.shape, F32)], "amplitude", 10, 1,
+                (core_at, factors, *parts, sources, column), whole,
+            )
+        sources, *rest = call(
             unpack_body,
-            [(right_side.shape, F32), ((rows, wide), BF16)],
+            [(right_side.shape, F32)] + ([] if last else [((rows, wide), BF16)]),
             "unpack", 4, 1, (place_z, right_side, *back),
         )
+        if not last:
+            (rounded,) = rest
     return (amplitude, sources)
 
 

time: 260 us -> 246 us (0.946)
  starting transfers between devices: 83.9 us -> 77.9 us
  local copies, waits for them, and re-layouts: 17 us -> 11.3 us
  Pallas kernels: 21.6 us -> 25.6 us
  matrix products: 16.1 us -> 13 us
  other arithmetic: 8 us -> 5.04 us
    ppermute x12, waiting for transfers between devices: 14.9 us -> 19.1 us  [reduce_all(): total = total + lax.ppermute(own, 'fac', along(d, False)).astype(F32)]
    pallas_call x9 -> x16, Pallas kernels: 21.6 us -> 25.6 us  [call(): pl.pallas_call(body, out_shape=[jax.ShapeDtypeStruct(s, t) for s, t in ou...]
    unnamed x53 -> x23, local copies, waits for them, and re-layouts: 10.7 us -> 7.4 us
    dot_general x2 -> x0, matrix products: 3 us -> none  [the longest x1 2.19 us: spread_of(): jnp.einsum('pa,afc->fpc', factors_keep, gathered.reshape(half, nf, cols),...]
    convert_element_type x12 -> x18, other arithmetic: 3.39 us -> 0.76 us  [exchange(): got[d] = lax.ppermute(sent[d].astype(F16), 'freq', swap(d)).astype(F32)]
  transfers between devices with their start and end apart: 56 -> 56, of which waited for: 53 -> 49; matrix products, arithmetic and copies ran while one was open for 4% -> 2% of each run, Pallas kernels for 0% -> 3%
where the time goes in v6:
time: 246 us; the launch traced here: 244 us
  waiting for transfers between devices  110 us (45%)
  starting transfers between devices  77.9 us (32%)
  Pallas kernels  25.6 us (10%)
  matrix products  13 us (5%)
  local copies, waits for them, and re-layouts  11.3 us (5%)
  other arithmetic  5.04 us (2%)
    ppermute x12, waiting for transfers between devices, exchange(): got[d] = lax.ppermute(sent[d].astype(F16), 'freq', swap(d)).astype(F32)  46.5 us
    pallas_call x16, Pallas kernels, call(): pl.pallas_call(body, out_shape=[jax.ShapeDtypeStruct(s, t) for s, t in ou...  25.6 us
    ppermute x12, waiting for transfers between devices, reduce_all(): total = total + lax.ppermute(own, 'fac', along(d, False)).astype(F32)  19.1 us
    ppermute x12, starting transfers between devices, exchange(): got[d] = lax.ppermute(sent[d].astype(F16), 'freq', swap(d)).astype(F32)  16.7 us
    ppermute x12, waiting for transfers between devices, reduce_all(): own = own + lax.ppermute(piece, 'fac', along(d, True)).astype(F32)  16.3 us
    ppermute x4, starting transfers between devices, reduce_all(): other = lax.ppermute(gathered, 'fac', CORES)  15.7 us
    ppermute x12, waiting for transfers between devices, reduce_all(): piece = lax.ppermute(total, 'fac', along(d, True))  13.9 us
    ppermute x12, starting transfers between devices, reduce_all(): own = own + lax.ppermute(piece, 'fac', along(d, True)).astype(F32)  13.8 us
  transfers between devices with their start and end apart: 56, of which 49 were waited for; matrix products, arithmetic and copies ran while one was open for 2% of the time, Pallas kernels for 3%

profile of v6, /device:TPU:1, one launch (start us, length us, event | category | flops | bytes accessed | tf_op | source)
XLA Modules:
  0.0 244.0 jit_solution(6173246003277347154)
XLA Ops:
  4.0 1.8 fusion.6
  7.3 2.6 %collective-permute-done = f32[512,512]{1,0:T(8,128)} collective-permute-done((f32[512,512]{1,0:T(8,128)}, f32[512,512]{1,0:T(8,128)}, u32[]{:S(2)}, u32[]{:S(2)}) %collective-permute-start) | collective-permute-done | bytes 1048608 | tf_op jit(solution)/shard_map/ppermute | solution.py:258
  9.9 3.1 %convolution_add_fusion.3 = f32[512,512]{1,0:T(8,128)} fusion(f32[512,512]{1,0:T(8,128)} %collective-permute-done, bf16[1152,512]{1,0:T(8,128)(2,1)S(1)} %round.1, bf16[1152,1024]{1,0:T(8,128)(2,1)S(1)} %copy-done.2, s32[]{:T(128)S(6)} %select_n.117), kind=kOutput, calls=%fused_computation.3 | convolution fusion | flops 604241920 | bytes 4456452 | tf_op jit(solution)/shard_map/dot_general | solution.py:252
  14.1 3.1 %collective-permute-start.1 = (bf16[128,512]{1,0:T(8,128)(2,1)S(1)}, bf16[128,512]{1,0:T(8,128)(2,1)S(1)}, u32[]{:S(2)}, u32[]{:S(2)}) collective-permute-start(bf16[128,512]{1,0:T(8,128)(2,1)S(1)} %get-tuple-element.33), channel_id=1, source_target_pairs={{0,16},{4,68},{8,24},{12,76},{16,0},{20,84},{24,8},{28,92},{32,48}... | collective-permute-start | bytes 393224 | tf_op jit(solution)/shard_map/ppermute | solution.py:265
  18.0 1.9 collective-permute-done.1
  24.0 2.5 %collective-permute-start.4 = (bf16[128,512]{1,0:T(8,128)(2,1)S(1)}, bf16[128,512]{1,0:T(8,128)(2,1)S(1)}, u32[]{:S(2)}, u32[]{:S(2)}) collective-permute-start(bf16[128,512]{1,0:T(8,128)(2,1)S(1)} %add_convert_fusion.7), channel_id=1, source_target_pairs={{0,64},{4,20},{8,72},{12,28},{16,80},{20,4},{24,88},{28,12},{32,96... | collective-permute-start | bytes 393224 | tf_op jit(solution)/shard_map/ppermute | solution.py:269
  27.4 2.0 collective-permute-done.4
  32.0 1.8 collective-permute-start.7
  35.3 2.1 collective-permute-done.7
  39.4 4.4 %collective-permute-start.10 = (bf16[512,512]{1,0:T(8,128)(2,1)S(1)}, bf16[512,512]{1,0:T(8,128)(2,1)}, u32[]{:S(2)}, u32[]{:S(2)}) collective-permute-start(bf16[512,512]{1,0:T(8,128)(2,1)S(1)} %constant_dynamic-update-slice_fusion.12.mine_ref), channel_id=1, source_target_pairs={{0,4},{4,0},{8,12},{12,8},{16,20},{20,16},{24,28},{28,24},{32,36},... | collective-permute-start | bytes 1572872 | tf_op jit(solution)/shard_map/ppermute | solution.py:278
  47.1 3.0 %ladder.2 = bf16[1152,512]{1,0:T(8,128)(2,1)S(1)} custom-call(s32[1]{0:T(128)} %bitcast.core_ref, bf16[1152,1024]{1,0:T(8,128)(2,1)S(1)} %copy-done.2, bf16[512,512]{1,0:T(8,128)(2,1)S(1)} %constant_dynamic-update-slice_fusion.12.mine_ref, bf16[512,512]{1,0:T(8,128)(2,1)} %collective-permute-done.10.other_ref, f32[4,1152,128]{2,1,0:T(8,128)S(1)} %copy-done.4, ...), custom_call_target="tpu_custom_call" | custom-call | tf_op jit(solution)/shard_map/ladder/pallas_call | solution.py:224
  51.6 2.3 collective-permute-done.11
  56.1 2.1 collective-permute-start.14
  58.2 2.4 collective-permute-done.12
  65.6 2.4 collective-permute-done.15
  71.0 1.8 constant_dynamic-update-slice_fusion.11
  81.6 3.2 %collective-permute-start.21 = (bf16[512,512]{1,0:T(8,128)(2,1)S(1)}, bf16[512,512]{1,0:T(8,128)(2,1)S(1)}, u32[]{:S(2)}, u32[]{:S(2)}) collective-permute-start(bf16[512,512]{1,0:T(8,128)(2,1)S(1)} %constant_dynamic-update-slice_fusion.8.mine_ref), channel_id=1, source_target_pairs={{0,4},{4,0},{8,12},{12,8},{16,20},{20,16},{24,28},{28,24},{32,36},... | collective-permute-start | bytes 1572872 | tf_op jit(solution)/shard_map/ppermute | solution.py:278
  88.9 4.0 %collective-permute-start.24 = (f16[1200,128]{1,0:T(8,128)(2,1)S(1)}, f16[1200,128]{1,0:T(8,128)(2,1)S(1)}, u32[]{:S(2)}, u32[]{:S(2)}) collective-permute-start(f16[1200,128]{1,0:T(8,128)(2,1)S(1)} %convert_element_type.260), channel_id=1, source_target_pairs={{0,3},{1,2},{2,1},{3,0},{4,7},{5,6},{6,5},{7,4},{8,11},{9,10},{10,... | collective-permute-start | bytes 921608 | tf_op jit(solution)/shard_map/ppermute | solution.py:284
  96.8 10.1 %collective-permute-done.24 = f16[1200,128]{1,0:T(8,128)(2,1)S(1)} collective-permute-done((f16[1200,128]{1,0:T(8,128)(2,1)S(1)}, f16[1200,128]{1,0:T(8,128)(2,1)S(1)}, u32[]{:S(2)}, u32[]{:S(2)}) %collective-permute-start.24) | collective-permute-done | bytes 307232 | tf_op jit(solution)/shard_map/ppermute | solution.py:284
  108.7 5.6 %mix.2 = (f32[4,1168,128]{2,1,0:T(8,128)S(1)}, f32[4608,128]{1,0:T(8,128)S(1)}) custom-call(f32[1200,128]{1,0:T(8,128)S(1)} %pack.8.own_ref, f32[1200,128]{1,0:T(8,128)S(1)} %convert_element_type.257.got1, f32[1200,128]{1,0:T(8,128)S(1)} %convert_element_type.259.got2, f32[1200,128]{1,0:T(8,128)S(1)} %convert_element_type.261.got3, ...), custom_call_target="tpu_custom_call" | custom-call | tf_op jit(solution)/shard_map/mix/pallas_call | solution.py:224
  115.4 2.3 collective-permute-start.26
  118.6 3.6 %collective-permute-done.25 = f16[1168,128]{1,0:T(8,128)(2,1)S(1)} collective-permute-done((f16[1168,128]{1,0:T(8,128)(2,1)S(1)}, f16[1168,128]{1,0:T(8,128)(2,1)S(1)}, u32[]{:S(2)}, u32[]{:S(2)}) %collective-permute-start.25) | collective-permute-done | bytes 299040 | tf_op jit(solution)/shard_map/ppermute | solution.py:284
  122.2 7.7 %collective-permute-done.26 = f16[1168,128]{1,0:T(8,128)(2,1)S(1)} collective-permute-done((f16[1168,128]{1,0:T(8,128)(2,1)S(1)}, f16[1168,128]{1,0:T(8,128)(2,1)S(1)}, u32[]{:S(2)}, u32[]{:S(2)}) %collective-permute-start.26) | collective-permute-done | bytes 299040 | tf_op jit(solution)/shard_map/ppermute | solution.py:284
  129.9 2.4 collective-permute-done.27
  133.8 2.6 %collective-permute-start.28 = (f32[512,512]{1,0:T(8,128)S(1)}, f32[512,512]{1,0:T(8,128)S(1)}, u32[]{:S(2)}, u32[]{:S(2)}) collective-permute-start(f32[512,512]{1,0:T(8,128)S(1)} %fusion.2), channel_id=1, source_target_pairs={{0,4},{4,0},{8,12},{12,8},{16,20},{20,16},{24,28},{28,24},{32,36},... | collective-permute-start | bytes 3145736 | tf_op jit(solution)/shard_map/ppermute | solution.py:258
  136.5 2.3 collective-permute-done.28
  143.0 2.4 collective-permute-done.29
  148.0 2.5 %collective-permute-start.33 = (bf16[128,512]{1,0:T(8,128)(2,1)S(1)}, bf16[128,512]{1,0:T(8,128)(2,1)S(1)}, u32[]{:S(2)}, u32[]{:S(2)}) collective-permute-start(bf16[128,512]{1,0:T(8,128)(2,1)S(1)} %add_convert_fusion.3), channel_id=1, source_target_pairs={{0,32},{4,12},{8,40},{12,4},{16,48},{20,28},{24,56},{28,20},{32,0}... | collective-permute-start | bytes 393224 | tf_op jit(solution)/shard_map/ppermute | solution.py:269
  150.9 2.1 collective-permute-done.32
  159.2 2.1 collective-permute-done.35
  162.8 4.5 %collective-permute-start.38 = (bf16[512,512]{1,0:T(8,128)(2,1)S(1)}, bf16[512,512]{1,0:T(8,128)(2,1)S(1)}, u32[]{:S(2)}, u32[]{:S(2)}) collective-permute-start(bf16[512,512]{1,0:T(8,128)(2,1)S(1)} %constant_dynamic-update-slice_fusion.4.mine_ref), channel_id=1, source_target_pairs={{0,4},{4,0},{8,12},{12,8},{16,20},{20,16},{24,28},{28,24},{32,36},... | collective-permute-start | bytes 1572872 | tf_op jit(solution)/shard_map/ppermute | solution.py:278
  168.8 2.0 ladder.3
  172.2 2.3 collective-permute-done.39
  176.7 2.1 collective-permute-start.42
  178.8 2.4 collective-permute-done.40
  182.7 2.6 %collective-permute-start.44 = (bf16[128,512]{1,0:T(8,128)(2,1)S(1)}, bf16[128,512]{1,0:T(8,128)(2,1)S(1)}, u32[]{:S(2)}, u32[]{:S(2)}) collective-permute-start(bf16[128,512]{1,0:T(8,128)(2,1)S(1)} %add_convert_fusion.1), channel_id=1, source_target_pairs={{0,32},{4,12},{8,40},{12,4},{16,48},{20,28},{24,56},{28,20},{32,0}... | collective-permute-start | bytes 393224 | tf_op jit(solution)/shard_map/ppermute | solution.py:269
  185.6 2.1 collective-permute-done.43
  190.9 2.0 collective-permute-start.47
  194.1 2.1 collective-permute-done.46
  198.0 3.6 %collective-permute-start.49 = (bf16[512,512]{1,0:T(8,128)(2,1)S(1)}, bf16[512,512]{1,0:T(8,128)(2,1)S(1)}, u32[]{:S(2)}, u32[]{:S(2)}) collective-permute-start(bf16[512,512]{1,0:T(8,128)(2,1)S(1)} %constant_dynamic-update-slice_fusion.mine_ref), channel_id=1, source_target_pairs={{0,4},{4,0},{8,12},{12,8},{16,20},{20,16},{24,28},{28,24},{32,36},... | collective-permute-start | bytes 1572872 | tf_op jit(solution)/shard_map/ppermute | solution.py:278
  206.6 2.4 collective-permute-start.50
  209.5 10.7 %collective-permute-done.52 = f16[1200,128]{1,0:T(8,128)(2,1)S(1)} collective-permute-done((f16[1200,128]{1,0:T(8,128)(2,1)S(1)}, f16[1200,128]{1,0:T(8,128)(2,1)S(1)}, u32[]{:S(2)}, u32[]{:S(2)}) %collective-permute-start.52) | collective-permute-done | bytes 307232 | tf_op jit(solution)/shard_map/ppermute | solution.py:284
  221.5 3.3 %mix.3.own_ref = f32[4,1168,128]{2,1,0:T(8,128)S(1)} custom-call(f32[1200,128]{1,0:T(8,128)S(1)} %pack.12.own_ref, f32[1200,128]{1,0:T(8,128)S(1)} %convert_element_type.293.got1, f32[1200,128]{1,0:T(8,128)S(1)} %convert_element_type.295.got2, f32[1200,128]{1,0:T(8,128)S(1)} %convert_element_type.297.got3, bf16[512,256]{1,0:T(8,128)(2,1)S(1)} %pad_maximum_fusion.into_ref, ...), custom_call_target="tpu_custom_call" | custom-call | tf_op jit(solution)/shard_map/mix/pallas_call | solution.py:224
  225.3 2.1 collective-permute-start.54
  229.1 3.4 %amplitude.1 = f32[4,1152,128]{2,1,0:T(8,128)} custom-call(s32[1]{0:T(128)} %bitcast.core_ref, bf16[1152,1024]{1,0:T(8,128)(2,1)S(1)} %copy-done.2, bf16[512,512]{1,0:T(8,128)(2,1)S(1)} %constant_dynamic-update-slice_fusion.mine_ref, bf16[512,512]{1,0:T(8,128)(2,1)S(1)} %collective-permute-done.49.other_ref, ...), custom_call_target="tpu_custom_call" | custom-call | tf_op jit(solution)/shard_map/amplitude/pallas_call | solution.py:224
  232.6 6.9 %collective-permute-done.54 = f16[1168,128]{1,0:T(8,128)(2,1)S(1)} collective-permute-done((f16[1168,128]{1,0:T(8,128)(2,1)S(1)}, f16[1168,128]{1,0:T(8,128)(2,1)S(1)}, u32[]{:S(2)}, u32[]{:S(2)}) %collective-permute-start.54) | collective-permute-done | bytes 299040 | tf_op jit(solution)/shard_map/ppermute | solution.py:284
  239.6 2.4 collective-permute-done.55
  242.0 1.9 unpack.3
  (173 shorter events, 91.8 us)
Async XLA Ops:
  14.1 5.7 %collective-permute-start.1 = (bf16[128,512]{1,0:T(8,128)(2,1)S(1)}, bf16[128,512]{1,0:T(8,128)(2,1)S(1)}, u32[]{:S(2)}, u32[]{:S(2)}) collective-permute-start(bf16[128,512]{1,0:T(8,128)(2,1)S(1)} %get-tuple-element.33), channel_id=1, source_target_pairs={{0,16},{4,68},{8,24},{12,76},{16,0},{20,84},{24,8},{28,92},{32,48}... | collective-permute-start | bytes 393224 | tf_op jit(solution)/shard_map/ppermute | solution.py:265
  17.6 5.3 %collective-permute-start.3 = (bf16[128,512]{1,0:T(8,128)(2,1)S(1)}, bf16[128,512]{1,0:T(8,128)(2,1)S(1)}, u32[]{:S(2)}, u32[]{:S(2)}) collective-permute-start(bf16[128,512]{1,0:T(8,128)(2,1)S(1)} %get-tuple-element.34), channel_id=1, source_target_pairs={{0,24},{4,100},{8,16},{12,108},{16,8},{20,116},{24,0},{28,124},{32... | collective-permute-start | bytes 393224 | tf_op jit(solution)/shard_map/ppermute | solution.py:265
  24.0 5.4 %collective-permute-start.4 = (bf16[128,512]{1,0:T(8,128)(2,1)S(1)}, bf16[128,512]{1,0:T(8,128)(2,1)S(1)}, u32[]{:S(2)}, u32[]{:S(2)}) collective-permute-start(bf16[128,512]{1,0:T(8,128)(2,1)S(1)} %add_convert_fusion.7), channel_id=1, source_target_pairs={{0,64},{4,20},{8,72},{12,28},{16,80},{20,4},{24,88},{28,12},{32,96... | collective-permute-start | bytes 393224 | tf_op jit(solution)/shard_map/ppermute | solution.py:269
  26.8 5.0 %collective-permute-start.6 = (bf16[128,512]{1,0:T(8,128)(2,1)S(1)}, bf16[128,512]{1,0:T(8,128)(2,1)S(1)}, u32[]{:S(2)}, u32[]{:S(2)}) collective-permute-start(bf16[128,512]{1,0:T(8,128)(2,1)S(1)} %add_convert_fusion.7), channel_id=1, source_target_pairs={{0,96},{4,28},{8,104},{12,20},{16,112},{20,12},{24,120},{28,4},{32... | collective-permute-start | bytes 393224 | tf_op jit(solution)/shard_map/ppermute | solution.py:269
  32.0 5.4 %collective-permute-start.7 = (bf16[128,512]{1,0:T(8,128)(2,1)S(1)}, bf16[128,512]{1,0:T(8,128)(2,1)S(1)}, u32[]{:S(2)}, u32[]{:S(2)}) collective-permute-start(bf16[128,512]{1,0:T(8,128)(2,1)S(1)} %get-tuple-element.17), channel_id=1, source_target_pairs={{0,16},{4,68},{8,24},{12,76},{16,0},{20,84},{24,8},{28,92},{32,48}... | collective-permute-start | bytes 393224 | tf_op jit(solution)/shard_map/ppermute | solution.py:274
  34.3 5.0 %collective-permute-start.9 = (bf16[128,512]{1,0:T(8,128)(2,1)S(1)}, bf16[128,512]{1,0:T(8,128)(2,1)S(1)}, u32[]{:S(2)}, u32[]{:S(2)}) collective-permute-start(bf16[128,512]{1,0:T(8,128)(2,1)S(1)} %get-tuple-element.17), channel_id=1, source_target_pairs={{0,24},{4,100},{8,16},{12,108},{16,8},{20,116},{24,0},{28,124},{32... | collective-permute-start | bytes 393224 | tf_op jit(solution)/shard_map/ppermute | solution.py:274
  39.4 6.1 %collective-permute-start.10 = (bf16[512,512]{1,0:T(8,128)(2,1)S(1)}, bf16[512,512]{1,0:T(8,128)(2,1)}, u32[]{:S(2)}, u32[]{:S(2)}) collective-permute-start(bf16[512,512]{1,0:T(8,128)(2,1)S(1)} %constant_dynamic-update-slice_fusion.12.mine_ref), channel_id=1, source_target_pairs={{0,4},{4,0},{8,12},{12,8},{16,20},{20,16},{24,28},{28,24},{32,36},... | collective-permute-start | bytes 1572872 | tf_op jit(solution)/shard_map/ppermute | solution.py:278
  54.8 5.7 %collective-permute-start.12 = (bf16[128,512]{1,0:T(8,128)(2,1)S(1)}, bf16[128,512]{1,0:T(8,128)(2,1)S(1)}, u32[]{:S(2)}, u32[]{:S(2)}) collective-permute-start(bf16[128,512]{1,0:T(8,128)(2,1)S(1)} %get-tuple-element.30), channel_id=1, source_target_pairs={{0,16},{4,68},{8,24},{12,76},{16,0},{20,84},{24,8},{28,92},{32,48}... | collective-permute-start | bytes 393224 | tf_op jit(solution)/shard_map/ppermute | solution.py:265
  56.1 5.6 %collective-permute-start.14 = (bf16[128,512]{1,0:T(8,128)(2,1)S(1)}, bf16[128,512]{1,0:T(8,128)(2,1)S(1)}, u32[]{:S(2)}, u32[]{:S(2)}) collective-permute-start(bf16[128,512]{1,0:T(8,128)(2,1)S(1)} %get-tuple-element.31), channel_id=1, source_target_pairs={{0,24},{4,100},{8,16},{12,108},{16,8},{20,116},{24,0},{28,124},{32... | collective-permute-start | bytes 393224 | tf_op jit(solution)/shard_map/ppermute | solution.py:265
  62.4 5.6 %collective-permute-start.15 = (bf16[128,512]{1,0:T(8,128)(2,1)}, bf16[128,512]{1,0:T(8,128)(2,1)}, u32[]{:S(2)}, u32[]{:S(2)}) collective-permute-start(bf16[128,512]{1,0:T(8,128)(2,1)} %add_convert_fusion.5), channel_id=1, source_target_pairs={{0,64},{4,20},{8,72},{12,28},{16,80},{20,4},{24,88},{28,12},{32,96... | collective-permute-start | bytes 393224 | tf_op jit(solution)/shard_map/ppermute | solution.py:269
  63.5 5.8 %collective-permute-start.16 = (bf16[128,512]{1,0:T(8,128)(2,1)}, bf16[128,512]{1,0:T(8,128)(2,1)S(1)}, u32[]{:S(2)}, u32[]{:S(2)}) collective-permute-start(bf16[128,512]{1,0:T(8,128)(2,1)} %add_convert_fusion.5), channel_id=1, source_target_pairs={{0,32},{4,12},{8,40},{12,4},{16,48},{20,28},{24,56},{28,20},{32,0}... | collective-permute-start | bytes 393224 | tf_op jit(solution)/shard_map/ppermute | solution.py:269
  65.3 5.6 %collective-permute-start.17 = (bf16[128,512]{1,0:T(8,128)(2,1)}, bf16[128,512]{1,0:T(8,128)(2,1)}, u32[]{:S(2)}, u32[]{:S(2)}) collective-permute-start(bf16[128,512]{1,0:T(8,128)(2,1)} %add_convert_fusion.5), channel_id=1, source_target_pairs={{0,96},{4,28},{8,104},{12,20},{16,112},{20,12},{24,120},{28,4},{32... | collective-permute-start | bytes 393224 | tf_op jit(solution)/shard_map/ppermute | solution.py:269
  72.9 5.6 %collective-permute-start.18 = (bf16[128,512]{1,0:T(8,128)(2,1)}, bf16[128,512]{1,0:T(8,128)(2,1)}, u32[]{:S(2)}, u32[]{:S(2)}) collective-permute-start(bf16[128,512]{1,0:T(8,128)(2,1)} %get-tuple-element.15), channel_id=1, source_target_pairs={{0,16},{4,68},{8,24},{12,76},{16,0},{20,84},{24,8},{28,92},{32,48}... | collective-permute-start | bytes 393224 | tf_op jit(solution)/shard_map/ppermute | solution.py:274
  73.4 6.0 %collective-permute-start.19 = (bf16[128,512]{1,0:T(8,128)(2,1)}, bf16[128,512]{1,0:T(8,128)(2,1)}, u32[]{:S(2)}, u32[]{:S(2)}) collective-permute-start(bf16[128,512]{1,0:T(8,128)(2,1)} %get-tuple-element.15), channel_id=1, source_target_pairs={{0,8},{4,36},{8,0},{12,44},{16,24},{20,52},{24,16},{28,60},{32,40}... | collective-permute-start | bytes 393224 | tf_op jit(solution)/shard_map/ppermute | solution.py:274
  75.9 5.7 %collective-permute-start.20 = (bf16[128,512]{1,0:T(8,128)(2,1)}, bf16[128,512]{1,0:T(8,128)(2,1)S(1)}, u32[]{:S(2)}, u32[]{:S(2)}) collective-permute-start(bf16[128,512]{1,0:T(8,128)(2,1)} %get-tuple-element.15), channel_id=1, source_target_pairs={{0,24},{4,100},{8,16},{12,108},{16,8},{20,116},{24,0},{28,124},{32... | collective-permute-start | bytes 393224 | tf_op jit(solution)/shard_map/ppermute | solution.py:274
  88.9 18.0 %collective-permute-start.24 = (f16[1200,128]{1,0:T(8,128)(2,1)S(1)}, f16[1200,128]{1,0:T(8,128)(2,1)S(1)}, u32[]{:S(2)}, u32[]{:S(2)}) collective-permute-start(f16[1200,128]{1,0:T(8,128)(2,1)S(1)} %convert_element_type.260), channel_id=1, source_target_pairs={{0,3},{1,2},{2,1},{3,0},{4,7},{5,6},{6,5},{7,4},{8,11},{9,10},{10,... | collective-permute-start | bytes 921608 | tf_op jit(solution)/shard_map/ppermute | solution.py:284
  93.7 13.2 %collective-permute-start.23 = (f16[1200,128]{1,0:T(8,128)(2,1)S(1)}, f16[1200,128]{1,0:T(8,128)(2,1)S(1)}, u32[]{:S(2)}, u32[]{:S(2)}) collective-permute-start(f16[1200,128]{1,0:T(8,128)(2,1)S(1)} %convert_element_type.258), channel_id=1, source_target_pairs={{0,2},{1,3},{2,0},{3,1},{4,6},{5,7},{6,4},{7,5},{8,10},{9,11},{10,... | collective-permute-start | bytes 921608 | tf_op jit(solution)/shard_map/ppermute | solution.py:284
  95.0 13.6 %collective-permute-start.22 = (f16[1200,128]{1,0:T(8,128)(2,1)S(1)}, f16[1200,128]{1,0:T(8,128)(2,1)S(1)}, u32[]{:S(2)}, u32[]{:S(2)}) collective-permute-start(f16[1200,128]{1,0:T(8,128)(2,1)S(1)} %convert_element_type.256), channel_id=1, source_target_pairs={{0,1},{1,0},{2,3},{3,2},{4,5},{5,4},{6,7},{7,6},{8,9},{9,8},{10,11... | collective-permute-start | bytes 921608 | tf_op jit(solution)/shard_map/ppermute | solution.py:284
  114.6 7.5 %collective-permute-start.25 = (f16[1168,128]{1,0:T(8,128)(2,1)S(1)}, f16[1168,128]{1,0:T(8,128)(2,1)S(1)}, u32[]{:S(2)}, u32[]{:S(2)}) collective-permute-start(f16[1168,128]{1,0:T(8,128)(2,1)S(1)} %get-tuple-element.23), channel_id=1, source_target_pairs={{0,1},{1,0},{2,3},{3,2},{4,5},{5,4},{6,7},{7,6},{8,9},{9,8},{10,11... | collective-permute-start | bytes 897032 | tf_op jit(solution)/shard_map/ppermute | solution.py:284
  115.4 14.4 %collective-permute-start.26 = (f16[1168,128]{1,0:T(8,128)(2,1)S(1)}, f16[1168,128]{1,0:T(8,128)(2,1)S(1)}, u32[]{:S(2)}, u32[]{:S(2)}) collective-permute-start(f16[1168,128]{1,0:T(8,128)(2,1)S(1)} %get-tuple-element.22), channel_id=1, source_target_pairs={{0,2},{1,3},{2,0},{3,1},{4,6},{5,7},{6,4},{7,5},{8,10},{9,11},{10,... | collective-permute-start | bytes 897032 | tf_op jit(solution)/shard_map/ppermute | solution.py:284
  117.7 14.6 %collective-permute-start.27 = (f16[1168,128]{1,0:T(8,128)(2,1)S(1)}, f16[1168,128]{1,0:T(8,128)(2,1)S(1)}, u32[]{:S(2)}, u32[]{:S(2)}) collective-permute-start(f16[1168,128]{1,0:T(8,128)(2,1)S(1)} %get-tuple-element.21), channel_id=1, source_target_pairs={{0,3},{1,2},{2,1},{3,0},{4,7},{5,6},{6,5},{7,4},{8,11},{9,10},{10,... | collective-permute-start | bytes 897032 | tf_op jit(solution)/shard_map/ppermute | solution.py:284
  133.8 4.9 %collective-permute-start.28 = (f32[512,512]{1,0:T(8,128)S(1)}, f32[512,512]{1,0:T(8,128)S(1)}, u32[]{:S(2)}, u32[]{:S(2)}) collective-permute-start(f32[512,512]{1,0:T(8,128)S(1)} %fusion.2), channel_id=1, source_target_pairs={{0,4},{4,0},{8,12},{12,8},{16,20},{20,16},{24,28},{28,24},{32,36},... | collective-permute-start | bytes 3145736 | tf_op jit(solution)/shard_map/ppermute | solution.py:258
  139.7 5.7 %collective-permute-start.29 = (bf16[128,512]{1,0:T(8,128)(2,1)S(1)}, bf16[128,512]{1,0:T(8,128)(2,1)S(1)}, u32[]{:S(2)}, u32[]{:S(2)}) collective-permute-start(bf16[128,512]{1,0:T(8,128)(2,1)S(1)} %get-tuple-element.27), channel_id=1, source_target_pairs={{0,16},{4,68},{8,24},{12,76},{16,0},{20,84},{24,8},{28,92},{32,48}... | collective-permute-start | bytes 393224 | tf_op jit(solution)/shard_map/ppermute | solution.py:265
  140.8 5.7 %collective-permute-start.30 = (bf16[128,512]{1,0:T(8,128)(2,1)S(1)}, bf16[128,512]{1,0:T(8,128)(2,1)S(1)}, u32[]{:S(2)}, u32[]{:S(2)}) collective-permute-start(bf16[128,512]{1,0:T(8,128)(2,1)S(1)} %get-tuple-element.29), channel_id=1, source_target_pairs={{0,8},{4,36},{8,0},{12,44},{16,24},{20,52},{24,16},{28,60},{32,40}... | collective-permute-start | bytes 393224 | tf_op jit(solution)/shard_map/ppermute | solution.py:265
  142.4 5.0 %collective-permute-start.31 = (bf16[128,512]{1,0:T(8,128)(2,1)S(1)}, bf16[128,512]{1,0:T(8,128)(2,1)S(1)}, u32[]{:S(2)}, u32[]{:S(2)}) collective-permute-start(bf16[128,512]{1,0:T(8,128)(2,1)S(1)} %get-tuple-element.28), channel_id=1, source_target_pairs={{0,24},{4,100},{8,16},{12,108},{16,8},{20,116},{24,0},{28,124},{32... | collective-permute-start | bytes 393224 | tf_op jit(solution)/shard_map/ppermute | solution.py:265
  147.5 5.4 %collective-permute-start.32 = (bf16[128,512]{1,0:T(8,128)(2,1)S(1)}, bf16[128,512]{1,0:T(8,128)(2,1)S(1)}, u32[]{:S(2)}, u32[]{:S(2)}) collective-permute-start(bf16[128,512]{1,0:T(8,128)(2,1)S(1)} %add_convert_fusion.3), channel_id=1, source_target_pairs={{0,64},{4,20},{8,72},{12,28},{16,80},{20,4},{24,88},{28,12},{32,96... | collective-permute-start | bytes 393224 | tf_op jit(solution)/shard_map/ppermute | solution.py:269
  148.0 6.6 %collective-permute-start.33 = (bf16[128,512]{1,0:T(8,128)(2,1)S(1)}, bf16[128,512]{1,0:T(8,128)(2,1)S(1)}, u32[]{:S(2)}, u32[]{:S(2)}) collective-permute-start(bf16[128,512]{1,0:T(8,128)(2,1)S(1)} %add_convert_fusion.3), channel_id=1, source_target_pairs={{0,32},{4,12},{8,40},{12,4},{16,48},{20,28},{24,56},{28,20},{32,0}... | collective-permute-start | bytes 393224 | tf_op jit(solution)/shard_map/ppermute | solution.py:269
  150.5 5.3 %collective-permute-start.34 = (bf16[128,512]{1,0:T(8,128)(2,1)S(1)}, bf16[128,512]{1,0:T(8,128)(2,1)S(1)}, u32[]{:S(2)}, u32[]{:S(2)}) collective-permute-start(bf16[128,512]{1,0:T(8,128)(2,1)S(1)} %add_convert_fusion.3), channel_id=1, source_target_pairs={{0,96},{4,28},{8,104},{12,20},{16,112},{20,12},{24,120},{28,4},{32... | collective-permute-start | bytes 393224 | tf_op jit(solution)/shard_map/ppermute | solution.py:269
  155.9 5.4 %collective-permute-start.35 = (bf16[128,512]{1,0:T(8,128)(2,1)S(1)}, bf16[128,512]{1,0:T(8,128)(2,1)S(1)}, u32[]{:S(2)}, u32[]{:S(2)}) collective-permute-start(bf16[128,512]{1,0:T(8,128)(2,1)S(1)} %get-tuple-element.13), channel_id=1, source_target_pairs={{0,16},{4,68},{8,24},{12,76},{16,0},{20,84},{24,8},{28,92},{32,48}... | collective-permute-start | bytes 393224 | tf_op jit(solution)/shard_map/ppermute | solution.py:274
  156.1 5.5 %collective-permute-start.36 = (bf16[128,512]{1,0:T(8,128)(2,1)S(1)}, bf16[128,512]{1,0:T(8,128)(2,1)S(1)}, u32[]{:S(2)}, u32[]{:S(2)}) collective-permute-start(bf16[128,512]{1,0:T(8,128)(2,1)S(1)} %get-tuple-element.13), channel_id=1, source_target_pairs={{0,8},{4,36},{8,0},{12,44},{16,24},{20,52},{24,16},{28,60},{32,40}... | collective-permute-start | bytes 393224 | tf_op jit(solution)/shard_map/ppermute | solution.py:274
  157.8 5.0 %collective-permute-start.37 = (bf16[128,512]{1,0:T(8,128)(2,1)S(1)}, bf16[128,512]{1,0:T(8,128)(2,1)S(1)}, u32[]{:S(2)}, u32[]{:S(2)}) collective-permute-start(bf16[128,512]{1,0:T(8,128)(2,1)S(1)} %get-tuple-element.13), channel_id=1, source_target_pairs={{0,24},{4,100},{8,16},{12,108},{16,8},{20,116},{24,0},{28,124},{32... | collective-permute-start | bytes 393224 | tf_op jit(solution)/shard_map/ppermute | solution.py:274
  162.8 6.0 %collective-permute-start.38 = (bf16[512,512]{1,0:T(8,128)(2,1)S(1)}, bf16[512,512]{1,0:T(8,128)(2,1)S(1)}, u32[]{:S(2)}, u32[]{:S(2)}) collective-permute-start(bf16[512,512]{1,0:T(8,128)(2,1)S(1)} %constant_dynamic-update-slice_fusion.4.mine_ref), channel_id=1, source_target_pairs={{0,4},{4,0},{8,12},{12,8},{16,20},{20,16},{24,28},{28,24},{32,36},... | collective-permute-start | bytes 1572872 | tf_op jit(solution)/shard_map/ppermute | solution.py:278
  175.4 5.7 %collective-permute-start.40 = (bf16[128,512]{1,0:T(8,128)(2,1)S(1)}, bf16[128,512]{1,0:T(8,128)(2,1)S(1)}, u32[]{:S(2)}, u32[]{:S(2)}) collective-permute-start(bf16[128,512]{1,0:T(8,128)(2,1)S(1)} %get-tuple-element.24), channel_id=1, source_target_pairs={{0,16},{4,68},{8,24},{12,76},{16,0},{20,84},{24,8},{28,92},{32,48}... | collective-permute-start | bytes 393224 | tf_op jit(solution)/shard_map/ppermute | solution.py:265
  175.5 5.6 %collective-permute-start.41 = (bf16[128,512]{1,0:T(8,128)(2,1)S(1)}, bf16[128,512]{1,0:T(8,128)(2,1)S(1)}, u32[]{:S(2)}, u32[]{:S(2)}) collective-permute-start(bf16[128,512]{1,0:T(8,128)(2,1)S(1)} %get-tuple-element.26), channel_id=1, source_target_pairs={{0,8},{4,36},{8,0},{12,44},{16,24},{20,52},{24,16},{28,60},{32,40}... | collective-permute-start | bytes 393224 | tf_op jit(solution)/shard_map/ppermute | solution.py:265
  176.7 5.5 %collective-permute-start.42 = (bf16[128,512]{1,0:T(8,128)(2,1)S(1)}, bf16[128,512]{1,0:T(8,128)(2,1)S(1)}, u32[]{:S(2)}, u32[]{:S(2)}) collective-permute-start(bf16[128,512]{1,0:T(8,128)(2,1)S(1)} %get-tuple-element.25), channel_id=1, source_target_pairs={{0,24},{4,100},{8,16},{12,108},{16,8},{20,116},{24,0},{28,124},{32... | collective-permute-start | bytes 393224 | tf_op jit(solution)/shard_map/ppermute | solution.py:265
  182.3 5.4 %collective-permute-start.43 = (bf16[128,512]{1,0:T(8,128)(2,1)S(1)}, bf16[128,512]{1,0:T(8,128)(2,1)S(1)}, u32[]{:S(2)}, u32[]{:S(2)}) collective-permute-start(bf16[128,512]{1,0:T(8,128)(2,1)S(1)} %add_convert_fusion.1), channel_id=1, source_target_pairs={{0,64},{4,20},{8,72},{12,28},{16,80},{20,4},{24,88},{28,12},{32,96... | collective-permute-start | bytes 393224 | tf_op jit(solution)/shard_map/ppermute | solution.py:269
  182.7 6.4 %collective-permute-start.44 = (bf16[128,512]{1,0:T(8,128)(2,1)S(1)}, bf16[128,512]{1,0:T(8,128)(2,1)S(1)}, u32[]{:S(2)}, u32[]{:S(2)}) collective-permute-start(bf16[128,512]{1,0:T(8,128)(2,1)S(1)} %add_convert_fusion.1), channel_id=1, source_target_pairs={{0,32},{4,12},{8,40},{12,4},{16,48},{20,28},{24,56},{28,20},{32,0}... | collective-permute-start | bytes 393224 | tf_op jit(solution)/shard_map/ppermute | solution.py:269
  185.3 5.3 %collective-permute-start.45 = (bf16[128,512]{1,0:T(8,128)(2,1)S(1)}, bf16[128,512]{1,0:T(8,128)(2,1)S(1)}, u32[]{:S(2)}, u32[]{:S(2)}) collective-permute-start(bf16[128,512]{1,0:T(8,128)(2,1)S(1)} %add_convert_fusion.1), channel_id=1, source_target_pairs={{0,96},{4,28},{8,104},{12,20},{16,112},{20,12},{24,120},{28,4},{32... | collective-permute-start | bytes 393224 | tf_op jit(solution)/shard_map/ppermute | solution.py:269
  190.8 5.4 %collective-permute-start.46 = (bf16[128,512]{1,0:T(8,128)(2,1)S(1)}, bf16[128,512]{1,0:T(8,128)(2,1)S(1)}, u32[]{:S(2)}, u32[]{:S(2)}) collective-permute-start(bf16[128,512]{1,0:T(8,128)(2,1)S(1)} %get-tuple-element.11), channel_id=1, source_target_pairs={{0,16},{4,68},{8,24},{12,76},{16,0},{20,84},{24,8},{28,92},{32,48}... | collective-permute-start | bytes 393224 | tf_op jit(solution)/shard_map/ppermute | solution.py:274
  190.9 5.8 %collective-permute-start.47 = (bf16[128,512]{1,0:T(8,128)(2,1)S(1)}, bf16[128,512]{1,0:T(8,128)(2,1)S(1)}, u32[]{:S(2)}, u32[]{:S(2)}) collective-permute-start(bf16[128,512]{1,0:T(8,128)(2,1)S(1)} %get-tuple-element.11), channel_id=1, source_target_pairs={{0,8},{4,36},{8,0},{12,44},{16,24},{20,52},{24,16},{28,60},{32,40}... | collective-permute-start | bytes 393224 | tf_op jit(solution)/shard_map/ppermute | solution.py:274
  192.9 5.0 %collective-permute-start.48 = (bf16[128,512]{1,0:T(8,128)(2,1)S(1)}, bf16[128,512]{1,0:T(8,128)(2,1)S(1)}, u32[]{:S(2)}, u32[]{:S(2)}) collective-permute-start(bf16[128,512]{1,0:T(8,128)(2,1)S(1)} %get-tuple-element.11), channel_id=1, source_target_pairs={{0,24},{4,100},{8,16},{12,108},{16,8},{20,116},{24,0},{28,124},{32... | collective-permute-start | bytes 393224 | tf_op jit(solution)/shard_map/ppermute | solution.py:274
  198.0 5.1 %collective-permute-start.49 = (bf16[512,512]{1,0:T(8,128)(2,1)S(1)}, bf16[512,512]{1,0:T(8,128)(2,1)S(1)}, u32[]{:S(2)}, u32[]{:S(2)}) collective-permute-start(bf16[512,512]{1,0:T(8,128)(2,1)S(1)} %constant_dynamic-update-slice_fusion.mine_ref), channel_id=1, source_target_pairs={{0,4},{4,0},{8,12},{12,8},{16,20},{20,16},{24,28},{28,24},{32,36},... | collective-permute-start | bytes 1572872 | tf_op jit(solution)/shard_map/ppermute | solution.py:278
  203.9 16.3 %collective-permute-start.52 = (f16[1200,128]{1,0:T(8,128)(2,1)S(1)}, f16[1200,128]{1,0:T(8,128)(2,1)S(1)}, u32[]{:S(2)}, u32[]{:S(2)}) collective-permute-start(f16[1200,128]{1,0:T(8,128)(2,1)S(1)} %convert_element_type.296), channel_id=1, source_target_pairs={{0,3},{1,2},{2,1},{3,0},{4,7},{5,6},{6,5},{7,4},{8,11},{9,10},{10,... | collective-permute-start | bytes 921608 | tf_op jit(solution)/shard_map/ppermute | solution.py:284
  205.7 14.6 %collective-permute-start.51 = (f16[1200,128]{1,0:T(8,128)(2,1)S(1)}, f16[1200,128]{1,0:T(8,128)(2,1)S(1)}, u32[]{:S(2)}, u32[]{:S(2)}) collective-permute-start(f16[1200,128]{1,0:T(8,128)(2,1)S(1)} %convert_element_type.294), channel_id=1, source_target_pairs={{0,2},{1,3},{2,0},{3,1},{4,6},{5,7},{6,4},{7,5},{8,10},{9,11},{10,... | collective-permute-start | bytes 921608 | tf_op jit(solution)/shard_map/ppermute | solution.py:284
  206.6 14.9 %collective-permute-start.50 = (f16[1200,128]{1,0:T(8,128)(2,1)S(1)}, f16[1200,128]{1,0:T(8,128)(2,1)S(1)}, u32[]{:S(2)}, u32[]{:S(2)}) collective-permute-start(f16[1200,128]{1,0:T(8,128)(2,1)S(1)} %convert_element_type.292), channel_id=1, source_target_pairs={{0,1},{1,0},{2,3},{3,2},{4,5},{5,4},{6,7},{7,6},{8,9},{9,8},{10,11... | collective-permute-start | bytes 921608 | tf_op jit(solution)/shard_map/ppermute | solution.py:284
  225.2 7.4 %collective-permute-start.53 = (f16[1168,128]{1,0:T(8,128)(2,1)S(1)}, f16[1168,128]{1,0:T(8,128)(2,1)S(1)}, u32[]{:S(2)}, u32[]{:S(2)}) collective-permute-start(f16[1168,128]{1,0:T(8,128)(2,1)S(1)} %get-tuple-element.20), channel_id=1, source_target_pairs={{0,1},{1,0},{2,3},{3,2},{4,5},{5,4},{6,7},{7,6},{8,9},{9,8},{10,11... | collective-permute-start | bytes 897032 | tf_op jit(solution)/shard_map/ppermute | solution.py:284
  225.3 14.3 %collective-permute-start.54 = (f16[1168,128]{1,0:T(8,128)(2,1)S(1)}, f16[1168,128]{1,0:T(8,128)(2,1)S(1)}, u32[]{:S(2)}, u32[]{:S(2)}) collective-permute-start(f16[1168,128]{1,0:T(8,128)(2,1)S(1)} %get-tuple-element.19), channel_id=1, source_target_pairs={{0,2},{1,3},{2,0},{3,1},{4,6},{5,7},{6,4},{7,5},{8,10},{9,11},{10,... | collective-permute-start | bytes 897032 | tf_op jit(solution)/shard_map/ppermute | solution.py:284
  227.4 14.6 %collective-permute-start.55 = (f16[1168,128]{1,0:T(8,128)(2,1)S(1)}, f16[1168,128]{1,0:T(8,128)(2,1)S(1)}, u32[]{:S(2)}, u32[]{:S(2)}) collective-permute-start(f16[1168,128]{1,0:T(8,128)(2,1)S(1)} %get-tuple-element.18), channel_id=1, source_target_pairs={{0,3},{1,2},{2,1},{3,0},{4,7},{5,6},{6,5},{7,4},{8,11},{9,10},{10,... | collective-permute-start | bytes 897032 | tf_op jit(solution)/shard_map/ppermute | solution.py:284
  (19 other events, 174.7 us)

commit v7 on v6

--- a/solution.py
+++ b/solution.py
@@ -16,6 +16,7 @@
 RUN = 16
 LANES = 128
 PARTNERS = (2, 1, 3)
+ARRIVALS = (0, 1, 3, 2)
 INTERPRET = False
 
 
@@ -59,6 +60,13 @@
     whole[pl.ds(pl.multiple_of((1 - core) * half, half), half), :] = other_ref[...]
 
 
+def join_body(spot_ref, piece0, piece1, piece3, piece2, out_ref):
+    chunk = piece0.shape[0]
+    for d, piece in enumerate((piece0, piece1, piece2, piece3)):
+        at = pl.ds(pl.multiple_of((spot_ref[0] ^ d) * chunk, chunk), chunk)
+        out_ref[at, :] = piece[...]
+
+
 def ladder_body(core_ref, factors_ref, mine_ref, other_ref, sources_ref, weight_ref,
                 rounded_ref, whole):
     nf, rows, cols = sources_ref.shape
@@ -82,9 +90,9 @@
     nf, rows, cols = sources_ref.shape
     quarter = rows // SIDE
     body = nf * quarter
-    gather_parts(core_ref, mine_ref, other_ref, whole)
     there = z_ref[0] ^ d
     at = pl.ds(pl.multiple_of(there * quarter, RUN), quarter)
+    gather_parts(core_ref, mine_ref, other_ref, whole)
     spread = jnp.dot(factors_ref[at, :], whole[...], preferred_element_type=F32)
     peak = jnp.zeros((RUN, cols), F32)
     for f in range(nf):
@@ -122,7 +130,7 @@
     lax.fori_loop(0, SIDE, step, 0)
 
 
-def mix_body(first, own_ref, got1, got2, got3, into_ref, out_ref, *refs):
+def mix_body(first, own_ref, got1, got3, got2, into_ref, out_ref, *refs):
     if first:
         sent_ref, kernel_ref, turned = refs
     else:
@@ -195,7 +203,7 @@
         sent_ref[d, body:, :] = jnp.broadcast_to(power, (RUN, cols))
 
 
-def unpack_body(z_ref, right_ref, own_ref, got1, got2, got3, sources_ref, *rounded):
+def unpack_body(z_ref, right_ref, own_ref, got1, got3, got2, sources_ref, *rounded):
     nf, rows, cols = right_ref.shape
     quarter = rows // SIDE
     z = z_ref[0]
@@ -221,10 +229,11 @@
 def call(body, outs, name, limit, scalars=0, args=(), scratch=()):
     spec = pl.BlockSpec(memory_space=pltpu.VMEM)
     flat = pl.BlockSpec(memory_space=pltpu.SMEM)
+    specs = [flat] * scalars + [spec] * (len(args) - scalars)
     return pl.pallas_call(
         body,
         out_shape=[jax.ShapeDtypeStruct(s, t) for s, t in outs],
-        in_specs=[flat] * scalars + [spec] * (len(args) - scalars),
+        in_specs=specs,
         out_specs=[spec] * len(outs),
         scratch_shapes=list(scratch),
         compiler_params=pltpu.CompilerParams(vmem_limit_bytes=limit << 20),
@@ -245,6 +254,7 @@
     core = me % 2
     chip = me // 2
     spot = jnp.where(core == 0, chip % SIDE, chip // SIDE)
+    spot_at = jnp.full((1,), spot, jnp.int32)
     factors_keep = lax.dynamic_slice(factors, (0, core * half), (rows, half))
     factors_send = lax.dynamic_slice(factors, (0, (1 - core) * half), (rows, half))
 
@@ -268,13 +278,13 @@
         for d in PARTNERS:
             total = total + lax.ppermute(own, "fac", along(d, False)).astype(F32)
         total = total.astype(BF16)
-        gathered = jnp.zeros((half, wide), BF16)
-        gathered = lax.dynamic_update_slice(gathered, total, (spot * chunk, 0))
+        pieces = {0: total}
         for d in PARTNERS:
-            piece = lax.ppermute(total, "fac", along(d, True))
-            gathered = lax.dynamic_update_slice(
-                gathered, piece, ((spot ^ d) * chunk, 0)
-            )
+            pieces[d] = lax.ppermute(total, "fac", along(d, True))
+        (gathered,) = call(
+            join_body, [((half, wide), BF16)], "join", 4, 1,
+            (spot_at, *[pieces[d] for d in ARRIVALS]),
+        )
         other = lax.ppermute(gathered, "fac", CORES)
         return gathered, other
 
@@ -282,7 +292,7 @@
         got = {}
         for d in PARTNERS:
             got[d] = lax.ppermute(sent[d].astype(F16), "freq", swap(d)).astype(F32)
-        return [got[d] for d in range(1, SIDE)]
+        return [got[d] for d in ARRIVALS[1:]]
 
     body = nf * quarter
     size = SIDE * nf * RUN
@@ -319,14 +329,16 @@
             parts = reduce_all(rounded)
             (rounded,) = call(
                 ladder_body, [((rows, wide), BF16)], "ladder", 10, 1,
-                (core_at, factors, *parts, sources, column), whole,
+                (core_at, factors, *parts, sources, column),
+                whole,
             )
         parts = reduce_all(rounded)
         sent = {}
         for d in (*PARTNERS, 0):
             (value,) = call(
                 partial(pack_body, d), [((body + 3 * RUN, cols), F32)], "pack", 10, 2,
-                (core_at, place_z, factors, *parts, sources, column, kernel), whole,
+                (core_at, place_z, factors, *parts, sources, column, kernel),
+                whole,
             )
             sent[d] = value
         got = exchange(sent)

time: 246 us -> 232 us (0.943)
  local copies, waits for them, and re-layouts: 11.3 us -> 6.9 us
  starting transfers between devices: 77.9 us -> 73.9 us
    ppermute x4, starting transfers between devices: 15.7 us -> 12.2 us  [reduce_all(): other = lax.ppermute(gathered, 'fac', CORES)]
    ppermute x12, waiting for transfers between devices: 19.1 us -> 15.7 us  [reduce_all(): total = total + lax.ppermute(own, 'fac', along(d, False)).astype(F32)]
    ppermute x12, waiting for transfers between devices: 13.9 us -> 16.8 us  [reduce_all(): pieces[d] = lax.ppermute(total, 'fac', along(d, True))]
    unnamed x23 -> x19, local copies, waits for them, and re-layouts: 7.4 us -> 5.08 us
    pallas_call x16 -> x20, Pallas kernels: 25.6 us -> 25.7 us  [call(): pl.pallas_call(body, out_shape=[jax.ShapeDtypeStruct(s, t) for s, t in ou...]
  transfers between devices with their start and end apart: 56 -> 56, of which waited for: 49 -> 47; matrix products, arithmetic and copies ran while one was open for 2% -> 1% of each run, Pallas kernels for 3% -> 3%
where the time goes in v7:
time: 232 us
  waiting for transfers between devices  110 us (47%)
  starting transfers between devices  73.9 us (32%)
  Pallas kernels  25.7 us (11%)
  matrix products  11.5 us (5%)
  local copies, waits for them, and re-layouts  6.9 us (3%)
  other arithmetic  2.63 us (1%)
    ppermute x12, waiting for transfers between devices, exchange(): got[d] = lax.ppermute(sent[d].astype(F16), 'freq', swap(d)).astype(F32)  45.9 us
    pallas_call x20, Pallas kernels, call(): pl.pallas_call(body, out_shape=[jax.ShapeDtypeStruct(s, t) for s, t in ou...  25.7 us
    ppermute x12, waiting for transfers between devices, reduce_all(): own = own + lax.ppermute(piece, 'fac', along(d, True)).astype(F32)  16.9 us
    ppermute x12, waiting for transfers between devices, reduce_all(): pieces[d] = lax.ppermute(total, 'fac', along(d, True))  16.8 us
    ppermute x12, starting transfers between devices, reduce_all(): own = own + lax.ppermute(piece, 'fac', along(d, True)).astype(F32)  16.1 us
    ppermute x12, starting transfers between devices, reduce_all(): total = total + lax.ppermute(own, 'fac', along(d, False)).astype(F32)  15.8 us
    ppermute x12, waiting for transfers between devices, reduce_all(): total = total + lax.ppermute(own, 'fac', along(d, False)).astype(F32)  15.7 us
    ppermute x12, starting transfers between devices, exchange(): got[d] = lax.ppermute(sent[d].astype(F16), 'freq', swap(d)).astype(F32)  15.2 us
  transfers between devices with their start and end apart: 56, of which 47 were waited for; matrix products, arithmetic and copies ran while one was open for 1% of the time, Pallas kernels for 3%

profile of v7, /device:TPU:1, one launch (start us, length us, event | category | flops | bytes accessed | tf_op | source)
XLA Modules:
  0.0 232.0 jit_solution(9748514790093540177)
XLA Ops:
  4.0 1.8 fusion.6
  7.3 2.6 %collective-permute-done = f32[512,512]{1,0:T(8,128)} collective-permute-done((f32[512,512]{1,0:T(8,128)}, f32[512,512]{1,0:T(8,128)}, u32[]{:S(2)}, u32[]{:S(2)}) %collective-permute-start) | collective-permute-done | bytes 1048608 | tf_op jit(solution)/shard_map/ppermute | solution.py:268
  9.9 3.1 %convolution_add_fusion.3 = f32[512,512]{1,0:T(8,128)} fusion(f32[512,512]{1,0:T(8,128)} %collective-permute-done, bf16[1152,512]{1,0:T(8,128)(2,1)S(1)} %round.1, bf16[1152,1024]{1,0:T(8,128)(2,1)S(1)} %copy-done.2, s32[]{:T(128)S(6)} %select_n.105), kind=kOutput, calls=%fused_computation.3 | convolution fusion | flops 604241920 | bytes 4456452 | tf_op jit(solution)/shard_map/dot_general | solution.py:262
  14.1 3.1 %collective-permute-start.1 = (bf16[128,512]{1,0:T(8,128)(2,1)S(1)}, bf16[128,512]{1,0:T(8,128)(2,1)S(1)}, u32[]{:S(2)}, u32[]{:S(2)}) collective-permute-start(bf16[128,512]{1,0:T(8,128)(2,1)S(1)} %get-tuple-element.25), channel_id=1, source_target_pairs={{0,16},{4,68},{8,24},{12,76},{16,0},{20,84},{24,8},{28,92},{32,48}... | collective-permute-start | bytes 393224 | tf_op jit(solution)/shard_map/ppermute | solution.py:275
  18.0 1.9 collective-permute-done.1
  19.9 2.7 %collective-permute-done.3 = bf16[128,512]{1,0:T(8,128)(2,1)S(1)} collective-permute-done((bf16[128,512]{1,0:T(8,128)(2,1)S(1)}, bf16[128,512]{1,0:T(8,128)(2,1)S(1)}, u32[]{:S(2)}, u32[]{:S(2)}) %collective-permute-start.3) | collective-permute-done | bytes 131104 | tf_op jit(solution)/shard_map/ppermute | solution.py:275
  23.6 2.3 collective-permute-start.6
  34.2 2.5 %collective-permute-done.9.piece2 = bf16[128,512]{1,0:T(8,128)(2,1)S(1)} collective-permute-done((bf16[128,512]{1,0:T(8,128)(2,1)S(1)}, bf16[128,512]{1,0:T(8,128)(2,1)S(1)}, u32[]{:S(2)}, u32[]{:S(2)}) %collective-permute-start.9) | collective-permute-done | bytes 131104 | tf_op jit(solution)/shard_map/ppermute | solution.py:283
  38.2 4.6 %collective-permute-start.10 = (bf16[512,512]{1,0:T(8,128)(2,1)S(1)}, bf16[512,512]{1,0:T(8,128)(2,1)}, u32[]{:S(2)}, u32[]{:S(2)}) collective-permute-start(bf16[512,512]{1,0:T(8,128)(2,1)S(1)} %join.4.mine_ref), channel_id=1, source_target_pairs={{0,4},{4,0},{8,12},{12,8},{16,20},{20,16},{24,28},{28,24},{32,36},... | collective-permute-start | bytes 1572872 | tf_op jit(solution)/shard_map/ppermute | solution.py:288
  46.1 3.1 %ladder.2 = bf16[1152,512]{1,0:T(8,128)(2,1)S(1)} custom-call(s32[1]{0:T(128)} %bitcast.core_ref, bf16[1152,1024]{1,0:T(8,128)(2,1)S(1)} %copy-done.2, bf16[512,512]{1,0:T(8,128)(2,1)S(1)} %join.4.mine_ref, bf16[512,512]{1,0:T(8,128)(2,1)} %collective-permute-done.10.other_ref, f32[4,1152,128]{2,1,0:T(8,128)S(1)} %copy-done.4, f32[1152,4]{1,0:T(8,128)S(1)} %bitcast.31), custom_call_target="tpu_custom_call" | custom-call | tf_op jit(solution)/shard_map/ladder/pallas_call | solution.py:233
  50.5 2.3 collective-permute-done.11
  55.1 2.7 %collective-permute-start.14 = (bf16[128,512]{1,0:T(8,128)(2,1)S(1)}, bf16[128,512]{1,0:T(8,128)(2,1)S(1)}, u32[]{:S(2)}, u32[]{:S(2)}) collective-permute-start(bf16[128,512]{1,0:T(8,128)(2,1)S(1)} %get-tuple-element.23), channel_id=1, source_target_pairs={{0,24},{4,100},{8,16},{12,108},{16,8},{20,116},{24,0},{28,124},{32... | collective-permute-start | bytes 393224 | tf_op jit(solution)/shard_map/ppermute | solution.py:275
  62.0 1.8 collective-permute-start.17
  63.9 2.1 collective-permute-start.15
  68.0 2.0 collective-permute-done.15
  73.1 2.5 %collective-permute-done.20.piece2 = bf16[128,512]{1,0:T(8,128)(2,1)S(1)} collective-permute-done((bf16[128,512]{1,0:T(8,128)(2,1)S(1)}, bf16[128,512]{1,0:T(8,128)(2,1)S(1)}, u32[]{:S(2)}, u32[]{:S(2)}) %collective-permute-start.20) | collective-permute-done | bytes 131104 | tf_op jit(solution)/shard_map/ppermute | solution.py:283
  77.3 2.5 %collective-permute-start.21 = (bf16[512,512]{1,0:T(8,128)(2,1)S(1)}, bf16[512,512]{1,0:T(8,128)(2,1)S(1)}, u32[]{:S(2)}, u32[]{:S(2)}) collective-permute-start(bf16[512,512]{1,0:T(8,128)(2,1)S(1)} %join.5.mine_ref), channel_id=1, source_target_pairs={{0,4},{4,0},{8,12},{12,8},{16,20},{20,16},{24,28},{28,24},{32,36},... | collective-permute-start | bytes 1572872 | tf_op jit(solution)/shard_map/ppermute | solution.py:288
  82.1 3.7 %collective-permute-start.24 = (f16[1200,128]{1,0:T(8,128)(2,1)S(1)}, f16[1200,128]{1,0:T(8,128)(2,1)S(1)}, u32[]{:S(2)}, u32[]{:S(2)}) collective-permute-start(f16[1200,128]{1,0:T(8,128)(2,1)S(1)} %convert_element_type.260), channel_id=1, source_target_pairs={{0,2},{1,3},{2,0},{3,1},{4,6},{5,7},{6,4},{7,5},{8,10},{9,11},{10,... | collective-permute-start | bytes 921608 | tf_op jit(solution)/shard_map/ppermute | solution.py:294
  89.5 3.8 %collective-permute-done.24 = f16[1200,128]{1,0:T(8,128)(2,1)S(1)} collective-permute-done((f16[1200,128]{1,0:T(8,128)(2,1)S(1)}, f16[1200,128]{1,0:T(8,128)(2,1)S(1)}, u32[]{:S(2)}, u32[]{:S(2)}) %collective-permute-start.24) | collective-permute-done | bytes 307232 | tf_op jit(solution)/shard_map/ppermute | solution.py:294
  93.3 6.9 %collective-permute-done.23 = f16[1200,128]{1,0:T(8,128)(2,1)S(1)} collective-permute-done((f16[1200,128]{1,0:T(8,128)(2,1)S(1)}, f16[1200,128]{1,0:T(8,128)(2,1)S(1)}, u32[]{:S(2)}, u32[]{:S(2)}) %collective-permute-start.23) | collective-permute-done | bytes 307232 | tf_op jit(solution)/shard_map/ppermute | solution.py:294
  100.3 5.6 %mix.2 = (f32[4,1168,128]{2,1,0:T(8,128)S(1)}, f32[4608,128]{1,0:T(8,128)S(1)}) custom-call(f32[1200,128]{1,0:T(8,128)S(1)} %pack.8.own_ref, f32[1200,128]{1,0:T(8,128)S(1)} %convert_element_type.257.got1, f32[1200,128]{1,0:T(8,128)S(1)} %convert_element_type.259.got3, f32[1200,128]{1,0:T(8,128)S(1)} %convert_element_type.261.got2, ...), custom_call_target="tpu_custom_call" | custom-call | tf_op jit(solution)/shard_map/mix/pallas_call | solution.py:233
  106.2 3.1 %collective-permute-start.27 = (f16[1168,128]{1,0:T(8,128)(2,1)S(1)}, f16[1168,128]{1,0:T(8,128)(2,1)S(1)}, u32[]{:S(2)}, u32[]{:S(2)}) collective-permute-start(f16[1168,128]{1,0:T(8,128)(2,1)S(1)} %get-tuple-element.13), channel_id=1, source_target_pairs={{0,2},{1,3},{2,0},{3,1},{4,6},{5,7},{6,4},{7,5},{8,10},{9,11},{10,... | collective-permute-start | bytes 897032 | tf_op jit(solution)/shard_map/ppermute | solution.py:294
  110.0 5.3 %collective-permute-done.27 = f16[1168,128]{1,0:T(8,128)(2,1)S(1)} collective-permute-done((f16[1168,128]{1,0:T(8,128)(2,1)S(1)}, f16[1168,128]{1,0:T(8,128)(2,1)S(1)}, u32[]{:S(2)}, u32[]{:S(2)}) %collective-permute-start.27) | collective-permute-done | bytes 299040 | tf_op jit(solution)/shard_map/ppermute | solution.py:294
  115.3 7.9 %collective-permute-done.26 = f16[1168,128]{1,0:T(8,128)(2,1)S(1)} collective-permute-done((f16[1168,128]{1,0:T(8,128)(2,1)S(1)}, f16[1168,128]{1,0:T(8,128)(2,1)S(1)}, u32[]{:S(2)}, u32[]{:S(2)}) %collective-permute-start.26) | collective-permute-done | bytes 299040 | tf_op jit(solution)/shard_map/ppermute | solution.py:294
  126.1 2.3 collective-permute-done.28
  129.3 1.9 collective-permute-start.29
  131.2 2.2 collective-permute-start.31
  139.4 2.1 collective-permute-start.32
  143.5 2.1 collective-permute-done.32
  148.4 2.8 %collective-permute-done.37.piece2 = bf16[128,512]{1,0:T(8,128)(2,1)S(1)} collective-permute-done((bf16[128,512]{1,0:T(8,128)(2,1)S(1)}, bf16[128,512]{1,0:T(8,128)(2,1)S(1)}, u32[]{:S(2)}, u32[]{:S(2)}) %collective-permute-start.37) | collective-permute-done | bytes 131104 | tf_op jit(solution)/shard_map/ppermute | solution.py:283
  152.8 2.5 %collective-permute-start.38 = (bf16[512,512]{1,0:T(8,128)(2,1)S(1)}, bf16[512,512]{1,0:T(8,128)(2,1)S(1)}, u32[]{:S(2)}, u32[]{:S(2)}) collective-permute-start(bf16[512,512]{1,0:T(8,128)(2,1)S(1)} %join.6.mine_ref), channel_id=1, source_target_pairs={{0,4},{4,0},{8,12},{12,8},{16,20},{20,16},{24,28},{28,24},{32,36},... | collective-permute-start | bytes 1572872 | tf_op jit(solution)/shard_map/ppermute | solution.py:288
  156.9 2.0 ladder.3
  160.2 2.3 collective-permute-done.39
  163.4 1.9 collective-permute-start.40
  165.4 2.2 collective-permute-start.42
  173.6 2.1 collective-permute-start.43
  177.7 2.1 collective-permute-done.43
  182.5 2.8 %collective-permute-done.48.piece2 = bf16[128,512]{1,0:T(8,128)(2,1)S(1)} collective-permute-done((bf16[128,512]{1,0:T(8,128)(2,1)S(1)}, bf16[128,512]{1,0:T(8,128)(2,1)S(1)}, u32[]{:S(2)}, u32[]{:S(2)}) %collective-permute-start.48) | collective-permute-done | bytes 131104 | tf_op jit(solution)/shard_map/ppermute | solution.py:283
  186.9 2.5 %collective-permute-start.49 = (bf16[512,512]{1,0:T(8,128)(2,1)S(1)}, bf16[512,512]{1,0:T(8,128)(2,1)S(1)}, u32[]{:S(2)}, u32[]{:S(2)}) collective-permute-start(bf16[512,512]{1,0:T(8,128)(2,1)S(1)} %join.7.mine_ref), channel_id=1, source_target_pairs={{0,4},{4,0},{8,12},{12,8},{16,20},{20,16},{24,28},{28,24},{32,36},... | collective-permute-start | bytes 1572872 | tf_op jit(solution)/shard_map/ppermute | solution.py:288
  191.8 1.9 collective-permute-start.52
  197.4 4.5 %collective-permute-done.52 = f16[1200,128]{1,0:T(8,128)(2,1)S(1)} collective-permute-done((f16[1200,128]{1,0:T(8,128)(2,1)S(1)}, f16[1200,128]{1,0:T(8,128)(2,1)S(1)}, u32[]{:S(2)}, u32[]{:S(2)}) %collective-permute-start.52) | collective-permute-done | bytes 307232 | tf_op jit(solution)/shard_map/ppermute | solution.py:294
  202.0 7.2 %collective-permute-done.51 = f16[1200,128]{1,0:T(8,128)(2,1)S(1)} collective-permute-done((f16[1200,128]{1,0:T(8,128)(2,1)S(1)}, f16[1200,128]{1,0:T(8,128)(2,1)S(1)}, u32[]{:S(2)}, u32[]{:S(2)}) %collective-permute-start.51) | collective-permute-done | bytes 307232 | tf_op jit(solution)/shard_map/ppermute | solution.py:294
  209.3 3.3 %mix.3.own_ref = f32[4,1168,128]{2,1,0:T(8,128)S(1)} custom-call(f32[1200,128]{1,0:T(8,128)S(1)} %pack.12.own_ref, f32[1200,128]{1,0:T(8,128)S(1)} %convert_element_type.293.got1, f32[1200,128]{1,0:T(8,128)S(1)} %convert_element_type.295.got3, f32[1200,128]{1,0:T(8,128)S(1)} %convert_element_type.297.got2, bf16[512,256]{1,0:T(8,128)(2,1)S(1)} %pad_maximum_fusion.into_ref, ...), custom_call_target="tpu_custom_call" | custom-call | tf_op jit(solution)/shard_map/mix/pallas_call | solution.py:233
  213.0 1.9 collective-permute-start.55
  216.2 3.4 %amplitude.1 = f32[4,1152,128]{2,1,0:T(8,128)} custom-call(s32[1]{0:T(128)} %bitcast.core_ref, bf16[1152,1024]{1,0:T(8,128)(2,1)S(1)} %copy-done.2, bf16[512,512]{1,0:T(8,128)(2,1)S(1)} %join.7.mine_ref, bf16[512,512]{1,0:T(8,128)(2,1)S(1)} %collective-permute-done.49.other_ref, f32[4,1152,128]{2,1,0:T(8,128)S(1)} %get-tuple-element.8.sources_ref, ...), custom_call_target="tpu_custom_call" | custom-call | tf_op jit(solution)/shard_map/amplitude/pallas_call | solution.py:233
  219.6 3.1 %collective-permute-done.55 = f16[1168,128]{1,0:T(8,128)(2,1)S(1)} collective-permute-done((f16[1168,128]{1,0:T(8,128)(2,1)S(1)}, f16[1168,128]{1,0:T(8,128)(2,1)S(1)}, u32[]{:S(2)}, u32[]{:S(2)}) %collective-permute-start.55) | collective-permute-done | bytes 299040 | tf_op jit(solution)/shard_map/ppermute | solution.py:294
  222.8 7.2 %collective-permute-done.54 = f16[1168,128]{1,0:T(8,128)(2,1)S(1)} collective-permute-done((f16[1168,128]{1,0:T(8,128)(2,1)S(1)}, f16[1168,128]{1,0:T(8,128)(2,1)S(1)}, u32[]{:S(2)}, u32[]{:S(2)}) %collective-permute-start.54) | collective-permute-done | bytes 299040 | tf_op jit(solution)/shard_map/ppermute | solution.py:294
  230.1 1.9 unpack.3
  (157 shorter events, 82.7 us)
Async XLA Ops:
  14.1 5.7 %collective-permute-start.1 = (bf16[128,512]{1,0:T(8,128)(2,1)S(1)}, bf16[128,512]{1,0:T(8,128)(2,1)S(1)}, u32[]{:S(2)}, u32[]{:S(2)}) collective-permute-start(bf16[128,512]{1,0:T(8,128)(2,1)S(1)} %get-tuple-element.25), channel_id=1, source_target_pairs={{0,16},{4,68},{8,24},{12,76},{16,0},{20,84},{24,8},{28,92},{32,48}... | collective-permute-start | bytes 393224 | tf_op jit(solution)/shard_map/ppermute | solution.py:275
  17.2 5.3 %collective-permute-start.3 = (bf16[128,512]{1,0:T(8,128)(2,1)S(1)}, bf16[128,512]{1,0:T(8,128)(2,1)S(1)}, u32[]{:S(2)}, u32[]{:S(2)}) collective-permute-start(bf16[128,512]{1,0:T(8,128)(2,1)S(1)} %get-tuple-element.26), channel_id=1, source_target_pairs={{0,24},{4,100},{8,16},{12,108},{16,8},{20,116},{24,0},{28,124},{32... | collective-permute-start | bytes 393224 | tf_op jit(solution)/shard_map/ppermute | solution.py:275
  18.0 4.5 %collective-permute-start.2 = (bf16[128,512]{1,0:T(8,128)(2,1)S(1)}, bf16[128,512]{1,0:T(8,128)(2,1)S(1)}, u32[]{:S(2)}, u32[]{:S(2)}) collective-permute-start(bf16[128,512]{1,0:T(8,128)(2,1)S(1)} %get-tuple-element.27), channel_id=1, source_target_pairs={{0,8},{4,36},{8,0},{12,44},{16,24},{20,52},{24,16},{28,60},{32,40}... | collective-permute-start | bytes 393224 | tf_op jit(solution)/shard_map/ppermute | solution.py:275
  23.6 5.1 %collective-permute-start.6 = (bf16[128,512]{1,0:T(8,128)(2,1)S(1)}, bf16[128,512]{1,0:T(8,128)(2,1)S(1)}, u32[]{:S(2)}, u32[]{:S(2)}) collective-permute-start(bf16[128,512]{1,0:T(8,128)(2,1)S(1)} %add_convert_fusion.7), channel_id=1, source_target_pairs={{0,96},{4,28},{8,104},{12,20},{16,112},{20,12},{24,120},{28,4},{32... | collective-permute-start | bytes 393224 | tf_op jit(solution)/shard_map/ppermute | solution.py:279
  25.8 4.1 %collective-permute-start.5 = (bf16[128,512]{1,0:T(8,128)(2,1)S(1)}, bf16[128,512]{1,0:T(8,128)(2,1)S(1)}, u32[]{:S(2)}, u32[]{:S(2)}) collective-permute-start(bf16[128,512]{1,0:T(8,128)(2,1)S(1)} %add_convert_fusion.7), channel_id=1, source_target_pairs={{0,32},{4,12},{8,40},{12,4},{16,48},{20,28},{24,56},{28,20},{32,0}... | collective-permute-start | bytes 393224 | tf_op jit(solution)/shard_map/ppermute | solution.py:279
  25.8 5.4 %collective-permute-start.4 = (bf16[128,512]{1,0:T(8,128)(2,1)S(1)}, bf16[128,512]{1,0:T(8,128)(2,1)S(1)}, u32[]{:S(2)}, u32[]{:S(2)}) collective-permute-start(bf16[128,512]{1,0:T(8,128)(2,1)S(1)} %add_convert_fusion.7), channel_id=1, source_target_pairs={{0,64},{4,20},{8,72},{12,28},{16,80},{20,4},{24,88},{28,12},{32,96... | collective-permute-start | bytes 393224 | tf_op jit(solution)/shard_map/ppermute | solution.py:279
  31.3 5.4 %collective-permute-start.9 = (bf16[128,512]{1,0:T(8,128)(2,1)S(1)}, bf16[128,512]{1,0:T(8,128)(2,1)S(1)}, u32[]{:S(2)}, u32[]{:S(2)}) collective-permute-start(bf16[128,512]{1,0:T(8,128)(2,1)S(1)} %add_convert_fusion.6.piece0), channel_id=1, source_target_pairs={{0,16},{4,68},{8,24},{12,76},{16,0},{20,84},{24,8},{28,92},{32,48}... | collective-permute-start | bytes 393224 | tf_op jit(solution)/shard_map/ppermute | solution.py:283
  32.8 5.4 %collective-permute-start.8 = (bf16[128,512]{1,0:T(8,128)(2,1)S(1)}, bf16[128,512]{1,0:T(8,128)(2,1)S(1)}, u32[]{:S(2)}, u32[]{:S(2)}) collective-permute-start(bf16[128,512]{1,0:T(8,128)(2,1)S(1)} %add_convert_fusion.6.piece0), channel_id=1, source_target_pairs={{0,24},{4,100},{8,16},{12,108},{16,8},{20,116},{24,0},{28,124},{32... | collective-permute-start | bytes 393224 | tf_op jit(solution)/shard_map/ppermute | solution.py:283
  38.2 6.2 %collective-permute-start.10 = (bf16[512,512]{1,0:T(8,128)(2,1)S(1)}, bf16[512,512]{1,0:T(8,128)(2,1)}, u32[]{:S(2)}, u32[]{:S(2)}) collective-permute-start(bf16[512,512]{1,0:T(8,128)(2,1)S(1)} %join.4.mine_ref), channel_id=1, source_target_pairs={{0,4},{4,0},{8,12},{12,8},{16,20},{20,16},{24,28},{28,24},{32,36},... | collective-permute-start | bytes 1572872 | tf_op jit(solution)/shard_map/ppermute | solution.py:288
  53.8 5.7 %collective-permute-start.12 = (bf16[128,512]{1,0:T(8,128)(2,1)S(1)}, bf16[128,512]{1,0:T(8,128)(2,1)S(1)}, u32[]{:S(2)}, u32[]{:S(2)}) collective-permute-start(bf16[128,512]{1,0:T(8,128)(2,1)S(1)} %get-tuple-element.22), channel_id=1, source_target_pairs={{0,16},{4,68},{8,24},{12,76},{16,0},{20,84},{24,8},{28,92},{32,48}... | collective-permute-start | bytes 393224 | tf_op jit(solution)/shard_map/ppermute | solution.py:275
  55.1 5.8 %collective-permute-start.14 = (bf16[128,512]{1,0:T(8,128)(2,1)S(1)}, bf16[128,512]{1,0:T(8,128)(2,1)S(1)}, u32[]{:S(2)}, u32[]{:S(2)}) collective-permute-start(bf16[128,512]{1,0:T(8,128)(2,1)S(1)} %get-tuple-element.23), channel_id=1, source_target_pairs={{0,24},{4,100},{8,16},{12,108},{16,8},{20,116},{24,0},{28,124},{32... | collective-permute-start | bytes 393224 | tf_op jit(solution)/shard_map/ppermute | solution.py:275
  57.9 4.1 %collective-permute-start.13 = (bf16[128,512]{1,0:T(8,128)(2,1)S(1)}, bf16[128,512]{1,0:T(8,128)(2,1)S(1)}, u32[]{:S(2)}, u32[]{:S(2)}) collective-permute-start(bf16[128,512]{1,0:T(8,128)(2,1)S(1)} %get-tuple-element.24), channel_id=1, source_target_pairs={{0,8},{4,36},{8,0},{12,44},{16,24},{20,52},{24,16},{28,60},{32,40}... | collective-permute-start | bytes 393224 | tf_op jit(solution)/shard_map/ppermute | solution.py:275
  62.0 5.4 %collective-permute-start.17 = (bf16[128,512]{1,0:T(8,128)(2,1)S(1)}, bf16[128,512]{1,0:T(8,128)(2,1)S(1)}, u32[]{:S(2)}, u32[]{:S(2)}) collective-permute-start(bf16[128,512]{1,0:T(8,128)(2,1)S(1)} %add_convert_fusion.5), channel_id=1, source_target_pairs={{0,96},{4,28},{8,104},{12,20},{16,112},{20,12},{24,120},{28,4},{32... | collective-permute-start | bytes 393224 | tf_op jit(solution)/shard_map/ppermute | solution.py:279
  63.9 4.1 %collective-permute-start.16 = (bf16[128,512]{1,0:T(8,128)(2,1)S(1)}, bf16[128,512]{1,0:T(8,128)(2,1)S(1)}, u32[]{:S(2)}, u32[]{:S(2)}) collective-permute-start(bf16[128,512]{1,0:T(8,128)(2,1)S(1)} %add_convert_fusion.5), channel_id=1, source_target_pairs={{0,32},{4,12},{8,40},{12,4},{16,48},{20,28},{24,56},{28,20},{32,0}... | collective-permute-start | bytes 393224 | tf_op jit(solution)/shard_map/ppermute | solution.py:279
  63.9 6.1 %collective-permute-start.15 = (bf16[128,512]{1,0:T(8,128)(2,1)S(1)}, bf16[128,512]{1,0:T(8,128)(2,1)S(1)}, u32[]{:S(2)}, u32[]{:S(2)}) collective-permute-start(bf16[128,512]{1,0:T(8,128)(2,1)S(1)} %add_convert_fusion.5), channel_id=1, source_target_pairs={{0,64},{4,20},{8,72},{12,28},{16,80},{20,4},{24,88},{28,12},{32,96... | collective-permute-start | bytes 393224 | tf_op jit(solution)/shard_map/ppermute | solution.py:279
  70.1 5.5 %collective-permute-start.20 = (bf16[128,512]{1,0:T(8,128)(2,1)S(1)}, bf16[128,512]{1,0:T(8,128)(2,1)S(1)}, u32[]{:S(2)}, u32[]{:S(2)}) collective-permute-start(bf16[128,512]{1,0:T(8,128)(2,1)S(1)} %add_convert_fusion.4.piece0), channel_id=1, source_target_pairs={{0,16},{4,68},{8,24},{12,76},{16,0},{20,84},{24,8},{28,92},{32,48}... | collective-permute-start | bytes 393224 | tf_op jit(solution)/shard_map/ppermute | solution.py:283
  71.1 6.1 %collective-permute-start.19 = (bf16[128,512]{1,0:T(8,128)(2,1)S(1)}, bf16[128,512]{1,0:T(8,128)(2,1)S(1)}, u32[]{:S(2)}, u32[]{:S(2)}) collective-permute-start(bf16[128,512]{1,0:T(8,128)(2,1)S(1)} %add_convert_fusion.4.piece0), channel_id=1, source_target_pairs={{0,24},{4,100},{8,16},{12,108},{16,8},{20,116},{24,0},{28,124},{32... | collective-permute-start | bytes 393224 | tf_op jit(solution)/shard_map/ppermute | solution.py:283
  72.2 5.0 %collective-permute-start.18 = (bf16[128,512]{1,0:T(8,128)(2,1)S(1)}, bf16[128,512]{1,0:T(8,128)(2,1)S(1)}, u32[]{:S(2)}, u32[]{:S(2)}) collective-permute-start(bf16[128,512]{1,0:T(8,128)(2,1)S(1)} %add_convert_fusion.4.piece0), channel_id=1, source_target_pairs={{0,8},{4,36},{8,0},{12,44},{16,24},{20,52},{24,16},{28,60},{32,40}... | collective-permute-start | bytes 393224 | tf_op jit(solution)/shard_map/ppermute | solution.py:283
  82.1 11.1 %collective-permute-start.24 = (f16[1200,128]{1,0:T(8,128)(2,1)S(1)}, f16[1200,128]{1,0:T(8,128)(2,1)S(1)}, u32[]{:S(2)}, u32[]{:S(2)}) collective-permute-start(f16[1200,128]{1,0:T(8,128)(2,1)S(1)} %convert_element_type.260), channel_id=1, source_target_pairs={{0,2},{1,3},{2,0},{3,1},{4,6},{5,7},{6,4},{7,5},{8,10},{9,11},{10,... | collective-permute-start | bytes 921608 | tf_op jit(solution)/shard_map/ppermute | solution.py:294
  86.6 13.5 %collective-permute-start.23 = (f16[1200,128]{1,0:T(8,128)(2,1)S(1)}, f16[1200,128]{1,0:T(8,128)(2,1)S(1)}, u32[]{:S(2)}, u32[]{:S(2)}) collective-permute-start(f16[1200,128]{1,0:T(8,128)(2,1)S(1)} %convert_element_type.258), channel_id=1, source_target_pairs={{0,3},{1,2},{2,1},{3,0},{4,7},{5,6},{6,5},{7,4},{8,11},{9,10},{10,... | collective-permute-start | bytes 921608 | tf_op jit(solution)/shard_map/ppermute | solution.py:294
  88.1 12.1 %collective-permute-start.22 = (f16[1200,128]{1,0:T(8,128)(2,1)S(1)}, f16[1200,128]{1,0:T(8,128)(2,1)S(1)}, u32[]{:S(2)}, u32[]{:S(2)}) collective-permute-start(f16[1200,128]{1,0:T(8,128)(2,1)S(1)} %convert_element_type.256), channel_id=1, source_target_pairs={{0,1},{1,0},{2,3},{3,2},{4,5},{5,4},{6,7},{7,6},{8,9},{9,8},{10,11... | collective-permute-start | bytes 921608 | tf_op jit(solution)/shard_map/ppermute | solution.py:294
  106.2 9.1 %collective-permute-start.27 = (f16[1168,128]{1,0:T(8,128)(2,1)S(1)}, f16[1168,128]{1,0:T(8,128)(2,1)S(1)}, u32[]{:S(2)}, u32[]{:S(2)}) collective-permute-start(f16[1168,128]{1,0:T(8,128)(2,1)S(1)} %get-tuple-element.13), channel_id=1, source_target_pairs={{0,2},{1,3},{2,0},{3,1},{4,6},{5,7},{6,4},{7,5},{8,10},{9,11},{10,... | collective-permute-start | bytes 897032 | tf_op jit(solution)/shard_map/ppermute | solution.py:294
  109.2 14.0 %collective-permute-start.26 = (f16[1168,128]{1,0:T(8,128)(2,1)S(1)}, f16[1168,128]{1,0:T(8,128)(2,1)S(1)}, u32[]{:S(2)}, u32[]{:S(2)}) collective-permute-start(f16[1168,128]{1,0:T(8,128)(2,1)S(1)} %get-tuple-element.14), channel_id=1, source_target_pairs={{0,3},{1,2},{2,1},{3,0},{4,7},{5,6},{6,5},{7,4},{8,11},{9,10},{10,... | collective-permute-start | bytes 897032 | tf_op jit(solution)/shard_map/ppermute | solution.py:294
  109.6 13.6 %collective-permute-start.25 = (f16[1168,128]{1,0:T(8,128)(2,1)S(1)}, f16[1168,128]{1,0:T(8,128)(2,1)S(1)}, u32[]{:S(2)}, u32[]{:S(2)}) collective-permute-start(f16[1168,128]{1,0:T(8,128)(2,1)S(1)} %get-tuple-element.15), channel_id=1, source_target_pairs={{0,1},{1,0},{2,3},{3,2},{4,5},{5,4},{6,7},{7,6},{8,9},{9,8},{10,11... | collective-permute-start | bytes 897032 | tf_op jit(solution)/shard_map/ppermute | solution.py:294
  129.3 5.7 %collective-permute-start.29 = (bf16[128,512]{1,0:T(8,128)(2,1)S(1)}, bf16[128,512]{1,0:T(8,128)(2,1)S(1)}, u32[]{:S(2)}, u32[]{:S(2)}) collective-permute-start(bf16[128,512]{1,0:T(8,128)(2,1)S(1)} %get-tuple-element.19), channel_id=1, source_target_pairs={{0,16},{4,68},{8,24},{12,76},{16,0},{20,84},{24,8},{28,92},{32,48}... | collective-permute-start | bytes 393224 | tf_op jit(solution)/shard_map/ppermute | solution.py:275
  131.2 5.3 %collective-permute-start.31 = (bf16[128,512]{1,0:T(8,128)(2,1)S(1)}, bf16[128,512]{1,0:T(8,128)(2,1)S(1)}, u32[]{:S(2)}, u32[]{:S(2)}) collective-permute-start(bf16[128,512]{1,0:T(8,128)(2,1)S(1)} %get-tuple-element.20), channel_id=1, source_target_pairs={{0,24},{4,100},{8,16},{12,108},{16,8},{20,116},{24,0},{28,124},{32... | collective-permute-start | bytes 393224 | tf_op jit(solution)/shard_map/ppermute | solution.py:275
  133.4 4.1 %collective-permute-start.30 = (bf16[128,512]{1,0:T(8,128)(2,1)S(1)}, bf16[128,512]{1,0:T(8,128)(2,1)S(1)}, u32[]{:S(2)}, u32[]{:S(2)}) collective-permute-start(bf16[128,512]{1,0:T(8,128)(2,1)S(1)} %get-tuple-element.21), channel_id=1, source_target_pairs={{0,8},{4,36},{8,0},{12,44},{16,24},{20,52},{24,16},{28,60},{32,40}... | collective-permute-start | bytes 393224 | tf_op jit(solution)/shard_map/ppermute | solution.py:275
  137.6 5.4 %collective-permute-start.34 = (bf16[128,512]{1,0:T(8,128)(2,1)S(1)}, bf16[128,512]{1,0:T(8,128)(2,1)S(1)}, u32[]{:S(2)}, u32[]{:S(2)}) collective-permute-start(bf16[128,512]{1,0:T(8,128)(2,1)S(1)} %add_convert_fusion.3), channel_id=1, source_target_pairs={{0,96},{4,28},{8,104},{12,20},{16,112},{20,12},{24,120},{28,4},{32... | collective-permute-start | bytes 393224 | tf_op jit(solution)/shard_map/ppermute | solution.py:279
  139.4 4.1 %collective-permute-start.33 = (bf16[128,512]{1,0:T(8,128)(2,1)S(1)}, bf16[128,512]{1,0:T(8,128)(2,1)S(1)}, u32[]{:S(2)}, u32[]{:S(2)}) collective-permute-start(bf16[128,512]{1,0:T(8,128)(2,1)S(1)} %add_convert_fusion.3), channel_id=1, source_target_pairs={{0,32},{4,12},{8,40},{12,4},{16,48},{20,28},{24,56},{28,20},{32,0}... | collective-permute-start | bytes 393224 | tf_op jit(solution)/shard_map/ppermute | solution.py:279
  139.4 6.2 %collective-permute-start.32 = (bf16[128,512]{1,0:T(8,128)(2,1)S(1)}, bf16[128,512]{1,0:T(8,128)(2,1)S(1)}, u32[]{:S(2)}, u32[]{:S(2)}) collective-permute-start(bf16[128,512]{1,0:T(8,128)(2,1)S(1)} %add_convert_fusion.3), channel_id=1, source_target_pairs={{0,64},{4,20},{8,72},{12,28},{16,80},{20,4},{24,88},{28,12},{32,96... | collective-permute-start | bytes 393224 | tf_op jit(solution)/shard_map/ppermute | solution.py:279
  145.6 5.5 %collective-permute-start.37 = (bf16[128,512]{1,0:T(8,128)(2,1)S(1)}, bf16[128,512]{1,0:T(8,128)(2,1)S(1)}, u32[]{:S(2)}, u32[]{:S(2)}) collective-permute-start(bf16[128,512]{1,0:T(8,128)(2,1)S(1)} %add_convert_fusion.2.piece0), channel_id=1, source_target_pairs={{0,16},{4,68},{8,24},{12,76},{16,0},{20,84},{24,8},{28,92},{32,48}... | collective-permute-start | bytes 393224 | tf_op jit(solution)/shard_map/ppermute | solution.py:283
  146.6 6.1 %collective-permute-start.36 = (bf16[128,512]{1,0:T(8,128)(2,1)S(1)}, bf16[128,512]{1,0:T(8,128)(2,1)S(1)}, u32[]{:S(2)}, u32[]{:S(2)}) collective-permute-start(bf16[128,512]{1,0:T(8,128)(2,1)S(1)} %add_convert_fusion.2.piece0), channel_id=1, source_target_pairs={{0,24},{4,100},{8,16},{12,108},{16,8},{20,116},{24,0},{28,124},{32... | collective-permute-start | bytes 393224 | tf_op jit(solution)/shard_map/ppermute | solution.py:283
  147.8 5.0 %collective-permute-start.35 = (bf16[128,512]{1,0:T(8,128)(2,1)S(1)}, bf16[128,512]{1,0:T(8,128)(2,1)S(1)}, u32[]{:S(2)}, u32[]{:S(2)}) collective-permute-start(bf16[128,512]{1,0:T(8,128)(2,1)S(1)} %add_convert_fusion.2.piece0), channel_id=1, source_target_pairs={{0,8},{4,36},{8,0},{12,44},{16,24},{20,52},{24,16},{28,60},{32,40}... | collective-permute-start | bytes 393224 | tf_op jit(solution)/shard_map/ppermute | solution.py:283
  163.4 5.7 %collective-permute-start.40 = (bf16[128,512]{1,0:T(8,128)(2,1)S(1)}, bf16[128,512]{1,0:T(8,128)(2,1)S(1)}, u32[]{:S(2)}, u32[]{:S(2)}) collective-permute-start(bf16[128,512]{1,0:T(8,128)(2,1)S(1)} %get-tuple-element.16), channel_id=1, source_target_pairs={{0,16},{4,68},{8,24},{12,76},{16,0},{20,84},{24,8},{28,92},{32,48}... | collective-permute-start | bytes 393224 | tf_op jit(solution)/shard_map/ppermute | solution.py:275
  165.4 5.3 %collective-permute-start.42 = (bf16[128,512]{1,0:T(8,128)(2,1)S(1)}, bf16[128,512]{1,0:T(8,128)(2,1)S(1)}, u32[]{:S(2)}, u32[]{:S(2)}) collective-permute-start(bf16[128,512]{1,0:T(8,128)(2,1)S(1)} %get-tuple-element.17), channel_id=1, source_target_pairs={{0,24},{4,100},{8,16},{12,108},{16,8},{20,116},{24,0},{28,124},{32... | collective-permute-start | bytes 393224 | tf_op jit(solution)/shard_map/ppermute | solution.py:275
  167.5 4.1 %collective-permute-start.41 = (bf16[128,512]{1,0:T(8,128)(2,1)S(1)}, bf16[128,512]{1,0:T(8,128)(2,1)S(1)}, u32[]{:S(2)}, u32[]{:S(2)}) collective-permute-start(bf16[128,512]{1,0:T(8,128)(2,1)S(1)} %get-tuple-element.18), channel_id=1, source_target_pairs={{0,8},{4,36},{8,0},{12,44},{16,24},{20,52},{24,16},{28,60},{32,40}... | collective-permute-start | bytes 393224 | tf_op jit(solution)/shard_map/ppermute | solution.py:275
  171.7 5.4 %collective-permute-start.45 = (bf16[128,512]{1,0:T(8,128)(2,1)S(1)}, bf16[128,512]{1,0:T(8,128)(2,1)S(1)}, u32[]{:S(2)}, u32[]{:S(2)}) collective-permute-start(bf16[128,512]{1,0:T(8,128)(2,1)S(1)} %add_convert_fusion.1), channel_id=1, source_target_pairs={{0,96},{4,28},{8,104},{12,20},{16,112},{20,12},{24,120},{28,4},{32... | collective-permute-start | bytes 393224 | tf_op jit(solution)/shard_map/ppermute | solution.py:279
  173.6 4.1 %collective-permute-start.44 = (bf16[128,512]{1,0:T(8,128)(2,1)S(1)}, bf16[128,512]{1,0:T(8,128)(2,1)S(1)}, u32[]{:S(2)}, u32[]{:S(2)}) collective-permute-start(bf16[128,512]{1,0:T(8,128)(2,1)S(1)} %add_convert_fusion.1), channel_id=1, source_target_pairs={{0,32},{4,12},{8,40},{12,4},{16,48},{20,28},{24,56},{28,20},{32,0}... | collective-permute-start | bytes 393224 | tf_op jit(solution)/shard_map/ppermute | solution.py:279
  173.6 6.2 %collective-permute-start.43 = (bf16[128,512]{1,0:T(8,128)(2,1)S(1)}, bf16[128,512]{1,0:T(8,128)(2,1)S(1)}, u32[]{:S(2)}, u32[]{:S(2)}) collective-permute-start(bf16[128,512]{1,0:T(8,128)(2,1)S(1)} %add_convert_fusion.1), channel_id=1, source_target_pairs={{0,64},{4,20},{8,72},{12,28},{16,80},{20,4},{24,88},{28,12},{32,96... | collective-permute-start | bytes 393224 | tf_op jit(solution)/shard_map/ppermute | solution.py:279
  179.8 5.5 %collective-permute-start.48 = (bf16[128,512]{1,0:T(8,128)(2,1)S(1)}, bf16[128,512]{1,0:T(8,128)(2,1)S(1)}, u32[]{:S(2)}, u32[]{:S(2)}) collective-permute-start(bf16[128,512]{1,0:T(8,128)(2,1)S(1)} %add_convert_fusion.piece0), channel_id=1, source_target_pairs={{0,16},{4,68},{8,24},{12,76},{16,0},{20,84},{24,8},{28,92},{32,48}... | collective-permute-start | bytes 393224 | tf_op jit(solution)/shard_map/ppermute | solution.py:283
  180.7 6.1 %collective-permute-start.47 = (bf16[128,512]{1,0:T(8,128)(2,1)S(1)}, bf16[128,512]{1,0:T(8,128)(2,1)S(1)}, u32[]{:S(2)}, u32[]{:S(2)}) collective-permute-start(bf16[128,512]{1,0:T(8,128)(2,1)S(1)} %add_convert_fusion.piece0), channel_id=1, source_target_pairs={{0,24},{4,100},{8,16},{12,108},{16,8},{20,116},{24,0},{28,124},{32... | collective-permute-start | bytes 393224 | tf_op jit(solution)/shard_map/ppermute | solution.py:283
  181.9 5.0 %collective-permute-start.46 = (bf16[128,512]{1,0:T(8,128)(2,1)S(1)}, bf16[128,512]{1,0:T(8,128)(2,1)S(1)}, u32[]{:S(2)}, u32[]{:S(2)}) collective-permute-start(bf16[128,512]{1,0:T(8,128)(2,1)S(1)} %add_convert_fusion.piece0), channel_id=1, source_target_pairs={{0,8},{4,36},{8,0},{12,44},{16,24},{20,52},{24,16},{28,60},{32,40}... | collective-permute-start | bytes 393224 | tf_op jit(solution)/shard_map/ppermute | solution.py:283
  191.8 10.1 %collective-permute-start.52 = (f16[1200,128]{1,0:T(8,128)(2,1)S(1)}, f16[1200,128]{1,0:T(8,128)(2,1)S(1)}, u32[]{:S(2)}, u32[]{:S(2)}) collective-permute-start(f16[1200,128]{1,0:T(8,128)(2,1)S(1)} %convert_element_type.296), channel_id=1, source_target_pairs={{0,2},{1,3},{2,0},{3,1},{4,6},{5,7},{6,4},{7,5},{8,10},{9,11},{10,... | collective-permute-start | bytes 921608 | tf_op jit(solution)/shard_map/ppermute | solution.py:294
  194.5 14.7 %collective-permute-start.51 = (f16[1200,128]{1,0:T(8,128)(2,1)S(1)}, f16[1200,128]{1,0:T(8,128)(2,1)S(1)}, u32[]{:S(2)}, u32[]{:S(2)}) collective-permute-start(f16[1200,128]{1,0:T(8,128)(2,1)S(1)} %convert_element_type.294), channel_id=1, source_target_pairs={{0,3},{1,2},{2,1},{3,0},{4,7},{5,6},{6,5},{7,4},{8,11},{9,10},{10,... | collective-permute-start | bytes 921608 | tf_op jit(solution)/shard_map/ppermute | solution.py:294
  196.7 12.5 %collective-permute-start.50 = (f16[1200,128]{1,0:T(8,128)(2,1)S(1)}, f16[1200,128]{1,0:T(8,128)(2,1)S(1)}, u32[]{:S(2)}, u32[]{:S(2)}) collective-permute-start(f16[1200,128]{1,0:T(8,128)(2,1)S(1)} %convert_element_type.292), channel_id=1, source_target_pairs={{0,1},{1,0},{2,3},{3,2},{4,5},{5,4},{6,7},{7,6},{8,9},{9,8},{10,11... | collective-permute-start | bytes 921608 | tf_op jit(solution)/shard_map/ppermute | solution.py:294
  213.0 9.8 %collective-permute-start.55 = (f16[1168,128]{1,0:T(8,128)(2,1)S(1)}, f16[1168,128]{1,0:T(8,128)(2,1)S(1)}, u32[]{:S(2)}, u32[]{:S(2)}) collective-permute-start(f16[1168,128]{1,0:T(8,128)(2,1)S(1)} %get-tuple-element.10), channel_id=1, source_target_pairs={{0,2},{1,3},{2,0},{3,1},{4,6},{5,7},{6,4},{7,5},{8,10},{9,11},{10,... | collective-permute-start | bytes 897032 | tf_op jit(solution)/shard_map/ppermute | solution.py:294
  214.9 15.1 %collective-permute-start.54 = (f16[1168,128]{1,0:T(8,128)(2,1)S(1)}, f16[1168,128]{1,0:T(8,128)(2,1)S(1)}, u32[]{:S(2)}, u32[]{:S(2)}) collective-permute-start(f16[1168,128]{1,0:T(8,128)(2,1)S(1)} %get-tuple-element.11), channel_id=1, source_target_pairs={{0,3},{1,2},{2,1},{3,0},{4,7},{5,6},{6,5},{7,4},{8,11},{9,10},{10,... | collective-permute-start | bytes 897032 | tf_op jit(solution)/shard_map/ppermute | solution.py:294
  216.2 13.8 %collective-permute-start.53 = (f16[1168,128]{1,0:T(8,128)(2,1)S(1)}, f16[1168,128]{1,0:T(8,128)(2,1)S(1)}, u32[]{:S(2)}, u32[]{:S(2)}) collective-permute-start(f16[1168,128]{1,0:T(8,128)(2,1)S(1)} %get-tuple-element.12), channel_id=1, source_target_pairs={{0,1},{1,0},{2,3},{3,2},{4,5},{5,4},{6,7},{7,6},{8,9},{9,8},{10,11... | collective-permute-start | bytes 897032 | tf_op jit(solution)/shard_map/ppermute | solution.py:294
  (17 other events, 166.9 us)

commit v8 on v7

--- a/solution.py
+++ b/solution.py
@@ -130,36 +130,33 @@
     lax.fori_loop(0, SIDE, step, 0)
 
 
-def mix_body(first, own_ref, got1, got3, got2, into_ref, out_ref, *refs):
-    if first:
-        sent_ref, kernel_ref, turned = refs
-    else:
-        kernel_ref, sent_ref = refs
-    body, cols = own_ref.shape[0] - 3 * RUN, own_ref.shape[1]
+def expand_body(nf, strips, table_ref, kernel_ref, turned):
+    body, cols = kernel_ref.shape
+    table = table_ref[body + RUN : body + 2 * RUN, :] + table_ref[body + 2 * RUN :, :]
+    turned[...] = table.T
+    each = LANES // RUN
+    groups = body // (nf * RUN)
+    for strip in range(strips):
+
+        def step(j, carry, strip=strip):
+            rows = turned[pl.ds(pl.multiple_of(j * RUN, RUN), RUN), :]
+            for f in range(nf):
+                column = rows[:, f * strips + strip : f * strips + strip + 1]
+                spot = ((strip * each + j) * nf + f) * RUN
+                kernel_ref[pl.ds(pl.multiple_of(spot, RUN), RUN), :] = jnp.broadcast_to(column, (RUN, cols))
+            return carry
+
+        lax.fori_loop(0, min(each, groups - strip * each), step, 0)
+
+
+def mix_body(own_ref, got1, got3, got2, into_ref, out_ref, kernel0, kernel1, kernel3, kernel2, sent_ref):
+    body, cols = kernel0.shape
     size = into_ref.shape[1]
     part = size // SIDE
     got = (got1, got2, got3)
-    nf = part // RUN
+    kernel_refs = (kernel0, kernel1, kernel2, kernel3)
     groups = body // part
-    each = LANES // RUN
-    strips = -(-groups // each)
-    if first:
-        for d, ref in enumerate((own_ref, *got)):
-            table = ref[body + RUN : body + 2 * RUN, :] + ref[body + 2 * RUN :, :]
-            turned[d] = table.T
-        for strip in range(strips):
-
-            def expand(j, carry, strip=strip):
-                for d in range(SIDE):
-                    rows = turned[d, pl.ds(pl.multiple_of(j * RUN, RUN), RUN), :]
-                    for f in range(nf):
-                        column = rows[:, f * strips + strip : f * strips + strip + 1]
-                        spot = (strip * each + j) * size + (d * nf + f) * RUN
-                        kernel_ref[pl.ds(pl.multiple_of(spot, RUN), RUN), :] = jnp.broadcast_to(column, (RUN, cols))
-                return carry
-
-            lax.fori_loop(0, min(each, groups - strip * each), expand, 0)
-    wide = 6 if groups % 6 == 0 else 2
+    wide = max(w for w in (2, 4, 6, 9) if groups % w == 0)
     gains = [jnp.exp2(jnp.broadcast_to(g[body : body + 1, :], (part, cols))) for g in got]
 
     def apply(table, value):
@@ -179,9 +176,7 @@
                     [own_ref[at, :]] + [r[at, :] * s for r, s in zip(got, gains)], axis=0
                 )
             )
-            kernels.append(
-                kernel_ref[pl.ds(pl.multiple_of((wide * g + half) * size, size), size), :]
-            )
+            kernels.append(jnp.concatenate([r[at, :] for r in kernel_refs], axis=0))
         timed = apply(into_ref, jnp.concatenate(sides, axis=1))
         renewed = apply(out_ref, jnp.concatenate(kernels, axis=1) * timed)
         fresh = list(peaks)
@@ -275,7 +270,7 @@
             own = own + lax.ppermute(piece, "fac", along(d, True)).astype(F32)
         own = own.astype(BF16)
         total = own.astype(F32)
-        for d in PARTNERS:
+        for d in ARRIVALS[1:]:
             total = total + lax.ppermute(own, "fac", along(d, False)).astype(F32)
         total = total.astype(BF16)
         pieces = {0: total}
@@ -343,18 +338,16 @@
             sent[d] = value
         got = exchange(sent)
         sent = sent[0]
-        mixed = [((SIDE, body + RUN, cols), F32)]
-        tables = (table_in, table_out)
         if outer == 0:
-            sent, spread_kernel = call(
-                partial(mix_body, True), mixed + [((SIDE * body, cols), F32)], "mix", 16, 0,
-                (sent, *got, *tables), [pltpu.VMEM((SIDE, LANES, RUN), F32)],
-            )
-        else:
-            (sent,) = call(
-                partial(mix_body, False), mixed, "mix", 16, 0,
-                (sent, *got, *tables, spread_kernel),
-            )
+            kernels = [
+                call(partial(expand_body, nf, strips), [((body, cols), F32)], "expand", 4, 0,
+                     (block,), [pltpu.VMEM((LANES, RUN), F32)])[0]
+                for block in (sent, *got)
+            ]
+        (sent,) = call(
+            mix_body, [((SIDE, body + RUN, cols), F32)], "mix", 24, 0,
+            (sent, *got, table_in, table_out, *kernels),
+        )
         back = [sent, *exchange(sent)]
         last = outer == OUTER - 1
         if last:

time: 232 us -> 229 us (0.987)
  starting transfers between devices: 73.9 us -> 67.9 us
  Pallas kernels: 25.7 us -> 28.6 us
    ppermute x12, starting transfers between devices: 15.8 us -> 11.6 us  [reduce_all(): total = total + lax.ppermute(own, 'fac', along(d, False)).astype(F32)]
    ppermute x12, starting transfers between devices: 16.1 us -> 12.3 us  [reduce_all(): own = own + lax.ppermute(piece, 'fac', along(d, True)).astype(F32)]
    ppermute x4, starting transfers between devices: 12.2 us -> 15.6 us  [reduce_all(): other = lax.ppermute(gathered, 'fac', CORES)]
    pallas_call x20 -> x24, Pallas kernels: 25.7 us -> 28.6 us  [call(): pl.pallas_call(body, out_shape=[jax.ShapeDtypeStruct(s, t) for s, t in ou...]
  transfers between devices with their start and end apart: 56 -> 56, of which waited for: 47 -> 41; matrix products, arithmetic and copies ran while one was open for 1% -> 1% of each run, Pallas kernels for 3% -> 5%
where the time goes in v8:
time: 229 us; the launch traced here: 228 us
  waiting for transfers between devices  110 us (48%)
  starting transfers between devices  67.9 us (30%)
  Pallas kernels  28.6 us (12%)
  matrix products  11.5 us (5%)
  local copies, waits for them, and re-layouts  6.9 us (3%)
  other arithmetic  2.68 us (1%)
    ppermute x12, waiting for transfers between devices, exchange(): got[d] = lax.ppermute(sent[d].astype(F16), 'freq', swap(d)).astype(F32)  44.3 us
    pallas_call x24, Pallas kernels, call(): pl.pallas_call(body, out_shape=[jax.ShapeDtypeStruct(s, t) for s, t in ou...  28.6 us
    ppermute x12, waiting for transfers between devices, reduce_all(): own = own + lax.ppermute(piece, 'fac', along(d, True)).astype(F32)  17.6 us
    ppermute x12, waiting for transfers between devices, reduce_all(): total = total + lax.ppermute(own, 'fac', along(d, False)).astype(F32)  17.1 us
    ppermute x12, waiting for transfers between devices, reduce_all(): pieces[d] = lax.ppermute(total, 'fac', along(d, True))  15.8 us
    ppermute x4, starting transfers between devices, reduce_all(): other = lax.ppermute(gathered, 'fac', CORES)  15.6 us
    ppermute x12, starting transfers between devices, exchange(): got[d] = lax.ppermute(sent[d].astype(F16), 'freq', swap(d)).astype(F32)  14.2 us
    ppermute x12, starting transfers between devices, reduce_all(): own = own + lax.ppermute(piece, 'fac', along(d, True)).astype(F32)  12.3 us
  transfers between devices with their start and end apart: 56, of which 41 were waited for; matrix products, arithmetic and copies ran while one was open for 1% of the time, Pallas kernels for 5%

profile of v8, /device:TPU:1, one launch (start us, length us, event | category | flops | bytes accessed | tf_op | source)
XLA Modules:
  0.0 228.5 jit_solution(4886656095680875431)
XLA Ops:
  4.0 1.8 fusion.6
  7.3 2.6 %collective-permute-done = f32[512,512]{1,0:T(8,128)} collective-permute-done((f32[512,512]{1,0:T(8,128)}, f32[512,512]{1,0:T(8,128)}, u32[]{:S(2)}, u32[]{:S(2)}) %collective-permute-start) | collective-permute-done | bytes 1048608 | tf_op jit(solution)/shard_map/ppermute | solution.py:263
  9.9 3.1 %convolution_add_fusion.3 = f32[512,512]{1,0:T(8,128)} fusion(f32[512,512]{1,0:T(8,128)} %collective-permute-done, bf16[1152,512]{1,0:T(8,128)(2,1)S(1)} %round.1, bf16[1152,1024]{1,0:T(8,128)(2,1)S(1)} %copy-done.2, s32[]{:T(128)S(6)} %select_n.105), kind=kOutput, calls=%fused_computation.3 | convolution fusion | flops 604241920 | bytes 4456452 | tf_op jit(solution)/shard_map/dot_general | solution.py:257
  14.1 3.1 %collective-permute-start.1 = (bf16[128,512]{1,0:T(8,128)(2,1)S(1)}, bf16[128,512]{1,0:T(8,128)(2,1)S(1)}, u32[]{:S(2)}, u32[]{:S(2)}) collective-permute-start(bf16[128,512]{1,0:T(8,128)(2,1)S(1)} %get-tuple-element.21), channel_id=1, source_target_pairs={{0,16},{4,68},{8,24},{12,76},{16,0},{20,84},{24,8},{28,92},{32,48}... | collective-permute-start | bytes 393224 | tf_op jit(solution)/shard_map/ppermute | solution.py:270
  18.0 1.9 collective-permute-done.1
  19.9 2.7 %collective-permute-done.3 = bf16[128,512]{1,0:T(8,128)(2,1)S(1)} collective-permute-done((bf16[128,512]{1,0:T(8,128)(2,1)S(1)}, bf16[128,512]{1,0:T(8,128)(2,1)S(1)}, u32[]{:S(2)}, u32[]{:S(2)}) %collective-permute-start.3) | collective-permute-done | bytes 131104 | tf_op jit(solution)/shard_map/ppermute | solution.py:270
  23.6 2.5 %collective-permute-start.6 = (bf16[128,512]{1,0:T(8,128)(2,1)S(1)}, bf16[128,512]{1,0:T(8,128)(2,1)S(1)}, u32[]{:S(2)}, u32[]{:S(2)}) collective-permute-start(bf16[128,512]{1,0:T(8,128)(2,1)S(1)} %add_convert_fusion.7), channel_id=1, source_target_pairs={{0,64},{4,20},{8,72},{12,28},{16,80},{20,4},{24,88},{28,12},{32,96... | collective-permute-start | bytes 393224 | tf_op jit(solution)/shard_map/ppermute | solution.py:274
  27.0 2.0 collective-permute-done.6
  29.0 2.2 collective-permute-done.5
  31.2 1.7 collective-permute-start.9
  34.3 2.3 collective-permute-done.9.piece2
  38.2 4.3 %collective-permute-start.10 = (bf16[512,512]{1,0:T(8,128)(2,1)S(1)}, bf16[512,512]{1,0:T(8,128)(2,1)}, u32[]{:S(2)}, u32[]{:S(2)}) collective-permute-start(bf16[512,512]{1,0:T(8,128)(2,1)S(1)} %join.4.mine_ref), channel_id=1, source_target_pairs={{0,4},{4,0},{8,12},{12,8},{16,20},{20,16},{24,28},{28,24},{32,36},... | collective-permute-start | bytes 1572872 | tf_op jit(solution)/shard_map/ppermute | solution.py:283
  45.8 3.0 %ladder.2 = bf16[1152,512]{1,0:T(8,128)(2,1)S(1)} custom-call(s32[1]{0:T(128)} %bitcast.core_ref, bf16[1152,1024]{1,0:T(8,128)(2,1)S(1)} %copy-done.2, bf16[512,512]{1,0:T(8,128)(2,1)S(1)} %join.4.mine_ref, bf16[512,512]{1,0:T(8,128)(2,1)} %collective-permute-done.10.other_ref, f32[4,1152,128]{2,1,0:T(8,128)S(1)} %copy-done.4, f32[1152,4]{1,0:T(8,128)S(1)} %bitcast.31), custom_call_target="tpu_custom_call" | custom-call | tf_op jit(solution)/shard_map/ladder/pallas_call | solution.py:228
  50.2 2.3 %collective-permute-done.11 = f32[512,512]{1,0:T(8,128)S(1)} collective-permute-done((f32[512,512]{1,0:T(8,128)S(1)}, f32[512,512]{1,0:T(8,128)S(1)}, u32[]{:S(2)}, u32[]{:S(2)}) %collective-permute-start.11) | collective-permute-done | bytes 1048608 | tf_op jit(solution)/shard_map/ppermute | solution.py:263
  56.3 3.0 %collective-permute-done.12 = bf16[128,512]{1,0:T(8,128)(2,1)S(1)} collective-permute-done((bf16[128,512]{1,0:T(8,128)(2,1)S(1)}, bf16[128,512]{1,0:T(8,128)(2,1)S(1)}, u32[]{:S(2)}, u32[]{:S(2)}) %collective-permute-start.12) | collective-permute-done | bytes 131104 | tf_op jit(solution)/shard_map/ppermute | solution.py:270
  63.6 2.5 %collective-permute-done.17 = bf16[128,512]{1,0:T(8,128)(2,1)S(1)} collective-permute-done((bf16[128,512]{1,0:T(8,128)(2,1)S(1)}, bf16[128,512]{1,0:T(8,128)(2,1)S(1)}, u32[]{:S(2)}, u32[]{:S(2)}) %collective-permute-start.17) | collective-permute-done | bytes 131104 | tf_op jit(solution)/shard_map/ppermute | solution.py:274
  66.1 1.7 collective-permute-done.16
  70.9 2.5 %collective-permute-done.20.piece2 = bf16[128,512]{1,0:T(8,128)(2,1)S(1)} collective-permute-done((bf16[128,512]{1,0:T(8,128)(2,1)S(1)}, bf16[128,512]{1,0:T(8,128)(2,1)S(1)}, u32[]{:S(2)}, u32[]{:S(2)}) %collective-permute-start.20) | collective-permute-done | bytes 131104 | tf_op jit(solution)/shard_map/ppermute | solution.py:278
  74.7 3.7 %collective-permute-start.21 = (bf16[512,512]{1,0:T(8,128)(2,1)S(1)}, bf16[512,512]{1,0:T(8,128)(2,1)S(1)}, u32[]{:S(2)}, u32[]{:S(2)}) collective-permute-start(bf16[512,512]{1,0:T(8,128)(2,1)S(1)} %join.5.mine_ref), channel_id=1, source_target_pairs={{0,4},{4,0},{8,12},{12,8},{16,20},{20,16},{24,28},{28,24},{32,36},... | collective-permute-start | bytes 1572872 | tf_op jit(solution)/shard_map/ppermute | solution.py:283
  80.7 3.9 %collective-permute-start.24 = (f16[1200,128]{1,0:T(8,128)(2,1)S(1)}, f16[1200,128]{1,0:T(8,128)(2,1)S(1)}, u32[]{:S(2)}, u32[]{:S(2)}) collective-permute-start(f16[1200,128]{1,0:T(8,128)(2,1)S(1)} %convert_element_type.260), channel_id=1, source_target_pairs={{0,2},{1,3},{2,0},{3,1},{4,6},{5,7},{6,4},{7,5},{8,10},{9,11},{10,... | collective-permute-start | bytes 921608 | tf_op jit(solution)/shard_map/ppermute | solution.py:289
  89.5 2.5 %collective-permute-done.24 = f16[1200,128]{1,0:T(8,128)(2,1)S(1)} collective-permute-done((f16[1200,128]{1,0:T(8,128)(2,1)S(1)}, f16[1200,128]{1,0:T(8,128)(2,1)S(1)}, u32[]{:S(2)}, u32[]{:S(2)}) %collective-permute-start.24) | collective-permute-done | bytes 307232 | tf_op jit(solution)/shard_map/ppermute | solution.py:289
  93.4 5.6 %collective-permute-done.22 = f16[1200,128]{1,0:T(8,128)(2,1)S(1)} collective-permute-done((f16[1200,128]{1,0:T(8,128)(2,1)S(1)}, f16[1200,128]{1,0:T(8,128)(2,1)S(1)}, u32[]{:S(2)}, u32[]{:S(2)}) %collective-permute-start.22) | collective-permute-done | bytes 307232 | tf_op jit(solution)/shard_map/ppermute | solution.py:289
  102.0 3.1 %mix.2.own_ref = f32[4,1168,128]{2,1,0:T(8,128)S(1)} custom-call(f32[1200,128]{1,0:T(8,128)S(1)} %pack.8.table_ref.own_ref, f32[1200,128]{1,0:T(8,128)S(1)} %convert_element_type.257.table_ref.got1, f32[1200,128]{1,0:T(8,128)S(1)} %convert_element_type.259.table_ref.got3, f32[1200,128]{1,0:T(8,128)S(1)} %convert_element_type.261.table_ref.got2, ...), custom_call_target="tpu_custom_call" | custom-call | tf_op jit(solution)/shard_map/mix/pallas_call | solution.py:228
  106.8 1.7 collective-permute-start.26
  108.6 5.8 %collective-permute-done.27 = f16[1168,128]{1,0:T(8,128)(2,1)S(1)} collective-permute-done((f16[1168,128]{1,0:T(8,128)(2,1)S(1)}, f16[1168,128]{1,0:T(8,128)(2,1)S(1)}, u32[]{:S(2)}, u32[]{:S(2)}) %collective-permute-start.27) | collective-permute-done | bytes 299040 | tf_op jit(solution)/shard_map/ppermute | solution.py:289
  114.5 7.9 %collective-permute-done.26 = f16[1168,128]{1,0:T(8,128)(2,1)S(1)} collective-permute-done((f16[1168,128]{1,0:T(8,128)(2,1)S(1)}, f16[1168,128]{1,0:T(8,128)(2,1)S(1)}, u32[]{:S(2)}, u32[]{:S(2)}) %collective-permute-start.26) | collective-permute-done | bytes 299040 | tf_op jit(solution)/shard_map/ppermute | solution.py:289
  124.6 2.3 %collective-permute-done.28 = f32[512,512]{1,0:T(8,128)S(1)} collective-permute-done((f32[512,512]{1,0:T(8,128)S(1)}, f32[512,512]{1,0:T(8,128)S(1)}, u32[]{:S(2)}, u32[]{:S(2)}) %collective-permute-start.28) | collective-permute-done | bytes 1048608 | tf_op jit(solution)/shard_map/ppermute | solution.py:263
  127.8 1.8 collective-permute-start.29
  130.6 2.9 %collective-permute-done.29 = bf16[128,512]{1,0:T(8,128)(2,1)S(1)} collective-permute-done((bf16[128,512]{1,0:T(8,128)(2,1)S(1)}, bf16[128,512]{1,0:T(8,128)(2,1)S(1)}, u32[]{:S(2)}, u32[]{:S(2)}) %collective-permute-start.29) | collective-permute-done | bytes 131104 | tf_op jit(solution)/shard_map/ppermute | solution.py:270
  137.8 2.7 %collective-permute-done.34 = bf16[128,512]{1,0:T(8,128)(2,1)S(1)} collective-permute-done((bf16[128,512]{1,0:T(8,128)(2,1)S(1)}, bf16[128,512]{1,0:T(8,128)(2,1)S(1)}, u32[]{:S(2)}, u32[]{:S(2)}) %collective-permute-start.34) | collective-permute-done | bytes 131104 | tf_op jit(solution)/shard_map/ppermute | solution.py:274
  144.9 2.7 %collective-permute-done.37.piece2 = bf16[128,512]{1,0:T(8,128)(2,1)S(1)} collective-permute-done((bf16[128,512]{1,0:T(8,128)(2,1)S(1)}, bf16[128,512]{1,0:T(8,128)(2,1)S(1)}, u32[]{:S(2)}, u32[]{:S(2)}) %collective-permute-start.37) | collective-permute-done | bytes 131104 | tf_op jit(solution)/shard_map/ppermute | solution.py:278
  149.1 4.0 %collective-permute-start.38 = (bf16[512,512]{1,0:T(8,128)(2,1)S(1)}, bf16[512,512]{1,0:T(8,128)(2,1)S(1)}, u32[]{:S(2)}, u32[]{:S(2)}) collective-permute-start(bf16[512,512]{1,0:T(8,128)(2,1)S(1)} %join.6.mine_ref), channel_id=1, source_target_pairs={{0,4},{4,0},{8,12},{12,8},{16,20},{20,16},{24,28},{28,24},{32,36},... | collective-permute-start | bytes 1572872 | tf_op jit(solution)/shard_map/ppermute | solution.py:283
  154.6 2.0 ladder.3
  157.9 2.3 %collective-permute-done.39 = f32[512,512]{1,0:T(8,128)S(1)} collective-permute-done((f32[512,512]{1,0:T(8,128)S(1)}, f32[512,512]{1,0:T(8,128)S(1)}, u32[]{:S(2)}, u32[]{:S(2)}) %collective-permute-start.39) | collective-permute-done | bytes 1048608 | tf_op jit(solution)/shard_map/ppermute | solution.py:263
  161.2 1.7 collective-permute-start.40
  164.1 3.0 %collective-permute-done.40 = bf16[128,512]{1,0:T(8,128)(2,1)S(1)} collective-permute-done((bf16[128,512]{1,0:T(8,128)(2,1)S(1)}, bf16[128,512]{1,0:T(8,128)(2,1)S(1)}, u32[]{:S(2)}, u32[]{:S(2)}) %collective-permute-start.40) | collective-permute-done | bytes 131104 | tf_op jit(solution)/shard_map/ppermute | solution.py:270
  171.3 2.7 %collective-permute-done.45 = bf16[128,512]{1,0:T(8,128)(2,1)S(1)} collective-permute-done((bf16[128,512]{1,0:T(8,128)(2,1)S(1)}, bf16[128,512]{1,0:T(8,128)(2,1)S(1)}, u32[]{:S(2)}, u32[]{:S(2)}) %collective-permute-start.45) | collective-permute-done | bytes 131104 | tf_op jit(solution)/shard_map/ppermute | solution.py:274
  174.0 1.7 collective-permute-done.44
  178.5 2.7 %collective-permute-done.48.piece2 = bf16[128,512]{1,0:T(8,128)(2,1)S(1)} collective-permute-done((bf16[128,512]{1,0:T(8,128)(2,1)S(1)}, bf16[128,512]{1,0:T(8,128)(2,1)S(1)}, u32[]{:S(2)}, u32[]{:S(2)}) %collective-permute-start.48) | collective-permute-done | bytes 131104 | tf_op jit(solution)/shard_map/ppermute | solution.py:278
  182.6 3.7 %collective-permute-start.49 = (bf16[512,512]{1,0:T(8,128)(2,1)S(1)}, bf16[512,512]{1,0:T(8,128)(2,1)S(1)}, u32[]{:S(2)}, u32[]{:S(2)}) collective-permute-start(bf16[512,512]{1,0:T(8,128)(2,1)S(1)} %join.7.mine_ref), channel_id=1, source_target_pairs={{0,4},{4,0},{8,12},{12,8},{16,20},{20,16},{24,28},{28,24},{32,36},... | collective-permute-start | bytes 1572872 | tf_op jit(solution)/shard_map/ppermute | solution.py:283
  190.8 1.7 collective-permute-start.51
  194.0 4.7 %collective-permute-done.52 = f16[1200,128]{1,0:T(8,128)(2,1)S(1)} collective-permute-done((f16[1200,128]{1,0:T(8,128)(2,1)S(1)}, f16[1200,128]{1,0:T(8,128)(2,1)S(1)}, u32[]{:S(2)}, u32[]{:S(2)}) %collective-permute-start.52) | collective-permute-done | bytes 307232 | tf_op jit(solution)/shard_map/ppermute | solution.py:289
  198.8 7.2 %collective-permute-done.51 = f16[1200,128]{1,0:T(8,128)(2,1)S(1)} collective-permute-done((f16[1200,128]{1,0:T(8,128)(2,1)S(1)}, f16[1200,128]{1,0:T(8,128)(2,1)S(1)}, u32[]{:S(2)}, u32[]{:S(2)}) %collective-permute-start.51) | collective-permute-done | bytes 307232 | tf_op jit(solution)/shard_map/ppermute | solution.py:289
  206.1 3.0 %mix.3.own_ref = f32[4,1168,128]{2,1,0:T(8,128)S(1)} custom-call(f32[1200,128]{1,0:T(8,128)S(1)} %pack.12.own_ref, f32[1200,128]{1,0:T(8,128)S(1)} %convert_element_type.293.got1, f32[1200,128]{1,0:T(8,128)S(1)} %convert_element_type.295.got3, f32[1200,128]{1,0:T(8,128)S(1)} %convert_element_type.297.got2, bf16[512,256]{1,0:T(8,128)(2,1)S(1)} %pad_maximum_fusion.into_ref, ...), custom_call_target="tpu_custom_call" | custom-call | tf_op jit(solution)/shard_map/mix/pallas_call | solution.py:228
  212.5 3.4 %amplitude.1 = f32[4,1152,128]{2,1,0:T(8,128)} custom-call(s32[1]{0:T(128)} %bitcast.core_ref, bf16[1152,1024]{1,0:T(8,128)(2,1)S(1)} %copy-done.2, bf16[512,512]{1,0:T(8,128)(2,1)S(1)} %join.7.mine_ref, bf16[512,512]{1,0:T(8,128)(2,1)S(1)} %collective-permute-done.49.other_ref, f32[4,1152,128]{2,1,0:T(8,128)S(1)} %get-tuple-element.5.sources_ref, ...), custom_call_target="tpu_custom_call" | custom-call | tf_op jit(solution)/shard_map/amplitude/pallas_call | solution.py:228
  215.9 3.3 %collective-permute-done.55 = f16[1168,128]{1,0:T(8,128)(2,1)S(1)} collective-permute-done((f16[1168,128]{1,0:T(8,128)(2,1)S(1)}, f16[1168,128]{1,0:T(8,128)(2,1)S(1)}, u32[]{:S(2)}, u32[]{:S(2)}) %collective-permute-start.55) | collective-permute-done | bytes 299040 | tf_op jit(solution)/shard_map/ppermute | solution.py:289
  219.3 7.2 %collective-permute-done.54 = f16[1168,128]{1,0:T(8,128)(2,1)S(1)} collective-permute-done((f16[1168,128]{1,0:T(8,128)(2,1)S(1)}, f16[1168,128]{1,0:T(8,128)(2,1)S(1)}, u32[]{:S(2)}, u32[]{:S(2)}) %collective-permute-start.54) | collective-permute-done | bytes 299040 | tf_op jit(solution)/shard_map/ppermute | solution.py:289
  226.5 1.9 unpack.3
  (161 shorter events, 79.4 us)
Async XLA Ops:
  14.1 5.7 %collective-permute-start.1 = (bf16[128,512]{1,0:T(8,128)(2,1)S(1)}, bf16[128,512]{1,0:T(8,128)(2,1)S(1)}, u32[]{:S(2)}, u32[]{:S(2)}) collective-permute-start(bf16[128,512]{1,0:T(8,128)(2,1)S(1)} %get-tuple-element.21), channel_id=1, source_target_pairs={{0,16},{4,68},{8,24},{12,76},{16,0},{20,84},{24,8},{28,92},{32,48}... | collective-permute-start | bytes 393224 | tf_op jit(solution)/shard_map/ppermute | solution.py:270
  17.2 5.3 %collective-permute-start.3 = (bf16[128,512]{1,0:T(8,128)(2,1)S(1)}, bf16[128,512]{1,0:T(8,128)(2,1)S(1)}, u32[]{:S(2)}, u32[]{:S(2)}) collective-permute-start(bf16[128,512]{1,0:T(8,128)(2,1)S(1)} %get-tuple-element.22), channel_id=1, source_target_pairs={{0,24},{4,100},{8,16},{12,108},{16,8},{20,116},{24,0},{28,124},{32... | collective-permute-start | bytes 393224 | tf_op jit(solution)/shard_map/ppermute | solution.py:270
  18.0 4.5 %collective-permute-start.2 = (bf16[128,512]{1,0:T(8,128)(2,1)S(1)}, bf16[128,512]{1,0:T(8,128)(2,1)S(1)}, u32[]{:S(2)}, u32[]{:S(2)}) collective-permute-start(bf16[128,512]{1,0:T(8,128)(2,1)S(1)} %get-tuple-element.23), channel_id=1, source_target_pairs={{0,8},{4,36},{8,0},{12,44},{16,24},{20,52},{24,16},{28,60},{32,40}... | collective-permute-start | bytes 393224 | tf_op jit(solution)/shard_map/ppermute | solution.py:270
  23.6 5.4 %collective-permute-start.6 = (bf16[128,512]{1,0:T(8,128)(2,1)S(1)}, bf16[128,512]{1,0:T(8,128)(2,1)S(1)}, u32[]{:S(2)}, u32[]{:S(2)}) collective-permute-start(bf16[128,512]{1,0:T(8,128)(2,1)S(1)} %add_convert_fusion.7), channel_id=1, source_target_pairs={{0,64},{4,20},{8,72},{12,28},{16,80},{20,4},{24,88},{28,12},{32,96... | collective-permute-start | bytes 393224 | tf_op jit(solution)/shard_map/ppermute | solution.py:274
  26.1 5.0 %collective-permute-start.5 = (bf16[128,512]{1,0:T(8,128)(2,1)S(1)}, bf16[128,512]{1,0:T(8,128)(2,1)S(1)}, u32[]{:S(2)}, u32[]{:S(2)}) collective-permute-start(bf16[128,512]{1,0:T(8,128)(2,1)S(1)} %add_convert_fusion.7), channel_id=1, source_target_pairs={{0,96},{4,28},{8,104},{12,20},{16,112},{20,12},{24,120},{28,4},{32... | collective-permute-start | bytes 393224 | tf_op jit(solution)/shard_map/ppermute | solution.py:274
  31.2 5.4 %collective-permute-start.9 = (bf16[128,512]{1,0:T(8,128)(2,1)S(1)}, bf16[128,512]{1,0:T(8,128)(2,1)S(1)}, u32[]{:S(2)}, u32[]{:S(2)}) collective-permute-start(bf16[128,512]{1,0:T(8,128)(2,1)S(1)} %add_convert_fusion.6.piece0), channel_id=1, source_target_pairs={{0,16},{4,68},{8,24},{12,76},{16,0},{20,84},{24,8},{28,92},{32,48}... | collective-permute-start | bytes 393224 | tf_op jit(solution)/shard_map/ppermute | solution.py:278
  32.9 5.1 %collective-permute-start.8 = (bf16[128,512]{1,0:T(8,128)(2,1)S(1)}, bf16[128,512]{1,0:T(8,128)(2,1)S(1)}, u32[]{:S(2)}, u32[]{:S(2)}) collective-permute-start(bf16[128,512]{1,0:T(8,128)(2,1)S(1)} %add_convert_fusion.6.piece0), channel_id=1, source_target_pairs={{0,24},{4,100},{8,16},{12,108},{16,8},{20,116},{24,0},{28,124},{32... | collective-permute-start | bytes 393224 | tf_op jit(solution)/shard_map/ppermute | solution.py:278
  38.2 6.0 %collective-permute-start.10 = (bf16[512,512]{1,0:T(8,128)(2,1)S(1)}, bf16[512,512]{1,0:T(8,128)(2,1)}, u32[]{:S(2)}, u32[]{:S(2)}) collective-permute-start(bf16[512,512]{1,0:T(8,128)(2,1)S(1)} %join.4.mine_ref), channel_id=1, source_target_pairs={{0,4},{4,0},{8,12},{12,8},{16,20},{20,16},{24,28},{28,24},{32,36},... | collective-permute-start | bytes 1572872 | tf_op jit(solution)/shard_map/ppermute | solution.py:283
  53.5 5.7 %collective-permute-start.12 = (bf16[128,512]{1,0:T(8,128)(2,1)S(1)}, bf16[128,512]{1,0:T(8,128)(2,1)S(1)}, u32[]{:S(2)}, u32[]{:S(2)}) collective-permute-start(bf16[128,512]{1,0:T(8,128)(2,1)S(1)} %get-tuple-element.18), channel_id=1, source_target_pairs={{0,16},{4,68},{8,24},{12,76},{16,0},{20,84},{24,8},{28,92},{32,48}... | collective-permute-start | bytes 393224 | tf_op jit(solution)/shard_map/ppermute | solution.py:270
  54.9 5.8 %collective-permute-start.14 = (bf16[128,512]{1,0:T(8,128)(2,1)S(1)}, bf16[128,512]{1,0:T(8,128)(2,1)S(1)}, u32[]{:S(2)}, u32[]{:S(2)}) collective-permute-start(bf16[128,512]{1,0:T(8,128)(2,1)S(1)} %get-tuple-element.19), channel_id=1, source_target_pairs={{0,24},{4,100},{8,16},{12,108},{16,8},{20,116},{24,0},{28,124},{32... | collective-permute-start | bytes 393224 | tf_op jit(solution)/shard_map/ppermute | solution.py:270
  55.9 4.7 %collective-permute-start.13 = (bf16[128,512]{1,0:T(8,128)(2,1)S(1)}, bf16[128,512]{1,0:T(8,128)(2,1)S(1)}, u32[]{:S(2)}, u32[]{:S(2)}) collective-permute-start(bf16[128,512]{1,0:T(8,128)(2,1)S(1)} %get-tuple-element.20), channel_id=1, source_target_pairs={{0,8},{4,36},{8,0},{12,44},{16,24},{20,52},{24,16},{28,60},{32,40}... | collective-permute-start | bytes 393224 | tf_op jit(solution)/shard_map/ppermute | solution.py:270
  60.7 5.4 %collective-permute-start.17 = (bf16[128,512]{1,0:T(8,128)(2,1)S(1)}, bf16[128,512]{1,0:T(8,128)(2,1)S(1)}, u32[]{:S(2)}, u32[]{:S(2)}) collective-permute-start(bf16[128,512]{1,0:T(8,128)(2,1)S(1)} %add_convert_fusion.5), channel_id=1, source_target_pairs={{0,64},{4,20},{8,72},{12,28},{16,80},{20,4},{24,88},{28,12},{32,96... | collective-permute-start | bytes 393224 | tf_op jit(solution)/shard_map/ppermute | solution.py:274
  62.3 5.5 %collective-permute-start.16 = (bf16[128,512]{1,0:T(8,128)(2,1)S(1)}, bf16[128,512]{1,0:T(8,128)(2,1)S(1)}, u32[]{:S(2)}, u32[]{:S(2)}) collective-permute-start(bf16[128,512]{1,0:T(8,128)(2,1)S(1)} %add_convert_fusion.5), channel_id=1, source_target_pairs={{0,96},{4,28},{8,104},{12,20},{16,112},{20,12},{24,120},{28,4},{32... | collective-permute-start | bytes 393224 | tf_op jit(solution)/shard_map/ppermute | solution.py:274
  63.2 4.6 %collective-permute-start.15 = (bf16[128,512]{1,0:T(8,128)(2,1)S(1)}, bf16[128,512]{1,0:T(8,128)(2,1)S(1)}, u32[]{:S(2)}, u32[]{:S(2)}) collective-permute-start(bf16[128,512]{1,0:T(8,128)(2,1)S(1)} %add_convert_fusion.5), channel_id=1, source_target_pairs={{0,32},{4,12},{8,40},{12,4},{16,48},{20,28},{24,56},{28,20},{32,0}... | collective-permute-start | bytes 393224 | tf_op jit(solution)/shard_map/ppermute | solution.py:274
  67.9 5.5 %collective-permute-start.20 = (bf16[128,512]{1,0:T(8,128)(2,1)S(1)}, bf16[128,512]{1,0:T(8,128)(2,1)S(1)}, u32[]{:S(2)}, u32[]{:S(2)}) collective-permute-start(bf16[128,512]{1,0:T(8,128)(2,1)S(1)} %add_convert_fusion.4.piece0), channel_id=1, source_target_pairs={{0,16},{4,68},{8,24},{12,76},{16,0},{20,84},{24,8},{28,92},{32,48}... | collective-permute-start | bytes 393224 | tf_op jit(solution)/shard_map/ppermute | solution.py:278
  69.1 5.6 %collective-permute-start.19 = (bf16[128,512]{1,0:T(8,128)(2,1)S(1)}, bf16[128,512]{1,0:T(8,128)(2,1)S(1)}, u32[]{:S(2)}, u32[]{:S(2)}) collective-permute-start(bf16[128,512]{1,0:T(8,128)(2,1)S(1)} %add_convert_fusion.4.piece0), channel_id=1, source_target_pairs={{0,24},{4,100},{8,16},{12,108},{16,8},{20,116},{24,0},{28,124},{32... | collective-permute-start | bytes 393224 | tf_op jit(solution)/shard_map/ppermute | solution.py:278
  70.2 4.5 %collective-permute-start.18 = (bf16[128,512]{1,0:T(8,128)(2,1)S(1)}, bf16[128,512]{1,0:T(8,128)(2,1)S(1)}, u32[]{:S(2)}, u32[]{:S(2)}) collective-permute-start(bf16[128,512]{1,0:T(8,128)(2,1)S(1)} %add_convert_fusion.4.piece0), channel_id=1, source_target_pairs={{0,8},{4,36},{8,0},{12,44},{16,24},{20,52},{24,16},{28,60},{32,40}... | collective-permute-start | bytes 393224 | tf_op jit(solution)/shard_map/ppermute | solution.py:278
  74.7 5.2 %collective-permute-start.21 = (bf16[512,512]{1,0:T(8,128)(2,1)S(1)}, bf16[512,512]{1,0:T(8,128)(2,1)S(1)}, u32[]{:S(2)}, u32[]{:S(2)}) collective-permute-start(bf16[512,512]{1,0:T(8,128)(2,1)S(1)} %join.5.mine_ref), channel_id=1, source_target_pairs={{0,4},{4,0},{8,12},{12,8},{16,20},{20,16},{24,28},{28,24},{32,36},... | collective-permute-start | bytes 1572872 | tf_op jit(solution)/shard_map/ppermute | solution.py:283
  80.7 11.2 %collective-permute-start.24 = (f16[1200,128]{1,0:T(8,128)(2,1)S(1)}, f16[1200,128]{1,0:T(8,128)(2,1)S(1)}, u32[]{:S(2)}, u32[]{:S(2)}) collective-permute-start(f16[1200,128]{1,0:T(8,128)(2,1)S(1)} %convert_element_type.260), channel_id=1, source_target_pairs={{0,2},{1,3},{2,0},{3,1},{4,6},{5,7},{6,4},{7,5},{8,10},{9,11},{10,... | collective-permute-start | bytes 921608 | tf_op jit(solution)/shard_map/ppermute | solution.py:289
  86.2 14.3 %collective-permute-start.23 = (f16[1200,128]{1,0:T(8,128)(2,1)S(1)}, f16[1200,128]{1,0:T(8,128)(2,1)S(1)}, u32[]{:S(2)}, u32[]{:S(2)}) collective-permute-start(f16[1200,128]{1,0:T(8,128)(2,1)S(1)} %convert_element_type.258), channel_id=1, source_target_pairs={{0,3},{1,2},{2,1},{3,0},{4,7},{5,6},{6,5},{7,4},{8,11},{9,10},{10,... | collective-permute-start | bytes 921608 | tf_op jit(solution)/shard_map/ppermute | solution.py:289
  86.7 12.3 %collective-permute-start.22 = (f16[1200,128]{1,0:T(8,128)(2,1)S(1)}, f16[1200,128]{1,0:T(8,128)(2,1)S(1)}, u32[]{:S(2)}, u32[]{:S(2)}) collective-permute-start(f16[1200,128]{1,0:T(8,128)(2,1)S(1)} %convert_element_type.256), channel_id=1, source_target_pairs={{0,1},{1,0},{2,3},{3,2},{4,5},{5,4},{6,7},{7,6},{8,9},{9,8},{10,11... | collective-permute-start | bytes 921608 | tf_op jit(solution)/shard_map/ppermute | solution.py:289
  105.4 9.0 %collective-permute-start.27 = (f16[1168,128]{1,0:T(8,128)(2,1)S(1)}, f16[1168,128]{1,0:T(8,128)(2,1)S(1)}, u32[]{:S(2)}, u32[]{:S(2)}) collective-permute-start(f16[1168,128]{1,0:T(8,128)(2,1)S(1)} %get-tuple-element.9), channel_id=1, source_target_pairs={{0,2},{1,3},{2,0},{3,1},{4,6},{5,7},{6,4},{7,5},{8,10},{9,11},{10,... | collective-permute-start | bytes 897032 | tf_op jit(solution)/shard_map/ppermute | solution.py:289
  106.8 15.6 %collective-permute-start.26 = (f16[1168,128]{1,0:T(8,128)(2,1)S(1)}, f16[1168,128]{1,0:T(8,128)(2,1)S(1)}, u32[]{:S(2)}, u32[]{:S(2)}) collective-permute-start(f16[1168,128]{1,0:T(8,128)(2,1)S(1)} %get-tuple-element.10), channel_id=1, source_target_pairs={{0,3},{1,2},{2,1},{3,0},{4,7},{5,6},{6,5},{7,4},{8,11},{9,10},{10,... | collective-permute-start | bytes 897032 | tf_op jit(solution)/shard_map/ppermute | solution.py:289
  108.6 13.9 %collective-permute-start.25 = (f16[1168,128]{1,0:T(8,128)(2,1)S(1)}, f16[1168,128]{1,0:T(8,128)(2,1)S(1)}, u32[]{:S(2)}, u32[]{:S(2)}) collective-permute-start(f16[1168,128]{1,0:T(8,128)(2,1)S(1)} %get-tuple-element.11), channel_id=1, source_target_pairs={{0,1},{1,0},{2,3},{3,2},{4,5},{5,4},{6,7},{7,6},{8,9},{9,8},{10,11... | collective-permute-start | bytes 897032 | tf_op jit(solution)/shard_map/ppermute | solution.py:289
  127.8 5.7 %collective-permute-start.29 = (bf16[128,512]{1,0:T(8,128)(2,1)S(1)}, bf16[128,512]{1,0:T(8,128)(2,1)S(1)}, u32[]{:S(2)}, u32[]{:S(2)}) collective-permute-start(bf16[128,512]{1,0:T(8,128)(2,1)S(1)} %get-tuple-element.15), channel_id=1, source_target_pairs={{0,16},{4,68},{8,24},{12,76},{16,0},{20,84},{24,8},{28,92},{32,48}... | collective-permute-start | bytes 393224 | tf_op jit(solution)/shard_map/ppermute | solution.py:270
  129.6 5.3 %collective-permute-start.31 = (bf16[128,512]{1,0:T(8,128)(2,1)S(1)}, bf16[128,512]{1,0:T(8,128)(2,1)S(1)}, u32[]{:S(2)}, u32[]{:S(2)}) collective-permute-start(bf16[128,512]{1,0:T(8,128)(2,1)S(1)} %get-tuple-element.16), channel_id=1, source_target_pairs={{0,24},{4,100},{8,16},{12,108},{16,8},{20,116},{24,0},{28,124},{32... | collective-permute-start | bytes 393224 | tf_op jit(solution)/shard_map/ppermute | solution.py:270
  135.0 5.4 %collective-permute-start.34 = (bf16[128,512]{1,0:T(8,128)(2,1)S(1)}, bf16[128,512]{1,0:T(8,128)(2,1)S(1)}, u32[]{:S(2)}, u32[]{:S(2)}) collective-permute-start(bf16[128,512]{1,0:T(8,128)(2,1)S(1)} %add_convert_fusion.3), channel_id=1, source_target_pairs={{0,64},{4,20},{8,72},{12,28},{16,80},{20,4},{24,88},{28,12},{32,96... | collective-permute-start | bytes 393224 | tf_op jit(solution)/shard_map/ppermute | solution.py:274
  136.6 5.5 %collective-permute-start.33 = (bf16[128,512]{1,0:T(8,128)(2,1)S(1)}, bf16[128,512]{1,0:T(8,128)(2,1)S(1)}, u32[]{:S(2)}, u32[]{:S(2)}) collective-permute-start(bf16[128,512]{1,0:T(8,128)(2,1)S(1)} %add_convert_fusion.3), channel_id=1, source_target_pairs={{0,96},{4,28},{8,104},{12,20},{16,112},{20,12},{24,120},{28,4},{32... | collective-permute-start | bytes 393224 | tf_op jit(solution)/shard_map/ppermute | solution.py:274
  137.6 4.6 %collective-permute-start.32 = (bf16[128,512]{1,0:T(8,128)(2,1)S(1)}, bf16[128,512]{1,0:T(8,128)(2,1)S(1)}, u32[]{:S(2)}, u32[]{:S(2)}) collective-permute-start(bf16[128,512]{1,0:T(8,128)(2,1)S(1)} %add_convert_fusion.3), channel_id=1, source_target_pairs={{0,32},{4,12},{8,40},{12,4},{16,48},{20,28},{24,56},{28,20},{32,0}... | collective-permute-start | bytes 393224 | tf_op jit(solution)/shard_map/ppermute | solution.py:274
  142.2 5.4 %collective-permute-start.37 = (bf16[128,512]{1,0:T(8,128)(2,1)S(1)}, bf16[128,512]{1,0:T(8,128)(2,1)S(1)}, u32[]{:S(2)}, u32[]{:S(2)}) collective-permute-start(bf16[128,512]{1,0:T(8,128)(2,1)S(1)} %add_convert_fusion.2.piece0), channel_id=1, source_target_pairs={{0,16},{4,68},{8,24},{12,76},{16,0},{20,84},{24,8},{28,92},{32,48}... | collective-permute-start | bytes 393224 | tf_op jit(solution)/shard_map/ppermute | solution.py:278
  143.7 5.4 %collective-permute-start.36 = (bf16[128,512]{1,0:T(8,128)(2,1)S(1)}, bf16[128,512]{1,0:T(8,128)(2,1)S(1)}, u32[]{:S(2)}, u32[]{:S(2)}) collective-permute-start(bf16[128,512]{1,0:T(8,128)(2,1)S(1)} %add_convert_fusion.2.piece0), channel_id=1, source_target_pairs={{0,24},{4,100},{8,16},{12,108},{16,8},{20,116},{24,0},{28,124},{32... | collective-permute-start | bytes 393224 | tf_op jit(solution)/shard_map/ppermute | solution.py:278
  149.1 5.5 %collective-permute-start.38 = (bf16[512,512]{1,0:T(8,128)(2,1)S(1)}, bf16[512,512]{1,0:T(8,128)(2,1)S(1)}, u32[]{:S(2)}, u32[]{:S(2)}) collective-permute-start(bf16[512,512]{1,0:T(8,128)(2,1)S(1)} %join.6.mine_ref), channel_id=1, source_target_pairs={{0,4},{4,0},{8,12},{12,8},{16,20},{20,16},{24,28},{28,24},{32,36},... | collective-permute-start | bytes 1572872 | tf_op jit(solution)/shard_map/ppermute | solution.py:283
  161.2 5.9 %collective-permute-start.40 = (bf16[128,512]{1,0:T(8,128)(2,1)S(1)}, bf16[128,512]{1,0:T(8,128)(2,1)S(1)}, u32[]{:S(2)}, u32[]{:S(2)}) collective-permute-start(bf16[128,512]{1,0:T(8,128)(2,1)S(1)} %get-tuple-element.12), channel_id=1, source_target_pairs={{0,16},{4,68},{8,24},{12,76},{16,0},{20,84},{24,8},{28,92},{32,48}... | collective-permute-start | bytes 393224 | tf_op jit(solution)/shard_map/ppermute | solution.py:270
  162.9 5.6 %collective-permute-start.42 = (bf16[128,512]{1,0:T(8,128)(2,1)S(1)}, bf16[128,512]{1,0:T(8,128)(2,1)S(1)}, u32[]{:S(2)}, u32[]{:S(2)}) collective-permute-start(bf16[128,512]{1,0:T(8,128)(2,1)S(1)} %get-tuple-element.13), channel_id=1, source_target_pairs={{0,24},{4,100},{8,16},{12,108},{16,8},{20,116},{24,0},{28,124},{32... | collective-permute-start | bytes 393224 | tf_op jit(solution)/shard_map/ppermute | solution.py:270
  163.8 4.7 %collective-permute-start.41 = (bf16[128,512]{1,0:T(8,128)(2,1)S(1)}, bf16[128,512]{1,0:T(8,128)(2,1)S(1)}, u32[]{:S(2)}, u32[]{:S(2)}) collective-permute-start(bf16[128,512]{1,0:T(8,128)(2,1)S(1)} %get-tuple-element.14), channel_id=1, source_target_pairs={{0,8},{4,36},{8,0},{12,44},{16,24},{20,52},{24,16},{28,60},{32,40}... | collective-permute-start | bytes 393224 | tf_op jit(solution)/shard_map/ppermute | solution.py:270
  168.6 5.4 %collective-permute-start.45 = (bf16[128,512]{1,0:T(8,128)(2,1)S(1)}, bf16[128,512]{1,0:T(8,128)(2,1)S(1)}, u32[]{:S(2)}, u32[]{:S(2)}) collective-permute-start(bf16[128,512]{1,0:T(8,128)(2,1)S(1)} %add_convert_fusion.1), channel_id=1, source_target_pairs={{0,64},{4,20},{8,72},{12,28},{16,80},{20,4},{24,88},{28,12},{32,96... | collective-permute-start | bytes 393224 | tf_op jit(solution)/shard_map/ppermute | solution.py:274
  170.1 5.6 %collective-permute-start.44 = (bf16[128,512]{1,0:T(8,128)(2,1)S(1)}, bf16[128,512]{1,0:T(8,128)(2,1)S(1)}, u32[]{:S(2)}, u32[]{:S(2)}) collective-permute-start(bf16[128,512]{1,0:T(8,128)(2,1)S(1)} %add_convert_fusion.1), channel_id=1, source_target_pairs={{0,96},{4,28},{8,104},{12,20},{16,112},{20,12},{24,120},{28,4},{32... | collective-permute-start | bytes 393224 | tf_op jit(solution)/shard_map/ppermute | solution.py:274
  171.0 4.6 %collective-permute-start.43 = (bf16[128,512]{1,0:T(8,128)(2,1)S(1)}, bf16[128,512]{1,0:T(8,128)(2,1)S(1)}, u32[]{:S(2)}, u32[]{:S(2)}) collective-permute-start(bf16[128,512]{1,0:T(8,128)(2,1)S(1)} %add_convert_fusion.1), channel_id=1, source_target_pairs={{0,32},{4,12},{8,40},{12,4},{16,48},{20,28},{24,56},{28,20},{32,0}... | collective-permute-start | bytes 393224 | tf_op jit(solution)/shard_map/ppermute | solution.py:274
  175.7 5.4 %collective-permute-start.48 = (bf16[128,512]{1,0:T(8,128)(2,1)S(1)}, bf16[128,512]{1,0:T(8,128)(2,1)S(1)}, u32[]{:S(2)}, u32[]{:S(2)}) collective-permute-start(bf16[128,512]{1,0:T(8,128)(2,1)S(1)} %add_convert_fusion.piece0), channel_id=1, source_target_pairs={{0,16},{4,68},{8,24},{12,76},{16,0},{20,84},{24,8},{28,92},{32,48}... | collective-permute-start | bytes 393224 | tf_op jit(solution)/shard_map/ppermute | solution.py:278
  177.1 5.4 %collective-permute-start.47 = (bf16[128,512]{1,0:T(8,128)(2,1)S(1)}, bf16[128,512]{1,0:T(8,128)(2,1)S(1)}, u32[]{:S(2)}, u32[]{:S(2)}) collective-permute-start(bf16[128,512]{1,0:T(8,128)(2,1)S(1)} %add_convert_fusion.piece0), channel_id=1, source_target_pairs={{0,24},{4,100},{8,16},{12,108},{16,8},{20,116},{24,0},{28,124},{32... | collective-permute-start | bytes 393224 | tf_op jit(solution)/shard_map/ppermute | solution.py:278
  178.1 4.5 %collective-permute-start.46 = (bf16[128,512]{1,0:T(8,128)(2,1)S(1)}, bf16[128,512]{1,0:T(8,128)(2,1)S(1)}, u32[]{:S(2)}, u32[]{:S(2)}) collective-permute-start(bf16[128,512]{1,0:T(8,128)(2,1)S(1)} %add_convert_fusion.piece0), channel_id=1, source_target_pairs={{0,8},{4,36},{8,0},{12,44},{16,24},{20,52},{24,16},{28,60},{32,40}... | collective-permute-start | bytes 393224 | tf_op jit(solution)/shard_map/ppermute | solution.py:278
  182.6 5.2 %collective-permute-start.49 = (bf16[512,512]{1,0:T(8,128)(2,1)S(1)}, bf16[512,512]{1,0:T(8,128)(2,1)S(1)}, u32[]{:S(2)}, u32[]{:S(2)}) collective-permute-start(bf16[512,512]{1,0:T(8,128)(2,1)S(1)} %join.7.mine_ref), channel_id=1, source_target_pairs={{0,4},{4,0},{8,12},{12,8},{16,20},{20,16},{24,28},{28,24},{32,36},... | collective-permute-start | bytes 1572872 | tf_op jit(solution)/shard_map/ppermute | solution.py:283
  188.6 10.1 %collective-permute-start.52 = (f16[1200,128]{1,0:T(8,128)(2,1)S(1)}, f16[1200,128]{1,0:T(8,128)(2,1)S(1)}, u32[]{:S(2)}, u32[]{:S(2)}) collective-permute-start(f16[1200,128]{1,0:T(8,128)(2,1)S(1)} %convert_element_type.296), channel_id=1, source_target_pairs={{0,2},{1,3},{2,0},{3,1},{4,6},{5,7},{6,4},{7,5},{8,10},{9,11},{10,... | collective-permute-start | bytes 921608 | tf_op jit(solution)/shard_map/ppermute | solution.py:289
  190.8 15.1 %collective-permute-start.51 = (f16[1200,128]{1,0:T(8,128)(2,1)S(1)}, f16[1200,128]{1,0:T(8,128)(2,1)S(1)}, u32[]{:S(2)}, u32[]{:S(2)}) collective-permute-start(f16[1200,128]{1,0:T(8,128)(2,1)S(1)} %convert_element_type.294), channel_id=1, source_target_pairs={{0,3},{1,2},{2,1},{3,0},{4,7},{5,6},{6,5},{7,4},{8,11},{9,10},{10,... | collective-permute-start | bytes 921608 | tf_op jit(solution)/shard_map/ppermute | solution.py:289
  193.3 12.7 %collective-permute-start.50 = (f16[1200,128]{1,0:T(8,128)(2,1)S(1)}, f16[1200,128]{1,0:T(8,128)(2,1)S(1)}, u32[]{:S(2)}, u32[]{:S(2)}) collective-permute-start(f16[1200,128]{1,0:T(8,128)(2,1)S(1)} %convert_element_type.292), channel_id=1, source_target_pairs={{0,1},{1,0},{2,3},{3,2},{4,5},{5,4},{6,7},{7,6},{8,9},{9,8},{10,11... | collective-permute-start | bytes 921608 | tf_op jit(solution)/shard_map/ppermute | solution.py:289
  209.4 9.8 %collective-permute-start.55 = (f16[1168,128]{1,0:T(8,128)(2,1)S(1)}, f16[1168,128]{1,0:T(8,128)(2,1)S(1)}, u32[]{:S(2)}, u32[]{:S(2)}) collective-permute-start(f16[1168,128]{1,0:T(8,128)(2,1)S(1)} %get-tuple-element.6), channel_id=1, source_target_pairs={{0,2},{1,3},{2,0},{3,1},{4,6},{5,7},{6,4},{7,5},{8,10},{9,11},{10,... | collective-permute-start | bytes 897032 | tf_op jit(solution)/shard_map/ppermute | solution.py:289
  210.9 15.6 %collective-permute-start.54 = (f16[1168,128]{1,0:T(8,128)(2,1)S(1)}, f16[1168,128]{1,0:T(8,128)(2,1)S(1)}, u32[]{:S(2)}, u32[]{:S(2)}) collective-permute-start(f16[1168,128]{1,0:T(8,128)(2,1)S(1)} %get-tuple-element.7), channel_id=1, source_target_pairs={{0,3},{1,2},{2,1},{3,0},{4,7},{5,6},{6,5},{7,4},{8,11},{9,10},{10,... | collective-permute-start | bytes 897032 | tf_op jit(solution)/shard_map/ppermute | solution.py:289
  212.5 14.0 %collective-permute-start.53 = (f16[1168,128]{1,0:T(8,128)(2,1)S(1)}, f16[1168,128]{1,0:T(8,128)(2,1)S(1)}, u32[]{:S(2)}, u32[]{:S(2)}) collective-permute-start(f16[1168,128]{1,0:T(8,128)(2,1)S(1)} %get-tuple-element.8), channel_id=1, source_target_pairs={{0,1},{1,0},{2,3},{3,2},{4,5},{5,4},{6,7},{7,6},{8,9},{9,8},{10,11... | collective-permute-start | bytes 897032 | tf_op jit(solution)/shard_map/ppermute | solution.py:289
  (17 other events, 163.5 us)

commit v9 on v8

--- a/solution.py
+++ b/solution.py
@@ -259,9 +259,9 @@
         )
 
     def reduce_all(rounded):
-        sent = project(factors_send, rounded)
+        sent = project(factors_send, rounded).astype(BF16)
         got = lax.ppermute(sent, "fac", CORES)
-        mine = project(factors_keep, rounded) + got
+        mine = project(factors_keep, rounded) + got.astype(F32)
         own = lax.dynamic_slice(mine, (spot * chunk, 0), (chunk, wide))
         for d in PARTNERS:
             piece = lax.dynamic_slice(

time: 229 us -> 225 us (0.983)
  waiting for transfers between devices: 110 us -> 107 us
    ppermute x4, waiting for transfers between devices: 9.5 us -> 6.5 us  [reduce_all(): got = lax.ppermute(sent, 'fac', CORES)]
where the time goes in v9:
time: 225 us
  waiting for transfers between devices  107 us (48%)
  starting transfers between devices  67.9 us (30%)
  Pallas kernels  28.5 us (13%)
  matrix products  11.1 us (5%)
  local copies, waits for them, and re-layouts  6.9 us (3%)
  other arithmetic  2.68 us (1%)
    ppermute x12, waiting for transfers between devices, exchange(): got[d] = lax.ppermute(sent[d].astype(F16), 'freq', swap(d)).astype(F32)  44.3 us
    pallas_call x24, Pallas kernels, call(): pl.pallas_call(body, out_shape=[jax.ShapeDtypeStruct(s, t) for s, t in ou...  28.5 us
    ppermute x12, waiting for transfers between devices, reduce_all(): own = own + lax.ppermute(piece, 'fac', along(d, True)).astype(F32)  17.7 us
    ppermute x12, waiting for transfers between devices, reduce_all(): total = total + lax.ppermute(own, 'fac', along(d, False)).astype(F32)  17.1 us
    ppermute x12, waiting for transfers between devices, reduce_all(): pieces[d] = lax.ppermute(total, 'fac', along(d, True))  15.8 us
    ppermute x4, starting transfers between devices, reduce_all(): other = lax.ppermute(gathered, 'fac', CORES)  15.6 us
    ppermute x12, starting transfers between devices, exchange(): got[d] = lax.ppermute(sent[d].astype(F16), 'freq', swap(d)).astype(F32)  14.2 us
    ppermute x12, starting transfers between devices, reduce_all(): own = own + lax.ppermute(piece, 'fac', along(d, True)).astype(F32)  12.3 us
  transfers between devices with their start and end apart: 56, of which 41 were waited for; matrix products, arithmetic and copies ran while one was open for 1% of the time, Pallas kernels for 5%

profile of v9, /device:TPU:1, one launch (start us, length us, event | category | flops | bytes accessed | tf_op | source)
XLA Modules:
  0.0 225.1 jit_solution(3524576435088793018)
XLA Ops:
  0.7 1.7 copy-done.3
  4.0 1.7 convolution_convert_fusion.3
  7.1 1.9 collective-permute-done
  9.0 2.9 %convert_add_fusion = f32[512,512]{1,0:T(8,128)} fusion(bf16[512,512]{1,0:T(8,128)(2,1)} %collective-permute-done, bf16[1152,512]{1,0:T(8,128)(2,1)S(1)} %round.1, bf16[1152,1024]{1,0:T(8,128)(2,1)S(1)} %copy-done.2, s32[]{:T(128)S(6)} %select_n.105), kind=kOutput, calls=%fused_computation.9 | convolution fusion | flops 604504064 | bytes 3932164 | tf_op jit(solution)/shard_map/dot_general | solution.py:257
  13.0 3.1 %collective-permute-start.1 = (bf16[128,512]{1,0:T(8,128)(2,1)S(1)}, bf16[128,512]{1,0:T(8,128)(2,1)S(1)}, u32[]{:S(2)}, u32[]{:S(2)}) collective-permute-start(bf16[128,512]{1,0:T(8,128)(2,1)S(1)} %get-tuple-element.21), channel_id=1, source_target_pairs={{0,16},{4,68},{8,24},{12,76},{16,0},{20,84},{24,8},{28,92},{32,48}... | collective-permute-start | bytes 393224 | tf_op jit(solution)/shard_map/ppermute | solution.py:270
  16.9 1.9 collective-permute-done.1
  18.8 2.7 %collective-permute-done.3 = bf16[128,512]{1,0:T(8,128)(2,1)S(1)} collective-permute-done((bf16[128,512]{1,0:T(8,128)(2,1)S(1)}, bf16[128,512]{1,0:T(8,128)(2,1)S(1)}, u32[]{:S(2)}, u32[]{:S(2)}) %collective-permute-start.3) | collective-permute-done | bytes 131104 | tf_op jit(solution)/shard_map/ppermute | solution.py:270
  22.4 2.5 %collective-permute-start.6 = (bf16[128,512]{1,0:T(8,128)(2,1)S(1)}, bf16[128,512]{1,0:T(8,128)(2,1)S(1)}, u32[]{:S(2)}, u32[]{:S(2)}) collective-permute-start(bf16[128,512]{1,0:T(8,128)(2,1)S(1)} %add_convert_fusion.7), channel_id=1, source_target_pairs={{0,64},{4,20},{8,72},{12,28},{16,80},{20,4},{24,88},{28,12},{32,96... | collective-permute-start | bytes 393224 | tf_op jit(solution)/shard_map/ppermute | solution.py:274
  25.8 2.0 collective-permute-done.6
  27.9 2.2 collective-permute-done.5
  30.1 1.7 collective-permute-start.9
  33.2 2.3 %collective-permute-done.9.piece2 = bf16[128,512]{1,0:T(8,128)(2,1)S(1)} collective-permute-done((bf16[128,512]{1,0:T(8,128)(2,1)S(1)}, bf16[128,512]{1,0:T(8,128)(2,1)S(1)}, u32[]{:S(2)}, u32[]{:S(2)}) %collective-permute-start.9) | collective-permute-done | bytes 131104 | tf_op jit(solution)/shard_map/ppermute | solution.py:278
  37.1 4.3 %collective-permute-start.10 = (bf16[512,512]{1,0:T(8,128)(2,1)S(1)}, bf16[512,512]{1,0:T(8,128)(2,1)}, u32[]{:S(2)}, u32[]{:S(2)}) collective-permute-start(bf16[512,512]{1,0:T(8,128)(2,1)S(1)} %join.4.mine_ref), channel_id=1, source_target_pairs={{0,4},{4,0},{8,12},{12,8},{16,20},{20,16},{24,28},{28,24},{32,36},... | collective-permute-start | bytes 1572872 | tf_op jit(solution)/shard_map/ppermute | solution.py:283
  43.1 1.7 copy-done.4
  44.7 3.1 %ladder.2 = bf16[1152,512]{1,0:T(8,128)(2,1)S(1)} custom-call(s32[1]{0:T(128)} %bitcast.core_ref, bf16[1152,1024]{1,0:T(8,128)(2,1)S(1)} %copy-done.2, bf16[512,512]{1,0:T(8,128)(2,1)S(1)} %join.4.mine_ref, bf16[512,512]{1,0:T(8,128)(2,1)} %collective-permute-done.10.other_ref, f32[4,1152,128]{2,1,0:T(8,128)S(1)} %copy-done.4, f32[1152,4]{1,0:T(8,128)S(1)} %bitcast.31), custom_call_target="tpu_custom_call" | custom-call | tf_op jit(solution)/shard_map/ladder/pallas_call | solution.py:228
  54.4 3.0 %collective-permute-done.12 = bf16[128,512]{1,0:T(8,128)(2,1)S(1)} collective-permute-done((bf16[128,512]{1,0:T(8,128)(2,1)S(1)}, bf16[128,512]{1,0:T(8,128)(2,1)S(1)}, u32[]{:S(2)}, u32[]{:S(2)}) %collective-permute-start.12) | collective-permute-done | bytes 131104 | tf_op jit(solution)/shard_map/ppermute | solution.py:270
  61.8 2.5 %collective-permute-done.17 = bf16[128,512]{1,0:T(8,128)(2,1)S(1)} collective-permute-done((bf16[128,512]{1,0:T(8,128)(2,1)S(1)}, bf16[128,512]{1,0:T(8,128)(2,1)S(1)}, u32[]{:S(2)}, u32[]{:S(2)}) %collective-permute-start.17) | collective-permute-done | bytes 131104 | tf_op jit(solution)/shard_map/ppermute | solution.py:274
  64.3 1.7 collective-permute-done.16
  69.0 2.5 %collective-permute-done.20.piece2 = bf16[128,512]{1,0:T(8,128)(2,1)S(1)} collective-permute-done((bf16[128,512]{1,0:T(8,128)(2,1)S(1)}, bf16[128,512]{1,0:T(8,128)(2,1)S(1)}, u32[]{:S(2)}, u32[]{:S(2)}) %collective-permute-start.20) | collective-permute-done | bytes 131104 | tf_op jit(solution)/shard_map/ppermute | solution.py:278
  72.9 3.7 %collective-permute-start.21 = (bf16[512,512]{1,0:T(8,128)(2,1)S(1)}, bf16[512,512]{1,0:T(8,128)(2,1)S(1)}, u32[]{:S(2)}, u32[]{:S(2)}) collective-permute-start(bf16[512,512]{1,0:T(8,128)(2,1)S(1)} %join.5.mine_ref), channel_id=1, source_target_pairs={{0,4},{4,0},{8,12},{12,8},{16,20},{20,16},{24,28},{28,24},{32,36},... | collective-permute-start | bytes 1572872 | tf_op jit(solution)/shard_map/ppermute | solution.py:283
  78.9 3.8 %collective-permute-start.24 = (f16[1200,128]{1,0:T(8,128)(2,1)S(1)}, f16[1200,128]{1,0:T(8,128)(2,1)S(1)}, u32[]{:S(2)}, u32[]{:S(2)}) collective-permute-start(f16[1200,128]{1,0:T(8,128)(2,1)S(1)} %convert_element_type.288), channel_id=1, source_target_pairs={{0,2},{1,3},{2,0},{3,1},{4,6},{5,7},{6,4},{7,5},{8,10},{9,11},{10,... | collective-permute-start | bytes 921608 | tf_op jit(solution)/shard_map/ppermute | solution.py:289
  87.6 2.5 %collective-permute-done.24 = f16[1200,128]{1,0:T(8,128)(2,1)S(1)} collective-permute-done((f16[1200,128]{1,0:T(8,128)(2,1)S(1)}, f16[1200,128]{1,0:T(8,128)(2,1)S(1)}, u32[]{:S(2)}, u32[]{:S(2)}) %collective-permute-start.24) | collective-permute-done | bytes 307232 | tf_op jit(solution)/shard_map/ppermute | solution.py:289
  91.6 5.5 %collective-permute-done.22 = f16[1200,128]{1,0:T(8,128)(2,1)S(1)} collective-permute-done((f16[1200,128]{1,0:T(8,128)(2,1)S(1)}, f16[1200,128]{1,0:T(8,128)(2,1)S(1)}, u32[]{:S(2)}, u32[]{:S(2)}) %collective-permute-start.22) | collective-permute-done | bytes 307232 | tf_op jit(solution)/shard_map/ppermute | solution.py:289
  100.1 3.0 %mix.2.own_ref = f32[4,1168,128]{2,1,0:T(8,128)S(1)} custom-call(f32[1200,128]{1,0:T(8,128)S(1)} %pack.8.table_ref.own_ref, f32[1200,128]{1,0:T(8,128)S(1)} %convert_element_type.285.table_ref.got1, f32[1200,128]{1,0:T(8,128)S(1)} %convert_element_type.287.table_ref.got3, f32[1200,128]{1,0:T(8,128)S(1)} %convert_element_type.289.table_ref.got2, ...), custom_call_target="tpu_custom_call" | custom-call | tf_op jit(solution)/shard_map/mix/pallas_call | solution.py:228
  105.0 1.7 collective-permute-start.26
  106.8 5.8 %collective-permute-done.27 = f16[1168,128]{1,0:T(8,128)(2,1)S(1)} collective-permute-done((f16[1168,128]{1,0:T(8,128)(2,1)S(1)}, f16[1168,128]{1,0:T(8,128)(2,1)S(1)}, u32[]{:S(2)}, u32[]{:S(2)}) %collective-permute-start.27) | collective-permute-done | bytes 299040 | tf_op jit(solution)/shard_map/ppermute | solution.py:289
  112.6 8.0 %collective-permute-done.26 = f16[1168,128]{1,0:T(8,128)(2,1)S(1)} collective-permute-done((f16[1168,128]{1,0:T(8,128)(2,1)S(1)}, f16[1168,128]{1,0:T(8,128)(2,1)S(1)}, u32[]{:S(2)}, u32[]{:S(2)}) %collective-permute-start.26) | collective-permute-done | bytes 299040 | tf_op jit(solution)/shard_map/ppermute | solution.py:289
  125.2 1.8 collective-permute-start.29
  128.0 2.9 %collective-permute-done.29 = bf16[128,512]{1,0:T(8,128)(2,1)S(1)} collective-permute-done((bf16[128,512]{1,0:T(8,128)(2,1)S(1)}, bf16[128,512]{1,0:T(8,128)(2,1)S(1)}, u32[]{:S(2)}, u32[]{:S(2)}) %collective-permute-start.29) | collective-permute-done | bytes 131104 | tf_op jit(solution)/shard_map/ppermute | solution.py:270
  135.2 2.7 %collective-permute-done.34 = bf16[128,512]{1,0:T(8,128)(2,1)S(1)} collective-permute-done((bf16[128,512]{1,0:T(8,128)(2,1)S(1)}, bf16[128,512]{1,0:T(8,128)(2,1)S(1)}, u32[]{:S(2)}, u32[]{:S(2)}) %collective-permute-start.34) | collective-permute-done | bytes 131104 | tf_op jit(solution)/shard_map/ppermute | solution.py:274
  137.9 1.7 collective-permute-done.33
  142.4 2.7 %collective-permute-done.37.piece2 = bf16[128,512]{1,0:T(8,128)(2,1)S(1)} collective-permute-done((bf16[128,512]{1,0:T(8,128)(2,1)S(1)}, bf16[128,512]{1,0:T(8,128)(2,1)S(1)}, u32[]{:S(2)}, u32[]{:S(2)}) %collective-permute-start.37) | collective-permute-done | bytes 131104 | tf_op jit(solution)/shard_map/ppermute | solution.py:278
  146.5 3.9 %collective-permute-start.38 = (bf16[512,512]{1,0:T(8,128)(2,1)S(1)}, bf16[512,512]{1,0:T(8,128)(2,1)S(1)}, u32[]{:S(2)}, u32[]{:S(2)}) collective-permute-start(bf16[512,512]{1,0:T(8,128)(2,1)S(1)} %join.6.mine_ref), channel_id=1, source_target_pairs={{0,4},{4,0},{8,12},{12,8},{16,20},{20,16},{24,28},{28,24},{32,36},... | collective-permute-start | bytes 1572872 | tf_op jit(solution)/shard_map/ppermute | solution.py:283
  152.0 2.0 ladder.3
  157.8 1.7 collective-permute-start.40
  160.7 3.0 %collective-permute-done.40 = bf16[128,512]{1,0:T(8,128)(2,1)S(1)} collective-permute-done((bf16[128,512]{1,0:T(8,128)(2,1)S(1)}, bf16[128,512]{1,0:T(8,128)(2,1)S(1)}, u32[]{:S(2)}, u32[]{:S(2)}) %collective-permute-start.40) | collective-permute-done | bytes 131104 | tf_op jit(solution)/shard_map/ppermute | solution.py:270
  167.9 2.7 %collective-permute-done.45 = bf16[128,512]{1,0:T(8,128)(2,1)S(1)} collective-permute-done((bf16[128,512]{1,0:T(8,128)(2,1)S(1)}, bf16[128,512]{1,0:T(8,128)(2,1)S(1)}, u32[]{:S(2)}, u32[]{:S(2)}) %collective-permute-start.45) | collective-permute-done | bytes 131104 | tf_op jit(solution)/shard_map/ppermute | solution.py:274
  170.6 1.7 collective-permute-done.44
  175.1 2.7 %collective-permute-done.48.piece2 = bf16[128,512]{1,0:T(8,128)(2,1)S(1)} collective-permute-done((bf16[128,512]{1,0:T(8,128)(2,1)S(1)}, bf16[128,512]{1,0:T(8,128)(2,1)S(1)}, u32[]{:S(2)}, u32[]{:S(2)}) %collective-permute-start.48) | collective-permute-done | bytes 131104 | tf_op jit(solution)/shard_map/ppermute | solution.py:278
  179.2 3.7 %collective-permute-start.49 = (bf16[512,512]{1,0:T(8,128)(2,1)S(1)}, bf16[512,512]{1,0:T(8,128)(2,1)S(1)}, u32[]{:S(2)}, u32[]{:S(2)}) collective-permute-start(bf16[512,512]{1,0:T(8,128)(2,1)S(1)} %join.7.mine_ref), channel_id=1, source_target_pairs={{0,4},{4,0},{8,12},{12,8},{16,20},{20,16},{24,28},{28,24},{32,36},... | collective-permute-start | bytes 1572872 | tf_op jit(solution)/shard_map/ppermute | solution.py:283
  187.5 1.7 collective-permute-start.51
  190.6 4.7 %collective-permute-done.52 = f16[1200,128]{1,0:T(8,128)(2,1)S(1)} collective-permute-done((f16[1200,128]{1,0:T(8,128)(2,1)S(1)}, f16[1200,128]{1,0:T(8,128)(2,1)S(1)}, u32[]{:S(2)}, u32[]{:S(2)}) %collective-permute-start.52) | collective-permute-done | bytes 307232 | tf_op jit(solution)/shard_map/ppermute | solution.py:289
  195.4 7.2 %collective-permute-done.51 = f16[1200,128]{1,0:T(8,128)(2,1)S(1)} collective-permute-done((f16[1200,128]{1,0:T(8,128)(2,1)S(1)}, f16[1200,128]{1,0:T(8,128)(2,1)S(1)}, u32[]{:S(2)}, u32[]{:S(2)}) %collective-permute-start.51) | collective-permute-done | bytes 307232 | tf_op jit(solution)/shard_map/ppermute | solution.py:289
  202.7 3.0 %mix.3.own_ref = f32[4,1168,128]{2,1,0:T(8,128)S(1)} custom-call(f32[1200,128]{1,0:T(8,128)S(1)} %pack.12.own_ref, f32[1200,128]{1,0:T(8,128)S(1)} %convert_element_type.325.got1, f32[1200,128]{1,0:T(8,128)S(1)} %convert_element_type.327.got3, f32[1200,128]{1,0:T(8,128)S(1)} %convert_element_type.329.got2, bf16[512,256]{1,0:T(8,128)(2,1)S(1)} %pad_maximum_fusion.into_ref, ...), custom_call_target="tpu_custom_call" | custom-call | tf_op jit(solution)/shard_map/mix/pallas_call | solution.py:228
  209.1 3.4 %amplitude.1 = f32[4,1152,128]{2,1,0:T(8,128)} custom-call(s32[1]{0:T(128)} %bitcast.core_ref, bf16[1152,1024]{1,0:T(8,128)(2,1)S(1)} %copy-done.2, bf16[512,512]{1,0:T(8,128)(2,1)S(1)} %join.7.mine_ref, bf16[512,512]{1,0:T(8,128)(2,1)S(1)} %collective-permute-done.49.other_ref, f32[4,1152,128]{2,1,0:T(8,128)S(1)} %get-tuple-element.5.sources_ref, ...), custom_call_target="tpu_custom_call" | custom-call | tf_op jit(solution)/shard_map/amplitude/pallas_call | solution.py:228
  212.5 3.3 %collective-permute-done.55 = f16[1168,128]{1,0:T(8,128)(2,1)S(1)} collective-permute-done((f16[1168,128]{1,0:T(8,128)(2,1)S(1)}, f16[1168,128]{1,0:T(8,128)(2,1)S(1)}, u32[]{:S(2)}, u32[]{:S(2)}) %collective-permute-start.55) | collective-permute-done | bytes 299040 | tf_op jit(solution)/shard_map/ppermute | solution.py:289
  215.9 7.2 %collective-permute-done.54 = f16[1168,128]{1,0:T(8,128)(2,1)S(1)} collective-permute-done((f16[1168,128]{1,0:T(8,128)(2,1)S(1)}, f16[1168,128]{1,0:T(8,128)(2,1)S(1)}, u32[]{:S(2)}, u32[]{:S(2)}) %collective-permute-start.54) | collective-permute-done | bytes 299040 | tf_op jit(solution)/shard_map/ppermute | solution.py:289
  223.2 1.9 unpack.3
  (161 shorter events, 79.0 us)
Async XLA Ops:
  13.0 5.7 %collective-permute-start.1 = (bf16[128,512]{1,0:T(8,128)(2,1)S(1)}, bf16[128,512]{1,0:T(8,128)(2,1)S(1)}, u32[]{:S(2)}, u32[]{:S(2)}) collective-permute-start(bf16[128,512]{1,0:T(8,128)(2,1)S(1)} %get-tuple-element.21), channel_id=1, source_target_pairs={{0,16},{4,68},{8,24},{12,76},{16,0},{20,84},{24,8},{28,92},{32,48}... | collective-permute-start | bytes 393224 | tf_op jit(solution)/shard_map/ppermute | solution.py:270
  16.1 5.3 %collective-permute-start.3 = (bf16[128,512]{1,0:T(8,128)(2,1)S(1)}, bf16[128,512]{1,0:T(8,128)(2,1)S(1)}, u32[]{:S(2)}, u32[]{:S(2)}) collective-permute-start(bf16[128,512]{1,0:T(8,128)(2,1)S(1)} %get-tuple-element.22), channel_id=1, source_target_pairs={{0,24},{4,100},{8,16},{12,108},{16,8},{20,116},{24,0},{28,124},{32... | collective-permute-start | bytes 393224 | tf_op jit(solution)/shard_map/ppermute | solution.py:270
  16.9 4.6 %collective-permute-start.2 = (bf16[128,512]{1,0:T(8,128)(2,1)S(1)}, bf16[128,512]{1,0:T(8,128)(2,1)S(1)}, u32[]{:S(2)}, u32[]{:S(2)}) collective-permute-start(bf16[128,512]{1,0:T(8,128)(2,1)S(1)} %get-tuple-element.23), channel_id=1, source_target_pairs={{0,8},{4,36},{8,0},{12,44},{16,24},{20,52},{24,16},{28,60},{32,40}... | collective-permute-start | bytes 393224 | tf_op jit(solution)/shard_map/ppermute | solution.py:270
  22.4 5.4 %collective-permute-start.6 = (bf16[128,512]{1,0:T(8,128)(2,1)S(1)}, bf16[128,512]{1,0:T(8,128)(2,1)S(1)}, u32[]{:S(2)}, u32[]{:S(2)}) collective-permute-start(bf16[128,512]{1,0:T(8,128)(2,1)S(1)} %add_convert_fusion.7), channel_id=1, source_target_pairs={{0,64},{4,20},{8,72},{12,28},{16,80},{20,4},{24,88},{28,12},{32,96... | collective-permute-start | bytes 393224 | tf_op jit(solution)/shard_map/ppermute | solution.py:274
  25.0 5.0 %collective-permute-start.5 = (bf16[128,512]{1,0:T(8,128)(2,1)S(1)}, bf16[128,512]{1,0:T(8,128)(2,1)S(1)}, u32[]{:S(2)}, u32[]{:S(2)}) collective-permute-start(bf16[128,512]{1,0:T(8,128)(2,1)S(1)} %add_convert_fusion.7), channel_id=1, source_target_pairs={{0,96},{4,28},{8,104},{12,20},{16,112},{20,12},{24,120},{28,4},{32... | collective-permute-start | bytes 393224 | tf_op jit(solution)/shard_map/ppermute | solution.py:274
  30.1 5.4 %collective-permute-start.9 = (bf16[128,512]{1,0:T(8,128)(2,1)S(1)}, bf16[128,512]{1,0:T(8,128)(2,1)S(1)}, u32[]{:S(2)}, u32[]{:S(2)}) collective-permute-start(bf16[128,512]{1,0:T(8,128)(2,1)S(1)} %add_convert_fusion.6.piece0), channel_id=1, source_target_pairs={{0,16},{4,68},{8,24},{12,76},{16,0},{20,84},{24,8},{28,92},{32,48}... | collective-permute-start | bytes 393224 | tf_op jit(solution)/shard_map/ppermute | solution.py:278
  31.8 5.1 %collective-permute-start.8 = (bf16[128,512]{1,0:T(8,128)(2,1)S(1)}, bf16[128,512]{1,0:T(8,128)(2,1)S(1)}, u32[]{:S(2)}, u32[]{:S(2)}) collective-permute-start(bf16[128,512]{1,0:T(8,128)(2,1)S(1)} %add_convert_fusion.6.piece0), channel_id=1, source_target_pairs={{0,24},{4,100},{8,16},{12,108},{16,8},{20,116},{24,0},{28,124},{32... | collective-permute-start | bytes 393224 | tf_op jit(solution)/shard_map/ppermute | solution.py:278
  37.1 6.0 %collective-permute-start.10 = (bf16[512,512]{1,0:T(8,128)(2,1)S(1)}, bf16[512,512]{1,0:T(8,128)(2,1)}, u32[]{:S(2)}, u32[]{:S(2)}) collective-permute-start(bf16[512,512]{1,0:T(8,128)(2,1)S(1)} %join.4.mine_ref), channel_id=1, source_target_pairs={{0,4},{4,0},{8,12},{12,8},{16,20},{20,16},{24,28},{28,24},{32,36},... | collective-permute-start | bytes 1572872 | tf_op jit(solution)/shard_map/ppermute | solution.py:283
  51.7 5.7 %collective-permute-start.12 = (bf16[128,512]{1,0:T(8,128)(2,1)S(1)}, bf16[128,512]{1,0:T(8,128)(2,1)S(1)}, u32[]{:S(2)}, u32[]{:S(2)}) collective-permute-start(bf16[128,512]{1,0:T(8,128)(2,1)S(1)} %get-tuple-element.18), channel_id=1, source_target_pairs={{0,16},{4,68},{8,24},{12,76},{16,0},{20,84},{24,8},{28,92},{32,48}... | collective-permute-start | bytes 393224 | tf_op jit(solution)/shard_map/ppermute | solution.py:270
  53.0 5.8 %collective-permute-start.14 = (bf16[128,512]{1,0:T(8,128)(2,1)S(1)}, bf16[128,512]{1,0:T(8,128)(2,1)S(1)}, u32[]{:S(2)}, u32[]{:S(2)}) collective-permute-start(bf16[128,512]{1,0:T(8,128)(2,1)S(1)} %get-tuple-element.19), channel_id=1, source_target_pairs={{0,24},{4,100},{8,16},{12,108},{16,8},{20,116},{24,0},{28,124},{32... | collective-permute-start | bytes 393224 | tf_op jit(solution)/shard_map/ppermute | solution.py:270
  54.1 4.7 %collective-permute-start.13 = (bf16[128,512]{1,0:T(8,128)(2,1)S(1)}, bf16[128,512]{1,0:T(8,128)(2,1)S(1)}, u32[]{:S(2)}, u32[]{:S(2)}) collective-permute-start(bf16[128,512]{1,0:T(8,128)(2,1)S(1)} %get-tuple-element.20), channel_id=1, source_target_pairs={{0,8},{4,36},{8,0},{12,44},{16,24},{20,52},{24,16},{28,60},{32,40}... | collective-permute-start | bytes 393224 | tf_op jit(solution)/shard_map/ppermute | solution.py:270
  58.9 5.4 %collective-permute-start.17 = (bf16[128,512]{1,0:T(8,128)(2,1)S(1)}, bf16[128,512]{1,0:T(8,128)(2,1)S(1)}, u32[]{:S(2)}, u32[]{:S(2)}) collective-permute-start(bf16[128,512]{1,0:T(8,128)(2,1)S(1)} %add_convert_fusion.5), channel_id=1, source_target_pairs={{0,64},{4,20},{8,72},{12,28},{16,80},{20,4},{24,88},{28,12},{32,96... | collective-permute-start | bytes 393224 | tf_op jit(solution)/shard_map/ppermute | solution.py:274
  60.4 5.6 %collective-permute-start.16 = (bf16[128,512]{1,0:T(8,128)(2,1)S(1)}, bf16[128,512]{1,0:T(8,128)(2,1)S(1)}, u32[]{:S(2)}, u32[]{:S(2)}) collective-permute-start(bf16[128,512]{1,0:T(8,128)(2,1)S(1)} %add_convert_fusion.5), channel_id=1, source_target_pairs={{0,96},{4,28},{8,104},{12,20},{16,112},{20,12},{24,120},{28,4},{32... | collective-permute-start | bytes 393224 | tf_op jit(solution)/shard_map/ppermute | solution.py:274
  61.3 4.6 %collective-permute-start.15 = (bf16[128,512]{1,0:T(8,128)(2,1)S(1)}, bf16[128,512]{1,0:T(8,128)(2,1)S(1)}, u32[]{:S(2)}, u32[]{:S(2)}) collective-permute-start(bf16[128,512]{1,0:T(8,128)(2,1)S(1)} %add_convert_fusion.5), channel_id=1, source_target_pairs={{0,32},{4,12},{8,40},{12,4},{16,48},{20,28},{24,56},{28,20},{32,0}... | collective-permute-start | bytes 393224 | tf_op jit(solution)/shard_map/ppermute | solution.py:274
  66.0 5.5 %collective-permute-start.20 = (bf16[128,512]{1,0:T(8,128)(2,1)S(1)}, bf16[128,512]{1,0:T(8,128)(2,1)S(1)}, u32[]{:S(2)}, u32[]{:S(2)}) collective-permute-start(bf16[128,512]{1,0:T(8,128)(2,1)S(1)} %add_convert_fusion.4.piece0), channel_id=1, source_target_pairs={{0,16},{4,68},{8,24},{12,76},{16,0},{20,84},{24,8},{28,92},{32,48}... | collective-permute-start | bytes 393224 | tf_op jit(solution)/shard_map/ppermute | solution.py:278
  67.3 5.6 %collective-permute-start.19 = (bf16[128,512]{1,0:T(8,128)(2,1)S(1)}, bf16[128,512]{1,0:T(8,128)(2,1)S(1)}, u32[]{:S(2)}, u32[]{:S(2)}) collective-permute-start(bf16[128,512]{1,0:T(8,128)(2,1)S(1)} %add_convert_fusion.4.piece0), channel_id=1, source_target_pairs={{0,24},{4,100},{8,16},{12,108},{16,8},{20,116},{24,0},{28,124},{32... | collective-permute-start | bytes 393224 | tf_op jit(solution)/shard_map/ppermute | solution.py:278
  68.4 4.5 %collective-permute-start.18 = (bf16[128,512]{1,0:T(8,128)(2,1)S(1)}, bf16[128,512]{1,0:T(8,128)(2,1)S(1)}, u32[]{:S(2)}, u32[]{:S(2)}) collective-permute-start(bf16[128,512]{1,0:T(8,128)(2,1)S(1)} %add_convert_fusion.4.piece0), channel_id=1, source_target_pairs={{0,8},{4,36},{8,0},{12,44},{16,24},{20,52},{24,16},{28,60},{32,40}... | collective-permute-start | bytes 393224 | tf_op jit(solution)/shard_map/ppermute | solution.py:278
  72.9 5.2 %collective-permute-start.21 = (bf16[512,512]{1,0:T(8,128)(2,1)S(1)}, bf16[512,512]{1,0:T(8,128)(2,1)S(1)}, u32[]{:S(2)}, u32[]{:S(2)}) collective-permute-start(bf16[512,512]{1,0:T(8,128)(2,1)S(1)} %join.5.mine_ref), channel_id=1, source_target_pairs={{0,4},{4,0},{8,12},{12,8},{16,20},{20,16},{24,28},{28,24},{32,36},... | collective-permute-start | bytes 1572872 | tf_op jit(solution)/shard_map/ppermute | solution.py:283
  78.9 11.2 %collective-permute-start.24 = (f16[1200,128]{1,0:T(8,128)(2,1)S(1)}, f16[1200,128]{1,0:T(8,128)(2,1)S(1)}, u32[]{:S(2)}, u32[]{:S(2)}) collective-permute-start(f16[1200,128]{1,0:T(8,128)(2,1)S(1)} %convert_element_type.288), channel_id=1, source_target_pairs={{0,2},{1,3},{2,0},{3,1},{4,6},{5,7},{6,4},{7,5},{8,10},{9,11},{10,... | collective-permute-start | bytes 921608 | tf_op jit(solution)/shard_map/ppermute | solution.py:289
  84.3 14.3 %collective-permute-start.23 = (f16[1200,128]{1,0:T(8,128)(2,1)S(1)}, f16[1200,128]{1,0:T(8,128)(2,1)S(1)}, u32[]{:S(2)}, u32[]{:S(2)}) collective-permute-start(f16[1200,128]{1,0:T(8,128)(2,1)S(1)} %convert_element_type.286), channel_id=1, source_target_pairs={{0,3},{1,2},{2,1},{3,0},{4,7},{5,6},{6,5},{7,4},{8,11},{9,10},{10,... | collective-permute-start | bytes 921608 | tf_op jit(solution)/shard_map/ppermute | solution.py:289
  84.8 12.3 %collective-permute-start.22 = (f16[1200,128]{1,0:T(8,128)(2,1)S(1)}, f16[1200,128]{1,0:T(8,128)(2,1)S(1)}, u32[]{:S(2)}, u32[]{:S(2)}) collective-permute-start(f16[1200,128]{1,0:T(8,128)(2,1)S(1)} %convert_element_type.284), channel_id=1, source_target_pairs={{0,1},{1,0},{2,3},{3,2},{4,5},{5,4},{6,7},{7,6},{8,9},{9,8},{10,11... | collective-permute-start | bytes 921608 | tf_op jit(solution)/shard_map/ppermute | solution.py:289
  103.5 9.0 %collective-permute-start.27 = (f16[1168,128]{1,0:T(8,128)(2,1)S(1)}, f16[1168,128]{1,0:T(8,128)(2,1)S(1)}, u32[]{:S(2)}, u32[]{:S(2)}) collective-permute-start(f16[1168,128]{1,0:T(8,128)(2,1)S(1)} %get-tuple-element.9), channel_id=1, source_target_pairs={{0,2},{1,3},{2,0},{3,1},{4,6},{5,7},{6,4},{7,5},{8,10},{9,11},{10,... | collective-permute-start | bytes 897032 | tf_op jit(solution)/shard_map/ppermute | solution.py:289
  105.0 15.5 %collective-permute-start.26 = (f16[1168,128]{1,0:T(8,128)(2,1)S(1)}, f16[1168,128]{1,0:T(8,128)(2,1)S(1)}, u32[]{:S(2)}, u32[]{:S(2)}) collective-permute-start(f16[1168,128]{1,0:T(8,128)(2,1)S(1)} %get-tuple-element.10), channel_id=1, source_target_pairs={{0,3},{1,2},{2,1},{3,0},{4,7},{5,6},{6,5},{7,4},{8,11},{9,10},{10,... | collective-permute-start | bytes 897032 | tf_op jit(solution)/shard_map/ppermute | solution.py:289
  106.7 13.8 %collective-permute-start.25 = (f16[1168,128]{1,0:T(8,128)(2,1)S(1)}, f16[1168,128]{1,0:T(8,128)(2,1)S(1)}, u32[]{:S(2)}, u32[]{:S(2)}) collective-permute-start(f16[1168,128]{1,0:T(8,128)(2,1)S(1)} %get-tuple-element.11), channel_id=1, source_target_pairs={{0,1},{1,0},{2,3},{3,2},{4,5},{5,4},{6,7},{7,6},{8,9},{9,8},{10,11... | collective-permute-start | bytes 897032 | tf_op jit(solution)/shard_map/ppermute | solution.py:289
  125.2 5.7 %collective-permute-start.29 = (bf16[128,512]{1,0:T(8,128)(2,1)S(1)}, bf16[128,512]{1,0:T(8,128)(2,1)S(1)}, u32[]{:S(2)}, u32[]{:S(2)}) collective-permute-start(bf16[128,512]{1,0:T(8,128)(2,1)S(1)} %get-tuple-element.15), channel_id=1, source_target_pairs={{0,16},{4,68},{8,24},{12,76},{16,0},{20,84},{24,8},{28,92},{32,48}... | collective-permute-start | bytes 393224 | tf_op jit(solution)/shard_map/ppermute | solution.py:270
  127.1 5.3 %collective-permute-start.31 = (bf16[128,512]{1,0:T(8,128)(2,1)S(1)}, bf16[128,512]{1,0:T(8,128)(2,1)S(1)}, u32[]{:S(2)}, u32[]{:S(2)}) collective-permute-start(bf16[128,512]{1,0:T(8,128)(2,1)S(1)} %get-tuple-element.16), channel_id=1, source_target_pairs={{0,24},{4,100},{8,16},{12,108},{16,8},{20,116},{24,0},{28,124},{32... | collective-permute-start | bytes 393224 | tf_op jit(solution)/shard_map/ppermute | solution.py:270
  132.5 5.4 %collective-permute-start.34 = (bf16[128,512]{1,0:T(8,128)(2,1)S(1)}, bf16[128,512]{1,0:T(8,128)(2,1)S(1)}, u32[]{:S(2)}, u32[]{:S(2)}) collective-permute-start(bf16[128,512]{1,0:T(8,128)(2,1)S(1)} %add_convert_fusion.3), channel_id=1, source_target_pairs={{0,64},{4,20},{8,72},{12,28},{16,80},{20,4},{24,88},{28,12},{32,96... | collective-permute-start | bytes 393224 | tf_op jit(solution)/shard_map/ppermute | solution.py:274
  134.0 5.6 %collective-permute-start.33 = (bf16[128,512]{1,0:T(8,128)(2,1)S(1)}, bf16[128,512]{1,0:T(8,128)(2,1)S(1)}, u32[]{:S(2)}, u32[]{:S(2)}) collective-permute-start(bf16[128,512]{1,0:T(8,128)(2,1)S(1)} %add_convert_fusion.3), channel_id=1, source_target_pairs={{0,96},{4,28},{8,104},{12,20},{16,112},{20,12},{24,120},{28,4},{32... | collective-permute-start | bytes 393224 | tf_op jit(solution)/shard_map/ppermute | solution.py:274
  135.0 4.6 %collective-permute-start.32 = (bf16[128,512]{1,0:T(8,128)(2,1)S(1)}, bf16[128,512]{1,0:T(8,128)(2,1)S(1)}, u32[]{:S(2)}, u32[]{:S(2)}) collective-permute-start(bf16[128,512]{1,0:T(8,128)(2,1)S(1)} %add_convert_fusion.3), channel_id=1, source_target_pairs={{0,32},{4,12},{8,40},{12,4},{16,48},{20,28},{24,56},{28,20},{32,0}... | collective-permute-start | bytes 393224 | tf_op jit(solution)/shard_map/ppermute | solution.py:274
  139.6 5.4 %collective-permute-start.37 = (bf16[128,512]{1,0:T(8,128)(2,1)S(1)}, bf16[128,512]{1,0:T(8,128)(2,1)S(1)}, u32[]{:S(2)}, u32[]{:S(2)}) collective-permute-start(bf16[128,512]{1,0:T(8,128)(2,1)S(1)} %add_convert_fusion.2.piece0), channel_id=1, source_target_pairs={{0,16},{4,68},{8,24},{12,76},{16,0},{20,84},{24,8},{28,92},{32,48}... | collective-permute-start | bytes 393224 | tf_op jit(solution)/shard_map/ppermute | solution.py:278
  141.0 5.4 %collective-permute-start.36 = (bf16[128,512]{1,0:T(8,128)(2,1)S(1)}, bf16[128,512]{1,0:T(8,128)(2,1)S(1)}, u32[]{:S(2)}, u32[]{:S(2)}) collective-permute-start(bf16[128,512]{1,0:T(8,128)(2,1)S(1)} %add_convert_fusion.2.piece0), channel_id=1, source_target_pairs={{0,24},{4,100},{8,16},{12,108},{16,8},{20,116},{24,0},{28,124},{32... | collective-permute-start | bytes 393224 | tf_op jit(solution)/shard_map/ppermute | solution.py:278
  146.5 5.5 %collective-permute-start.38 = (bf16[512,512]{1,0:T(8,128)(2,1)S(1)}, bf16[512,512]{1,0:T(8,128)(2,1)S(1)}, u32[]{:S(2)}, u32[]{:S(2)}) collective-permute-start(bf16[512,512]{1,0:T(8,128)(2,1)S(1)} %join.6.mine_ref), channel_id=1, source_target_pairs={{0,4},{4,0},{8,12},{12,8},{16,20},{20,16},{24,28},{28,24},{32,36},... | collective-permute-start | bytes 1572872 | tf_op jit(solution)/shard_map/ppermute | solution.py:283
  157.8 5.9 %collective-permute-start.40 = (bf16[128,512]{1,0:T(8,128)(2,1)S(1)}, bf16[128,512]{1,0:T(8,128)(2,1)S(1)}, u32[]{:S(2)}, u32[]{:S(2)}) collective-permute-start(bf16[128,512]{1,0:T(8,128)(2,1)S(1)} %get-tuple-element.12), channel_id=1, source_target_pairs={{0,16},{4,68},{8,24},{12,76},{16,0},{20,84},{24,8},{28,92},{32,48}... | collective-permute-start | bytes 393224 | tf_op jit(solution)/shard_map/ppermute | solution.py:270
  159.5 5.6 %collective-permute-start.42 = (bf16[128,512]{1,0:T(8,128)(2,1)S(1)}, bf16[128,512]{1,0:T(8,128)(2,1)S(1)}, u32[]{:S(2)}, u32[]{:S(2)}) collective-permute-start(bf16[128,512]{1,0:T(8,128)(2,1)S(1)} %get-tuple-element.13), channel_id=1, source_target_pairs={{0,24},{4,100},{8,16},{12,108},{16,8},{20,116},{24,0},{28,124},{32... | collective-permute-start | bytes 393224 | tf_op jit(solution)/shard_map/ppermute | solution.py:270
  160.5 4.6 %collective-permute-start.41 = (bf16[128,512]{1,0:T(8,128)(2,1)S(1)}, bf16[128,512]{1,0:T(8,128)(2,1)S(1)}, u32[]{:S(2)}, u32[]{:S(2)}) collective-permute-start(bf16[128,512]{1,0:T(8,128)(2,1)S(1)} %get-tuple-element.14), channel_id=1, source_target_pairs={{0,8},{4,36},{8,0},{12,44},{16,24},{20,52},{24,16},{28,60},{32,40}... | collective-permute-start | bytes 393224 | tf_op jit(solution)/shard_map/ppermute | solution.py:270
  165.2 5.4 %collective-permute-start.45 = (bf16[128,512]{1,0:T(8,128)(2,1)S(1)}, bf16[128,512]{1,0:T(8,128)(2,1)S(1)}, u32[]{:S(2)}, u32[]{:S(2)}) collective-permute-start(bf16[128,512]{1,0:T(8,128)(2,1)S(1)} %add_convert_fusion.1), channel_id=1, source_target_pairs={{0,64},{4,20},{8,72},{12,28},{16,80},{20,4},{24,88},{28,12},{32,96... | collective-permute-start | bytes 393224 | tf_op jit(solution)/shard_map/ppermute | solution.py:274
  166.7 5.6 %collective-permute-start.44 = (bf16[128,512]{1,0:T(8,128)(2,1)S(1)}, bf16[128,512]{1,0:T(8,128)(2,1)S(1)}, u32[]{:S(2)}, u32[]{:S(2)}) collective-permute-start(bf16[128,512]{1,0:T(8,128)(2,1)S(1)} %add_convert_fusion.1), channel_id=1, source_target_pairs={{0,96},{4,28},{8,104},{12,20},{16,112},{20,12},{24,120},{28,4},{32... | collective-permute-start | bytes 393224 | tf_op jit(solution)/shard_map/ppermute | solution.py:274
  167.7 4.6 %collective-permute-start.43 = (bf16[128,512]{1,0:T(8,128)(2,1)S(1)}, bf16[128,512]{1,0:T(8,128)(2,1)S(1)}, u32[]{:S(2)}, u32[]{:S(2)}) collective-permute-start(bf16[128,512]{1,0:T(8,128)(2,1)S(1)} %add_convert_fusion.1), channel_id=1, source_target_pairs={{0,32},{4,12},{8,40},{12,4},{16,48},{20,28},{24,56},{28,20},{32,0}... | collective-permute-start | bytes 393224 | tf_op jit(solution)/shard_map/ppermute | solution.py:274
  172.4 5.4 %collective-permute-start.48 = (bf16[128,512]{1,0:T(8,128)(2,1)S(1)}, bf16[128,512]{1,0:T(8,128)(2,1)S(1)}, u32[]{:S(2)}, u32[]{:S(2)}) collective-permute-start(bf16[128,512]{1,0:T(8,128)(2,1)S(1)} %add_convert_fusion.piece0), channel_id=1, source_target_pairs={{0,16},{4,68},{8,24},{12,76},{16,0},{20,84},{24,8},{28,92},{32,48}... | collective-permute-start | bytes 393224 | tf_op jit(solution)/shard_map/ppermute | solution.py:278
  173.8 5.4 %collective-permute-start.47 = (bf16[128,512]{1,0:T(8,128)(2,1)S(1)}, bf16[128,512]{1,0:T(8,128)(2,1)S(1)}, u32[]{:S(2)}, u32[]{:S(2)}) collective-permute-start(bf16[128,512]{1,0:T(8,128)(2,1)S(1)} %add_convert_fusion.piece0), channel_id=1, source_target_pairs={{0,24},{4,100},{8,16},{12,108},{16,8},{20,116},{24,0},{28,124},{32... | collective-permute-start | bytes 393224 | tf_op jit(solution)/shard_map/ppermute | solution.py:278
  174.7 4.5 %collective-permute-start.46 = (bf16[128,512]{1,0:T(8,128)(2,1)S(1)}, bf16[128,512]{1,0:T(8,128)(2,1)S(1)}, u32[]{:S(2)}, u32[]{:S(2)}) collective-permute-start(bf16[128,512]{1,0:T(8,128)(2,1)S(1)} %add_convert_fusion.piece0), channel_id=1, source_target_pairs={{0,8},{4,36},{8,0},{12,44},{16,24},{20,52},{24,16},{28,60},{32,40}... | collective-permute-start | bytes 393224 | tf_op jit(solution)/shard_map/ppermute | solution.py:278
  179.2 5.2 %collective-permute-start.49 = (bf16[512,512]{1,0:T(8,128)(2,1)S(1)}, bf16[512,512]{1,0:T(8,128)(2,1)S(1)}, u32[]{:S(2)}, u32[]{:S(2)}) collective-permute-start(bf16[512,512]{1,0:T(8,128)(2,1)S(1)} %join.7.mine_ref), channel_id=1, source_target_pairs={{0,4},{4,0},{8,12},{12,8},{16,20},{20,16},{24,28},{28,24},{32,36},... | collective-permute-start | bytes 1572872 | tf_op jit(solution)/shard_map/ppermute | solution.py:283
  185.2 10.1 %collective-permute-start.52 = (f16[1200,128]{1,0:T(8,128)(2,1)S(1)}, f16[1200,128]{1,0:T(8,128)(2,1)S(1)}, u32[]{:S(2)}, u32[]{:S(2)}) collective-permute-start(f16[1200,128]{1,0:T(8,128)(2,1)S(1)} %convert_element_type.328), channel_id=1, source_target_pairs={{0,2},{1,3},{2,0},{3,1},{4,6},{5,7},{6,4},{7,5},{8,10},{9,11},{10,... | collective-permute-start | bytes 921608 | tf_op jit(solution)/shard_map/ppermute | solution.py:289
  187.5 15.1 %collective-permute-start.51 = (f16[1200,128]{1,0:T(8,128)(2,1)S(1)}, f16[1200,128]{1,0:T(8,128)(2,1)S(1)}, u32[]{:S(2)}, u32[]{:S(2)}) collective-permute-start(f16[1200,128]{1,0:T(8,128)(2,1)S(1)} %convert_element_type.326), channel_id=1, source_target_pairs={{0,3},{1,2},{2,1},{3,0},{4,7},{5,6},{6,5},{7,4},{8,11},{9,10},{10,... | collective-permute-start | bytes 921608 | tf_op jit(solution)/shard_map/ppermute | solution.py:289
  189.9 12.7 %collective-permute-start.50 = (f16[1200,128]{1,0:T(8,128)(2,1)S(1)}, f16[1200,128]{1,0:T(8,128)(2,1)S(1)}, u32[]{:S(2)}, u32[]{:S(2)}) collective-permute-start(f16[1200,128]{1,0:T(8,128)(2,1)S(1)} %convert_element_type.324), channel_id=1, source_target_pairs={{0,1},{1,0},{2,3},{3,2},{4,5},{5,4},{6,7},{7,6},{8,9},{9,8},{10,11... | collective-permute-start | bytes 921608 | tf_op jit(solution)/shard_map/ppermute | solution.py:289
  206.1 9.8 %collective-permute-start.55 = (f16[1168,128]{1,0:T(8,128)(2,1)S(1)}, f16[1168,128]{1,0:T(8,128)(2,1)S(1)}, u32[]{:S(2)}, u32[]{:S(2)}) collective-permute-start(f16[1168,128]{1,0:T(8,128)(2,1)S(1)} %get-tuple-element.6), channel_id=1, source_target_pairs={{0,2},{1,3},{2,0},{3,1},{4,6},{5,7},{6,4},{7,5},{8,10},{9,11},{10,... | collective-permute-start | bytes 897032 | tf_op jit(solution)/shard_map/ppermute | solution.py:289
  207.5 15.6 %collective-permute-start.54 = (f16[1168,128]{1,0:T(8,128)(2,1)S(1)}, f16[1168,128]{1,0:T(8,128)(2,1)S(1)}, u32[]{:S(2)}, u32[]{:S(2)}) collective-permute-start(f16[1168,128]{1,0:T(8,128)(2,1)S(1)} %get-tuple-element.7), channel_id=1, source_target_pairs={{0,3},{1,2},{2,1},{3,0},{4,7},{5,6},{6,5},{7,4},{8,11},{9,10},{10,... | collective-permute-start | bytes 897032 | tf_op jit(solution)/shard_map/ppermute | solution.py:289
  209.1 14.0 %collective-permute-start.53 = (f16[1168,128]{1,0:T(8,128)(2,1)S(1)}, f16[1168,128]{1,0:T(8,128)(2,1)S(1)}, u32[]{:S(2)}, u32[]{:S(2)}) collective-permute-start(f16[1168,128]{1,0:T(8,128)(2,1)S(1)} %get-tuple-element.8), channel_id=1, source_target_pairs={{0,1},{1,0},{2,3},{3,2},{4,5},{5,4},{6,7},{7,6},{8,9},{9,8},{10,11... | collective-permute-start | bytes 897032 | tf_op jit(solution)/shard_map/ppermute | solution.py:289
  (17 other events, 158.7 us)

commit v10 on v9

--- a/solution.py
+++ b/solution.py
@@ -47,8 +47,12 @@
     return power, jnp.exp2(-power)
 
 
-def round_body(right_ref, rounded_ref):
+def round_body(core_ref, right_ref, factors_ref, rounded_ref, keep_ref, send_ref):
     nf, rows, cols = right_ref.shape
+    half = keep_ref.shape[1]
+    core = core_ref[0]
+    keep_ref[...] = factors_ref[:, pl.ds(pl.multiple_of(core * half, half), half)]
+    send_ref[...] = factors_ref[:, pl.ds(pl.multiple_of((1 - core) * half, half), half)]
     for f in range(nf):
         rounded_ref[:, f * cols : (f + 1) * cols] = right_ref[f].astype(BF16)
 
@@ -250,6 +254,12 @@
     chip = me // 2
     spot = jnp.where(core == 0, chip % SIDE, chip // SIDE)
     spot_at = jnp.full((1,), spot, jnp.int32)
+    core_at = jnp.full((1,), core, jnp.int32)
+    rounded, first_keep, first_send = call(
+        round_body, [((rows, wide), BF16)] + [((rows, half), BF16)] * 2, "round", 6, 1,
+        (core_at, right_side, factors),
+    )
+
     factors_keep = lax.dynamic_slice(factors, (0, core * half), (rows, half))
     factors_send = lax.dynamic_slice(factors, (0, (1 - core) * half), (rows, half))
 
@@ -258,10 +268,10 @@
             table, rounded, (((0,), (0,)), ((), ())), preferred_element_type=F32
         )
 
-    def reduce_all(rounded):
-        sent = project(factors_send, rounded).astype(BF16)
+    def reduce_all(rounded, keep=factors_keep, send=factors_send):
+        sent = project(send, rounded).astype(BF16)
         got = lax.ppermute(sent, "fac", CORES)
-        mine = project(factors_keep, rounded) + got.astype(F32)
+        mine = project(keep, rounded) + got.astype(F32)
         own = lax.dynamic_slice(mine, (spot * chunk, 0), (chunk, wide))
         for d in PARTNERS:
             piece = lax.dynamic_slice(
@@ -314,14 +324,15 @@
     table_in = spread_table(source, forward, source)
     table_out = spread_table(source, backward, source)
 
-    core_at = jnp.full((1,), core, jnp.int32)
     column = pair_weight.T
     whole = [pltpu.VMEM((naux, wide), BF16)]
     sources = right_side
-    (rounded,) = call(round_body, [((rows, wide), BF16)], "round", 4, 0, (right_side,))
     for outer in range(OUTER):
         for inner in range(INNER - 1):
-            parts = reduce_all(rounded)
+            if outer + inner == 0:
+                parts = reduce_all(rounded, first_keep, first_send)
+            else:
+                parts = reduce_all(rounded)
             (rounded,) = call(
                 ladder_body, [((rows, wide), BF16)], "ladder", 10, 1,
                 (core_at, factors, *parts, sources, column),

time: 225 us -> 226 us (level)
    unnamed x19 -> x31, local copies, waits for them, and re-layouts: 5.08 us -> 6.44 us
where the time goes in v10:
time: 226 us
  waiting for transfers between devices  106 us (47%)
  starting transfers between devices  67.9 us (30%)
  Pallas kernels  28.8 us (13%)
  matrix products  11.6 us (5%)
  local copies, waits for them, and re-layouts  7.17 us (3%)
  other arithmetic  2.85 us (1%)
    ppermute x12, waiting for transfers between devices, exchange(): got[d] = lax.ppermute(sent[d].astype(F16), 'freq', swap(d)).astype(F32)  44 us
    pallas_call x24, Pallas kernels, call(): pl.pallas_call(body, out_shape=[jax.ShapeDtypeStruct(s, t) for s, t in ou...  28.8 us
    ppermute x12, waiting for transfers between devices, reduce_all(): own = own + lax.ppermute(piece, 'fac', along(d, True)).astype(F32)  17.7 us
    ppermute x12, waiting for transfers between devices, reduce_all(): total = total + lax.ppermute(own, 'fac', along(d, False)).astype(F32)  17.1 us
    ppermute x12, waiting for transfers between devices, reduce_all(): pieces[d] = lax.ppermute(total, 'fac', along(d, True))  15.8 us
    ppermute x4, starting transfers between devices, reduce_all(): other = lax.ppermute(gathered, 'fac', CORES)  15.6 us
    ppermute x12, starting transfers between devices, exchange(): got[d] = lax.ppermute(sent[d].astype(F16), 'freq', swap(d)).astype(F32)  14.3 us
    ppermute x12, starting transfers between devices, reduce_all(): own = own + lax.ppermute(piece, 'fac', along(d, True)).astype(F32)  12.3 us
  transfers between devices with their start and end apart: 56, of which 41 were waited for; matrix products, arithmetic and copies ran while one was open for 1% of the time, Pallas kernels for 5%

profile of v10, /device:TPU:1, one launch (start us, length us, event | category | flops | bytes accessed | tf_op | source)
XLA Modules:
  0.0 225.9 jit_solution(15542508595083760284)
XLA Ops:
  9.3 2.1 convert_add_fusion
  11.5 3.1 %collective-permute-start.1 = (bf16[128,512]{1,0:T(8,128)(2,1)S(1)}, bf16[128,512]{1,0:T(8,128)(2,1)S(1)}, u32[]{:S(2)}, u32[]{:S(2)}) collective-permute-start(bf16[128,512]{1,0:T(8,128)(2,1)S(1)} %get-tuple-element.27), channel_id=1, source_target_pairs={{0,16},{4,68},{8,24},{12,76},{16,0},{20,84},{24,8},{28,92},{32,48}... | collective-permute-start | bytes 393224 | tf_op jit(solution)/shard_map/ppermute | solution.py:280
  15.4 1.9 collective-permute-done.1
  17.3 2.7 %collective-permute-done.3 = bf16[128,512]{1,0:T(8,128)(2,1)S(1)} collective-permute-done((bf16[128,512]{1,0:T(8,128)(2,1)S(1)}, bf16[128,512]{1,0:T(8,128)(2,1)S(1)}, u32[]{:S(2)}, u32[]{:S(2)}) %collective-permute-start.3) | collective-permute-done | bytes 131104 | tf_op jit(solution)/shard_map/ppermute | solution.py:280
  21.1 2.5 %collective-permute-start.6 = (bf16[128,512]{1,0:T(8,128)(2,1)S(1)}, bf16[128,512]{1,0:T(8,128)(2,1)S(1)}, u32[]{:S(2)}, u32[]{:S(2)}) collective-permute-start(bf16[128,512]{1,0:T(8,128)(2,1)S(1)} %add_convert_fusion.7), channel_id=1, source_target_pairs={{0,64},{4,20},{8,72},{12,28},{16,80},{20,4},{24,88},{28,12},{32,96... | collective-permute-start | bytes 393224 | tf_op jit(solution)/shard_map/ppermute | solution.py:284
  24.5 2.0 collective-permute-done.6
  26.5 2.2 collective-permute-done.5
  28.8 1.7 collective-permute-start.9
  31.9 2.3 %collective-permute-done.9.piece2 = bf16[128,512]{1,0:T(8,128)(2,1)S(1)} collective-permute-done((bf16[128,512]{1,0:T(8,128)(2,1)S(1)}, bf16[128,512]{1,0:T(8,128)(2,1)S(1)}, u32[]{:S(2)}, u32[]{:S(2)}) %collective-permute-start.9) | collective-permute-done | bytes 131104 | tf_op jit(solution)/shard_map/ppermute | solution.py:288
  35.8 4.3 %collective-permute-start.10 = (bf16[512,512]{1,0:T(8,128)(2,1)S(1)}, bf16[512,512]{1,0:T(8,128)(2,1)}, u32[]{:S(2)}, u32[]{:S(2)}) collective-permute-start(bf16[512,512]{1,0:T(8,128)(2,1)S(1)} %join.4.mine_ref), channel_id=1, source_target_pairs={{0,4},{4,0},{8,12},{12,8},{16,20},{20,16},{24,28},{28,24},{32,36},... | collective-permute-start | bytes 1572872 | tf_op jit(solution)/shard_map/ppermute | solution.py:293
  41.8 1.7 copy-done.5
  43.4 3.0 %ladder.2 = bf16[1152,512]{1,0:T(8,128)(2,1)S(1)} custom-call(s32[1]{0:T(128)} %bitcast.core_ref, bf16[1152,1024]{1,0:T(8,128)(2,1)S(1)} %copy-done.3, bf16[512,512]{1,0:T(8,128)(2,1)S(1)} %join.4.mine_ref, bf16[512,512]{1,0:T(8,128)(2,1)} %collective-permute-done.10.other_ref, f32[4,1152,128]{2,1,0:T(8,128)S(1)} %copy-done.5, f32[1152,4]{1,0:T(8,128)S(1)} %bitcast.33), custom_call_target="tpu_custom_call" | custom-call | tf_op jit(solution)/shard_map/ladder/pallas_call | solution.py:232
  46.5 1.7 convolution_convert_fusion.2
  48.5 1.7 collective-permute-done.11
  50.3 2.1 convolution_add_fusion.2
  55.3 3.0 %collective-permute-done.12 = bf16[128,512]{1,0:T(8,128)(2,1)S(1)} collective-permute-done((bf16[128,512]{1,0:T(8,128)(2,1)S(1)}, bf16[128,512]{1,0:T(8,128)(2,1)S(1)}, u32[]{:S(2)}, u32[]{:S(2)}) %collective-permute-start.12) | collective-permute-done | bytes 131104 | tf_op jit(solution)/shard_map/ppermute | solution.py:280
  62.6 2.5 %collective-permute-done.17 = bf16[128,512]{1,0:T(8,128)(2,1)S(1)} collective-permute-done((bf16[128,512]{1,0:T(8,128)(2,1)S(1)}, bf16[128,512]{1,0:T(8,128)(2,1)S(1)}, u32[]{:S(2)}, u32[]{:S(2)}) %collective-permute-start.17) | collective-permute-done | bytes 131104 | tf_op jit(solution)/shard_map/ppermute | solution.py:284
  65.1 1.7 collective-permute-done.16
  69.9 2.5 %collective-permute-done.20.piece2 = bf16[128,512]{1,0:T(8,128)(2,1)S(1)} collective-permute-done((bf16[128,512]{1,0:T(8,128)(2,1)S(1)}, bf16[128,512]{1,0:T(8,128)(2,1)S(1)}, u32[]{:S(2)}, u32[]{:S(2)}) %collective-permute-start.20) | collective-permute-done | bytes 131104 | tf_op jit(solution)/shard_map/ppermute | solution.py:288
  73.8 3.7 %collective-permute-start.21 = (bf16[512,512]{1,0:T(8,128)(2,1)S(1)}, bf16[512,512]{1,0:T(8,128)(2,1)S(1)}, u32[]{:S(2)}, u32[]{:S(2)}) collective-permute-start(bf16[512,512]{1,0:T(8,128)(2,1)S(1)} %join.5.mine_ref), channel_id=1, source_target_pairs={{0,4},{4,0},{8,12},{12,8},{16,20},{20,16},{24,28},{28,24},{32,36},... | collective-permute-start | bytes 1572872 | tf_op jit(solution)/shard_map/ppermute | solution.py:293
  79.7 3.9 %collective-permute-start.24 = (f16[1200,128]{1,0:T(8,128)(2,1)S(1)}, f16[1200,128]{1,0:T(8,128)(2,1)S(1)}, u32[]{:S(2)}, u32[]{:S(2)}) collective-permute-start(f16[1200,128]{1,0:T(8,128)(2,1)S(1)} %convert_element_type.288), channel_id=1, source_target_pairs={{0,2},{1,3},{2,0},{3,1},{4,6},{5,7},{6,4},{7,5},{8,10},{9,11},{10,... | collective-permute-start | bytes 921608 | tf_op jit(solution)/shard_map/ppermute | solution.py:299
  88.5 2.5 %collective-permute-done.24 = f16[1200,128]{1,0:T(8,128)(2,1)S(1)} collective-permute-done((f16[1200,128]{1,0:T(8,128)(2,1)S(1)}, f16[1200,128]{1,0:T(8,128)(2,1)S(1)}, u32[]{:S(2)}, u32[]{:S(2)}) %collective-permute-start.24) | collective-permute-done | bytes 307232 | tf_op jit(solution)/shard_map/ppermute | solution.py:299
  92.4 5.5 %collective-permute-done.22 = f16[1200,128]{1,0:T(8,128)(2,1)S(1)} collective-permute-done((f16[1200,128]{1,0:T(8,128)(2,1)S(1)}, f16[1200,128]{1,0:T(8,128)(2,1)S(1)}, u32[]{:S(2)}, u32[]{:S(2)}) %collective-permute-start.22) | collective-permute-done | bytes 307232 | tf_op jit(solution)/shard_map/ppermute | solution.py:299
  101.0 3.0 %mix.2.own_ref = f32[4,1168,128]{2,1,0:T(8,128)S(1)} custom-call(f32[1200,128]{1,0:T(8,128)S(1)} %pack.8.table_ref.own_ref, f32[1200,128]{1,0:T(8,128)S(1)} %convert_element_type.285.table_ref.got1, f32[1200,128]{1,0:T(8,128)S(1)} %convert_element_type.287.table_ref.got3, f32[1200,128]{1,0:T(8,128)S(1)} %convert_element_type.289.table_ref.got2, ...), custom_call_target="tpu_custom_call" | custom-call | tf_op jit(solution)/shard_map/mix/pallas_call | solution.py:232
  105.8 1.7 collective-permute-start.26
  107.6 5.8 %collective-permute-done.27 = f16[1168,128]{1,0:T(8,128)(2,1)S(1)} collective-permute-done((f16[1168,128]{1,0:T(8,128)(2,1)S(1)}, f16[1168,128]{1,0:T(8,128)(2,1)S(1)}, u32[]{:S(2)}, u32[]{:S(2)}) %collective-permute-start.27) | collective-permute-done | bytes 299040 | tf_op jit(solution)/shard_map/ppermute | solution.py:299
  113.4 8.0 %collective-permute-done.26 = f16[1168,128]{1,0:T(8,128)(2,1)S(1)} collective-permute-done((f16[1168,128]{1,0:T(8,128)(2,1)S(1)}, f16[1168,128]{1,0:T(8,128)(2,1)S(1)}, u32[]{:S(2)}, u32[]{:S(2)}) %collective-permute-start.26) | collective-permute-done | bytes 299040 | tf_op jit(solution)/shard_map/ppermute | solution.py:299
  126.0 1.9 collective-permute-start.29
  128.8 2.9 %collective-permute-done.29 = bf16[128,512]{1,0:T(8,128)(2,1)S(1)} collective-permute-done((bf16[128,512]{1,0:T(8,128)(2,1)S(1)}, bf16[128,512]{1,0:T(8,128)(2,1)S(1)}, u32[]{:S(2)}, u32[]{:S(2)}) %collective-permute-start.29) | collective-permute-done | bytes 131104 | tf_op jit(solution)/shard_map/ppermute | solution.py:280
  136.0 2.7 %collective-permute-done.34 = bf16[128,512]{1,0:T(8,128)(2,1)S(1)} collective-permute-done((bf16[128,512]{1,0:T(8,128)(2,1)S(1)}, bf16[128,512]{1,0:T(8,128)(2,1)S(1)}, u32[]{:S(2)}, u32[]{:S(2)}) %collective-permute-start.34) | collective-permute-done | bytes 131104 | tf_op jit(solution)/shard_map/ppermute | solution.py:284
  138.7 1.7 collective-permute-done.33
  143.2 2.7 %collective-permute-done.37.piece2 = bf16[128,512]{1,0:T(8,128)(2,1)S(1)} collective-permute-done((bf16[128,512]{1,0:T(8,128)(2,1)S(1)}, bf16[128,512]{1,0:T(8,128)(2,1)S(1)}, u32[]{:S(2)}, u32[]{:S(2)}) %collective-permute-start.37) | collective-permute-done | bytes 131104 | tf_op jit(solution)/shard_map/ppermute | solution.py:288
  147.3 3.9 %collective-permute-start.38 = (bf16[512,512]{1,0:T(8,128)(2,1)S(1)}, bf16[512,512]{1,0:T(8,128)(2,1)S(1)}, u32[]{:S(2)}, u32[]{:S(2)}) collective-permute-start(bf16[512,512]{1,0:T(8,128)(2,1)S(1)} %join.6.mine_ref), channel_id=1, source_target_pairs={{0,4},{4,0},{8,12},{12,8},{16,20},{20,16},{24,28},{28,24},{32,36},... | collective-permute-start | bytes 1572872 | tf_op jit(solution)/shard_map/ppermute | solution.py:293
  152.8 2.0 ladder.3
  158.6 1.7 collective-permute-start.40
  161.6 3.0 %collective-permute-done.40 = bf16[128,512]{1,0:T(8,128)(2,1)S(1)} collective-permute-done((bf16[128,512]{1,0:T(8,128)(2,1)S(1)}, bf16[128,512]{1,0:T(8,128)(2,1)S(1)}, u32[]{:S(2)}, u32[]{:S(2)}) %collective-permute-start.40) | collective-permute-done | bytes 131104 | tf_op jit(solution)/shard_map/ppermute | solution.py:280
  168.8 2.7 %collective-permute-done.45 = bf16[128,512]{1,0:T(8,128)(2,1)S(1)} collective-permute-done((bf16[128,512]{1,0:T(8,128)(2,1)S(1)}, bf16[128,512]{1,0:T(8,128)(2,1)S(1)}, u32[]{:S(2)}, u32[]{:S(2)}) %collective-permute-start.45) | collective-permute-done | bytes 131104 | tf_op jit(solution)/shard_map/ppermute | solution.py:284
  171.5 1.7 collective-permute-done.44
  175.9 2.7 %collective-permute-done.48.piece2 = bf16[128,512]{1,0:T(8,128)(2,1)S(1)} collective-permute-done((bf16[128,512]{1,0:T(8,128)(2,1)S(1)}, bf16[128,512]{1,0:T(8,128)(2,1)S(1)}, u32[]{:S(2)}, u32[]{:S(2)}) %collective-permute-start.48) | collective-permute-done | bytes 131104 | tf_op jit(solution)/shard_map/ppermute | solution.py:288
  180.1 3.6 %collective-permute-start.49 = (bf16[512,512]{1,0:T(8,128)(2,1)S(1)}, bf16[512,512]{1,0:T(8,128)(2,1)S(1)}, u32[]{:S(2)}, u32[]{:S(2)}) collective-permute-start(bf16[512,512]{1,0:T(8,128)(2,1)S(1)} %join.7.mine_ref), channel_id=1, source_target_pairs={{0,4},{4,0},{8,12},{12,8},{16,20},{20,16},{24,28},{28,24},{32,36},... | collective-permute-start | bytes 1572872 | tf_op jit(solution)/shard_map/ppermute | solution.py:293
  188.3 1.7 collective-permute-start.51
  191.5 4.7 %collective-permute-done.52 = f16[1200,128]{1,0:T(8,128)(2,1)S(1)} collective-permute-done((f16[1200,128]{1,0:T(8,128)(2,1)S(1)}, f16[1200,128]{1,0:T(8,128)(2,1)S(1)}, u32[]{:S(2)}, u32[]{:S(2)}) %collective-permute-start.52) | collective-permute-done | bytes 307232 | tf_op jit(solution)/shard_map/ppermute | solution.py:299
  196.2 7.2 %collective-permute-done.51 = f16[1200,128]{1,0:T(8,128)(2,1)S(1)} collective-permute-done((f16[1200,128]{1,0:T(8,128)(2,1)S(1)}, f16[1200,128]{1,0:T(8,128)(2,1)S(1)}, u32[]{:S(2)}, u32[]{:S(2)}) %collective-permute-start.51) | collective-permute-done | bytes 307232 | tf_op jit(solution)/shard_map/ppermute | solution.py:299
  203.5 3.0 %mix.3.own_ref = f32[4,1168,128]{2,1,0:T(8,128)S(1)} custom-call(f32[1200,128]{1,0:T(8,128)S(1)} %pack.12.own_ref, f32[1200,128]{1,0:T(8,128)S(1)} %convert_element_type.325.got1, f32[1200,128]{1,0:T(8,128)S(1)} %convert_element_type.327.got3, f32[1200,128]{1,0:T(8,128)S(1)} %convert_element_type.329.got2, bf16[512,256]{1,0:T(8,128)(2,1)S(1)} %pad_maximum_fusion.into_ref, ...), custom_call_target="tpu_custom_call" | custom-call | tf_op jit(solution)/shard_map/mix/pallas_call | solution.py:232
  209.9 3.5 %amplitude.1 = f32[4,1152,128]{2,1,0:T(8,128)} custom-call(s32[1]{0:T(128)} %bitcast.core_ref, bf16[1152,1024]{1,0:T(8,128)(2,1)S(1)} %copy-done.3, bf16[512,512]{1,0:T(8,128)(2,1)S(1)} %join.7.mine_ref, bf16[512,512]{1,0:T(8,128)(2,1)S(1)} %collective-permute-done.49.other_ref, f32[4,1152,128]{2,1,0:T(8,128)S(1)} %get-tuple-element.11.sources_ref, ...), custom_call_target="tpu_custom_call" | custom-call | tf_op jit(solution)/shard_map/amplitude/pallas_call | solution.py:232
  213.4 3.2 %collective-permute-done.55 = f16[1168,128]{1,0:T(8,128)(2,1)S(1)} collective-permute-done((f16[1168,128]{1,0:T(8,128)(2,1)S(1)}, f16[1168,128]{1,0:T(8,128)(2,1)S(1)}, u32[]{:S(2)}, u32[]{:S(2)}) %collective-permute-start.55) | collective-permute-done | bytes 299040 | tf_op jit(solution)/shard_map/ppermute | solution.py:299
  216.7 7.2 %collective-permute-done.54 = f16[1168,128]{1,0:T(8,128)(2,1)S(1)} collective-permute-done((f16[1168,128]{1,0:T(8,128)(2,1)S(1)}, f16[1168,128]{1,0:T(8,128)(2,1)S(1)}, u32[]{:S(2)}, u32[]{:S(2)}) %collective-permute-start.54) | collective-permute-done | bytes 299040 | tf_op jit(solution)/shard_map/ppermute | solution.py:299
  224.0 1.9 unpack.3
  (173 shorter events, 80.4 us)
Async XLA Ops:
  11.5 5.7 %collective-permute-start.1 = (bf16[128,512]{1,0:T(8,128)(2,1)S(1)}, bf16[128,512]{1,0:T(8,128)(2,1)S(1)}, u32[]{:S(2)}, u32[]{:S(2)}) collective-permute-start(bf16[128,512]{1,0:T(8,128)(2,1)S(1)} %get-tuple-element.27), channel_id=1, source_target_pairs={{0,16},{4,68},{8,24},{12,76},{16,0},{20,84},{24,8},{28,92},{32,48}... | collective-permute-start | bytes 393224 | tf_op jit(solution)/shard_map/ppermute | solution.py:280
  14.6 5.3 %collective-permute-start.3 = (bf16[128,512]{1,0:T(8,128)(2,1)S(1)}, bf16[128,512]{1,0:T(8,128)(2,1)S(1)}, u32[]{:S(2)}, u32[]{:S(2)}) collective-permute-start(bf16[128,512]{1,0:T(8,128)(2,1)S(1)} %get-tuple-element.28), channel_id=1, source_target_pairs={{0,24},{4,100},{8,16},{12,108},{16,8},{20,116},{24,0},{28,124},{32... | collective-permute-start | bytes 393224 | tf_op jit(solution)/shard_map/ppermute | solution.py:280
  15.4 4.6 %collective-permute-start.2 = (bf16[128,512]{1,0:T(8,128)(2,1)S(1)}, bf16[128,512]{1,0:T(8,128)(2,1)S(1)}, u32[]{:S(2)}, u32[]{:S(2)}) collective-permute-start(bf16[128,512]{1,0:T(8,128)(2,1)S(1)} %get-tuple-element.29), channel_id=1, source_target_pairs={{0,8},{4,36},{8,0},{12,44},{16,24},{20,52},{24,16},{28,60},{32,40}... | collective-permute-start | bytes 393224 | tf_op jit(solution)/shard_map/ppermute | solution.py:280
  21.1 5.4 %collective-permute-start.6 = (bf16[128,512]{1,0:T(8,128)(2,1)S(1)}, bf16[128,512]{1,0:T(8,128)(2,1)S(1)}, u32[]{:S(2)}, u32[]{:S(2)}) collective-permute-start(bf16[128,512]{1,0:T(8,128)(2,1)S(1)} %add_convert_fusion.7), channel_id=1, source_target_pairs={{0,64},{4,20},{8,72},{12,28},{16,80},{20,4},{24,88},{28,12},{32,96... | collective-permute-start | bytes 393224 | tf_op jit(solution)/shard_map/ppermute | solution.py:284
  23.7 5.0 %collective-permute-start.5 = (bf16[128,512]{1,0:T(8,128)(2,1)S(1)}, bf16[128,512]{1,0:T(8,128)(2,1)S(1)}, u32[]{:S(2)}, u32[]{:S(2)}) collective-permute-start(bf16[128,512]{1,0:T(8,128)(2,1)S(1)} %add_convert_fusion.7), channel_id=1, source_target_pairs={{0,96},{4,28},{8,104},{12,20},{16,112},{20,12},{24,120},{28,4},{32... | collective-permute-start | bytes 393224 | tf_op jit(solution)/shard_map/ppermute | solution.py:284
  28.8 5.4 %collective-permute-start.9 = (bf16[128,512]{1,0:T(8,128)(2,1)S(1)}, bf16[128,512]{1,0:T(8,128)(2,1)S(1)}, u32[]{:S(2)}, u32[]{:S(2)}) collective-permute-start(bf16[128,512]{1,0:T(8,128)(2,1)S(1)} %add_convert_fusion.6.piece0), channel_id=1, source_target_pairs={{0,16},{4,68},{8,24},{12,76},{16,0},{20,84},{24,8},{28,92},{32,48}... | collective-permute-start | bytes 393224 | tf_op jit(solution)/shard_map/ppermute | solution.py:288
  30.5 5.1 %collective-permute-start.8 = (bf16[128,512]{1,0:T(8,128)(2,1)S(1)}, bf16[128,512]{1,0:T(8,128)(2,1)S(1)}, u32[]{:S(2)}, u32[]{:S(2)}) collective-permute-start(bf16[128,512]{1,0:T(8,128)(2,1)S(1)} %add_convert_fusion.6.piece0), channel_id=1, source_target_pairs={{0,24},{4,100},{8,16},{12,108},{16,8},{20,116},{24,0},{28,124},{32... | collective-permute-start | bytes 393224 | tf_op jit(solution)/shard_map/ppermute | solution.py:288
  35.8 6.0 %collective-permute-start.10 = (bf16[512,512]{1,0:T(8,128)(2,1)S(1)}, bf16[512,512]{1,0:T(8,128)(2,1)}, u32[]{:S(2)}, u32[]{:S(2)}) collective-permute-start(bf16[512,512]{1,0:T(8,128)(2,1)S(1)} %join.4.mine_ref), channel_id=1, source_target_pairs={{0,4},{4,0},{8,12},{12,8},{16,20},{20,16},{24,28},{28,24},{32,36},... | collective-permute-start | bytes 1572872 | tf_op jit(solution)/shard_map/ppermute | solution.py:293
  52.5 5.7 %collective-permute-start.12 = (bf16[128,512]{1,0:T(8,128)(2,1)S(1)}, bf16[128,512]{1,0:T(8,128)(2,1)S(1)}, u32[]{:S(2)}, u32[]{:S(2)}) collective-permute-start(bf16[128,512]{1,0:T(8,128)(2,1)S(1)} %get-tuple-element.24), channel_id=1, source_target_pairs={{0,16},{4,68},{8,24},{12,76},{16,0},{20,84},{24,8},{28,92},{32,48}... | collective-permute-start | bytes 393224 | tf_op jit(solution)/shard_map/ppermute | solution.py:280
  53.9 5.8 %collective-permute-start.14 = (bf16[128,512]{1,0:T(8,128)(2,1)S(1)}, bf16[128,512]{1,0:T(8,128)(2,1)S(1)}, u32[]{:S(2)}, u32[]{:S(2)}) collective-permute-start(bf16[128,512]{1,0:T(8,128)(2,1)S(1)} %get-tuple-element.25), channel_id=1, source_target_pairs={{0,24},{4,100},{8,16},{12,108},{16,8},{20,116},{24,0},{28,124},{32... | collective-permute-start | bytes 393224 | tf_op jit(solution)/shard_map/ppermute | solution.py:280
  55.0 4.7 %collective-permute-start.13 = (bf16[128,512]{1,0:T(8,128)(2,1)S(1)}, bf16[128,512]{1,0:T(8,128)(2,1)S(1)}, u32[]{:S(2)}, u32[]{:S(2)}) collective-permute-start(bf16[128,512]{1,0:T(8,128)(2,1)S(1)} %get-tuple-element.26), channel_id=1, source_target_pairs={{0,8},{4,36},{8,0},{12,44},{16,24},{20,52},{24,16},{28,60},{32,40}... | collective-permute-start | bytes 393224 | tf_op jit(solution)/shard_map/ppermute | solution.py:280
  59.7 5.4 %collective-permute-start.17 = (bf16[128,512]{1,0:T(8,128)(2,1)S(1)}, bf16[128,512]{1,0:T(8,128)(2,1)S(1)}, u32[]{:S(2)}, u32[]{:S(2)}) collective-permute-start(bf16[128,512]{1,0:T(8,128)(2,1)S(1)} %add_convert_fusion.5), channel_id=1, source_target_pairs={{0,64},{4,20},{8,72},{12,28},{16,80},{20,4},{24,88},{28,12},{32,96... | collective-permute-start | bytes 393224 | tf_op jit(solution)/shard_map/ppermute | solution.py:284
  61.2 5.6 %collective-permute-start.16 = (bf16[128,512]{1,0:T(8,128)(2,1)S(1)}, bf16[128,512]{1,0:T(8,128)(2,1)S(1)}, u32[]{:S(2)}, u32[]{:S(2)}) collective-permute-start(bf16[128,512]{1,0:T(8,128)(2,1)S(1)} %add_convert_fusion.5), channel_id=1, source_target_pairs={{0,96},{4,28},{8,104},{12,20},{16,112},{20,12},{24,120},{28,4},{32... | collective-permute-start | bytes 393224 | tf_op jit(solution)/shard_map/ppermute | solution.py:284
  62.2 4.6 %collective-permute-start.15 = (bf16[128,512]{1,0:T(8,128)(2,1)S(1)}, bf16[128,512]{1,0:T(8,128)(2,1)S(1)}, u32[]{:S(2)}, u32[]{:S(2)}) collective-permute-start(bf16[128,512]{1,0:T(8,128)(2,1)S(1)} %add_convert_fusion.5), channel_id=1, source_target_pairs={{0,32},{4,12},{8,40},{12,4},{16,48},{20,28},{24,56},{28,20},{32,0}... | collective-permute-start | bytes 393224 | tf_op jit(solution)/shard_map/ppermute | solution.py:284
  66.9 5.5 %collective-permute-start.20 = (bf16[128,512]{1,0:T(8,128)(2,1)S(1)}, bf16[128,512]{1,0:T(8,128)(2,1)S(1)}, u32[]{:S(2)}, u32[]{:S(2)}) collective-permute-start(bf16[128,512]{1,0:T(8,128)(2,1)S(1)} %add_convert_fusion.4.piece0), channel_id=1, source_target_pairs={{0,16},{4,68},{8,24},{12,76},{16,0},{20,84},{24,8},{28,92},{32,48}... | collective-permute-start | bytes 393224 | tf_op jit(solution)/shard_map/ppermute | solution.py:288
  68.1 5.6 %collective-permute-start.19 = (bf16[128,512]{1,0:T(8,128)(2,1)S(1)}, bf16[128,512]{1,0:T(8,128)(2,1)S(1)}, u32[]{:S(2)}, u32[]{:S(2)}) collective-permute-start(bf16[128,512]{1,0:T(8,128)(2,1)S(1)} %add_convert_fusion.4.piece0), channel_id=1, source_target_pairs={{0,24},{4,100},{8,16},{12,108},{16,8},{20,116},{24,0},{28,124},{32... | collective-permute-start | bytes 393224 | tf_op jit(solution)/shard_map/ppermute | solution.py:288
  69.2 4.5 %collective-permute-start.18 = (bf16[128,512]{1,0:T(8,128)(2,1)S(1)}, bf16[128,512]{1,0:T(8,128)(2,1)S(1)}, u32[]{:S(2)}, u32[]{:S(2)}) collective-permute-start(bf16[128,512]{1,0:T(8,128)(2,1)S(1)} %add_convert_fusion.4.piece0), channel_id=1, source_target_pairs={{0,8},{4,36},{8,0},{12,44},{16,24},{20,52},{24,16},{28,60},{32,40}... | collective-permute-start | bytes 393224 | tf_op jit(solution)/shard_map/ppermute | solution.py:288
  73.8 5.2 %collective-permute-start.21 = (bf16[512,512]{1,0:T(8,128)(2,1)S(1)}, bf16[512,512]{1,0:T(8,128)(2,1)S(1)}, u32[]{:S(2)}, u32[]{:S(2)}) collective-permute-start(bf16[512,512]{1,0:T(8,128)(2,1)S(1)} %join.5.mine_ref), channel_id=1, source_target_pairs={{0,4},{4,0},{8,12},{12,8},{16,20},{20,16},{24,28},{28,24},{32,36},... | collective-permute-start | bytes 1572872 | tf_op jit(solution)/shard_map/ppermute | solution.py:293
  79.7 11.2 %collective-permute-start.24 = (f16[1200,128]{1,0:T(8,128)(2,1)S(1)}, f16[1200,128]{1,0:T(8,128)(2,1)S(1)}, u32[]{:S(2)}, u32[]{:S(2)}) collective-permute-start(f16[1200,128]{1,0:T(8,128)(2,1)S(1)} %convert_element_type.288), channel_id=1, source_target_pairs={{0,2},{1,3},{2,0},{3,1},{4,6},{5,7},{6,4},{7,5},{8,10},{9,11},{10,... | collective-permute-start | bytes 921608 | tf_op jit(solution)/shard_map/ppermute | solution.py:299
  85.2 14.2 %collective-permute-start.23 = (f16[1200,128]{1,0:T(8,128)(2,1)S(1)}, f16[1200,128]{1,0:T(8,128)(2,1)S(1)}, u32[]{:S(2)}, u32[]{:S(2)}) collective-permute-start(f16[1200,128]{1,0:T(8,128)(2,1)S(1)} %convert_element_type.286), channel_id=1, source_target_pairs={{0,3},{1,2},{2,1},{3,0},{4,7},{5,6},{6,5},{7,4},{8,11},{9,10},{10,... | collective-permute-start | bytes 921608 | tf_op jit(solution)/shard_map/ppermute | solution.py:299
  85.7 12.2 %collective-permute-start.22 = (f16[1200,128]{1,0:T(8,128)(2,1)S(1)}, f16[1200,128]{1,0:T(8,128)(2,1)S(1)}, u32[]{:S(2)}, u32[]{:S(2)}) collective-permute-start(f16[1200,128]{1,0:T(8,128)(2,1)S(1)} %convert_element_type.284), channel_id=1, source_target_pairs={{0,1},{1,0},{2,3},{3,2},{4,5},{5,4},{6,7},{7,6},{8,9},{9,8},{10,11... | collective-permute-start | bytes 921608 | tf_op jit(solution)/shard_map/ppermute | solution.py:299
  104.3 9.0 %collective-permute-start.27 = (f16[1168,128]{1,0:T(8,128)(2,1)S(1)}, f16[1168,128]{1,0:T(8,128)(2,1)S(1)}, u32[]{:S(2)}, u32[]{:S(2)}) collective-permute-start(f16[1168,128]{1,0:T(8,128)(2,1)S(1)} %get-tuple-element.15), channel_id=1, source_target_pairs={{0,2},{1,3},{2,0},{3,1},{4,6},{5,7},{6,4},{7,5},{8,10},{9,11},{10,... | collective-permute-start | bytes 897032 | tf_op jit(solution)/shard_map/ppermute | solution.py:299
  105.8 15.5 %collective-permute-start.26 = (f16[1168,128]{1,0:T(8,128)(2,1)S(1)}, f16[1168,128]{1,0:T(8,128)(2,1)S(1)}, u32[]{:S(2)}, u32[]{:S(2)}) collective-permute-start(f16[1168,128]{1,0:T(8,128)(2,1)S(1)} %get-tuple-element.16), channel_id=1, source_target_pairs={{0,3},{1,2},{2,1},{3,0},{4,7},{5,6},{6,5},{7,4},{8,11},{9,10},{10,... | collective-permute-start | bytes 897032 | tf_op jit(solution)/shard_map/ppermute | solution.py:299
  107.6 13.8 %collective-permute-start.25 = (f16[1168,128]{1,0:T(8,128)(2,1)S(1)}, f16[1168,128]{1,0:T(8,128)(2,1)S(1)}, u32[]{:S(2)}, u32[]{:S(2)}) collective-permute-start(f16[1168,128]{1,0:T(8,128)(2,1)S(1)} %get-tuple-element.17), channel_id=1, source_target_pairs={{0,1},{1,0},{2,3},{3,2},{4,5},{5,4},{6,7},{7,6},{8,9},{9,8},{10,11... | collective-permute-start | bytes 897032 | tf_op jit(solution)/shard_map/ppermute | solution.py:299
  126.0 5.7 %collective-permute-start.29 = (bf16[128,512]{1,0:T(8,128)(2,1)S(1)}, bf16[128,512]{1,0:T(8,128)(2,1)S(1)}, u32[]{:S(2)}, u32[]{:S(2)}) collective-permute-start(bf16[128,512]{1,0:T(8,128)(2,1)S(1)} %get-tuple-element.21), channel_id=1, source_target_pairs={{0,16},{4,68},{8,24},{12,76},{16,0},{20,84},{24,8},{28,92},{32,48}... | collective-permute-start | bytes 393224 | tf_op jit(solution)/shard_map/ppermute | solution.py:280
  127.9 5.3 %collective-permute-start.31 = (bf16[128,512]{1,0:T(8,128)(2,1)S(1)}, bf16[128,512]{1,0:T(8,128)(2,1)S(1)}, u32[]{:S(2)}, u32[]{:S(2)}) collective-permute-start(bf16[128,512]{1,0:T(8,128)(2,1)S(1)} %get-tuple-element.22), channel_id=1, source_target_pairs={{0,24},{4,100},{8,16},{12,108},{16,8},{20,116},{24,0},{28,124},{32... | collective-permute-start | bytes 393224 | tf_op jit(solution)/shard_map/ppermute | solution.py:280
  133.3 5.4 %collective-permute-start.34 = (bf16[128,512]{1,0:T(8,128)(2,1)S(1)}, bf16[128,512]{1,0:T(8,128)(2,1)S(1)}, u32[]{:S(2)}, u32[]{:S(2)}) collective-permute-start(bf16[128,512]{1,0:T(8,128)(2,1)S(1)} %add_convert_fusion.3), channel_id=1, source_target_pairs={{0,64},{4,20},{8,72},{12,28},{16,80},{20,4},{24,88},{28,12},{32,96... | collective-permute-start | bytes 393224 | tf_op jit(solution)/shard_map/ppermute | solution.py:284
  134.8 5.6 %collective-permute-start.33 = (bf16[128,512]{1,0:T(8,128)(2,1)S(1)}, bf16[128,512]{1,0:T(8,128)(2,1)S(1)}, u32[]{:S(2)}, u32[]{:S(2)}) collective-permute-start(bf16[128,512]{1,0:T(8,128)(2,1)S(1)} %add_convert_fusion.3), channel_id=1, source_target_pairs={{0,96},{4,28},{8,104},{12,20},{16,112},{20,12},{24,120},{28,4},{32... | collective-permute-start | bytes 393224 | tf_op jit(solution)/shard_map/ppermute | solution.py:284
  135.8 4.6 %collective-permute-start.32 = (bf16[128,512]{1,0:T(8,128)(2,1)S(1)}, bf16[128,512]{1,0:T(8,128)(2,1)S(1)}, u32[]{:S(2)}, u32[]{:S(2)}) collective-permute-start(bf16[128,512]{1,0:T(8,128)(2,1)S(1)} %add_convert_fusion.3), channel_id=1, source_target_pairs={{0,32},{4,12},{8,40},{12,4},{16,48},{20,28},{24,56},{28,20},{32,0}... | collective-permute-start | bytes 393224 | tf_op jit(solution)/shard_map/ppermute | solution.py:284
  140.5 5.4 %collective-permute-start.37 = (bf16[128,512]{1,0:T(8,128)(2,1)S(1)}, bf16[128,512]{1,0:T(8,128)(2,1)S(1)}, u32[]{:S(2)}, u32[]{:S(2)}) collective-permute-start(bf16[128,512]{1,0:T(8,128)(2,1)S(1)} %add_convert_fusion.2.piece0), channel_id=1, source_target_pairs={{0,16},{4,68},{8,24},{12,76},{16,0},{20,84},{24,8},{28,92},{32,48}... | collective-permute-start | bytes 393224 | tf_op jit(solution)/shard_map/ppermute | solution.py:288
  141.8 5.4 %collective-permute-start.36 = (bf16[128,512]{1,0:T(8,128)(2,1)S(1)}, bf16[128,512]{1,0:T(8,128)(2,1)S(1)}, u32[]{:S(2)}, u32[]{:S(2)}) collective-permute-start(bf16[128,512]{1,0:T(8,128)(2,1)S(1)} %add_convert_fusion.2.piece0), channel_id=1, source_target_pairs={{0,24},{4,100},{8,16},{12,108},{16,8},{20,116},{24,0},{28,124},{32... | collective-permute-start | bytes 393224 | tf_op jit(solution)/shard_map/ppermute | solution.py:288
  147.3 5.5 %collective-permute-start.38 = (bf16[512,512]{1,0:T(8,128)(2,1)S(1)}, bf16[512,512]{1,0:T(8,128)(2,1)S(1)}, u32[]{:S(2)}, u32[]{:S(2)}) collective-permute-start(bf16[512,512]{1,0:T(8,128)(2,1)S(1)} %join.6.mine_ref), channel_id=1, source_target_pairs={{0,4},{4,0},{8,12},{12,8},{16,20},{20,16},{24,28},{28,24},{32,36},... | collective-permute-start | bytes 1572872 | tf_op jit(solution)/shard_map/ppermute | solution.py:293
  158.6 5.9 %collective-permute-start.40 = (bf16[128,512]{1,0:T(8,128)(2,1)S(1)}, bf16[128,512]{1,0:T(8,128)(2,1)S(1)}, u32[]{:S(2)}, u32[]{:S(2)}) collective-permute-start(bf16[128,512]{1,0:T(8,128)(2,1)S(1)} %get-tuple-element.18), channel_id=1, source_target_pairs={{0,16},{4,68},{8,24},{12,76},{16,0},{20,84},{24,8},{28,92},{32,48}... | collective-permute-start | bytes 393224 | tf_op jit(solution)/shard_map/ppermute | solution.py:280
  160.3 5.6 %collective-permute-start.42 = (bf16[128,512]{1,0:T(8,128)(2,1)S(1)}, bf16[128,512]{1,0:T(8,128)(2,1)S(1)}, u32[]{:S(2)}, u32[]{:S(2)}) collective-permute-start(bf16[128,512]{1,0:T(8,128)(2,1)S(1)} %get-tuple-element.19), channel_id=1, source_target_pairs={{0,24},{4,100},{8,16},{12,108},{16,8},{20,116},{24,0},{28,124},{32... | collective-permute-start | bytes 393224 | tf_op jit(solution)/shard_map/ppermute | solution.py:280
  161.3 4.7 %collective-permute-start.41 = (bf16[128,512]{1,0:T(8,128)(2,1)S(1)}, bf16[128,512]{1,0:T(8,128)(2,1)S(1)}, u32[]{:S(2)}, u32[]{:S(2)}) collective-permute-start(bf16[128,512]{1,0:T(8,128)(2,1)S(1)} %get-tuple-element.20), channel_id=1, source_target_pairs={{0,8},{4,36},{8,0},{12,44},{16,24},{20,52},{24,16},{28,60},{32,40}... | collective-permute-start | bytes 393224 | tf_op jit(solution)/shard_map/ppermute | solution.py:280
  166.0 5.4 %collective-permute-start.45 = (bf16[128,512]{1,0:T(8,128)(2,1)S(1)}, bf16[128,512]{1,0:T(8,128)(2,1)S(1)}, u32[]{:S(2)}, u32[]{:S(2)}) collective-permute-start(bf16[128,512]{1,0:T(8,128)(2,1)S(1)} %add_convert_fusion.1), channel_id=1, source_target_pairs={{0,64},{4,20},{8,72},{12,28},{16,80},{20,4},{24,88},{28,12},{32,96... | collective-permute-start | bytes 393224 | tf_op jit(solution)/shard_map/ppermute | solution.py:284
  167.5 5.6 %collective-permute-start.44 = (bf16[128,512]{1,0:T(8,128)(2,1)S(1)}, bf16[128,512]{1,0:T(8,128)(2,1)S(1)}, u32[]{:S(2)}, u32[]{:S(2)}) collective-permute-start(bf16[128,512]{1,0:T(8,128)(2,1)S(1)} %add_convert_fusion.1), channel_id=1, source_target_pairs={{0,96},{4,28},{8,104},{12,20},{16,112},{20,12},{24,120},{28,4},{32... | collective-permute-start | bytes 393224 | tf_op jit(solution)/shard_map/ppermute | solution.py:284
  168.5 4.6 %collective-permute-start.43 = (bf16[128,512]{1,0:T(8,128)(2,1)S(1)}, bf16[128,512]{1,0:T(8,128)(2,1)S(1)}, u32[]{:S(2)}, u32[]{:S(2)}) collective-permute-start(bf16[128,512]{1,0:T(8,128)(2,1)S(1)} %add_convert_fusion.1), channel_id=1, source_target_pairs={{0,32},{4,12},{8,40},{12,4},{16,48},{20,28},{24,56},{28,20},{32,0}... | collective-permute-start | bytes 393224 | tf_op jit(solution)/shard_map/ppermute | solution.py:284
  173.2 5.4 %collective-permute-start.48 = (bf16[128,512]{1,0:T(8,128)(2,1)S(1)}, bf16[128,512]{1,0:T(8,128)(2,1)S(1)}, u32[]{:S(2)}, u32[]{:S(2)}) collective-permute-start(bf16[128,512]{1,0:T(8,128)(2,1)S(1)} %add_convert_fusion.piece0), channel_id=1, source_target_pairs={{0,16},{4,68},{8,24},{12,76},{16,0},{20,84},{24,8},{28,92},{32,48}... | collective-permute-start | bytes 393224 | tf_op jit(solution)/shard_map/ppermute | solution.py:288
  174.6 5.4 %collective-permute-start.47 = (bf16[128,512]{1,0:T(8,128)(2,1)S(1)}, bf16[128,512]{1,0:T(8,128)(2,1)S(1)}, u32[]{:S(2)}, u32[]{:S(2)}) collective-permute-start(bf16[128,512]{1,0:T(8,128)(2,1)S(1)} %add_convert_fusion.piece0), channel_id=1, source_target_pairs={{0,24},{4,100},{8,16},{12,108},{16,8},{20,116},{24,0},{28,124},{32... | collective-permute-start | bytes 393224 | tf_op jit(solution)/shard_map/ppermute | solution.py:288
  175.5 4.5 %collective-permute-start.46 = (bf16[128,512]{1,0:T(8,128)(2,1)S(1)}, bf16[128,512]{1,0:T(8,128)(2,1)S(1)}, u32[]{:S(2)}, u32[]{:S(2)}) collective-permute-start(bf16[128,512]{1,0:T(8,128)(2,1)S(1)} %add_convert_fusion.piece0), channel_id=1, source_target_pairs={{0,8},{4,36},{8,0},{12,44},{16,24},{20,52},{24,16},{28,60},{32,40}... | collective-permute-start | bytes 393224 | tf_op jit(solution)/shard_map/ppermute | solution.py:288
  180.1 5.2 %collective-permute-start.49 = (bf16[512,512]{1,0:T(8,128)(2,1)S(1)}, bf16[512,512]{1,0:T(8,128)(2,1)S(1)}, u32[]{:S(2)}, u32[]{:S(2)}) collective-permute-start(bf16[512,512]{1,0:T(8,128)(2,1)S(1)} %join.7.mine_ref), channel_id=1, source_target_pairs={{0,4},{4,0},{8,12},{12,8},{16,20},{20,16},{24,28},{28,24},{32,36},... | collective-permute-start | bytes 1572872 | tf_op jit(solution)/shard_map/ppermute | solution.py:293
  186.0 10.1 %collective-permute-start.52 = (f16[1200,128]{1,0:T(8,128)(2,1)S(1)}, f16[1200,128]{1,0:T(8,128)(2,1)S(1)}, u32[]{:S(2)}, u32[]{:S(2)}) collective-permute-start(f16[1200,128]{1,0:T(8,128)(2,1)S(1)} %convert_element_type.328), channel_id=1, source_target_pairs={{0,2},{1,3},{2,0},{3,1},{4,6},{5,7},{6,4},{7,5},{8,10},{9,11},{10,... | collective-permute-start | bytes 921608 | tf_op jit(solution)/shard_map/ppermute | solution.py:299
  188.3 15.1 %collective-permute-start.51 = (f16[1200,128]{1,0:T(8,128)(2,1)S(1)}, f16[1200,128]{1,0:T(8,128)(2,1)S(1)}, u32[]{:S(2)}, u32[]{:S(2)}) collective-permute-start(f16[1200,128]{1,0:T(8,128)(2,1)S(1)} %convert_element_type.326), channel_id=1, source_target_pairs={{0,3},{1,2},{2,1},{3,0},{4,7},{5,6},{6,5},{7,4},{8,11},{9,10},{10,... | collective-permute-start | bytes 921608 | tf_op jit(solution)/shard_map/ppermute | solution.py:299
  190.8 12.7 %collective-permute-start.50 = (f16[1200,128]{1,0:T(8,128)(2,1)S(1)}, f16[1200,128]{1,0:T(8,128)(2,1)S(1)}, u32[]{:S(2)}, u32[]{:S(2)}) collective-permute-start(f16[1200,128]{1,0:T(8,128)(2,1)S(1)} %convert_element_type.324), channel_id=1, source_target_pairs={{0,1},{1,0},{2,3},{3,2},{4,5},{5,4},{6,7},{7,6},{8,9},{9,8},{10,11... | collective-permute-start | bytes 921608 | tf_op jit(solution)/shard_map/ppermute | solution.py:299
  206.8 9.8 %collective-permute-start.55 = (f16[1168,128]{1,0:T(8,128)(2,1)S(1)}, f16[1168,128]{1,0:T(8,128)(2,1)S(1)}, u32[]{:S(2)}, u32[]{:S(2)}) collective-permute-start(f16[1168,128]{1,0:T(8,128)(2,1)S(1)} %get-tuple-element.12), channel_id=1, source_target_pairs={{0,2},{1,3},{2,0},{3,1},{4,6},{5,7},{6,4},{7,5},{8,10},{9,11},{10,... | collective-permute-start | bytes 897032 | tf_op jit(solution)/shard_map/ppermute | solution.py:299
  208.3 15.5 %collective-permute-start.54 = (f16[1168,128]{1,0:T(8,128)(2,1)S(1)}, f16[1168,128]{1,0:T(8,128)(2,1)S(1)}, u32[]{:S(2)}, u32[]{:S(2)}) collective-permute-start(f16[1168,128]{1,0:T(8,128)(2,1)S(1)} %get-tuple-element.13), channel_id=1, source_target_pairs={{0,3},{1,2},{2,1},{3,0},{4,7},{5,6},{6,5},{7,4},{8,11},{9,10},{10,... | collective-permute-start | bytes 897032 | tf_op jit(solution)/shard_map/ppermute | solution.py:299
  209.9 14.0 %collective-permute-start.53 = (f16[1168,128]{1,0:T(8,128)(2,1)S(1)}, f16[1168,128]{1,0:T(8,128)(2,1)S(1)}, u32[]{:S(2)}, u32[]{:S(2)}) collective-permute-start(f16[1168,128]{1,0:T(8,128)(2,1)S(1)} %get-tuple-element.14), channel_id=1, source_target_pairs={{0,1},{1,0},{2,3},{3,2},{4,5},{5,4},{6,7},{7,6},{8,9},{9,8},{10,11... | collective-permute-start | bytes 897032 | tf_op jit(solution)/shard_map/ppermute | solution.py:299
  (23 other events, 197.5 us)

commit v11 on v9

--- a/solution.py
+++ b/solution.py
@@ -102,10 +102,11 @@
             tile = value[g * RUN : (g + 1) * RUN]
             sent_ref[(g * nf + f) * RUN : (g * nf + f + 1) * RUN, :] = tile
             peak = jnp.maximum(peak, jnp.abs(tile))
-    kernel = kernel_ref[there]
-    high = kernel.astype(BF16).astype(F32)
-    sent_ref[body + RUN : body + 2 * RUN, :] = high
-    sent_ref[body + 2 * RUN :, :] = kernel - high
+    if sent_ref.shape[0] > body + RUN:
+        kernel = kernel_ref[there]
+        high = kernel.astype(BF16).astype(F32)
+        sent_ref[body + RUN : body + 2 * RUN, :] = high
+        sent_ref[body + 2 * RUN :, :] = kernel - high
     if d:
         peak = jnp.max(jnp.max(peak, axis=0, keepdims=True), axis=1, keepdims=True)
         power, scale = scale_of(jnp.broadcast_to(peak, (1, cols)))
@@ -331,7 +332,7 @@
         sent = {}
         for d in (*PARTNERS, 0):
             (value,) = call(
-                partial(pack_body, d), [((body + 3 * RUN, cols), F32)], "pack", 10, 2,
+                partial(pack_body, d), [((body + (1 if outer else 3) * RUN, cols), F32)], "pack", 10, 2,
                 (core_at, place_z, factors, *parts, sources, column, kernel),
                 whole,
             )

time: 225 us -> 225 us (level)
  no operation moved by 1% of the time
where the time goes in v11:
time: 225 us
  waiting for transfers between devices  106 us (47%)
  starting transfers between devices  67.9 us (30%)
  Pallas kernels  28.6 us (13%)
  matrix products  11.1 us (5%)
  local copies, waits for them, and re-layouts  6.9 us (3%)
  other arithmetic  2.67 us (1%)
    ppermute x12, waiting for transfers between devices, exchange(): got[d] = lax.ppermute(sent[d].astype(F16), 'freq', swap(d)).astype(F32)  43.9 us
    pallas_call x24, Pallas kernels, call(): pl.pallas_call(body, out_shape=[jax.ShapeDtypeStruct(s, t) for s, t in ou...  28.6 us
    ppermute x12, waiting for transfers between devices, reduce_all(): own = own + lax.ppermute(piece, 'fac', along(d, True)).astype(F32)  17.7 us
    ppermute x12, waiting for transfers between devices, reduce_all(): total = total + lax.ppermute(own, 'fac', along(d, False)).astype(F32)  17.1 us
    ppermute x12, waiting for transfers between devices, reduce_all(): pieces[d] = lax.ppermute(total, 'fac', along(d, True))  15.8 us
    ppermute x4, starting transfers between devices, reduce_all(): other = lax.ppermute(gathered, 'fac', CORES)  15.6 us
    ppermute x12, starting transfers between devices, exchange(): got[d] = lax.ppermute(sent[d].astype(F16), 'freq', swap(d)).astype(F32)  14.2 us
    ppermute x12, starting transfers between devices, reduce_all(): own = own + lax.ppermute(piece, 'fac', along(d, True)).astype(F32)  12.3 us
  transfers between devices with their start and end apart: 56, of which 41 were waited for; matrix products, arithmetic and copies ran while one was open for 1% of the time, Pallas kernels for 5%

profile of v11, /device:TPU:1, one launch (start us, length us, event | category | flops | bytes accessed | tf_op | source)
XLA Modules:
  0.0 224.8 jit_solution(17986601378522514332)
XLA Ops:
  0.7 1.7 copy-done.3
  4.0 1.7 convolution_convert_fusion.3
  7.1 1.9 collective-permute-done
  9.0 2.9 %convert_add_fusion = f32[512,512]{1,0:T(8,128)} fusion(bf16[512,512]{1,0:T(8,128)(2,1)} %collective-permute-done, bf16[1152,512]{1,0:T(8,128)(2,1)S(1)} %round.1, bf16[1152,1024]{1,0:T(8,128)(2,1)S(1)} %copy-done.2, s32[]{:T(128)S(6)} %select_n.105), kind=kOutput, calls=%fused_computation.9 | convolution fusion | flops 604504064 | bytes 3932164 | tf_op jit(solution)/shard_map/dot_general | solution.py:258
  13.0 3.1 %collective-permute-start.1 = (bf16[128,512]{1,0:T(8,128)(2,1)S(1)}, bf16[128,512]{1,0:T(8,128)(2,1)S(1)}, u32[]{:S(2)}, u32[]{:S(2)}) collective-permute-start(bf16[128,512]{1,0:T(8,128)(2,1)S(1)} %get-tuple-element.21), channel_id=1, source_target_pairs={{0,16},{4,68},{8,24},{12,76},{16,0},{20,84},{24,8},{28,92},{32,48}... | collective-permute-start | bytes 393224 | tf_op jit(solution)/shard_map/ppermute | solution.py:271
  16.9 1.9 collective-permute-done.1
  18.8 2.7 %collective-permute-done.3 = bf16[128,512]{1,0:T(8,128)(2,1)S(1)} collective-permute-done((bf16[128,512]{1,0:T(8,128)(2,1)S(1)}, bf16[128,512]{1,0:T(8,128)(2,1)S(1)}, u32[]{:S(2)}, u32[]{:S(2)}) %collective-permute-start.3) | collective-permute-done | bytes 131104 | tf_op jit(solution)/shard_map/ppermute | solution.py:271
  22.4 2.5 %collective-permute-start.6 = (bf16[128,512]{1,0:T(8,128)(2,1)S(1)}, bf16[128,512]{1,0:T(8,128)(2,1)S(1)}, u32[]{:S(2)}, u32[]{:S(2)}) collective-permute-start(bf16[128,512]{1,0:T(8,128)(2,1)S(1)} %add_convert_fusion.7), channel_id=1, source_target_pairs={{0,64},{4,20},{8,72},{12,28},{16,80},{20,4},{24,88},{28,12},{32,96... | collective-permute-start | bytes 393224 | tf_op jit(solution)/shard_map/ppermute | solution.py:275
  25.8 2.0 collective-permute-done.6
  27.9 2.2 collective-permute-done.5
  30.1 1.7 collective-permute-start.9
  33.2 2.3 %collective-permute-done.9.piece2 = bf16[128,512]{1,0:T(8,128)(2,1)S(1)} collective-permute-done((bf16[128,512]{1,0:T(8,128)(2,1)S(1)}, bf16[128,512]{1,0:T(8,128)(2,1)S(1)}, u32[]{:S(2)}, u32[]{:S(2)}) %collective-permute-start.9) | collective-permute-done | bytes 131104 | tf_op jit(solution)/shard_map/ppermute | solution.py:279
  37.1 4.3 %collective-permute-start.10 = (bf16[512,512]{1,0:T(8,128)(2,1)S(1)}, bf16[512,512]{1,0:T(8,128)(2,1)}, u32[]{:S(2)}, u32[]{:S(2)}) collective-permute-start(bf16[512,512]{1,0:T(8,128)(2,1)S(1)} %join.4.mine_ref), channel_id=1, source_target_pairs={{0,4},{4,0},{8,12},{12,8},{16,20},{20,16},{24,28},{28,24},{32,36},... | collective-permute-start | bytes 1572872 | tf_op jit(solution)/shard_map/ppermute | solution.py:284
  43.1 1.7 copy-done.4
  44.7 3.1 %ladder.2 = bf16[1152,512]{1,0:T(8,128)(2,1)S(1)} custom-call(s32[1]{0:T(128)} %bitcast.core_ref, bf16[1152,1024]{1,0:T(8,128)(2,1)S(1)} %copy-done.2, bf16[512,512]{1,0:T(8,128)(2,1)S(1)} %join.4.mine_ref, bf16[512,512]{1,0:T(8,128)(2,1)} %collective-permute-done.10.other_ref, f32[4,1152,128]{2,1,0:T(8,128)S(1)} %copy-done.4, f32[1152,4]{1,0:T(8,128)S(1)} %bitcast.31), custom_call_target="tpu_custom_call" | custom-call | tf_op jit(solution)/shard_map/ladder/pallas_call | solution.py:229
  54.4 3.0 %collective-permute-done.12 = bf16[128,512]{1,0:T(8,128)(2,1)S(1)} collective-permute-done((bf16[128,512]{1,0:T(8,128)(2,1)S(1)}, bf16[128,512]{1,0:T(8,128)(2,1)S(1)}, u32[]{:S(2)}, u32[]{:S(2)}) %collective-permute-start.12) | collective-permute-done | bytes 131104 | tf_op jit(solution)/shard_map/ppermute | solution.py:271
  61.8 2.5 %collective-permute-done.17 = bf16[128,512]{1,0:T(8,128)(2,1)S(1)} collective-permute-done((bf16[128,512]{1,0:T(8,128)(2,1)S(1)}, bf16[128,512]{1,0:T(8,128)(2,1)S(1)}, u32[]{:S(2)}, u32[]{:S(2)}) %collective-permute-start.17) | collective-permute-done | bytes 131104 | tf_op jit(solution)/shard_map/ppermute | solution.py:275
  64.3 1.7 collective-permute-done.16
  69.0 2.5 %collective-permute-done.20.piece2 = bf16[128,512]{1,0:T(8,128)(2,1)S(1)} collective-permute-done((bf16[128,512]{1,0:T(8,128)(2,1)S(1)}, bf16[128,512]{1,0:T(8,128)(2,1)S(1)}, u32[]{:S(2)}, u32[]{:S(2)}) %collective-permute-start.20) | collective-permute-done | bytes 131104 | tf_op jit(solution)/shard_map/ppermute | solution.py:279
  72.9 3.7 %collective-permute-start.21 = (bf16[512,512]{1,0:T(8,128)(2,1)S(1)}, bf16[512,512]{1,0:T(8,128)(2,1)S(1)}, u32[]{:S(2)}, u32[]{:S(2)}) collective-permute-start(bf16[512,512]{1,0:T(8,128)(2,1)S(1)} %join.5.mine_ref), channel_id=1, source_target_pairs={{0,4},{4,0},{8,12},{12,8},{16,20},{20,16},{24,28},{28,24},{32,36},... | collective-permute-start | bytes 1572872 | tf_op jit(solution)/shard_map/ppermute | solution.py:284
  78.9 3.8 %collective-permute-start.24 = (f16[1200,128]{1,0:T(8,128)(2,1)S(1)}, f16[1200,128]{1,0:T(8,128)(2,1)S(1)}, u32[]{:S(2)}, u32[]{:S(2)}) collective-permute-start(f16[1200,128]{1,0:T(8,128)(2,1)S(1)} %convert_element_type.288), channel_id=1, source_target_pairs={{0,2},{1,3},{2,0},{3,1},{4,6},{5,7},{6,4},{7,5},{8,10},{9,11},{10,... | collective-permute-start | bytes 921608 | tf_op jit(solution)/shard_map/ppermute | solution.py:290
  87.6 2.5 %collective-permute-done.24 = f16[1200,128]{1,0:T(8,128)(2,1)S(1)} collective-permute-done((f16[1200,128]{1,0:T(8,128)(2,1)S(1)}, f16[1200,128]{1,0:T(8,128)(2,1)S(1)}, u32[]{:S(2)}, u32[]{:S(2)}) %collective-permute-start.24) | collective-permute-done | bytes 307232 | tf_op jit(solution)/shard_map/ppermute | solution.py:290
  91.6 5.5 %collective-permute-done.22 = f16[1200,128]{1,0:T(8,128)(2,1)S(1)} collective-permute-done((f16[1200,128]{1,0:T(8,128)(2,1)S(1)}, f16[1200,128]{1,0:T(8,128)(2,1)S(1)}, u32[]{:S(2)}, u32[]{:S(2)}) %collective-permute-start.22) | collective-permute-done | bytes 307232 | tf_op jit(solution)/shard_map/ppermute | solution.py:290
  100.1 3.0 %mix.2.own_ref = f32[4,1168,128]{2,1,0:T(8,128)S(1)} custom-call(f32[1200,128]{1,0:T(8,128)S(1)} %pack.8.table_ref.own_ref, f32[1200,128]{1,0:T(8,128)S(1)} %convert_element_type.285.table_ref.got1, f32[1200,128]{1,0:T(8,128)S(1)} %convert_element_type.287.table_ref.got3, f32[1200,128]{1,0:T(8,128)S(1)} %convert_element_type.289.table_ref.got2, ...), custom_call_target="tpu_custom_call" | custom-call | tf_op jit(solution)/shard_map/mix/pallas_call | solution.py:229
  105.0 1.7 collective-permute-start.26
  106.8 5.8 %collective-permute-done.27 = f16[1168,128]{1,0:T(8,128)(2,1)S(1)} collective-permute-done((f16[1168,128]{1,0:T(8,128)(2,1)S(1)}, f16[1168,128]{1,0:T(8,128)(2,1)S(1)}, u32[]{:S(2)}, u32[]{:S(2)}) %collective-permute-start.27) | collective-permute-done | bytes 299040 | tf_op jit(solution)/shard_map/ppermute | solution.py:290
  112.6 8.0 %collective-permute-done.26 = f16[1168,128]{1,0:T(8,128)(2,1)S(1)} collective-permute-done((f16[1168,128]{1,0:T(8,128)(2,1)S(1)}, f16[1168,128]{1,0:T(8,128)(2,1)S(1)}, u32[]{:S(2)}, u32[]{:S(2)}) %collective-permute-start.26) | collective-permute-done | bytes 299040 | tf_op jit(solution)/shard_map/ppermute | solution.py:290
  125.2 1.8 collective-permute-start.29
  128.0 2.9 %collective-permute-done.29 = bf16[128,512]{1,0:T(8,128)(2,1)S(1)} collective-permute-done((bf16[128,512]{1,0:T(8,128)(2,1)S(1)}, bf16[128,512]{1,0:T(8,128)(2,1)S(1)}, u32[]{:S(2)}, u32[]{:S(2)}) %collective-permute-start.29) | collective-permute-done | bytes 131104 | tf_op jit(solution)/shard_map/ppermute | solution.py:271
  135.2 2.7 %collective-permute-done.34 = bf16[128,512]{1,0:T(8,128)(2,1)S(1)} collective-permute-done((bf16[128,512]{1,0:T(8,128)(2,1)S(1)}, bf16[128,512]{1,0:T(8,128)(2,1)S(1)}, u32[]{:S(2)}, u32[]{:S(2)}) %collective-permute-start.34) | collective-permute-done | bytes 131104 | tf_op jit(solution)/shard_map/ppermute | solution.py:275
  137.9 1.7 collective-permute-done.33
  142.4 2.7 %collective-permute-done.37.piece2 = bf16[128,512]{1,0:T(8,128)(2,1)S(1)} collective-permute-done((bf16[128,512]{1,0:T(8,128)(2,1)S(1)}, bf16[128,512]{1,0:T(8,128)(2,1)S(1)}, u32[]{:S(2)}, u32[]{:S(2)}) %collective-permute-start.37) | collective-permute-done | bytes 131104 | tf_op jit(solution)/shard_map/ppermute | solution.py:279
  146.5 3.9 %collective-permute-start.38 = (bf16[512,512]{1,0:T(8,128)(2,1)S(1)}, bf16[512,512]{1,0:T(8,128)(2,1)S(1)}, u32[]{:S(2)}, u32[]{:S(2)}) collective-permute-start(bf16[512,512]{1,0:T(8,128)(2,1)S(1)} %join.6.mine_ref), channel_id=1, source_target_pairs={{0,4},{4,0},{8,12},{12,8},{16,20},{20,16},{24,28},{28,24},{32,36},... | collective-permute-start | bytes 1572872 | tf_op jit(solution)/shard_map/ppermute | solution.py:284
  152.0 2.0 ladder.3
  157.8 1.7 collective-permute-start.40
  160.7 3.0 %collective-permute-done.40 = bf16[128,512]{1,0:T(8,128)(2,1)S(1)} collective-permute-done((bf16[128,512]{1,0:T(8,128)(2,1)S(1)}, bf16[128,512]{1,0:T(8,128)(2,1)S(1)}, u32[]{:S(2)}, u32[]{:S(2)}) %collective-permute-start.40) | collective-permute-done | bytes 131104 | tf_op jit(solution)/shard_map/ppermute | solution.py:271
  167.9 2.7 %collective-permute-done.45 = bf16[128,512]{1,0:T(8,128)(2,1)S(1)} collective-permute-done((bf16[128,512]{1,0:T(8,128)(2,1)S(1)}, bf16[128,512]{1,0:T(8,128)(2,1)S(1)}, u32[]{:S(2)}, u32[]{:S(2)}) %collective-permute-start.45) | collective-permute-done | bytes 131104 | tf_op jit(solution)/shard_map/ppermute | solution.py:275
  170.6 1.7 collective-permute-done.44
  175.1 2.7 %collective-permute-done.48.piece2 = bf16[128,512]{1,0:T(8,128)(2,1)S(1)} collective-permute-done((bf16[128,512]{1,0:T(8,128)(2,1)S(1)}, bf16[128,512]{1,0:T(8,128)(2,1)S(1)}, u32[]{:S(2)}, u32[]{:S(2)}) %collective-permute-start.48) | collective-permute-done | bytes 131104 | tf_op jit(solution)/shard_map/ppermute | solution.py:279
  179.2 3.7 %collective-permute-start.49 = (bf16[512,512]{1,0:T(8,128)(2,1)S(1)}, bf16[512,512]{1,0:T(8,128)(2,1)S(1)}, u32[]{:S(2)}, u32[]{:S(2)}) collective-permute-start(bf16[512,512]{1,0:T(8,128)(2,1)S(1)} %join.7.mine_ref), channel_id=1, source_target_pairs={{0,4},{4,0},{8,12},{12,8},{16,20},{20,16},{24,28},{28,24},{32,36},... | collective-permute-start | bytes 1572872 | tf_op jit(solution)/shard_map/ppermute | solution.py:284
  187.5 1.7 collective-permute-start.51
  190.6 4.6 %collective-permute-done.52 = f16[1168,128]{1,0:T(8,128)(2,1)S(1)} collective-permute-done((f16[1168,128]{1,0:T(8,128)(2,1)S(1)}, f16[1168,128]{1,0:T(8,128)(2,1)S(1)}, u32[]{:S(2)}, u32[]{:S(2)}) %collective-permute-start.52) | collective-permute-done | bytes 299040 | tf_op jit(solution)/shard_map/ppermute | solution.py:290
  195.2 7.0 %collective-permute-done.51 = f16[1168,128]{1,0:T(8,128)(2,1)S(1)} collective-permute-done((f16[1168,128]{1,0:T(8,128)(2,1)S(1)}, f16[1168,128]{1,0:T(8,128)(2,1)S(1)}, u32[]{:S(2)}, u32[]{:S(2)}) %collective-permute-start.51) | collective-permute-done | bytes 299040 | tf_op jit(solution)/shard_map/ppermute | solution.py:290
  202.4 3.0 %mix.3.own_ref = f32[4,1168,128]{2,1,0:T(8,128)S(1)} custom-call(f32[1168,128]{1,0:T(8,128)S(1)} %pack.12.own_ref, f32[1168,128]{1,0:T(8,128)S(1)} %convert_element_type.325.got1, f32[1168,128]{1,0:T(8,128)S(1)} %convert_element_type.327.got3, f32[1168,128]{1,0:T(8,128)S(1)} %convert_element_type.329.got2, bf16[512,256]{1,0:T(8,128)(2,1)S(1)} %pad_maximum_fusion.into_ref, ...), custom_call_target="tpu_custom_call" | custom-call | tf_op jit(solution)/shard_map/mix/pallas_call | solution.py:229
  208.7 3.4 %amplitude.1 = f32[4,1152,128]{2,1,0:T(8,128)} custom-call(s32[1]{0:T(128)} %bitcast.core_ref, bf16[1152,1024]{1,0:T(8,128)(2,1)S(1)} %copy-done.2, bf16[512,512]{1,0:T(8,128)(2,1)S(1)} %join.7.mine_ref, bf16[512,512]{1,0:T(8,128)(2,1)S(1)} %collective-permute-done.49.other_ref, f32[4,1152,128]{2,1,0:T(8,128)S(1)} %get-tuple-element.5.sources_ref, ...), custom_call_target="tpu_custom_call" | custom-call | tf_op jit(solution)/shard_map/amplitude/pallas_call | solution.py:229
  212.2 3.3 %collective-permute-done.55 = f16[1168,128]{1,0:T(8,128)(2,1)S(1)} collective-permute-done((f16[1168,128]{1,0:T(8,128)(2,1)S(1)}, f16[1168,128]{1,0:T(8,128)(2,1)S(1)}, u32[]{:S(2)}, u32[]{:S(2)}) %collective-permute-start.55) | collective-permute-done | bytes 299040 | tf_op jit(solution)/shard_map/ppermute | solution.py:290
  215.5 7.2 %collective-permute-done.54 = f16[1168,128]{1,0:T(8,128)(2,1)S(1)} collective-permute-done((f16[1168,128]{1,0:T(8,128)(2,1)S(1)}, f16[1168,128]{1,0:T(8,128)(2,1)S(1)}, u32[]{:S(2)}, u32[]{:S(2)}) %collective-permute-start.54) | collective-permute-done | bytes 299040 | tf_op jit(solution)/shard_map/ppermute | solution.py:290
  222.8 1.9 unpack.3
  (161 shorter events, 79.0 us)
Async XLA Ops:
  13.0 5.7 %collective-permute-start.1 = (bf16[128,512]{1,0:T(8,128)(2,1)S(1)}, bf16[128,512]{1,0:T(8,128)(2,1)S(1)}, u32[]{:S(2)}, u32[]{:S(2)}) collective-permute-start(bf16[128,512]{1,0:T(8,128)(2,1)S(1)} %get-tuple-element.21), channel_id=1, source_target_pairs={{0,16},{4,68},{8,24},{12,76},{16,0},{20,84},{24,8},{28,92},{32,48}... | collective-permute-start | bytes 393224 | tf_op jit(solution)/shard_map/ppermute | solution.py:271
  16.1 5.3 %collective-permute-start.3 = (bf16[128,512]{1,0:T(8,128)(2,1)S(1)}, bf16[128,512]{1,0:T(8,128)(2,1)S(1)}, u32[]{:S(2)}, u32[]{:S(2)}) collective-permute-start(bf16[128,512]{1,0:T(8,128)(2,1)S(1)} %get-tuple-element.22), channel_id=1, source_target_pairs={{0,24},{4,100},{8,16},{12,108},{16,8},{20,116},{24,0},{28,124},{32... | collective-permute-start | bytes 393224 | tf_op jit(solution)/shard_map/ppermute | solution.py:271
  16.9 4.6 %collective-permute-start.2 = (bf16[128,512]{1,0:T(8,128)(2,1)S(1)}, bf16[128,512]{1,0:T(8,128)(2,1)S(1)}, u32[]{:S(2)}, u32[]{:S(2)}) collective-permute-start(bf16[128,512]{1,0:T(8,128)(2,1)S(1)} %get-tuple-element.23), channel_id=1, source_target_pairs={{0,8},{4,36},{8,0},{12,44},{16,24},{20,52},{24,16},{28,60},{32,40}... | collective-permute-start | bytes 393224 | tf_op jit(solution)/shard_map/ppermute | solution.py:271
  22.4 5.4 %collective-permute-start.6 = (bf16[128,512]{1,0:T(8,128)(2,1)S(1)}, bf16[128,512]{1,0:T(8,128)(2,1)S(1)}, u32[]{:S(2)}, u32[]{:S(2)}) collective-permute-start(bf16[128,512]{1,0:T(8,128)(2,1)S(1)} %add_convert_fusion.7), channel_id=1, source_target_pairs={{0,64},{4,20},{8,72},{12,28},{16,80},{20,4},{24,88},{28,12},{32,96... | collective-permute-start | bytes 393224 | tf_op jit(solution)/shard_map/ppermute | solution.py:275
  25.0 5.0 %collective-permute-start.5 = (bf16[128,512]{1,0:T(8,128)(2,1)S(1)}, bf16[128,512]{1,0:T(8,128)(2,1)S(1)}, u32[]{:S(2)}, u32[]{:S(2)}) collective-permute-start(bf16[128,512]{1,0:T(8,128)(2,1)S(1)} %add_convert_fusion.7), channel_id=1, source_target_pairs={{0,96},{4,28},{8,104},{12,20},{16,112},{20,12},{24,120},{28,4},{32... | collective-permute-start | bytes 393224 | tf_op jit(solution)/shard_map/ppermute | solution.py:275
  30.1 5.4 %collective-permute-start.9 = (bf16[128,512]{1,0:T(8,128)(2,1)S(1)}, bf16[128,512]{1,0:T(8,128)(2,1)S(1)}, u32[]{:S(2)}, u32[]{:S(2)}) collective-permute-start(bf16[128,512]{1,0:T(8,128)(2,1)S(1)} %add_convert_fusion.6.piece0), channel_id=1, source_target_pairs={{0,16},{4,68},{8,24},{12,76},{16,0},{20,84},{24,8},{28,92},{32,48}... | collective-permute-start | bytes 393224 | tf_op jit(solution)/shard_map/ppermute | solution.py:279
  31.8 5.1 %collective-permute-start.8 = (bf16[128,512]{1,0:T(8,128)(2,1)S(1)}, bf16[128,512]{1,0:T(8,128)(2,1)S(1)}, u32[]{:S(2)}, u32[]{:S(2)}) collective-permute-start(bf16[128,512]{1,0:T(8,128)(2,1)S(1)} %add_convert_fusion.6.piece0), channel_id=1, source_target_pairs={{0,24},{4,100},{8,16},{12,108},{16,8},{20,116},{24,0},{28,124},{32... | collective-permute-start | bytes 393224 | tf_op jit(solution)/shard_map/ppermute | solution.py:279
  37.1 6.0 %collective-permute-start.10 = (bf16[512,512]{1,0:T(8,128)(2,1)S(1)}, bf16[512,512]{1,0:T(8,128)(2,1)}, u32[]{:S(2)}, u32[]{:S(2)}) collective-permute-start(bf16[512,512]{1,0:T(8,128)(2,1)S(1)} %join.4.mine_ref), channel_id=1, source_target_pairs={{0,4},{4,0},{8,12},{12,8},{16,20},{20,16},{24,28},{28,24},{32,36},... | collective-permute-start | bytes 1572872 | tf_op jit(solution)/shard_map/ppermute | solution.py:284
  51.7 5.7 %collective-permute-start.12 = (bf16[128,512]{1,0:T(8,128)(2,1)S(1)}, bf16[128,512]{1,0:T(8,128)(2,1)S(1)}, u32[]{:S(2)}, u32[]{:S(2)}) collective-permute-start(bf16[128,512]{1,0:T(8,128)(2,1)S(1)} %get-tuple-element.18), channel_id=1, source_target_pairs={{0,16},{4,68},{8,24},{12,76},{16,0},{20,84},{24,8},{28,92},{32,48}... | collective-permute-start | bytes 393224 | tf_op jit(solution)/shard_map/ppermute | solution.py:271
  53.0 5.8 %collective-permute-start.14 = (bf16[128,512]{1,0:T(8,128)(2,1)S(1)}, bf16[128,512]{1,0:T(8,128)(2,1)S(1)}, u32[]{:S(2)}, u32[]{:S(2)}) collective-permute-start(bf16[128,512]{1,0:T(8,128)(2,1)S(1)} %get-tuple-element.19), channel_id=1, source_target_pairs={{0,24},{4,100},{8,16},{12,108},{16,8},{20,116},{24,0},{28,124},{32... | collective-permute-start | bytes 393224 | tf_op jit(solution)/shard_map/ppermute | solution.py:271
  54.1 4.7 %collective-permute-start.13 = (bf16[128,512]{1,0:T(8,128)(2,1)S(1)}, bf16[128,512]{1,0:T(8,128)(2,1)S(1)}, u32[]{:S(2)}, u32[]{:S(2)}) collective-permute-start(bf16[128,512]{1,0:T(8,128)(2,1)S(1)} %get-tuple-element.20), channel_id=1, source_target_pairs={{0,8},{4,36},{8,0},{12,44},{16,24},{20,52},{24,16},{28,60},{32,40}... | collective-permute-start | bytes 393224 | tf_op jit(solution)/shard_map/ppermute | solution.py:271
  58.9 5.4 %collective-permute-start.17 = (bf16[128,512]{1,0:T(8,128)(2,1)S(1)}, bf16[128,512]{1,0:T(8,128)(2,1)S(1)}, u32[]{:S(2)}, u32[]{:S(2)}) collective-permute-start(bf16[128,512]{1,0:T(8,128)(2,1)S(1)} %add_convert_fusion.5), channel_id=1, source_target_pairs={{0,64},{4,20},{8,72},{12,28},{16,80},{20,4},{24,88},{28,12},{32,96... | collective-permute-start | bytes 393224 | tf_op jit(solution)/shard_map/ppermute | solution.py:275
  60.4 5.6 %collective-permute-start.16 = (bf16[128,512]{1,0:T(8,128)(2,1)S(1)}, bf16[128,512]{1,0:T(8,128)(2,1)S(1)}, u32[]{:S(2)}, u32[]{:S(2)}) collective-permute-start(bf16[128,512]{1,0:T(8,128)(2,1)S(1)} %add_convert_fusion.5), channel_id=1, source_target_pairs={{0,96},{4,28},{8,104},{12,20},{16,112},{20,12},{24,120},{28,4},{32... | collective-permute-start | bytes 393224 | tf_op jit(solution)/shard_map/ppermute | solution.py:275
  61.3 4.6 %collective-permute-start.15 = (bf16[128,512]{1,0:T(8,128)(2,1)S(1)}, bf16[128,512]{1,0:T(8,128)(2,1)S(1)}, u32[]{:S(2)}, u32[]{:S(2)}) collective-permute-start(bf16[128,512]{1,0:T(8,128)(2,1)S(1)} %add_convert_fusion.5), channel_id=1, source_target_pairs={{0,32},{4,12},{8,40},{12,4},{16,48},{20,28},{24,56},{28,20},{32,0}... | collective-permute-start | bytes 393224 | tf_op jit(solution)/shard_map/ppermute | solution.py:275
  66.0 5.5 %collective-permute-start.20 = (bf16[128,512]{1,0:T(8,128)(2,1)S(1)}, bf16[128,512]{1,0:T(8,128)(2,1)S(1)}, u32[]{:S(2)}, u32[]{:S(2)}) collective-permute-start(bf16[128,512]{1,0:T(8,128)(2,1)S(1)} %add_convert_fusion.4.piece0), channel_id=1, source_target_pairs={{0,16},{4,68},{8,24},{12,76},{16,0},{20,84},{24,8},{28,92},{32,48}... | collective-permute-start | bytes 393224 | tf_op jit(solution)/shard_map/ppermute | solution.py:279
  67.3 5.6 %collective-permute-start.19 = (bf16[128,512]{1,0:T(8,128)(2,1)S(1)}, bf16[128,512]{1,0:T(8,128)(2,1)S(1)}, u32[]{:S(2)}, u32[]{:S(2)}) collective-permute-start(bf16[128,512]{1,0:T(8,128)(2,1)S(1)} %add_convert_fusion.4.piece0), channel_id=1, source_target_pairs={{0,24},{4,100},{8,16},{12,108},{16,8},{20,116},{24,0},{28,124},{32... | collective-permute-start | bytes 393224 | tf_op jit(solution)/shard_map/ppermute | solution.py:279
  68.4 4.5 %collective-permute-start.18 = (bf16[128,512]{1,0:T(8,128)(2,1)S(1)}, bf16[128,512]{1,0:T(8,128)(2,1)S(1)}, u32[]{:S(2)}, u32[]{:S(2)}) collective-permute-start(bf16[128,512]{1,0:T(8,128)(2,1)S(1)} %add_convert_fusion.4.piece0), channel_id=1, source_target_pairs={{0,8},{4,36},{8,0},{12,44},{16,24},{20,52},{24,16},{28,60},{32,40}... | collective-permute-start | bytes 393224 | tf_op jit(solution)/shard_map/ppermute | solution.py:279
  72.9 5.2 %collective-permute-start.21 = (bf16[512,512]{1,0:T(8,128)(2,1)S(1)}, bf16[512,512]{1,0:T(8,128)(2,1)S(1)}, u32[]{:S(2)}, u32[]{:S(2)}) collective-permute-start(bf16[512,512]{1,0:T(8,128)(2,1)S(1)} %join.5.mine_ref), channel_id=1, source_target_pairs={{0,4},{4,0},{8,12},{12,8},{16,20},{20,16},{24,28},{28,24},{32,36},... | collective-permute-start | bytes 1572872 | tf_op jit(solution)/shard_map/ppermute | solution.py:284
  78.9 11.2 %collective-permute-start.24 = (f16[1200,128]{1,0:T(8,128)(2,1)S(1)}, f16[1200,128]{1,0:T(8,128)(2,1)S(1)}, u32[]{:S(2)}, u32[]{:S(2)}) collective-permute-start(f16[1200,128]{1,0:T(8,128)(2,1)S(1)} %convert_element_type.288), channel_id=1, source_target_pairs={{0,2},{1,3},{2,0},{3,1},{4,6},{5,7},{6,4},{7,5},{8,10},{9,11},{10,... | collective-permute-start | bytes 921608 | tf_op jit(solution)/shard_map/ppermute | solution.py:290
  84.3 14.3 %collective-permute-start.23 = (f16[1200,128]{1,0:T(8,128)(2,1)S(1)}, f16[1200,128]{1,0:T(8,128)(2,1)S(1)}, u32[]{:S(2)}, u32[]{:S(2)}) collective-permute-start(f16[1200,128]{1,0:T(8,128)(2,1)S(1)} %convert_element_type.286), channel_id=1, source_target_pairs={{0,3},{1,2},{2,1},{3,0},{4,7},{5,6},{6,5},{7,4},{8,11},{9,10},{10,... | collective-permute-start | bytes 921608 | tf_op jit(solution)/shard_map/ppermute | solution.py:290
  84.8 12.3 %collective-permute-start.22 = (f16[1200,128]{1,0:T(8,128)(2,1)S(1)}, f16[1200,128]{1,0:T(8,128)(2,1)S(1)}, u32[]{:S(2)}, u32[]{:S(2)}) collective-permute-start(f16[1200,128]{1,0:T(8,128)(2,1)S(1)} %convert_element_type.284), channel_id=1, source_target_pairs={{0,1},{1,0},{2,3},{3,2},{4,5},{5,4},{6,7},{7,6},{8,9},{9,8},{10,11... | collective-permute-start | bytes 921608 | tf_op jit(solution)/shard_map/ppermute | solution.py:290
  103.5 9.0 %collective-permute-start.27 = (f16[1168,128]{1,0:T(8,128)(2,1)S(1)}, f16[1168,128]{1,0:T(8,128)(2,1)S(1)}, u32[]{:S(2)}, u32[]{:S(2)}) collective-permute-start(f16[1168,128]{1,0:T(8,128)(2,1)S(1)} %get-tuple-element.9), channel_id=1, source_target_pairs={{0,2},{1,3},{2,0},{3,1},{4,6},{5,7},{6,4},{7,5},{8,10},{9,11},{10,... | collective-permute-start | bytes 897032 | tf_op jit(solution)/shard_map/ppermute | solution.py:290
  105.0 15.5 %collective-permute-start.26 = (f16[1168,128]{1,0:T(8,128)(2,1)S(1)}, f16[1168,128]{1,0:T(8,128)(2,1)S(1)}, u32[]{:S(2)}, u32[]{:S(2)}) collective-permute-start(f16[1168,128]{1,0:T(8,128)(2,1)S(1)} %get-tuple-element.10), channel_id=1, source_target_pairs={{0,3},{1,2},{2,1},{3,0},{4,7},{5,6},{6,5},{7,4},{8,11},{9,10},{10,... | collective-permute-start | bytes 897032 | tf_op jit(solution)/shard_map/ppermute | solution.py:290
  106.7 13.8 %collective-permute-start.25 = (f16[1168,128]{1,0:T(8,128)(2,1)S(1)}, f16[1168,128]{1,0:T(8,128)(2,1)S(1)}, u32[]{:S(2)}, u32[]{:S(2)}) collective-permute-start(f16[1168,128]{1,0:T(8,128)(2,1)S(1)} %get-tuple-element.11), channel_id=1, source_target_pairs={{0,1},{1,0},{2,3},{3,2},{4,5},{5,4},{6,7},{7,6},{8,9},{9,8},{10,11... | collective-permute-start | bytes 897032 | tf_op jit(solution)/shard_map/ppermute | solution.py:290
  125.2 5.7 %collective-permute-start.29 = (bf16[128,512]{1,0:T(8,128)(2,1)S(1)}, bf16[128,512]{1,0:T(8,128)(2,1)S(1)}, u32[]{:S(2)}, u32[]{:S(2)}) collective-permute-start(bf16[128,512]{1,0:T(8,128)(2,1)S(1)} %get-tuple-element.15), channel_id=1, source_target_pairs={{0,16},{4,68},{8,24},{12,76},{16,0},{20,84},{24,8},{28,92},{32,48}... | collective-permute-start | bytes 393224 | tf_op jit(solution)/shard_map/ppermute | solution.py:271
  127.1 5.3 %collective-permute-start.31 = (bf16[128,512]{1,0:T(8,128)(2,1)S(1)}, bf16[128,512]{1,0:T(8,128)(2,1)S(1)}, u32[]{:S(2)}, u32[]{:S(2)}) collective-permute-start(bf16[128,512]{1,0:T(8,128)(2,1)S(1)} %get-tuple-element.16), channel_id=1, source_target_pairs={{0,24},{4,100},{8,16},{12,108},{16,8},{20,116},{24,0},{28,124},{32... | collective-permute-start | bytes 393224 | tf_op jit(solution)/shard_map/ppermute | solution.py:271
  132.5 5.4 %collective-permute-start.34 = (bf16[128,512]{1,0:T(8,128)(2,1)S(1)}, bf16[128,512]{1,0:T(8,128)(2,1)S(1)}, u32[]{:S(2)}, u32[]{:S(2)}) collective-permute-start(bf16[128,512]{1,0:T(8,128)(2,1)S(1)} %add_convert_fusion.3), channel_id=1, source_target_pairs={{0,64},{4,20},{8,72},{12,28},{16,80},{20,4},{24,88},{28,12},{32,96... | collective-permute-start | bytes 393224 | tf_op jit(solution)/shard_map/ppermute | solution.py:275
  134.0 5.6 %collective-permute-start.33 = (bf16[128,512]{1,0:T(8,128)(2,1)S(1)}, bf16[128,512]{1,0:T(8,128)(2,1)S(1)}, u32[]{:S(2)}, u32[]{:S(2)}) collective-permute-start(bf16[128,512]{1,0:T(8,128)(2,1)S(1)} %add_convert_fusion.3), channel_id=1, source_target_pairs={{0,96},{4,28},{8,104},{12,20},{16,112},{20,12},{24,120},{28,4},{32... | collective-permute-start | bytes 393224 | tf_op jit(solution)/shard_map/ppermute | solution.py:275
  135.0 4.6 %collective-permute-start.32 = (bf16[128,512]{1,0:T(8,128)(2,1)S(1)}, bf16[128,512]{1,0:T(8,128)(2,1)S(1)}, u32[]{:S(2)}, u32[]{:S(2)}) collective-permute-start(bf16[128,512]{1,0:T(8,128)(2,1)S(1)} %add_convert_fusion.3), channel_id=1, source_target_pairs={{0,32},{4,12},{8,40},{12,4},{16,48},{20,28},{24,56},{28,20},{32,0}... | collective-permute-start | bytes 393224 | tf_op jit(solution)/shard_map/ppermute | solution.py:275
  139.6 5.4 %collective-permute-start.37 = (bf16[128,512]{1,0:T(8,128)(2,1)S(1)}, bf16[128,512]{1,0:T(8,128)(2,1)S(1)}, u32[]{:S(2)}, u32[]{:S(2)}) collective-permute-start(bf16[128,512]{1,0:T(8,128)(2,1)S(1)} %add_convert_fusion.2.piece0), channel_id=1, source_target_pairs={{0,16},{4,68},{8,24},{12,76},{16,0},{20,84},{24,8},{28,92},{32,48}... | collective-permute-start | bytes 393224 | tf_op jit(solution)/shard_map/ppermute | solution.py:279
  141.0 5.4 %collective-permute-start.36 = (bf16[128,512]{1,0:T(8,128)(2,1)S(1)}, bf16[128,512]{1,0:T(8,128)(2,1)S(1)}, u32[]{:S(2)}, u32[]{:S(2)}) collective-permute-start(bf16[128,512]{1,0:T(8,128)(2,1)S(1)} %add_convert_fusion.2.piece0), channel_id=1, source_target_pairs={{0,24},{4,100},{8,16},{12,108},{16,8},{20,116},{24,0},{28,124},{32... | collective-permute-start | bytes 393224 | tf_op jit(solution)/shard_map/ppermute | solution.py:279
  146.5 5.5 %collective-permute-start.38 = (bf16[512,512]{1,0:T(8,128)(2,1)S(1)}, bf16[512,512]{1,0:T(8,128)(2,1)S(1)}, u32[]{:S(2)}, u32[]{:S(2)}) collective-permute-start(bf16[512,512]{1,0:T(8,128)(2,1)S(1)} %join.6.mine_ref), channel_id=1, source_target_pairs={{0,4},{4,0},{8,12},{12,8},{16,20},{20,16},{24,28},{28,24},{32,36},... | collective-permute-start | bytes 1572872 | tf_op jit(solution)/shard_map/ppermute | solution.py:284
  157.8 5.9 %collective-permute-start.40 = (bf16[128,512]{1,0:T(8,128)(2,1)S(1)}, bf16[128,512]{1,0:T(8,128)(2,1)S(1)}, u32[]{:S(2)}, u32[]{:S(2)}) collective-permute-start(bf16[128,512]{1,0:T(8,128)(2,1)S(1)} %get-tuple-element.12), channel_id=1, source_target_pairs={{0,16},{4,68},{8,24},{12,76},{16,0},{20,84},{24,8},{28,92},{32,48}... | collective-permute-start | bytes 393224 | tf_op jit(solution)/shard_map/ppermute | solution.py:271
  159.5 5.6 %collective-permute-start.42 = (bf16[128,512]{1,0:T(8,128)(2,1)S(1)}, bf16[128,512]{1,0:T(8,128)(2,1)S(1)}, u32[]{:S(2)}, u32[]{:S(2)}) collective-permute-start(bf16[128,512]{1,0:T(8,128)(2,1)S(1)} %get-tuple-element.13), channel_id=1, source_target_pairs={{0,24},{4,100},{8,16},{12,108},{16,8},{20,116},{24,0},{28,124},{32... | collective-permute-start | bytes 393224 | tf_op jit(solution)/shard_map/ppermute | solution.py:271
  160.5 4.6 %collective-permute-start.41 = (bf16[128,512]{1,0:T(8,128)(2,1)S(1)}, bf16[128,512]{1,0:T(8,128)(2,1)S(1)}, u32[]{:S(2)}, u32[]{:S(2)}) collective-permute-start(bf16[128,512]{1,0:T(8,128)(2,1)S(1)} %get-tuple-element.14), channel_id=1, source_target_pairs={{0,8},{4,36},{8,0},{12,44},{16,24},{20,52},{24,16},{28,60},{32,40}... | collective-permute-start | bytes 393224 | tf_op jit(solution)/shard_map/ppermute | solution.py:271
  165.2 5.4 %collective-permute-start.45 = (bf16[128,512]{1,0:T(8,128)(2,1)S(1)}, bf16[128,512]{1,0:T(8,128)(2,1)S(1)}, u32[]{:S(2)}, u32[]{:S(2)}) collective-permute-start(bf16[128,512]{1,0:T(8,128)(2,1)S(1)} %add_convert_fusion.1), channel_id=1, source_target_pairs={{0,64},{4,20},{8,72},{12,28},{16,80},{20,4},{24,88},{28,12},{32,96... | collective-permute-start | bytes 393224 | tf_op jit(solution)/shard_map/ppermute | solution.py:275
  166.7 5.6 %collective-permute-start.44 = (bf16[128,512]{1,0:T(8,128)(2,1)S(1)}, bf16[128,512]{1,0:T(8,128)(2,1)S(1)}, u32[]{:S(2)}, u32[]{:S(2)}) collective-permute-start(bf16[128,512]{1,0:T(8,128)(2,1)S(1)} %add_convert_fusion.1), channel_id=1, source_target_pairs={{0,96},{4,28},{8,104},{12,20},{16,112},{20,12},{24,120},{28,4},{32... | collective-permute-start | bytes 393224 | tf_op jit(solution)/shard_map/ppermute | solution.py:275
  167.7 4.6 %collective-permute-start.43 = (bf16[128,512]{1,0:T(8,128)(2,1)S(1)}, bf16[128,512]{1,0:T(8,128)(2,1)S(1)}, u32[]{:S(2)}, u32[]{:S(2)}) collective-permute-start(bf16[128,512]{1,0:T(8,128)(2,1)S(1)} %add_convert_fusion.1), channel_id=1, source_target_pairs={{0,32},{4,12},{8,40},{12,4},{16,48},{20,28},{24,56},{28,20},{32,0}... | collective-permute-start | bytes 393224 | tf_op jit(solution)/shard_map/ppermute | solution.py:275
  172.4 5.4 %collective-permute-start.48 = (bf16[128,512]{1,0:T(8,128)(2,1)S(1)}, bf16[128,512]{1,0:T(8,128)(2,1)S(1)}, u32[]{:S(2)}, u32[]{:S(2)}) collective-permute-start(bf16[128,512]{1,0:T(8,128)(2,1)S(1)} %add_convert_fusion.piece0), channel_id=1, source_target_pairs={{0,16},{4,68},{8,24},{12,76},{16,0},{20,84},{24,8},{28,92},{32,48}... | collective-permute-start | bytes 393224 | tf_op jit(solution)/shard_map/ppermute | solution.py:279
  173.8 5.4 %collective-permute-start.47 = (bf16[128,512]{1,0:T(8,128)(2,1)S(1)}, bf16[128,512]{1,0:T(8,128)(2,1)S(1)}, u32[]{:S(2)}, u32[]{:S(2)}) collective-permute-start(bf16[128,512]{1,0:T(8,128)(2,1)S(1)} %add_convert_fusion.piece0), channel_id=1, source_target_pairs={{0,24},{4,100},{8,16},{12,108},{16,8},{20,116},{24,0},{28,124},{32... | collective-permute-start | bytes 393224 | tf_op jit(solution)/shard_map/ppermute | solution.py:279
  174.7 4.5 %collective-permute-start.46 = (bf16[128,512]{1,0:T(8,128)(2,1)S(1)}, bf16[128,512]{1,0:T(8,128)(2,1)S(1)}, u32[]{:S(2)}, u32[]{:S(2)}) collective-permute-start(bf16[128,512]{1,0:T(8,128)(2,1)S(1)} %add_convert_fusion.piece0), channel_id=1, source_target_pairs={{0,8},{4,36},{8,0},{12,44},{16,24},{20,52},{24,16},{28,60},{32,40}... | collective-permute-start | bytes 393224 | tf_op jit(solution)/shard_map/ppermute | solution.py:279
  179.2 5.2 %collective-permute-start.49 = (bf16[512,512]{1,0:T(8,128)(2,1)S(1)}, bf16[512,512]{1,0:T(8,128)(2,1)S(1)}, u32[]{:S(2)}, u32[]{:S(2)}) collective-permute-start(bf16[512,512]{1,0:T(8,128)(2,1)S(1)} %join.7.mine_ref), channel_id=1, source_target_pairs={{0,4},{4,0},{8,12},{12,8},{16,20},{20,16},{24,28},{28,24},{32,36},... | collective-permute-start | bytes 1572872 | tf_op jit(solution)/shard_map/ppermute | solution.py:284
  185.2 9.9 %collective-permute-start.52 = (f16[1168,128]{1,0:T(8,128)(2,1)S(1)}, f16[1168,128]{1,0:T(8,128)(2,1)S(1)}, u32[]{:S(2)}, u32[]{:S(2)}) collective-permute-start(f16[1168,128]{1,0:T(8,128)(2,1)S(1)} %convert_element_type.328), channel_id=1, source_target_pairs={{0,2},{1,3},{2,0},{3,1},{4,6},{5,7},{6,4},{7,5},{8,10},{9,11},{10,... | collective-permute-start | bytes 897032 | tf_op jit(solution)/shard_map/ppermute | solution.py:290
  187.5 14.8 %collective-permute-start.51 = (f16[1168,128]{1,0:T(8,128)(2,1)S(1)}, f16[1168,128]{1,0:T(8,128)(2,1)S(1)}, u32[]{:S(2)}, u32[]{:S(2)}) collective-permute-start(f16[1168,128]{1,0:T(8,128)(2,1)S(1)} %convert_element_type.326), channel_id=1, source_target_pairs={{0,3},{1,2},{2,1},{3,0},{4,7},{5,6},{6,5},{7,4},{8,11},{9,10},{10,... | collective-permute-start | bytes 897032 | tf_op jit(solution)/shard_map/ppermute | solution.py:290
  189.9 12.4 %collective-permute-start.50 = (f16[1168,128]{1,0:T(8,128)(2,1)S(1)}, f16[1168,128]{1,0:T(8,128)(2,1)S(1)}, u32[]{:S(2)}, u32[]{:S(2)}) collective-permute-start(f16[1168,128]{1,0:T(8,128)(2,1)S(1)} %convert_element_type.324), channel_id=1, source_target_pairs={{0,1},{1,0},{2,3},{3,2},{4,5},{5,4},{6,7},{7,6},{8,9},{9,8},{10,11... | collective-permute-start | bytes 897032 | tf_op jit(solution)/shard_map/ppermute | solution.py:290
  205.7 9.8 %collective-permute-start.55 = (f16[1168,128]{1,0:T(8,128)(2,1)S(1)}, f16[1168,128]{1,0:T(8,128)(2,1)S(1)}, u32[]{:S(2)}, u32[]{:S(2)}) collective-permute-start(f16[1168,128]{1,0:T(8,128)(2,1)S(1)} %get-tuple-element.6), channel_id=1, source_target_pairs={{0,2},{1,3},{2,0},{3,1},{4,6},{5,7},{6,4},{7,5},{8,10},{9,11},{10,... | collective-permute-start | bytes 897032 | tf_op jit(solution)/shard_map/ppermute | solution.py:290
  207.2 15.6 %collective-permute-start.54 = (f16[1168,128]{1,0:T(8,128)(2,1)S(1)}, f16[1168,128]{1,0:T(8,128)(2,1)S(1)}, u32[]{:S(2)}, u32[]{:S(2)}) collective-permute-start(f16[1168,128]{1,0:T(8,128)(2,1)S(1)} %get-tuple-element.7), channel_id=1, source_target_pairs={{0,3},{1,2},{2,1},{3,0},{4,7},{5,6},{6,5},{7,4},{8,11},{9,10},{10,... | collective-permute-start | bytes 897032 | tf_op jit(solution)/shard_map/ppermute | solution.py:290
  208.7 14.0 %collective-permute-start.53 = (f16[1168,128]{1,0:T(8,128)(2,1)S(1)}, f16[1168,128]{1,0:T(8,128)(2,1)S(1)}, u32[]{:S(2)}, u32[]{:S(2)}) collective-permute-start(f16[1168,128]{1,0:T(8,128)(2,1)S(1)} %get-tuple-element.8), channel_id=1, source_target_pairs={{0,1},{1,0},{2,3},{3,2},{4,5},{5,4},{6,7},{7,6},{8,9},{9,8},{10,11... | collective-permute-start | bytes 897032 | tf_op jit(solution)/shard_map/ppermute | solution.py:290
  (17 other events, 158.7 us)
